TPU v7x, 32 devices: a whole 2x2x4 slice. The times are simulated.
32 devices in a mesh: dp: 4 (over x, core), mp: 8 (over z, y).
Axes of the slice: x: 2, y: 2, z: 4, core: 2. Of those that a mesh axis runs over, the one named last changes fastest.
Arguments:
- patches: bfloat16 [7680, 2048], P('dp'), may hold values from -6 to 6
- query_proj: bfloat16 [2048, 1024], P(None, 'mp'), may hold values from -0.3125 to 0.3125
- output_proj: bfloat16 [1024, 2048], P('mp'), may hold values from -0.1875 to 0.1875
- encoder_cache: bfloat16 [512, 128, 16, 128], P(('dp', 'mp')), may hold values from -28 to 28
- block_lengths: int32 [512], P(('dp', 'mp')), may hold values from 16 to 128
- neighbours: int32 [16, 32], replicated, may hold values from 0 to 511, as said below
- cotangent: bfloat16 [7680, 2048], P('dp'), may hold values from -6 to 6
Outputs:
- attended: bfloat16 [7680, 2048], P('dp', 'mp')
- patch_grad: bfloat16 [7680, 2048], P('dp', 'mp')
- query_grad: float32 [2048, 1024], P('dp', 'mp')
- output_grad: float32 [1024, 2048], P('mp', 'dp')
Inputs may be any that keep to these rules, and one draw needn't show every extreme that they name: `neighbours`: each row names 32 different blocks. Device k (in dp+mp order) holds blocks k * 16 to k * 16 + 15; the 4 rows of one index of dp name the blocks of any one device at most 8 times in all, and some device's blocks exactly 8 times.
All inputs are finite; a program needn't handle non-finite values.
Results may differ from a plain program's by a relative error of at most 0.02.
The roundings to bfloat16 on the way count: a program that leaves them out, or rounds other values in their place, can miss the bound.
Values may be sent and summed in bfloat16 or wider, within the bound.
No kernel may reach another device: no remote copies, remote signals or barrier semaphores. Data moves between devices by JAX's collectives and lax.ppermute only.
A program may use at most 128 MiB of HBM per device.

v0:
```python
import math

import jax
import jax.numpy as jnp
from jax import lax
from jax.sharding import PartitionSpec as P

masked_value = -1e30


def rounded(array):
    return lax.optimization_barrier(array.astype(jnp.bfloat16))


def local(patches, query_proj, output_proj, encoder_cache, block_lengths, neighbours, cotangent):
    group_count = lax.axis_size("dp")
    model_count = lax.axis_size("mp")
    owner_count = group_count * model_count
    group_index = lax.axis_index("dp")
    model_index = lax.axis_index("mp")
    my_owner = group_index * model_count + model_index
    local_blocks = encoder_cache.shape[0]
    block_rows = encoder_cache.shape[1]
    head_size = encoder_cache.shape[3] // 2
    local_heads = query_proj.shape[1] // head_size
    neighbour_count = neighbours.shape[1]
    patch_blocks = neighbours.shape[0] // group_count
    entry_count = patch_blocks * neighbour_count
    capacity = 2 * entry_count // owner_count
    row_count = patches.shape[0]
    patch_rows = row_count // patch_blocks
    head_scale = 1.0 / math.sqrt(head_size)
    grad_scale = 1.0 / math.sqrt(row_count * group_count)
    all_ids = neighbours.reshape(group_count, entry_count)
    match_int = (all_ids // local_blocks == my_owner).astype(jnp.int32)
    before = jnp.cumsum(match_int, axis=1) - match_int
    slot_range = jnp.arange(capacity, dtype=jnp.int32)
    placed = match_int[:, :, None] * (before[:, :, None] == slot_range[None, None, :]).astype(
        jnp.int32
    )
    chosen = jnp.sum(placed * (all_ids % local_blocks)[:, :, None], axis=1)
    send_lengths = block_lengths[chosen]
    head_groups = encoder_cache.reshape(
        local_blocks, block_rows, model_count, local_heads, 2 * head_size
    )
    member_range = jnp.arange(model_count, dtype=jnp.int32)
    outgoing = head_groups[chosen[:, None, :], :, member_range[None, :, None]]
    outgoing_len = jnp.broadcast_to(
        send_lengths[:, None, :], (group_count, model_count, capacity)
    ).astype(jnp.bfloat16)
    flat_out = outgoing.reshape(owner_count, capacity, block_rows, local_heads, 2 * head_size)
    flat_len = outgoing_len.reshape(owner_count, capacity)
    received, received_len = (
        lax.all_to_all(flat_out, ("dp", "mp"), split_axis=0, concat_axis=0, tiled=True),
        lax.all_to_all(flat_len, ("dp", "mp"), split_axis=0, concat_axis=0, tiled=True),
    )
    received = received.reshape(owner_count * capacity, block_rows, local_heads, 2 * head_size)
    received_len = received_len.reshape(owner_count * capacity)
    my_ids = lax.dynamic_slice_in_dim(
        neighbours, group_index * patch_blocks, patch_blocks, 0
    ).reshape(entry_count)
    owners = my_ids // local_blocks
    owner_hot = (owners[:, None] == jnp.arange(owner_count, dtype=jnp.int32)[None, :]).astype(
        jnp.int32
    )
    earlier = jnp.cumsum(owner_hot, axis=0) - owner_hot
    slot_of = jnp.sum(earlier * owner_hot, axis=1)
    rows_at = owners * capacity + slot_of
    fetched = received[rows_at].reshape(
        patch_blocks, neighbour_count, block_rows, local_heads, 2 * head_size
    )
    lengths = received_len[rows_at].astype(jnp.float32).reshape(patch_blocks, neighbour_count)
    queries = rounded(jnp.dot(patches, query_proj, preferred_element_type=jnp.float32) * head_scale)
    back_heads = rounded(jnp.dot(cotangent, output_proj.T, preferred_element_type=jnp.float32))
    queries = queries.reshape(patch_blocks, patch_rows, local_heads, head_size)
    back_heads = back_heads.reshape(patch_blocks, patch_rows, local_heads, head_size)

    def one_block(inputs):
        query_blk, back_blk, cache_blk, length_blk = inputs
        key_rows = cache_blk[..., :head_size]
        value_rows = cache_blk[..., head_size:]
        visible = jnp.arange(block_rows, dtype=jnp.float32)[None, :] < length_blk[:, None]
        scores = jnp.einsum(
            "rhd,sbhd->hrsb", query_blk, key_rows, preferred_element_type=jnp.float32
        )
        scores = jnp.where(visible[None, None], scores, masked_value)
        row_max = jnp.max(scores, axis=(2, 3), keepdims=True)
        weights = jnp.exp(scores - row_max)
        att_weights = weights / jnp.sum(weights, axis=(2, 3), keepdims=True)
        probs_low = rounded(att_weights)
        heads_blk = rounded(
            jnp.einsum("hrsb,sbhd->rhd", probs_low, value_rows, preferred_element_type=jnp.float32)
        )
        dprobs = jnp.einsum(
            "rhd,sbhd->hrsb", back_blk, value_rows, preferred_element_type=jnp.float32
        )
        row_inner = jnp.sum(att_weights * dprobs, axis=(2, 3), keepdims=True)
        dscores = rounded(att_weights * (dprobs - row_inner) * head_scale)
        dquery = rounded(
            jnp.einsum("hrsb,sbhd->rhd", dscores, key_rows, preferred_element_type=jnp.float32)
        )
        return (heads_blk, dquery)

    heads_all, dquery_all = lax.map(one_block, (queries, back_heads, fetched, lengths))
    heads_out = heads_all.reshape(row_count, local_heads * head_size)
    dquery_rows = dquery_all.reshape(row_count, local_heads * head_size)
    output_term = jnp.dot(heads_out, output_proj, preferred_element_type=jnp.float32)
    attended = lax.psum_scatter(output_term, "mp", scatter_dimension=1, tiled=True).astype(
        jnp.bfloat16
    )
    patch_term = jnp.dot(dquery_rows, query_proj.T, preferred_element_type=jnp.float32)
    patch_grad = lax.psum_scatter(patch_term, "mp", scatter_dimension=1, tiled=True).astype(
        jnp.bfloat16
    )
    query_term = jnp.dot(patches.T, dquery_rows, preferred_element_type=jnp.float32) * grad_scale
    output_wterm = jnp.dot(heads_out.T, cotangent, preferred_element_type=jnp.float32) * grad_scale
    query_grad, output_grad = (
        lax.psum_scatter(
            query_term.astype(jnp.bfloat16), "dp", scatter_dimension=0, tiled=True
        ).astype(jnp.float32),
        lax.psum_scatter(
            output_wterm.astype(jnp.bfloat16), "dp", scatter_dimension=1, tiled=True
        ).astype(jnp.float32),
    )
    return (attended, patch_grad, query_grad, output_grad)


def solution(mesh):
    return jax.shard_map(
        local,
        mesh=mesh,
        in_specs=(
            P("dp", None),
            P(None, "mp"),
            P("mp", None),
            P(("dp", "mp"), None, None, None),
            P(("dp", "mp")),
            P(),
            P("dp", None),
        ),
        out_specs=(P("dp", "mp"), P("dp", "mp"), P("dp", "mp"), P("mp", "dp")),
        check_vma=False,
    )
```

profile of v0, /device:TPU:0, one launch (start us, length us, event | category | flops | bytes accessed | tf_op | source)
XLA Modules:
  0.0 1281.2 jit_solution(9258895830291779024)
XLA Ops:
  11.1 7.3 all-to-all-start.1
  18.5 52.7 %gather_fusion = bf16[256,128,2,128]{3,2,1,0:T(2,128)(2,1)} fusion(bf16[16,128,8,2,128]{4,3,2,1,0:T(2,128)(2,1)} %bitcast.111, s32[256]{0:T(256)S(1)} %reshape.308), kind=kCustom, calls=%fused_computation | custom fusion | bytes 33556480 | tf_op jit(solution)/shard_map/gather | solution.py:47
  71.2 15.2 %copy.51 = bf16[256,128,2,128]{3,1,2,0:T(8,128)(2,1)} copy(bf16[256,128,2,128]{3,2,1,0:T(2,128)(2,1)} %gather_fusion) | data formatting | bytes 33554432 | tf_op jit(solution)/shard_map/gather | solution.py:47
  86.3 6.0 all-to-all-start
  109.6 357.7 %all-to-all-done = bf16[32,8,128,2,128]{4,2,3,1,0:T(8,128)(2,1)} async-done(((bf16[32,8,128,2,128]{4,2,3,1,0:T(8,128)(2,1)}), bf16[32,8,128,2,128]{4,2,3,1,0:T(8,128)(2,1)}, u32[]{:S(2)}, u32[]{:S(2)}) %all-to-all-start) | async-done | bytes 16777248 | tf_op jit(solution)/shard_map/all_to_all | solution.py:54
  467.3 12.4 gather_fusion.1
  479.7 232.8 %while.12 = (s32[]{:T(128)}, bf16[4,480,2,64]{1,3,2,0:T(8,128)(2,1)}, bf16[4,480,2,64]{1,3,2,0:T(8,128)(2,1)}, bf16[4,32,128,2,128]{4,2,3,1,0:T(8,128)(2,1)}, f3...) while((s32[]{:T(128)}, ...), condition=%wide.region_8.9_spmd, body=%wide.region_4.8_spmd.sunk | while | flops 2084168960 | bytes 186670928 | solution.py:104
  486.1 7.8 select_reduce_fusion.3
  493.9 8.4 fusion.61
  502.4 13.5 %multiply_reduce_fusion.3 = (f32[2,480]{1,0:T(2,128)S(1)}, f32[2,480,32,128]{3,1,2,0:T(8,128)}) fusion(f32[2,480]{1,0:T(2,128)S(1)} %fusion.61, f32[2,480]{1,0:T(2,128)S(1)} %get-tuple-element.184, f32[2,480,32,128]{3,1,2,0:T(8,128)} %get-tuple-element.183, pred[32,128]{1,0:T(8,128)(4,1)S(1)} %iota_compare_fusion.4, ...), kind=kOutput, calls=%fused_computation.5.clone.1 | convolution fusion | flops 522976320 | bytes 32653568 | tf_op jit(solution)/shard_map/while/body/eval_jaxpr/rhd,sbhd->hrsb/dot_general | solution.py:94
  517.9 11.4 multiply_convert_fusion.2
  529.3 5.6 fusion.63
  544.3 7.8 select_reduce_fusion.3
  552.1 8.4 fusion.61
  560.6 13.5 %multiply_reduce_fusion.3 = (f32[2,480]{1,0:T(2,128)S(1)}, f32[2,480,32,128]{3,1,2,0:T(8,128)}) fusion(f32[2,480]{1,0:T(2,128)S(1)} %fusion.61, f32[2,480]{1,0:T(2,128)S(1)} %get-tuple-element.184, f32[2,480,32,128]{3,1,2,0:T(8,128)} %get-tuple-element.183, pred[32,128]{1,0:T(8,128)(4,1)S(1)} %iota_compare_fusion.4, ...), kind=kOutput, calls=%fused_computation.5.clone.1 | convolution fusion | flops 522976320 | bytes 32653568 | tf_op jit(solution)/shard_map/while/body/eval_jaxpr/rhd,sbhd->hrsb/dot_general | solution.py:94
  576.1 11.4 multiply_convert_fusion.2
  587.5 5.6 fusion.63
  602.5 7.8 select_reduce_fusion.3
  610.3 8.4 fusion.61
  618.8 13.5 %multiply_reduce_fusion.3 = (f32[2,480]{1,0:T(2,128)S(1)}, f32[2,480,32,128]{3,1,2,0:T(8,128)}) fusion(f32[2,480]{1,0:T(2,128)S(1)} %fusion.61, f32[2,480]{1,0:T(2,128)S(1)} %get-tuple-element.184, f32[2,480,32,128]{3,1,2,0:T(8,128)} %get-tuple-element.183, pred[32,128]{1,0:T(8,128)(4,1)S(1)} %iota_compare_fusion.4, ...), kind=kOutput, calls=%fused_computation.5.clone.1 | convolution fusion | flops 522976320 | bytes 32653568 | tf_op jit(solution)/shard_map/while/body/eval_jaxpr/rhd,sbhd->hrsb/dot_general | solution.py:94
  634.3 11.4 multiply_convert_fusion.2
  645.7 5.6 fusion.63
  660.7 7.8 select_reduce_fusion.3
  668.5 8.4 fusion.61
  677.0 13.5 %multiply_reduce_fusion.3 = (f32[2,480]{1,0:T(2,128)S(1)}, f32[2,480,32,128]{3,1,2,0:T(8,128)}) fusion(f32[2,480]{1,0:T(2,128)S(1)} %fusion.61, f32[2,480]{1,0:T(2,128)S(1)} %get-tuple-element.184, f32[2,480,32,128]{3,1,2,0:T(8,128)} %get-tuple-element.183, pred[32,128]{1,0:T(8,128)(4,1)S(1)} %iota_compare_fusion.4, ...), kind=kOutput, calls=%fused_computation.5.clone.1 | convolution fusion | flops 522976320 | bytes 32653568 | tf_op jit(solution)/shard_map/while/body/eval_jaxpr/rhd,sbhd->hrsb/dot_general | solution.py:94
  692.5 11.4 multiply_convert_fusion.2
  703.9 5.6 fusion.63
  726.5 7.7 fusion.31
  735.3 7.8 fusion.32
  744.7 18.1 %reduce-scatter.9.cloned.1.call-done = bf16[512,128]{0,1:T(8,128)(2,1)} async-done(((bf16[2048,128]{0,1:T(8,128)(2,1)}), bf16[512,128]{0,1:T(8,128)(2,1)}) %reduce-scatter.9.cloned.1.call-update) | async-done | bytes 131088 | tf_op jit(solution)/shard_map/reduce_scatter | solution.py:118
  764.5 253.4 %reduce-scatter.5.cloned.1.call-done = f32[1920,256]{1,0:T(8,128)} async-done(((f32[1920,2048]{1,0:T(8,128)}), f32[1920,256]{1,0:T(8,128)}) %reduce-scatter.5.cloned.1.call-update) | async-done | bytes 1966096 | tf_op jit(solution)/shard_map/reduce_scatter | solution.py:108
  1020.5 251.6 %reduce-scatter.7.cloned.1.call-done = f32[1920,256]{1,0:T(8,128)} async-done(((f32[1920,2048]{1,0:T(8,128)}), f32[1920,256]{1,0:T(8,128)}) %reduce-scatter.7.cloned.1.call-update) | async-done | bytes 1966096 | tf_op jit(solution)/shard_map/reduce_scatter | solution.py:112
  (128 shorter events, 90.7 us)
Async XLA Ops:
  7.2 93.1 %copy-start = (bf16[128,2048]{1,0:T(8,128)(2,1)S(1)}, bf16[128,2048]{1,0:T(8,128)(2,1)}, u32[]{:S(2)}) copy-start(bf16[128,2048]{1,0:T(8,128)(2,1)} %param.11) | copy-start | bytes 1572868
  11.1 75.3 %all-to-all-start.1 = ((bf16[32,1,8]{2,1,0:T(2,128)(2,1)}), bf16[32,1,8]{2,1,0:T(2,128)(2,1)S(1)}, u32[]{:S(2)}, u32[]{:S(2)}) async-start(bf16[32,1,8]{2,1,0:T(2,128)(2,1)} %copy.53), calls=%async_computation.1 | async-start | bytes 32768 | tf_op jit(solution)/shard_map/all_to_all | solution.py:55
  86.3 7.4 copy-start.1
  86.3 381.0 %all-to-all-start = ((bf16[32,8,128,2,128]{4,2,3,1,0:T(8,128)(2,1)}), bf16[32,8,128,2,128]{4,2,3,1,0:T(8,128)(2,1)}, u32[]{:S(2)}, u32[]{:S(2)}) async-start(bf16[32,8,128,2,128]{4,2,3,1,0:T(8,128)(2,1)} %bitcast.109), calls=%async_computation | async-start | bytes 33554432 | tf_op jit(solution)/shard_map/all_to_all | solution.py:54
  92.3 650.8 %reduce-scatter.11.cloned.1.call-start = ((), (), s32[]{:S(2)}) async-start(), calls=%async_computation.9 | async-start | bytes 655360 | tf_op jit(solution)/shard_map/reduce_scatter | solution.py:121
  502.3 13.5 %slice-start = ((s8[15728640]{0:T(1024)(128)(4,1)}), s8[4194304]{0:T(1024)(128)(4,1)S(1)}, s32[]{:S(2)}) async-start(s8[15728640]{0:T(1024)(128)(4,1)} %bitcast.103), calls=%async_computation.10 | async-start | bytes 8388608 | tf_op jit(solution)/shard_map/while
  502.4 13.5 %slice-start.1 = ((s8[15728640]{0:T(1024)(128)(4,1)}), s8[4194304]{0:T(1024)(128)(4,1)S(1)}, s32[]{:S(2)}) async-start(s8[15728640]{0:T(1024)(128)(4,1)} %bitcast.103), calls=%async_computation.11 | async-start | bytes 8388608 | tf_op jit(solution)/shard_map/while
  502.4 14.6 %slice-start.2 = ((s8[15728640]{0:T(1024)(128)(4,1)}), s8[4194304]{0:T(1024)(128)(4,1)S(1)}, s32[]{:S(2)}) async-start(s8[15728640]{0:T(1024)(128)(4,1)} %bitcast.103), calls=%async_computation.12 | async-start | bytes 8388608 | tf_op jit(solution)/shard_map/while
  502.4 15.5 %slice-start.3 = ((s8[15728640]{0:T(1024)(128)(4,1)}), s8[3145728]{0:T(1024)(128)(4,1)S(1)}, s32[]{:S(2)}) async-start(s8[15728640]{0:T(1024)(128)(4,1)} %bitcast.103), calls=%async_computation.13 | async-start | bytes 6291456 | tf_op jit(solution)/shard_map/while
  560.5 13.5 %slice-start = ((s8[15728640]{0:T(1024)(128)(4,1)}), s8[4194304]{0:T(1024)(128)(4,1)S(1)}, s32[]{:S(2)}) async-start(s8[15728640]{0:T(1024)(128)(4,1)} %bitcast.103), calls=%async_computation.10 | async-start | bytes 8388608 | tf_op jit(solution)/shard_map/while
  560.6 13.5 %slice-start.1 = ((s8[15728640]{0:T(1024)(128)(4,1)}), s8[4194304]{0:T(1024)(128)(4,1)S(1)}, s32[]{:S(2)}) async-start(s8[15728640]{0:T(1024)(128)(4,1)} %bitcast.103), calls=%async_computation.11 | async-start | bytes 8388608 | tf_op jit(solution)/shard_map/while
  560.6 14.6 %slice-start.2 = ((s8[15728640]{0:T(1024)(128)(4,1)}), s8[4194304]{0:T(1024)(128)(4,1)S(1)}, s32[]{:S(2)}) async-start(s8[15728640]{0:T(1024)(128)(4,1)} %bitcast.103), calls=%async_computation.12 | async-start | bytes 8388608 | tf_op jit(solution)/shard_map/while
  560.6 15.5 %slice-start.3 = ((s8[15728640]{0:T(1024)(128)(4,1)}), s8[3145728]{0:T(1024)(128)(4,1)S(1)}, s32[]{:S(2)}) async-start(s8[15728640]{0:T(1024)(128)(4,1)} %bitcast.103), calls=%async_computation.13 | async-start | bytes 6291456 | tf_op jit(solution)/shard_map/while
  618.7 13.5 %slice-start = ((s8[15728640]{0:T(1024)(128)(4,1)}), s8[4194304]{0:T(1024)(128)(4,1)S(1)}, s32[]{:S(2)}) async-start(s8[15728640]{0:T(1024)(128)(4,1)} %bitcast.103), calls=%async_computation.10 | async-start | bytes 8388608 | tf_op jit(solution)/shard_map/while
  618.8 13.5 %slice-start.1 = ((s8[15728640]{0:T(1024)(128)(4,1)}), s8[4194304]{0:T(1024)(128)(4,1)S(1)}, s32[]{:S(2)}) async-start(s8[15728640]{0:T(1024)(128)(4,1)} %bitcast.103), calls=%async_computation.11 | async-start | bytes 8388608 | tf_op jit(solution)/shard_map/while
  618.8 14.6 %slice-start.2 = ((s8[15728640]{0:T(1024)(128)(4,1)}), s8[4194304]{0:T(1024)(128)(4,1)S(1)}, s32[]{:S(2)}) async-start(s8[15728640]{0:T(1024)(128)(4,1)} %bitcast.103), calls=%async_computation.12 | async-start | bytes 8388608 | tf_op jit(solution)/shard_map/while
  618.8 15.5 %slice-start.3 = ((s8[15728640]{0:T(1024)(128)(4,1)}), s8[3145728]{0:T(1024)(128)(4,1)S(1)}, s32[]{:S(2)}) async-start(s8[15728640]{0:T(1024)(128)(4,1)} %bitcast.103), calls=%async_computation.13 | async-start | bytes 6291456 | tf_op jit(solution)/shard_map/while
  676.9 13.5 %slice-start = ((s8[15728640]{0:T(1024)(128)(4,1)}), s8[4194304]{0:T(1024)(128)(4,1)S(1)}, s32[]{:S(2)}) async-start(s8[15728640]{0:T(1024)(128)(4,1)} %bitcast.103), calls=%async_computation.10 | async-start | bytes 8388608 | tf_op jit(solution)/shard_map/while
  677.0 13.5 %slice-start.1 = ((s8[15728640]{0:T(1024)(128)(4,1)}), s8[4194304]{0:T(1024)(128)(4,1)S(1)}, s32[]{:S(2)}) async-start(s8[15728640]{0:T(1024)(128)(4,1)} %bitcast.103), calls=%async_computation.11 | async-start | bytes 8388608 | tf_op jit(solution)/shard_map/while
  677.0 14.6 %slice-start.2 = ((s8[15728640]{0:T(1024)(128)(4,1)}), s8[4194304]{0:T(1024)(128)(4,1)S(1)}, s32[]{:S(2)}) async-start(s8[15728640]{0:T(1024)(128)(4,1)} %bitcast.103), calls=%async_computation.12 | async-start | bytes 8388608 | tf_op jit(solution)/shard_map/while
  677.0 15.5 %slice-start.3 = ((s8[15728640]{0:T(1024)(128)(4,1)}), s8[3145728]{0:T(1024)(128)(4,1)S(1)}, s32[]{:S(2)}) async-start(s8[15728640]{0:T(1024)(128)(4,1)} %bitcast.103), calls=%async_computation.13 | async-start | bytes 6291456 | tf_op jit(solution)/shard_map/while
  714.0 6.0 copy-start.3
  719.9 42.9 %reduce-scatter.9.cloned.1.call-start = ((), (), s32[]{:S(2)}) async-start(), calls=%async_computation.8 | async-start | bytes 655360 | tf_op jit(solution)/shard_map/reduce_scatter | solution.py:118
  726.4 291.5 %reduce-scatter.5.cloned.1.call-start = ((), (), s32[]{:S(2)}) async-start(), calls=%async_computation.6 | async-start | bytes 17694720 | tf_op jit(solution)/shard_map/reduce_scatter | solution.py:108
  734.2 1.0 copy-start.2
  734.2 537.8 %reduce-scatter.7.cloned.1.call-start = ((), (), s32[]{:S(2)}) async-start(), calls=%async_computation.7 | async-start | bytes 17694720 | tf_op jit(solution)/shard_map/reduce_scatter | solution.py:112
Sparse Core Ops, SparseCore 0:
  720.0 17.9 reduce-scatter.10
  741.2 21.6 reduce-scatter.8
  766.4 251.4 reduce-scatter.4
  1021.4 250.6 reduce-scatter.6
where the time goes:
time: 1280 us
  waiting for transfers between devices  881 us (69%)
  matrix products  154 us (12%)
  local copies, waits for them, and re-layouts  131 us (10%)
  other arithmetic  87.3 us (7%)
  between operations  14 us (1%)
  starting transfers between devices  13.6 us (1%)
    all_to_all x1, waiting for transfers between devices, local(): lax.all_to_all(flat_out, ('dp', 'mp'), split_axis=0, concat_axis=0, tiled...  358 us
    reduce_scatter x1, waiting for transfers between devices, local(): lax.psum_scatter(output_term, 'mp', scatter_dimension=1, tiled=True)  253 us
    reduce_scatter x1, waiting for transfers between devices, local(): lax.psum_scatter(patch_term, 'mp', scatter_dimension=1, tiled=True)  252 us
    gather x2, local copies, waits for them, and re-layouts, local(): outgoing = head_groups[chosen[:, None, :], :, member_range[None, :, None]]  67.8 us
    dot_general x4, matrix products, one_block(): jnp.einsum('rhd,sbhd->hrsb', back_blk, value_rows, preferred_element_type...  54 us
    convert_element_type x4, other arithmetic, rounded(): return lax.optimization_barrier(array.astype(jnp.bfloat16))  45.5 us
    reduce_sum x4, other arithmetic, one_block(): att_weights = weights / jnp.sum(weights, axis=(2, 3), keepdims=True)  33.7 us
    dot_general x4, matrix products, one_block(): jnp.einsum('rhd,sbhd->hrsb', query_blk, key_rows, preferred_element_type=...  31.1 us
  transfers between devices with their start and end apart: 6, of which 4 were waited for; matrix products, arithmetic and copies ran while one was open for 9% of the time, Pallas kernels for 0%

commit v1 on v0

v1 whole, which is shorter than its diff:
```python
import functools
import math

import jax
import jax.numpy as jnp
from jax import lax
from jax.experimental import pallas as pl
from jax.experimental.pallas import tpu as pltpu
from jax.sharding import Mesh
from jax.sharding import PartitionSpec as P

masked_value = -1e30
LANES = 128


def pack_kernel(chosen, counts, cache_ref, out_ref, *, chunk, local_heads, inner, capacity):
    slot = pl.program_id(0) * capacity + pl.program_id(1)

    @pl.when(pl.program_id(1) < counts[pl.program_id(0)])
    def _():
        by_head = pltpu.einshape("rhd->hrd", cache_ref[0])
        for r in range(inner):
            for half in range(2):
                out_ref[0, r, 0, half] = by_head[(half * inner + r) * local_heads + chunk]


def pack_blocks(chosen, counts, cache, chunk, groups, inner, capacity, local_heads):
    _, block_rows, heads, width = cache.shape
    return pl.pallas_call(
        functools.partial(
            pack_kernel, chunk=chunk, local_heads=local_heads, inner=inner, capacity=capacity
        ),
        grid_spec=pltpu.PrefetchScalarGridSpec(
            num_scalar_prefetch=2,
            grid=(groups, capacity),
            in_specs=[
                pl.BlockSpec(
                    (1, block_rows, heads, width),
                    lambda g, s, ch, ct: (ch[g * capacity + s], 0, 0, 0),
                )
            ],
            out_specs=pl.BlockSpec(
                (1, inner, 1, 2, block_rows, width), lambda g, s, ch, ct: (g, 0, s, 0, 0, 0)
            ),
        ),
        out_shape=jax.ShapeDtypeStruct(
            (groups, inner, capacity, 2, block_rows, width), cache.dtype
        ),
        compiler_params=pltpu.CompilerParams(vmem_limit_bytes=32 << 20),
        cost_estimate=pl.CostEstimate(
            flops=0, transcendentals=0, bytes_accessed=groups * capacity * 2 * 262144
        ),
    )(chosen, counts, cache)


def nt_dot(left, right):
    return lax.dot_general(
        left, right, (((1,), (1,)), ((), ())), preferred_element_type=jnp.float32
    )


def attention_kernel(
    places, lens, counts, q_ref, b_ref, recv_ref, co_ref, ds_ref,
    kv, scores, probs, top, acc, total, dacc, sems, *, slots, scale,
):
    patch = pl.program_id(0)
    patches = pl.num_programs(0)
    block_rows = recv_ref.shape[2]
    pair = 2 * block_rows

    def copy(which, j, place):
        return pltpu.make_async_copy(
            recv_ref.at[place],
            kv.at[which % 2, :, pl.ds(pl.multiple_of(j * block_rows, block_rows), block_rows), :],
            sems.at[which % 2, j],
        )

    def start(which):
        @pl.loop(0, counts[which])
        def _(j):
            copy(which, j, places[which * slots + j]).start()

    @pl.when(patch == 0)
    def _():
        start(patch)

    @pl.when(patch + 1 < patches)
    def _():
        start(patch + 1)

    here = counts[patch]
    tiles = jnp.maximum((here + 1) // 2, 1)

    @pl.loop(here, 2 * tiles)
    def _(j):
        kv[patch % 2, :, pl.ds(pl.multiple_of(j * block_rows, block_rows), block_rows), :] = (
            jnp.zeros((2, block_rows, kv.shape[3]), kv.dtype)
        )

    @pl.loop(0, here)
    def _(j):
        copy(patch, j, 0).wait()

    def key_tile(t, head):
        return kv[patch % 2, head, pl.ds(pl.multiple_of(t * pair, pair), pair), :]

    rows = q_ref.shape[0]
    for head in range(2):
        lanes = pl.ds(head * LANES, LANES)
        q = q_ref[:, lanes]
        back = b_ref[:, lanes]
        top[...] = jnp.full_like(top, masked_value)
        acc[...] = jnp.zeros_like(acc)
        total[...] = jnp.zeros_like(total)
        dacc[...] = jnp.zeros_like(dacc)

        @pl.loop(0, tiles)
        def _(t):
            place = lax.broadcasted_iota(jnp.int32, (1, block_rows), 1)
            seen_lo = place < lens[patch * slots + 2 * t]
            seen_hi = place < lens[patch * slots + 2 * t + 1]
            score = nt_dot(q, key_tile(t, head))
            low = jnp.where(seen_lo, score[:, :block_rows], masked_value)
            high = jnp.where(seen_hi, score[:, block_rows:], masked_value)
            scores[t, :, :block_rows] = low
            scores[t, :, block_rows:] = high
            top[...] = jnp.maximum(top[...], jnp.maximum(low, high))

        row_max = jnp.max(top[...], axis=1, keepdims=True)

        @pl.loop(0, tiles)
        def _(t):
            weights = jnp.exp(scores[t] - row_max).astype(jnp.bfloat16)
            probs[t] = weights
            wide = weights.astype(jnp.float32)
            total[...] += wide[:, :block_rows] + wide[:, block_rows:]
            acc[...] += jnp.dot(
                weights, key_tile(t, head), preferred_element_type=jnp.float32
            )

        row_sum = jnp.sum(total[...], axis=1, keepdims=True)
        inverse = 1.0 / row_sum
        outs = acc[...] * inverse
        inner = jnp.sum(outs * back.astype(jnp.float32), axis=1, keepdims=True)

        @pl.loop(0, tiles)
        def _(t):
            dprobs = nt_dot(back, key_tile(t, head))
            dscores = (probs[t].astype(jnp.float32) * (dprobs - inner)).astype(jnp.bfloat16)
            dacc[...] += jnp.dot(
                dscores, key_tile(t, head), preferred_element_type=jnp.float32
            )

        co_ref[:, lanes] = outs
        lane = lax.broadcasted_iota(jnp.int32, (rows, LANES), 1)
        stat = jnp.where(lane < 96, row_max + jnp.log(row_sum), inner)
        ds_ref[:, lanes] = jnp.where(lane < 64, dacc[...] * (inverse * scale), stat)


def attention(places, lens, counts, queries, backs, received, chunk, patch_blocks, slots, scale):
    rows = queries.shape[0] // patch_blocks
    total_rows = queries.shape[0]
    block_rows, width = received.shape[2:]
    wide = pl.BlockSpec((rows, 2 * LANES), lambda p, *_: (p, chunk))
    out = pl.BlockSpec((rows, 2 * LANES), lambda p, *_: (p, 0))
    tiles = (slots + 1) // 2
    return pl.pallas_call(
        functools.partial(attention_kernel, slots=slots, scale=scale),
        grid_spec=pltpu.PrefetchScalarGridSpec(
            num_scalar_prefetch=3,
            grid=(patch_blocks,),
            in_specs=[wide, wide, pl.BlockSpec(memory_space=pl.ANY)],
            out_specs=[out, out],
            scratch_shapes=[
                pltpu.VMEM((2, 2, tiles * 2 * block_rows, width), jnp.bfloat16),
                pltpu.VMEM((tiles, rows, 2 * block_rows), jnp.float32),
                pltpu.VMEM((tiles, rows, 2 * block_rows), jnp.bfloat16),
                pltpu.VMEM((rows, block_rows), jnp.float32),
                pltpu.VMEM((rows, width), jnp.float32),
                pltpu.VMEM((rows, block_rows), jnp.float32),
                pltpu.VMEM((rows, width), jnp.float32),
                pltpu.SemaphoreType.DMA((2, slots)),
            ],
        ),
        out_shape=[jax.ShapeDtypeStruct((total_rows, 2 * LANES), jnp.float32)] * 2,
        compiler_params=pltpu.CompilerParams(vmem_limit_bytes=44 << 20),
        cost_estimate=pl.CostEstimate(
            flops=8 * total_rows * slots * block_rows * width,
            transcendentals=total_rows * slots * block_rows,
            bytes_accessed=40 << 20,
        ),
    )(places, lens, counts, queries, backs, received)


def swap(x, axis):
    return lax.ppermute(x, axis, [(0, 1), (1, 0)])


def gather_half(x, zl_size, y_size):
    if zl_size == 2 and y_size == 2:
        place = 2 * lax.axis_index("zl") + lax.axis_index("y")
        cut = x.shape[0] // 2
        by_y = swap(x, "y")
        by_zl = swap(x, "zl")
        corner = jnp.concatenate([swap(by_y[:cut], "zl"), swap(by_zl[cut:], "y")], axis=0)
        return [x, by_y, by_zl, corner], jnp.stack([place, place ^ 1, place ^ 2, place ^ 3])
    whole = lax.all_gather(x, ("zl", "y"), axis=0, tiled=False)
    count = zl_size * y_size
    return [whole[i] for i in range(count)], jnp.arange(count, dtype=jnp.int32)


def scatter_sum(x, size, dim):
    index = lax.axis_index("dp")
    step = size // 2
    while step >= 1:
        half = x.shape[dim] // 2
        upper = (index // step) % 2
        keep = lax.dynamic_slice_in_dim(x, upper * half, half, dim)
        give = lax.dynamic_slice_in_dim(x, (1 - upper) * half, half, dim)
        got = lax.ppermute(
            give.astype(jnp.bfloat16), "dp", [(i, i ^ step) for i in range(size)]
        )
        x = keep + got.astype(jnp.float32)
        step //= 2
    return x


def local(
    patches, query_proj, output_proj, cache, block_lengths, neighbours, cotangent, *, sizes
):
    groups, zl_size, y_size = sizes
    inner = zl_size * y_size
    model = 2 * inner
    owner_count = groups * model
    group = lax.axis_index("dp")
    zh = lax.axis_index("zh")
    spot = lax.axis_index("zl") * y_size + lax.axis_index("y")
    me = group * model + zh * inner + spot
    local_blocks, block_rows, heads, width = cache.shape
    head_size = width // 2
    local_heads = query_proj.shape[1] // head_size
    features = patches.shape[1]
    columns = features // model
    slots = neighbours.shape[1]
    patch_blocks = neighbours.shape[0] // groups
    entry_count = patch_blocks * slots
    capacity = 2 * entry_count // owner_count
    row_count = patches.shape[0]
    head_scale = 1.0 / math.sqrt(head_size)
    grad_scale = 1.0 / math.sqrt(row_count * groups)

    all_ids = neighbours.reshape(groups, entry_count)
    match = all_ids // local_blocks == me
    order = jnp.arange(entry_count, dtype=jnp.int32)
    earlier = order[None, :] < order[:, None]
    rank = jnp.sum((match[:, None, :] & earlier[None]).astype(jnp.int32), axis=2)
    slot_range = jnp.arange(capacity, dtype=jnp.int32)
    placed = match[:, :, None] & (rank[:, :, None] == slot_range)
    chosen = jnp.sum(
        jnp.where(placed, (all_ids % local_blocks)[:, :, None], 0), axis=1
    ).reshape(groups * capacity)
    send_counts = jnp.sum(match.astype(jnp.int32), axis=1)

    packed = [
        pack_blocks(
            chosen, send_counts, cache, c, groups, inner, capacity, local_heads
        ).reshape(groups * inner, capacity * 2 * block_rows, width)
        for c in range(local_heads)
    ]
    received = [
        lax.all_to_all(x, ("dp", "zl", "y"), split_axis=0, concat_axis=0, tiled=True).reshape(
            groups * inner * capacity, 2, block_rows, width
        )
        for x in packed
    ]

    my_ids = lax.dynamic_slice_in_dim(
        neighbours, group * patch_blocks, patch_blocks, 0
    ).reshape(entry_count)
    owners = my_ids // local_blocks
    slot_of = jnp.sum(((owners[:, None] == owners[None, :]) & earlier).astype(jnp.int32), axis=1)
    source = (owners // model) * inner + owners % inner
    in_half = ((owners % model) // inner == zh).reshape(patch_blocks, slots)
    arrival = (source * capacity + slot_of).reshape(patch_blocks, slots)
    every_length = lax.all_gather(
        block_lengths, ("dp", "zh", "zl", "y"), axis=0, tiled=True
    )
    entry_length = every_length[my_ids].reshape(patch_blocks, slots)
    spots = jnp.arange(slots, dtype=jnp.int32)
    before = jnp.sum(
        (in_half[:, None, :] & (spots[None, :] < spots[:, None])[None]).astype(jnp.int32), axis=2
    )
    at = in_half[:, :, None] & (before[:, :, None] == spots)
    places = jnp.sum(jnp.where(at, arrival[:, :, None], 0), axis=1).reshape(entry_count)
    lens = jnp.sum(jnp.where(at, entry_length[:, :, None], 0), axis=1).reshape(entry_count)
    counts = jnp.sum(in_half.astype(jnp.int32), axis=1)

    def both_halves(own):
        other = swap(own, "zh")
        return jnp.where(zh == 0, own, other), jnp.where(zh == 0, other, own)

    q_halves = [
        w.reshape(features, local_heads, head_size) for w in both_halves(query_proj)
    ]
    q_wide = jnp.stack(q_halves, axis=2)
    q_wide = jnp.pad(q_wide, ((0, 0), (0, 0), (0, 0), (0, LANES - head_size)))
    q_wide = q_wide.reshape(features, local_heads * 2 * LANES)
    o_halves = [
        w.reshape(local_heads, head_size, features) for w in both_halves(output_proj)
    ]
    o_wide = jnp.stack(o_halves, axis=1)
    o_wide = jnp.pad(o_wide, ((0, 0), (0, 0), (LANES - head_size, 0), (0, 0)))
    o_wide = o_wide.reshape(local_heads * 2 * LANES, features)
    queries = (
        jnp.dot(patches, q_wide, preferred_element_type=jnp.float32) * head_scale
    ).astype(jnp.bfloat16)
    backs = nt_dot(cotangent, o_wide).astype(jnp.bfloat16)

    mp = ("zh", "zl", "y")
    o_cols = output_proj.reshape(local_heads * head_size, model, columns).transpose(1, 0, 2)
    o_cols = lax.all_to_all(o_cols, mp, split_axis=0, concat_axis=0, tiled=True)
    o_cols = o_cols.reshape(2, inner, local_heads, head_size, columns)
    q_cols = query_proj.reshape(model, columns, local_heads * head_size).transpose(0, 2, 1)
    q_cols = lax.all_to_all(q_cols, mp, split_axis=0, concat_axis=0, tiled=True)
    q_cols = q_cols.reshape(2, inner, local_heads, head_size, columns)

    def tail_weights(cols, c, first, order):
        piece = jnp.moveaxis(cols[:, :, c], 0, 1)
        empty = jnp.zeros_like(piece)
        pair = [piece, empty] if first else [empty, piece]
        stacked = jnp.stack(pair, axis=2).reshape(inner, 2 * LANES, columns)
        return stacked[order].reshape(inner * 2 * LANES, columns)

    lane = jnp.arange(2 * LANES, dtype=jnp.int32)
    lower = (lane % LANES < head_size)[None, :]
    first_head = (lane < LANES)[None, :]
    attended = None
    patch_grad = None
    own = []
    for c in range(local_heads):
        outs, douts = attention(
            places, lens, counts, queries, backs, received[c], c, patch_blocks, slots, head_scale
        )
        lse = douts[:, 64], douts[:, LANES + 64]
        inner_sum = douts[:, 96], douts[:, LANES + 96]
        theirs = swap(jnp.stack(lse + inner_sum), "zh")

        def per_head(pair):
            return jnp.where(first_head, pair[0][:, None], pair[1][:, None])

        weight = per_head([jax.nn.sigmoid(lse[i] - theirs[i]) for i in range(2)])
        shift = per_head(
            [
                jax.nn.sigmoid(theirs[i] - lse[i]) * (inner_sum[i] - theirs[2 + i]) * head_scale
                for i in range(2)
            ]
        )
        part = weight * jnp.where(lower, douts + shift * outs, outs)
        merged = (part + swap(part.astype(jnp.bfloat16), "zh").astype(jnp.float32)).astype(
            jnp.bfloat16
        )
        pieces, order = gather_half(merged, zl_size, y_size)
        every = jnp.concatenate(pieces, axis=1)
        att = jnp.dot(
            every, tail_weights(o_cols, c, False, order), preferred_element_type=jnp.float32
        )
        grad = jnp.dot(
            every, tail_weights(q_cols, c, True, order), preferred_element_type=jnp.float32
        )
        attended = att if attended is None else attended + att
        patch_grad = grad if patch_grad is None else patch_grad + grad
        own.append(lax.dynamic_slice_in_dim(merged, zh * LANES, LANES, 1))

    dquery = jnp.concatenate([x[:, :head_size] for x in own], axis=1)
    heads_out = jnp.concatenate([x[:, head_size:] for x in own], axis=1)
    query_term = (
        lax.dot_general(
            patches, dquery, (((0,), (0,)), ((), ())), preferred_element_type=jnp.float32
        )
        * grad_scale
    )
    output_term = (
        lax.dot_general(
            heads_out, cotangent, (((0,), (0,)), ((), ())), preferred_element_type=jnp.float32
        )
        * grad_scale
    )
    return (
        attended.astype(jnp.bfloat16),
        patch_grad.astype(jnp.bfloat16),
        scatter_sum(query_term, groups, 0),
        scatter_sum(output_term, groups, 1),
    )


def solution(mesh):
    groups, model = mesh.shape["dp"], mesh.shape["mp"]
    sizes = (groups, model // 4, 2)
    split = Mesh(
        mesh.devices.reshape(groups, 2, model // 4, 2), ("dp", "zh", "zl", "y")
    )
    mp = ("zh", "zl", "y")
    every = ("dp",) + mp
    return jax.shard_map(
        functools.partial(local, sizes=sizes),
        mesh=split,
        in_specs=(
            P("dp", None),
            P(None, mp),
            P(mp, None),
            P(every, None, None, None),
            P(every),
            P(),
            P("dp", None),
        ),
        out_specs=(P("dp", mp), P("dp", mp), P("dp", mp), P(mp, "dp")),
        check_vma=False,
    )
```

time: 1280 us -> 653 us (0.51)
  waiting for transfers between devices: 881 us -> 203 us
  Pallas kernels: 0 us -> 142 us
  blocking collectives: 0 us -> 141 us
  matrix products: 154 us -> 25.2 us
  local copies, waits for them, and re-layouts: 131 us -> 55.2 us
  other arithmetic: 87.3 us -> 30.7 us
  starting transfers between devices: 13.6 us -> 47.5 us
    reduce_scatter x4 -> x0, waiting for transfers between devices: 523 us -> none  [the longest x1 253 us: local(): lax.psum_scatter(output_term, 'mp', scatter_dimension=1, tiled=True)]
    all_to_all x2 -> x4, waiting for transfers between devices: 358 us -> 97.2 us  [the longest x2 97.2 us: local(): lax.all_to_all(x, ('dp', 'zl', 'y'), split_axis=0, concat_axis=0, tiled=T...]
    pallas_call x0 -> x4, Pallas kernels: none -> 142 us  [the longest x2 134 us: attention(): pl.pallas_call(functools.partial(attention_kernel, slots=slots, scale=sca...]
    unnamed x0 -> x1, blocking collectives: none -> 141 us
    dot_general x22 -> x8, matrix products: 154 us -> 25.2 us  [the longest x2 5.19 us: local(): jnp.dot(every, tail_weights(q_cols, c, True, order), preferred_element_ty...]
    ppermute x0 -> x18, waiting for transfers between devices: none -> 105 us  [the longest x14 97.2 us: swap(): return lax.ppermute(x, axis, [(0, 1), (1, 0)])]
    gather x5, local copies, waits for them, and re-layouts: 82.8 us -> 6.84 us  [the longest x4 5.58 us: tail_weights(): return stacked[order].reshape(inner * 2 * LANES, columns)]
    convert_element_type x10 -> x3, other arithmetic: 52.4 us -> 12.6 us  [the longest x1 8.01 us: local(): part.astype(jnp.bfloat16)]
  transfers between devices with their start and end apart: 6 -> 22, of which waited for: 4 -> 11; matrix products, arithmetic and copies ran while one was open for 9% -> 12% of each run, Pallas kernels for 0% -> 21%
where the time goes in v1:
time: 653 us; the launch traced here: 646 us
  waiting for transfers between devices  203 us (31%)
  Pallas kernels  142 us (22%)
  blocking collectives  141 us (22%)
  local copies, waits for them, and re-layouts  55.2 us (8%)
  starting transfers between devices  47.5 us (7%)
  other arithmetic  30.7 us (5%)
  matrix products  25.2 us (4%)
    unnamed x1, blocking collectives  141 us
    pallas_call x2, Pallas kernels, attention(): pl.pallas_call(functools.partial(attention_kernel, slots=slots, scale=sca...  134 us
    ppermute x14, waiting for transfers between devices, swap(): return lax.ppermute(x, axis, [(0, 1), (1, 0)])  97.2 us
    all_to_all x2, waiting for transfers between devices, local(): lax.all_to_all(x, ('dp', 'zl', 'y'), split_axis=0, concat_axis=0, tiled=T...  97.2 us
    unnamed x58, local copies, waits for them, and re-layouts  25.8 us
    ppermute x14, starting transfers between devices, swap(): return lax.ppermute(x, axis, [(0, 1), (1, 0)])  15.6 us
  transfers between devices with their start and end apart: 22, of which 11 were waited for; matrix products, arithmetic and copies ran while one was open for 12% of the time, Pallas kernels for 21%

profile of v1, /device:TPU:0, one launch (start us, length us, event | category | flops | bytes accessed | tf_op | source)
XLA Modules:
  0.0 646.3 jit_solution(8235758590072701357)
XLA Ops:
  2.9 3.4 copy-done.1
  6.3 4.4 shard_map.104
  10.7 3.2 copy-done.4
  13.9 6.8 %all-to-all-start.2 = ((bf16[16,2048,128]{2,1,0:T(8,128)(2,1)}), bf16[16,2048,128]{2,1,0:T(8,128)(2,1)}, u32[]{:S(2)}, u32[]{:S(2)}) async-start(bf16[16,2048,128]{2,1,0:T(8,128)(2,1)} %bitcast.95), calls=%async_computation.2 | async-start | bytes 16777216 | tf_op jit(solution)/shard_map/all_to_all | solution.py:271
  20.7 3.4 copy-done.2
  24.1 3.9 shard_map.102
  28.0 3.2 copy-done.3
  31.2 97.2 %all-to-all-done.2 = bf16[16,2048,128]{2,1,0:T(8,128)(2,1)} async-done(((bf16[16,2048,128]{2,1,0:T(8,128)(2,1)}), bf16[16,2048,128]{2,1,0:T(8,128)(2,1)}, u32[]{:S(2)}, u32[]{:S(2)}) %all-to-all-start.2) | async-done | bytes 8388640 | tf_op jit(solution)/shard_map/all_to_all | solution.py:271
  128.4 4.9 all-to-all-start
  140.0 141.0 %all-reduce.6 = s32[512]{0:T(512)S(1)} all-reduce(s32[512]{0:T(512)S(1)} %dynamic-update-slice), channel_id=1, replica_groups=mesh['dp'=4,'zh'=2,'zl'=2,'y'=2] {'dp','zh','zl','y'}, use_global_device_ids=true, to_apply=%add.6 | all-reduce | flops 512 | bytes 4096
  286.3 4.4 fusion.3.q_ref
  290.7 4.4 fusion.2.b_ref
  295.1 67.0 %shard_map.105 = (f32[1920,256]{1,0:T(8,128)S(1)}, f32[1920,256]{1,0:T(8,128)S(1)}) custom-call(s32[128]{0:T(128)S(1)} %reshape.579.places, s32[128]{0:T(128)S(1)} %reshape.581.lens, s32[4]{0:T(128)S(1)} %get-tuple-element.62.counts, bf16[1920,512]{1,0:T(8,128)(2,1)S(1)} %fusion.3.q_ref, bf16[1920,512]{1,0:T(8,128)(2,1)S(1)} %fusion.2.b_ref, ...), custom_call_target="tpu_custom_call" | custom-call | flops 8053063680 | bytes 41943040 | tf_op jit(solution)/shard_map/pallas_call | solution.py:167
  365.8 5.9 all-to-all-start.3
  374.8 66.9 %shard_map.103 = (f32[1920,256]{1,0:T(8,128)S(1)}, f32[1920,256]{1,0:T(8,128)S(1)}) custom-call(s32[128]{0:T(128)S(1)} %reshape.579.places, s32[128]{0:T(128)S(1)} %reshape.581.lens, s32[4]{0:T(128)S(1)} %get-tuple-element.62.counts, bf16[1920,512]{1,0:T(8,128)(2,1)S(1)} %copy-done.8, bf16[1920,512]{1,0:T(8,128)(2,1)S(1)} %copy-done.10, ...), custom_call_target="tpu_custom_call" | custom-call | flops 8053063680 | bytes 41943040 | tf_op jit(solution)/shard_map/pallas_call | solution.py:167
  450.8 3.9 fusion.9
  459.9 5.1 fusion.7
  465.1 5.7 all-to-all-start.1
  470.7 8.0 %fusion.41 = (bf16[1920,256]{1,0:T(8,128)(2,1)}, f32[1920,256]{1,0:T(8,128)}, bf16[1920,256]{1,0:T(8,128)(2,1)}, f32[1920,256]{1,0:T(8,128)}) fusion(f32[1920,256]{1,0:T(8,128)} %copy-done.6, f32[1920,256]{1,0:T(8,128)} %copy-done, f32[1920]{0:T(1024)S(1)} %get-tuple-element.44, f32[1920]{0:T(1024)S(1)} %get-tuple-element.37, ...), kind=kLoop, calls=%fused_computation.160 | loop fusion | flops 6881280 | bytes 13824512 | tf_op jit(solution)/shard_map/convert_element_type | solution.py:359
  488.9 59.3 %collective-permute-done.3 = bf16[1920,256]{1,0:T(8,128)(2,1)} collective-permute-done((bf16[1920,256]{1,0:T(8,128)(2,1)}, bf16[1920,256]{1,0:T(8,128)(2,1)}, u32[]{:S(2)}, u32[]{:S(2)}) %collective-permute-start.3) | collective-permute-done | bytes 983072 | tf_op jit(solution)/shard_map/ppermute | solution.py:196
  548.2 3.0 add_convert_fusion.1
  554.2 15.2 %collective-permute-done.9 = bf16[1920,256]{1,0:T(8,128)(2,1)} collective-permute-done((bf16[1920,256]{1,0:T(8,128)(2,1)}, bf16[1920,256]{1,0:T(8,128)(2,1)}, u32[]{:S(2)}, u32[]{:S(2)}) %collective-permute-start.9) | collective-permute-done | bytes 983072 | tf_op jit(solution)/shard_map/ppermute | solution.py:196
  572.8 4.8 convolution_multiply_fusion.1
  577.7 6.0 collective-permute-start.14
  585.1 3.9 collective-permute-done.14
  591.6 4.3 collective-permute-done.16
  599.4 13.5 %collective-permute-done.11 = bf16[1920,256]{1,0:T(8,128)(2,1)S(1)} collective-permute-done((bf16[1920,256]{1,0:T(8,128)(2,1)S(1)}, bf16[1920,256]{1,0:T(8,128)(2,1)S(1)}, u32[]{:S(2)}, u32[]{:S(2)}) %collective-permute-start.11) | collective-permute-done | bytes 983072 | tf_op jit(solution)/shard_map/ppermute | solution.py:196
  623.6 4.5 collective-permute-done.13
  628.1 3.4 maximum_maximum_fusion.1
  634.8 3.3 collective-permute-done.7
  638.0 4.0 fusion.5
  642.1 3.9 fusion.4
  (174 shorter events, 72.9 us)
Async XLA Ops:
  13.9 114.5 %all-to-all-start.2 = ((bf16[16,2048,128]{2,1,0:T(8,128)(2,1)}), bf16[16,2048,128]{2,1,0:T(8,128)(2,1)}, u32[]{:S(2)}, u32[]{:S(2)}) async-start(bf16[16,2048,128]{2,1,0:T(8,128)(2,1)} %bitcast.95), calls=%async_computation.2 | async-start | bytes 16777216 | tf_op jit(solution)/shard_map/all_to_all | solution.py:271
  128.4 8.5 %copy-start.12 = (bf16[128,2048]{1,0:T(8,128)(2,1)S(1)}, bf16[128,2048]{1,0:T(8,128)(2,1)}, u32[]{:S(2)}) copy-start(bf16[128,2048]{1,0:T(8,128)(2,1)} %param.9) | copy-start | bytes 1572868
  128.4 11.4 %copy-start.17 = (s32[16]{0:T(128)S(1)}, s32[16]{0:T(128)}, u32[]{:S(2)}) copy-start(s32[16]{0:T(128)} %param.11) | copy-start | bytes 196
  128.4 237.4 %all-to-all-start = ((bf16[16,2048,128]{2,1,0:T(8,128)(2,1)}), bf16[16,2048,128]{2,1,0:T(8,128)(2,1)}, u32[]{:S(2)}, u32[]{:S(2)}) async-start(bf16[16,2048,128]{2,1,0:T(8,128)(2,1)} %bitcast.94), calls=%async_computation | async-start | bytes 16777216 | tf_op jit(solution)/shard_map/all_to_all | solution.py:271
  134.5 148.4 %collective-permute-start = (bf16[2048,128]{0,1:T(8,128)(2,1)S(1)}, bf16[2048,128]{0,1:T(8,128)(2,1)S(1)}, u32[]{:S(2)}, u32[]{:S(2)}) collective-permute-start(bf16[2048,128]{0,1:T(8,128)(2,1)S(1)} %copy.113), channel_id=1, source_target_pairs={{0,4},{4,0},{1,5},{5,1},{2,6},{6,2},{3,7},{7,3},{8,12},{12,8},{9,1... | collective-permute-start | bytes 1572872 | tf_op jit(solution)/shard_map/ppermute | solution.py:196
  136.9 146.5 %collective-permute-start.1 = (bf16[128,2048]{1,0:T(8,128)(2,1)S(1)}, bf16[128,2048]{1,0:T(8,128)(2,1)S(1)}, u32[]{:S(2)}, u32[]{:S(2)}) collective-permute-start(bf16[128,2048]{1,0:T(8,128)(2,1)S(1)} %copy-done.12), channel_id=1, source_target_pairs={{0,4},{4,0},{1,5},{5,1},{2,6},{6,2},{3,7},{7,3},{8,12},{12,8},{9,1... | collective-permute-start | bytes 1572872 | tf_op jit(solution)/shard_map/ppermute | solution.py:196
  283.5 7.1 %slice-start.2 = ((s8[7864320]{0:T(1024)(128)(4,1)}), s8[4194304]{0:T(1024)(128)(4,1)S(1)}, s32[]{:S(2)}) async-start(s8[7864320]{0:T(1024)(128)(4,1)} %bitcast.98), calls=%async_computation.6 | async-start | bytes 8388608
  290.7 4.4 copy-start.7
  295.1 67.1 %copy-start.9 = (bf16[1920,512]{1,0:T(8,128)(2,1)}, bf16[1920,512]{1,0:T(8,128)(2,1)S(1)}, u32[]{:S(2)}) copy-start(bf16[1920,512]{1,0:T(8,128)(2,1)S(1)} %fusion.2.b_ref) | copy-start | bytes 5898244
  365.7 80.7 %collective-permute-start.8 = (f32[4,1920]{1,0:T(4,128)S(1)}, f32[4,1920]{1,0:T(4,128)S(1)}, u32[]{:S(2)}, u32[]{:S(2)}) collective-permute-start(f32[4,1920]{1,0:T(4,128)S(1)} %pad_maximum_fusion.2), channel_id=1, source_target_pairs={{0,4},{4,0},{1,5},{5,1},{2,6},{6,2},{3,7},{7,3},{8,12},{12,8},{9,1... | collective-permute-start | bytes 92168 | tf_op jit(solution)/shard_map/ppermute | solution.py:196
  365.8 99.3 %all-to-all-start.3 = ((bf16[8,128,256]{1,2,0:T(8,128)(2,1)}), bf16[8,128,256]{1,2,0:T(8,128)(2,1)S(1)}, u32[]{:S(2)}, u32[]{:S(2)}) async-start(bf16[8,128,256]{1,2,0:T(8,128)(2,1)} %bitcast.40), calls=%async_computation.3 | async-start | bytes 1048576 | tf_op jit(solution)/shard_map/all_to_all | solution.py:324
  445.2 9.5 %collective-permute-start.2 = (f32[4,1920]{1,0:T(4,128)S(1)}, f32[4,1920]{1,0:T(4,128)}, u32[]{:S(2)}, u32[]{:S(2)}) collective-permute-start(f32[4,1920]{1,0:T(4,128)S(1)} %pad_maximum_fusion.1), channel_id=1, source_target_pairs={{0,4},{4,0},{1,5},{5,1},{2,6},{6,2},{3,7},{7,3},{8,12},{12,8},{9,1... | collective-permute-start | bytes 92168 | tf_op jit(solution)/shard_map/ppermute | solution.py:196
  465.1 19.9 %all-to-all-start.1 = ((bf16[8,128,256]{1,2,0:T(8,128)(2,1)}), bf16[8,128,256]{1,2,0:T(8,128)(2,1)S(1)}, u32[]{:S(2)}, u32[]{:S(2)}) async-start(bf16[8,128,256]{1,2,0:T(8,128)(2,1)} %bitcast.16), calls=%async_computation.1 | async-start | bytes 1048576 | tf_op jit(solution)/shard_map/all_to_all | solution.py:321
  478.7 69.4 %collective-permute-start.3 = (bf16[1920,256]{1,0:T(8,128)(2,1)}, bf16[1920,256]{1,0:T(8,128)(2,1)}, u32[]{:S(2)}, u32[]{:S(2)}) collective-permute-start(bf16[1920,256]{1,0:T(8,128)(2,1)} %get-tuple-element.58), channel_id=1, source_target_pairs={{0,4},{4,0},{1,5},{5,1},{2,6},{6,2},{3,7},{7,3},{8,12},{12,8},{9,1... | collective-permute-start | bytes 2949128 | tf_op jit(solution)/shard_map/ppermute | solution.py:196
  485.1 84.2 %collective-permute-start.9 = (bf16[1920,256]{1,0:T(8,128)(2,1)}, bf16[1920,256]{1,0:T(8,128)(2,1)}, u32[]{:S(2)}, u32[]{:S(2)}) collective-permute-start(bf16[1920,256]{1,0:T(8,128)(2,1)} %get-tuple-element.85), channel_id=1, source_target_pairs={{0,4},{4,0},{1,5},{5,1},{2,6},{6,2},{3,7},{7,3},{8,12},{12,8},{9,1... | collective-permute-start | bytes 2949128 | tf_op jit(solution)/shard_map/ppermute | solution.py:196
  487.4 82.0 %copy-start.11 = (f32[1920,256]{1,0:T(8,128)S(1)}, f32[1920,256]{1,0:T(8,128)}, u32[]{:S(2)}) copy-start(f32[1920,256]{1,0:T(8,128)} %get-tuple-element.86) | copy-start | bytes 5898244
  551.2 69.0 %collective-permute-start.4 = (bf16[1920,256]{1,0:T(8,128)(2,1)}, bf16[1920,256]{1,0:T(8,128)(2,1)}, u32[]{:S(2)}, u32[]{:S(2)}) collective-permute-start(bf16[1920,256]{1,0:T(8,128)(2,1)} %add_convert_fusion.1), channel_id=1, source_target_pairs={{0,1},{1,0},{2,3},{3,2},{4,5},{5,4},{6,7},{7,6},{8,9},{9,8},{10,11... | collective-permute-start | bytes 2949128 | tf_op jit(solution)/shard_map/ppermute | solution.py:196
  552.6 68.7 %collective-permute-start.5 = (bf16[1920,256]{1,0:T(8,128)(2,1)}, bf16[1920,256]{1,0:T(8,128)(2,1)}, u32[]{:S(2)}, u32[]{:S(2)}) collective-permute-start(bf16[1920,256]{1,0:T(8,128)(2,1)} %add_convert_fusion.1), channel_id=1, source_target_pairs={{0,2},{2,0},{1,3},{3,1},{4,6},{6,4},{5,7},{7,5},{8,10},{10,8},{9,1... | collective-permute-start | bytes 2949128 | tf_op jit(solution)/shard_map/ppermute | solution.py:196
  569.4 14.3 %slice-start.4 = ((s8[7864320]{0:T(1024)(128)(4,1)}), s8[4194304]{0:T(1024)(128)(4,1)S(1)}, s32[]{:S(2)}) async-start(s8[7864320]{0:T(1024)(128)(4,1)} %bitcast.100), calls=%async_computation.8 | async-start | bytes 8388608
  571.3 24.8 %collective-permute-start.10 = (bf16[1920,256]{1,0:T(8,128)(2,1)S(1)}, bf16[1920,256]{1,0:T(8,128)(2,1)S(1)}, u32[]{:S(2)}, u32[]{:S(2)}) collective-permute-start(bf16[1920,256]{1,0:T(8,128)(2,1)S(1)} %add_convert_fusion), channel_id=1, source_target_pairs={{0,1},{1,0},{2,3},{3,2},{4,5},{5,4},{6,7},{7,6},{8,9},{9,8},{10,11... | collective-permute-start | bytes 2949128 | tf_op jit(solution)/shard_map/ppermute | solution.py:196
  572.8 40.1 %collective-permute-start.11 = (bf16[1920,256]{1,0:T(8,128)(2,1)S(1)}, bf16[1920,256]{1,0:T(8,128)(2,1)S(1)}, u32[]{:S(2)}, u32[]{:S(2)}) collective-permute-start(bf16[1920,256]{1,0:T(8,128)(2,1)S(1)} %add_convert_fusion), channel_id=1, source_target_pairs={{0,2},{2,0},{1,3},{3,1},{4,6},{6,4},{5,7},{7,5},{8,10},{10,8},{9,1... | collective-permute-start | bytes 2949128 | tf_op jit(solution)/shard_map/ppermute | solution.py:196
  572.8 10.8 %slice-start.5 = ((s8[7864320]{0:T(1024)(128)(4,1)}), s8[3670016]{0:T(1024)(128)(4,1)S(1)}, s32[]{:S(2)}) async-start(s8[7864320]{0:T(1024)(128)(4,1)} %bitcast.100), calls=%async_computation.9 | async-start | bytes 7340032
  577.7 11.4 %collective-permute-start.14 = (bf16[1024,128]{0,1:T(8,128)(2,1)S(1)}, bf16[1024,128]{0,1:T(8,128)(2,1)S(1)}, u32[]{:S(2)}, u32[]{:S(2)}) collective-permute-start(bf16[1024,128]{0,1:T(8,128)(2,1)S(1)} %fusion.17), channel_id=1, source_target_pairs={{0,16},{8,24},{16,0},{24,8},{1,17},{9,25},{17,1},{25,9},{2,18},{10... | collective-permute-start | bytes 786440 | tf_op jit(solution)/shard_map/ppermute | solution.py:220
  589.0 6.8 %collective-permute-start.16 = (bf16[128,1024]{1,0:T(8,128)(2,1)S(1)}, bf16[128,1024]{1,0:T(8,128)(2,1)S(1)}, u32[]{:S(2)}, u32[]{:S(2)}) collective-permute-start(bf16[128,1024]{1,0:T(8,128)(2,1)S(1)} %dynamic-slice_convert_fusion), channel_id=1, source_target_pairs={{0,16},{8,24},{16,0},{24,8},{1,17},{9,25},{17,1},{25,9},{2,18},{10... | collective-permute-start | bytes 786440 | tf_op jit(solution)/shard_map/ppermute | solution.py:220
  595.9 20.0 %collective-permute-start.15 = (bf16[512,128]{0,1:T(8,128)(2,1)S(1)}, bf16[512,128]{0,1:T(8,128)(2,1)S(1)}, u32[]{:S(2)}, u32[]{:S(2)}) collective-permute-start(bf16[512,128]{0,1:T(8,128)(2,1)S(1)} %dynamic-slice_convert_fusion.3), channel_id=1, source_target_pairs={{0,8},{8,0},{16,24},{24,16},{1,9},{9,1},{17,25},{25,17},{2,10},{10... | collective-permute-start | bytes 393224 | tf_op jit(solution)/shard_map/ppermute | solution.py:220
  596.9 26.7 %collective-permute-start.12 = (bf16[960,256]{1,0:T(8,128)(2,1)}, bf16[960,256]{1,0:T(8,128)(2,1)}, u32[]{:S(2)}, u32[]{:S(2)}) collective-permute-start(bf16[960,256]{1,0:T(8,128)(2,1)} %slice.137), channel_id=1, source_target_pairs={{0,2},{2,0},{1,3},{3,1},{4,6},{6,4},{5,7},{7,5},{8,10},{10,8},{9,1... | collective-permute-start | bytes 1474568 | tf_op jit(solution)/shard_map/ppermute | solution.py:196
  613.7 14.3 %collective-permute-start.13 = (bf16[960,256]{1,0:T(8,128)(2,1)}, bf16[960,256]{1,0:T(8,128)(2,1)}, u32[]{:S(2)}, u32[]{:S(2)}) collective-permute-start(bf16[960,256]{1,0:T(8,128)(2,1)} %slice.138), channel_id=1, source_target_pairs={{0,1},{1,0},{2,3},{3,2},{4,5},{5,4},{6,7},{7,6},{8,9},{9,8},{10,11... | collective-permute-start | bytes 1474568 | tf_op jit(solution)/shard_map/ppermute | solution.py:196
  615.8 2.7 collective-permute-start.17
  621.2 13.6 %collective-permute-start.6 = (bf16[960,256]{1,0:T(8,128)(2,1)S(1)}, bf16[960,256]{1,0:T(8,128)(2,1)S(1)}, u32[]{:S(2)}, u32[]{:S(2)}) collective-permute-start(bf16[960,256]{1,0:T(8,128)(2,1)S(1)} %slice.130), channel_id=1, source_target_pairs={{0,2},{2,0},{1,3},{3,1},{4,6},{6,4},{5,7},{7,5},{8,10},{10,8},{9,1... | collective-permute-start | bytes 1474568 | tf_op jit(solution)/shard_map/ppermute | solution.py:196
  622.4 9.1 %copy-start.14 = (bf16[4,256,256]{2,1,0:T(8,128)(2,1)S(1)}, bf16[4,256,256]{2,1,0:T(8,128)(2,1)}, u32[]{:S(2)}) copy-start(bf16[4,256,256]{2,1,0:T(8,128)(2,1)} %gather_fusion.4) | copy-start | bytes 1572868
  622.4 15.7 %collective-permute-start.7 = (bf16[960,256]{1,0:T(8,128)(2,1)S(1)}, bf16[960,256]{1,0:T(8,128)(2,1)S(1)}, u32[]{:S(2)}, u32[]{:S(2)}) collective-permute-start(bf16[960,256]{1,0:T(8,128)(2,1)S(1)} %slice.131), channel_id=1, source_target_pairs={{0,1},{1,0},{2,3},{3,2},{4,5},{5,4},{6,7},{7,6},{8,9},{9,8},{10,11... | collective-permute-start | bytes 1474568 | tf_op jit(solution)/shard_map/ppermute | solution.py:196
  632.7 5.3 copy-start.13
  (14 other events, 37.2 us)

commit v2 on v1

--- a/solution.py
+++ b/solution.py
@@ -60,8 +60,8 @@
 
 
 def attention_kernel(
-    places, lens, counts, q_ref, b_ref, recv_ref, co_ref, ds_ref,
-    kv, scores, probs, top, acc, total, dacc, sems, *, slots, scale,
+    places, lens, counts, q_ref, b_ref, recv_ref, co_ref, ds_ref, stat_ref,
+    kv, scores, probs, top, acc, total, dacc, columns, sems, *, slots, scale,
 ):
     patch = pl.program_id(0)
     patches = pl.num_programs(0)
@@ -105,61 +105,70 @@
         return kv[patch % 2, head, pl.ds(pl.multiple_of(t * pair, pair), pair), :]
 
     rows = q_ref.shape[0]
-    for head in range(2):
-        lanes = pl.ds(head * LANES, LANES)
-        q = q_ref[:, lanes]
-        back = b_ref[:, lanes]
-        top[...] = jnp.full_like(top, masked_value)
-        acc[...] = jnp.zeros_like(acc)
-        total[...] = jnp.zeros_like(total)
-        dacc[...] = jnp.zeros_like(dacc)
-
-        @pl.loop(0, tiles)
-        def _(t):
-            place = lax.broadcasted_iota(jnp.int32, (1, block_rows), 1)
-            seen_lo = place < lens[patch * slots + 2 * t]
-            seen_hi = place < lens[patch * slots + 2 * t + 1]
-            score = nt_dot(q, key_tile(t, head))
+    lanes = [pl.ds(head * LANES, LANES) for head in range(2)]
+    top[...] = jnp.full_like(top, masked_value)
+    acc[...] = jnp.zeros_like(acc)
+    total[...] = jnp.zeros_like(total)
+    dacc[...] = jnp.zeros_like(dacc)
+
+    @pl.loop(0, tiles)
+    def _(t):
+        place = lax.broadcasted_iota(jnp.int32, (1, block_rows), 1)
+        seen_lo = place < lens[patch * slots + 2 * t]
+        seen_hi = place < lens[patch * slots + 2 * t + 1]
+        for head in range(2):
+            score = nt_dot(q_ref[:, lanes[head]], key_tile(t, head))
             low = jnp.where(seen_lo, score[:, :block_rows], masked_value)
             high = jnp.where(seen_hi, score[:, block_rows:], masked_value)
-            scores[t, :, :block_rows] = low
-            scores[t, :, block_rows:] = high
-            top[...] = jnp.maximum(top[...], jnp.maximum(low, high))
-
-        row_max = jnp.max(top[...], axis=1, keepdims=True)
-
-        @pl.loop(0, tiles)
-        def _(t):
-            weights = jnp.exp(scores[t] - row_max).astype(jnp.bfloat16)
-            probs[t] = weights
+            scores[head, t, :, :block_rows] = low
+            scores[head, t, :, block_rows:] = high
+            top[head] = jnp.maximum(top[head], jnp.maximum(low, high))
+
+    row_max = [jnp.max(top[head], axis=1, keepdims=True) for head in range(2)]
+
+    @pl.loop(0, tiles)
+    def _(t):
+        for head in range(2):
+            weights = jnp.exp(scores[head, t] - row_max[head]).astype(jnp.bfloat16)
+            probs[head, t] = weights
             wide = weights.astype(jnp.float32)
-            total[...] += wide[:, :block_rows] + wide[:, block_rows:]
-            acc[...] += jnp.dot(
-                weights, key_tile(t, head), preferred_element_type=jnp.float32
+            total[head] += wide[:, :block_rows] + wide[:, block_rows:]
+            acc[head] += jnp.dot(weights, key_tile(t, head), preferred_element_type=jnp.float32)
+
+    inverse, inner, stats = [], [], []
+    for head in range(2):
+        row_sum = jnp.sum(total[head], axis=1, keepdims=True)
+        inverse.append(1.0 / row_sum)
+        outs = acc[head] * inverse[head]
+        co_ref[:, lanes[head]] = outs
+        inner.append(
+            jnp.sum(outs * b_ref[:, lanes[head]].astype(jnp.float32), axis=1, keepdims=True)
+        )
+        stats += [row_max[head] + jnp.log(row_sum), inner[head]]
+
+    @pl.loop(0, tiles)
+    def _(t):
+        for head in range(2):
+            dprobs = nt_dot(b_ref[:, lanes[head]], key_tile(t, head))
+            dscores = (probs[head, t].astype(jnp.float32) * (dprobs - inner[head])).astype(
+                jnp.bfloat16
             )
-
-        row_sum = jnp.sum(total[...], axis=1, keepdims=True)
-        inverse = 1.0 / row_sum
-        outs = acc[...] * inverse
-        inner = jnp.sum(outs * back.astype(jnp.float32), axis=1, keepdims=True)
-
-        @pl.loop(0, tiles)
-        def _(t):
-            dprobs = nt_dot(back, key_tile(t, head))
-            dscores = (probs[t].astype(jnp.float32) * (dprobs - inner)).astype(jnp.bfloat16)
-            dacc[...] += jnp.dot(
-                dscores, key_tile(t, head), preferred_element_type=jnp.float32
-            )
-
-        co_ref[:, lanes] = outs
-        lane = lax.broadcasted_iota(jnp.int32, (rows, LANES), 1)
-        stat = jnp.where(lane < 96, row_max + jnp.log(row_sum), inner)
-        ds_ref[:, lanes] = jnp.where(lane < 64, dacc[...] * (inverse * scale), stat)
+            dacc[head] += jnp.dot(dscores, key_tile(t, head), preferred_element_type=jnp.float32)
+
+    for head in range(2):
+        ds_ref[:, lanes[head]] = dacc[head] * (inverse[head] * scale)
+    lane = lax.broadcasted_iota(jnp.int32, (rows, LANES), 1)
+    columns[rows:, :] = jnp.zeros((columns.shape[0] - rows, LANES), jnp.float32)
+    picked = jnp.where(lane == 0, stats[0], stats[1])
+    picked = jnp.where(lane == 2, stats[2], picked)
+    columns[:rows, :] = jnp.where(lane == 3, stats[3], picked)
+    stat_ref[0] = jnp.transpose(columns[...])[:8]
 
 
 def attention(places, lens, counts, queries, backs, received, chunk, patch_blocks, slots, scale):
     rows = queries.shape[0] // patch_blocks
     total_rows = queries.shape[0]
+    padded = pl.cdiv(rows, LANES) * LANES
     block_rows, width = received.shape[2:]
     wide = pl.BlockSpec((rows, 2 * LANES), lambda p, *_: (p, chunk))
     out = pl.BlockSpec((rows, 2 * LANES), lambda p, *_: (p, 0))
@@ -170,20 +179,22 @@
             num_scalar_prefetch=3,
             grid=(patch_blocks,),
             in_specs=[wide, wide, pl.BlockSpec(memory_space=pl.ANY)],
-            out_specs=[out, out],
+            out_specs=[out, out, pl.BlockSpec((1, 8, padded), lambda p, *_: (p, 0, 0))],
             scratch_shapes=[
                 pltpu.VMEM((2, 2, tiles * 2 * block_rows, width), jnp.bfloat16),
-                pltpu.VMEM((tiles, rows, 2 * block_rows), jnp.float32),
-                pltpu.VMEM((tiles, rows, 2 * block_rows), jnp.bfloat16),
-                pltpu.VMEM((rows, block_rows), jnp.float32),
-                pltpu.VMEM((rows, width), jnp.float32),
-                pltpu.VMEM((rows, block_rows), jnp.float32),
-                pltpu.VMEM((rows, width), jnp.float32),
+                pltpu.VMEM((2, tiles, rows, 2 * block_rows), jnp.float32),
+                pltpu.VMEM((2, tiles, rows, 2 * block_rows), jnp.bfloat16),
+                pltpu.VMEM((2, rows, block_rows), jnp.float32),
+                pltpu.VMEM((2, rows, width), jnp.float32),
+                pltpu.VMEM((2, rows, block_rows), jnp.float32),
+                pltpu.VMEM((2, rows, width), jnp.float32),
+                pltpu.VMEM((padded, LANES), jnp.float32),
                 pltpu.SemaphoreType.DMA((2, slots)),
             ],
         ),
-        out_shape=[jax.ShapeDtypeStruct((total_rows, 2 * LANES), jnp.float32)] * 2,
-        compiler_params=pltpu.CompilerParams(vmem_limit_bytes=44 << 20),
+        out_shape=[jax.ShapeDtypeStruct((total_rows, 2 * LANES), jnp.float32)] * 2
+        + [jax.ShapeDtypeStruct((patch_blocks, 8, padded), jnp.float32)],
+        compiler_params=pltpu.CompilerParams(vmem_limit_bytes=48 << 20),
         cost_estimate=pl.CostEstimate(
             flops=8 * total_rows * slots * block_rows * width,
             transcendentals=total_rows * slots * block_rows,
@@ -192,21 +203,100 @@
     )(places, lens, counts, queries, backs, received)
 
 
+def merge_kernel(co_ref, ds_ref, mine_ref, theirs_ref, out_ref, *, scale, split):
+    rows = co_ref.shape[0]
+    mine, theirs = mine_ref[0], theirs_ref[0]
+    kind = lax.broadcasted_iota(jnp.int32, mine.shape, 0)
+    gap = mine - theirs
+    share = 1.0 / (1.0 + jnp.exp(-gap))
+    rest = 1.0 / (1.0 + jnp.exp(gap))
+    rest_below = jnp.concatenate([rest[:1], rest[:-1]], axis=0)
+    table = jnp.where(kind % 2 == 0, share, rest_below * gap * scale)
+    tall = jnp.transpose(
+        jnp.concatenate([table, jnp.zeros((LANES - 8, table.shape[1]), jnp.float32)], axis=0)
+    )[:rows]
+    lower = lax.broadcasted_iota(jnp.int32, (rows, LANES), 1) < split
+    for head in range(2):
+        lanes = pl.ds(head * LANES, LANES)
+        weight = tall[:, 2 * head : 2 * head + 1]
+        shift = tall[:, 2 * head + 1 : 2 * head + 2]
+        outs = co_ref[:, lanes]
+        value = weight * jnp.where(lower, ds_ref[:, lanes] + shift * outs, outs)
+        out_ref[:, lanes] = value.astype(jnp.bfloat16)
+
+
+def merge(outs, douts, mine, theirs, scale, split):
+    patch_blocks, _, padded = mine.shape
+    rows = outs.shape[0] // patch_blocks
+    wide = pl.BlockSpec((rows, 2 * LANES), lambda p: (p, 0))
+    flat = pl.BlockSpec((1, 8, padded), lambda p: (p, 0, 0))
+    return pl.pallas_call(
+        functools.partial(merge_kernel, scale=scale, split=split),
+        grid=(patch_blocks,),
+        in_specs=[wide, wide, flat, flat],
+        out_specs=wide,
+        out_shape=jax.ShapeDtypeStruct(outs.shape, jnp.bfloat16),
+        cost_estimate=pl.CostEstimate(
+            flops=10 * outs.size, transcendentals=0, bytes_accessed=10 * outs.size
+        ),
+    )(outs, douts, mine, theirs)
+
+
+def project_kernel(*refs, count, last):
+    pieces, weights = refs[:count], refs[count]
+    value = jnp.dot(pieces[0][...], weights[0], preferred_element_type=jnp.float32)
+    for i in range(1, count):
+        value += jnp.dot(pieces[i][...], weights[i], preferred_element_type=jnp.float32)
+    rest = refs[count + 1 :]
+    if not last:
+        rest[-1][...] = value if len(rest) == 1 else rest[0][...] + value
+        return
+    if len(rest) == 3:
+        value += rest[0][...]
+    width = rest[-1].shape[1]
+    rest[-2][...] = value[:, :width].astype(jnp.bfloat16)
+    rest[-1][...] = value[:, width:].astype(jnp.bfloat16)
+
+
+def project(pieces, weights, before, last):
+    count = len(pieces)
+    total_rows, depth = pieces[0].shape
+    width = weights.shape[2]
+    tile = total_rows // 4
+    rowwise = lambda w: pl.BlockSpec((tile, w), lambda i: (i, 0))
+    halves = jax.ShapeDtypeStruct((total_rows, width // 2), jnp.bfloat16)
+    return pl.pallas_call(
+        functools.partial(project_kernel, count=count, last=last),
+        grid=(4,),
+        in_specs=[rowwise(depth)] * count
+        + [pl.BlockSpec(weights.shape, lambda i: (0, 0, 0))]
+        + ([] if before is None else [rowwise(width)]),
+        out_specs=[rowwise(width // 2)] * 2 if last else rowwise(width),
+        out_shape=[halves] * 2
+        if last
+        else jax.ShapeDtypeStruct((total_rows, width), jnp.float32),
+        compiler_params=pltpu.CompilerParams(vmem_limit_bytes=40 << 20),
+        cost_estimate=pl.CostEstimate(
+            flops=2 * total_rows * depth * count * width,
+            transcendentals=0,
+            bytes_accessed=2 * total_rows * (depth * count + 2 * width),
+        ),
+    )(*pieces, weights, *([] if before is None else [before]))
+
+
 def swap(x, axis):
     return lax.ppermute(x, axis, [(0, 1), (1, 0)])
 
 
 def gather_half(x, zl_size, y_size):
     if zl_size == 2 and y_size == 2:
-        place = 2 * lax.axis_index("zl") + lax.axis_index("y")
         cut = x.shape[0] // 2
         by_y = swap(x, "y")
         by_zl = swap(x, "zl")
         corner = jnp.concatenate([swap(by_y[:cut], "zl"), swap(by_zl[cut:], "y")], axis=0)
-        return [x, by_y, by_zl, corner], jnp.stack([place, place ^ 1, place ^ 2, place ^ 3])
+        return [x, by_y, by_zl, corner]
     whole = lax.all_gather(x, ("zl", "y"), axis=0, tiled=False)
-    count = zl_size * y_size
-    return [whole[i] for i in range(count)], jnp.arange(count, dtype=jnp.int32)
+    return [whole[i] for i in range(zl_size * y_size)]
 
 
 def scatter_sum(x, size, dim):
@@ -261,18 +351,17 @@
     ).reshape(groups * capacity)
     send_counts = jnp.sum(match.astype(jnp.int32), axis=1)
 
-    packed = [
-        pack_blocks(
+    def pack(c):
+        return pack_blocks(
             chosen, send_counts, cache, c, groups, inner, capacity, local_heads
         ).reshape(groups * inner, capacity * 2 * block_rows, width)
-        for c in range(local_heads)
-    ]
-    received = [
-        lax.all_to_all(x, ("dp", "zl", "y"), split_axis=0, concat_axis=0, tiled=True).reshape(
-            groups * inner * capacity, 2, block_rows, width
-        )
-        for x in packed
-    ]
+
+    def exchange(x):
+        return lax.all_to_all(
+            x, ("dp", "zl", "y"), split_axis=0, concat_axis=0, tiled=True
+        ).reshape(groups * inner * capacity, 2, block_rows, width)
+
+    received = [exchange(pack(0))]
 
     my_ids = lax.dynamic_slice_in_dim(
         neighbours, group * patch_blocks, patch_blocks, 0
@@ -282,9 +371,16 @@
     source = (owners // model) * inner + owners % inner
     in_half = ((owners % model) // inner == zh).reshape(patch_blocks, slots)
     arrival = (source * capacity + slot_of).reshape(patch_blocks, slots)
-    every_length = lax.all_gather(
-        block_lengths, ("dp", "zh", "zl", "y"), axis=0, tiled=True
-    )
+    every_length = lax.dynamic_update_slice_in_dim(
+        jnp.zeros((owner_count * local_blocks,), jnp.int32), block_lengths, me * local_blocks, 0
+    )
+    for axis, size in (("y", y_size), ("zl", zl_size), ("dp", groups)):
+        step = 1
+        while step < size:
+            every_length += lax.ppermute(
+                every_length, axis, [(i, i ^ step) for i in range(size)]
+            )
+            step *= 2
     entry_length = every_length[my_ids].reshape(patch_blocks, slots)
     spots = jnp.arange(slots, dtype=jnp.int32)
     before = jnp.sum(
@@ -316,60 +412,52 @@
     ).astype(jnp.bfloat16)
     backs = nt_dot(cotangent, o_wide).astype(jnp.bfloat16)
 
-    mp = ("zh", "zl", "y")
-    o_cols = output_proj.reshape(local_heads * head_size, model, columns).transpose(1, 0, 2)
-    o_cols = lax.all_to_all(o_cols, mp, split_axis=0, concat_axis=0, tiled=True)
-    o_cols = o_cols.reshape(2, inner, local_heads, head_size, columns)
-    q_cols = query_proj.reshape(model, columns, local_heads * head_size).transpose(0, 2, 1)
-    q_cols = lax.all_to_all(q_cols, mp, split_axis=0, concat_axis=0, tiled=True)
-    q_cols = q_cols.reshape(2, inner, local_heads, head_size, columns)
-
-    def tail_weights(cols, c, first, order):
-        piece = jnp.moveaxis(cols[:, :, c], 0, 1)
-        empty = jnp.zeros_like(piece)
-        pair = [piece, empty] if first else [empty, piece]
-        stacked = jnp.stack(pair, axis=2).reshape(inner, 2 * LANES, columns)
-        return stacked[order].reshape(inner * 2 * LANES, columns)
-
-    lane = jnp.arange(2 * LANES, dtype=jnp.int32)
-    lower = (lane % LANES < head_size)[None, :]
-    first_head = (lane < LANES)[None, :]
-    attended = None
-    patch_grad = None
+    places, lens, counts, queries, backs, cache = lax.optimization_barrier(
+        (places, lens, counts, queries, backs, cache)
+    )
+    for c in range(1, local_heads):
+        received.append(exchange(pack(c)))
+
+    cols = jnp.concatenate(
+        [
+            output_proj.reshape(local_heads * head_size, model, columns).transpose(1, 0, 2),
+            query_proj.reshape(model, columns, local_heads * head_size).transpose(0, 2, 1),
+        ],
+        axis=2,
+    )
+    cols, received[-1] = lax.optimization_barrier((cols, received[-1]))
+    cols = lax.all_to_all(cols, ("zh", "zl", "y"), split_axis=0, concat_axis=0, tiled=True)
+    cols = cols.reshape(2, inner, local_heads, head_size, 2 * columns)
+    right = jnp.arange(2 * columns)[None, None, None, :] >= columns
+    if zl_size == 2 and y_size == 2:
+        order = jnp.stack([spot, spot ^ 1, spot ^ 2, spot ^ 3])
+    else:
+        order = jnp.arange(inner, dtype=jnp.int32)
+
+    def tail_weights(c):
+        both = jnp.moveaxis(cols[:, :, c], 0, 1)
+        pair = [jnp.where(right, both, 0), jnp.where(right, 0, both)]
+        return jnp.stack(pair, axis=2).reshape(inner, 2 * LANES, 2 * columns)[order]
+
+    finals = [tail_weights(c) for c in range(local_heads)]
+
+    result = None
     own = []
     for c in range(local_heads):
-        outs, douts = attention(
+        outs, douts, mine = attention(
             places, lens, counts, queries, backs, received[c], c, patch_blocks, slots, head_scale
         )
-        lse = douts[:, 64], douts[:, LANES + 64]
-        inner_sum = douts[:, 96], douts[:, LANES + 96]
-        theirs = swap(jnp.stack(lse + inner_sum), "zh")
-
-        def per_head(pair):
-            return jnp.where(first_head, pair[0][:, None], pair[1][:, None])
-
-        weight = per_head([jax.nn.sigmoid(lse[i] - theirs[i]) for i in range(2)])
-        shift = per_head(
-            [
-                jax.nn.sigmoid(theirs[i] - lse[i]) * (inner_sum[i] - theirs[2 + i]) * head_scale
-                for i in range(2)
-            ]
-        )
-        part = weight * jnp.where(lower, douts + shift * outs, outs)
-        merged = (part + swap(part.astype(jnp.bfloat16), "zh").astype(jnp.float32)).astype(
+        theirs = swap(mine, "zh")
+        part = merge(outs, douts, mine, theirs, head_scale, head_size)
+        merged = (part.astype(jnp.float32) + swap(part, "zh").astype(jnp.float32)).astype(
             jnp.bfloat16
         )
-        pieces, order = gather_half(merged, zl_size, y_size)
-        every = jnp.concatenate(pieces, axis=1)
-        att = jnp.dot(
-            every, tail_weights(o_cols, c, False, order), preferred_element_type=jnp.float32
-        )
-        grad = jnp.dot(
-            every, tail_weights(q_cols, c, True, order), preferred_element_type=jnp.float32
-        )
-        attended = att if attended is None else attended + att
-        patch_grad = grad if patch_grad is None else patch_grad + grad
+        if c + 1 < local_heads:
+            merged, received[c + 1] = lax.optimization_barrier((merged, received[c + 1]))
+        pieces = gather_half(merged, zl_size, y_size)
+        result = project(pieces, finals[c], result, c + 1 == local_heads)
         own.append(lax.dynamic_slice_in_dim(merged, zh * LANES, LANES, 1))
+    attended, patch_grad = result
 
     dquery = jnp.concatenate([x[:, :head_size] for x in own], axis=1)
     heads_out = jnp.concatenate([x[:, head_size:] for x in own], axis=1)
@@ -386,8 +474,8 @@
         * grad_scale
     )
     return (
-        attended.astype(jnp.bfloat16),
-        patch_grad.astype(jnp.bfloat16),
+        attended,
+        patch_grad,
         scatter_sum(query_term, groups, 0),
         scatter_sum(output_term, groups, 1),
     )

time: 653 us -> 502 us (0.77)
  blocking collectives: 141 us -> 0 us
  waiting for transfers between devices: 203 us -> 256 us
  Pallas kernels: 142 us -> 112 us
  other arithmetic: 30.7 us -> 12.9 us
  local copies, waits for them, and re-layouts: 55.2 us -> 43 us
  starting transfers between devices: 47.5 us -> 58.4 us
  matrix products: 25.2 us -> 16.1 us
    unnamed x1 -> x0, blocking collectives: 141 us -> none
    ppermute x0 -> x4, waiting for transfers between devices: none -> 117 us  [local(): lax.ppermute(every_length, axis, [(i, i ^ step) for i in range(size)])]
    all_to_all x4 -> x3, waiting for transfers between devices: 97.2 us -> 18.6 us  [the longest x2 18.6 us: exchange(): lax.all_to_all(x, ('dp', 'zl', 'y'), split_axis=0, concat_axis=0, tiled=T...]
    pallas_call x2, Pallas kernels: 134 us -> 85.7 us  [attention(): pl.pallas_call(functools.partial(attention_kernel, slots=slots, scale=sca...]
    ppermute x14, starting transfers between devices: 15.6 us -> 37.9 us  [swap(): return lax.ppermute(x, axis, [(0, 1), (1, 0)])]
    pallas_call x0 -> x4, Pallas kernels: none -> 17.4 us  [the longest x2 9.51 us: merge(): pl.pallas_call(functools.partial(merge_kernel, scale=scale, split=split),...]
    ppermute x14, waiting for transfers between devices: 97.2 us -> 110 us  [swap(): return lax.ppermute(x, axis, [(0, 1), (1, 0)])]
    dot_general x4 -> x0, matrix products: 10.3 us -> none  [the longest x2 5.19 us: local(): jnp.dot(every, tail_weights(q_cols, c, True, order), preferred_element_ty...]
  transfers between devices with their start and end apart: 22 -> 25, of which waited for: 11 -> 14; matrix products, arithmetic and copies ran while one was open for 12% -> 9% of each run, Pallas kernels for 21% -> 12%
where the time goes in v2:
time: 502 us; the launch traced here: 500 us
  waiting for transfers between devices  256 us (51%)
  Pallas kernels  112 us (22%)
  starting transfers between devices  58.4 us (12%)
  local copies, waits for them, and re-layouts  43 us (9%)
  matrix products  16.1 us (3%)
  other arithmetic  12.9 us (3%)
    ppermute x4, waiting for transfers between devices, local(): lax.ppermute(every_length, axis, [(i, i ^ step) for i in range(size)])  117 us
    ppermute x14, waiting for transfers between devices, swap(): return lax.ppermute(x, axis, [(0, 1), (1, 0)])  110 us
    pallas_call x2, Pallas kernels, attention(): pl.pallas_call(functools.partial(attention_kernel, slots=slots, scale=sca...  85.7 us
    ppermute x14, starting transfers between devices, swap(): return lax.ppermute(x, axis, [(0, 1), (1, 0)])  37.9 us
    unnamed x68, local copies, waits for them, and re-layouts  26.1 us
    all_to_all x2, waiting for transfers between devices, exchange(): lax.all_to_all(x, ('dp', 'zl', 'y'), split_axis=0, concat_axis=0, tiled=T...  18.6 us
    all_to_all x2, starting transfers between devices, exchange(): lax.all_to_all(x, ('dp', 'zl', 'y'), split_axis=0, concat_axis=0, tiled=T...  11.4 us
    ppermute x4, waiting for transfers between devices, scatter_sum(): lax.ppermute(give.astype(jnp.bfloat16), 'dp', [(i, i ^ step) for i in ran...  10.6 us
  transfers between devices with their start and end apart: 25, of which 14 were waited for; matrix products, arithmetic and copies ran while one was open for 9% of the time, Pallas kernels for 12%

profile of v2, /device:TPU:0, one launch (start us, length us, event | category | flops | bytes accessed | tf_op | source)
XLA Modules:
  0.0 500.1 jit_solution(8449436932040944537)
XLA Ops:
  2.9 3.4 copy-done
  6.3 4.4 shard_map.102
  10.7 3.3 copy-done.1
  14.0 6.5 %all-to-all-start = ((bf16[16,2048,128]{2,1,0:T(8,128)(2,1)}), bf16[16,2048,128]{2,1,0:T(8,128)(2,1)}, u32[]{:S(2)}, u32[]{:S(2)}) async-start(bf16[16,2048,128]{2,1,0:T(8,128)(2,1)} %bitcast.73), calls=%async_computation | async-start | bytes 16777216 | tf_op jit(solution)/shard_map/all_to_all | solution.py:360
  22.9 2.7 collective-permute-start.4
  27.2 19.0 %collective-permute-done = s32[512]{0:T(512)S(1)} collective-permute-done((s32[512]{0:T(512)S(1)}, s32[512]{0:T(512)S(1)}, u32[]{:S(2)}, u32[]{:S(2)}) %collective-permute-start) | collective-permute-done | bytes 2080 | tf_op jit(solution)/shard_map/ppermute | solution.py:380
  47.8 93.7 %collective-permute-done.1 = s32[512]{0:T(512)S(1)} collective-permute-done((s32[512]{0:T(512)S(1)}, s32[512]{0:T(512)S(1)}, u32[]{:S(2)}, u32[]{:S(2)}) %collective-permute-start.1) | collective-permute-done | bytes 2080 | tf_op jit(solution)/shard_map/ppermute | solution.py:380
  143.1 3.2 collective-permute-done.3
  151.4 4.3 fusion.3.q_ref
  155.7 5.6 %fusion.2.b_ref = bf16[1920,512]{1,0:T(8,128)(2,1)} fusion(bf16[512,2048]{1,0:T(8,128)(2,1)S(1)} %bitcast.84, bf16[1920,2048]{1,0:T(8,128)(2,1)S(1)} %bitcast.76), kind=kOutput, calls=%fused_computation.8 | convolution fusion | flops 4027514880 | bytes 11927552 | tf_op jit(solution)/shard_map/dot_general | solution.py:57
  161.4 5.0 shard_map.105
  166.3 3.3 copy-done.2
  169.6 4.9 all-to-all-start.1
  174.5 42.8 %shard_map.103 = (f32[1920,256]{1,0:T(8,128)S(1)}, f32[1920,256]{1,0:T(8,128)S(1)}, f32[4,8,512]{2,1,0:T(8,128)S(1)}) custom-call(s32[128]{0:T(128)S(1)} %reshape.537.places, s32[128]{0:T(128)S(1)} %reshape.539.lens, s32[4]{0:T(128)S(1)} %get-tuple-element.24.counts, bf16[1920,512]{1,0:T(8,128)(2,1)S(1)} %fusion.3.q_ref, bf16[1920,512]{1,0:T(8,128)(2,1)} %fusion.2.b_ref, ...), custom_call_target="tpu_custom_call" | custom-call | flops 8053063680 | bytes 41943040 | tf_op jit(solution)/shard_map/pallas_call | solution.py:176
  220.0 14.7 %collective-permute-start.6 = (f32[4,8,512]{2,1,0:T(8,128)S(1)}, f32[4,8,512]{2,1,0:T(8,128)S(1)}, u32[]{:S(2)}, u32[]{:S(2)}) collective-permute-start(f32[4,8,512]{2,1,0:T(8,128)S(1)} %get-tuple-element.29.mine_ref), channel_id=1, source_target_pairs={{0,4},{4,0},{1,5},{5,1},{2,6},{6,2},{3,7},{7,3},{8,12},{12,8},{9,1... | collective-permute-start | bytes 196616 | tf_op jit(solution)/shard_map/ppermute | solution.py:288
  234.7 32.9 %collective-permute-done.6.theirs_ref = f32[4,8,512]{2,1,0:T(8,128)S(1)} collective-permute-done((f32[4,8,512]{2,1,0:T(8,128)S(1)}, f32[4,8,512]{2,1,0:T(8,128)S(1)}, u32[]{:S(2)}, u32[]{:S(2)}) %collective-permute-start.6) | collective-permute-done | bytes 65568 | tf_op jit(solution)/shard_map/ppermute | solution.py:288
  268.2 4.8 shard_map.104
  272.9 3.4 collective-permute-start.7
  277.7 18.6 %all-to-all-done.1 = bf16[16,2048,128]{2,1,0:T(8,128)(2,1)} async-done(((bf16[16,2048,128]{2,1,0:T(8,128)(2,1)}), bf16[16,2048,128]{2,1,0:T(8,128)(2,1)}, u32[]{:S(2)}, u32[]{:S(2)}) %all-to-all-start.1) | async-done | bytes 8388640 | tf_op jit(solution)/shard_map/all_to_all | solution.py:360
  296.3 24.7 %collective-permute-done.7 = bf16[1920,256]{1,0:T(8,128)(2,1)} collective-permute-done((bf16[1920,256]{1,0:T(8,128)(2,1)}, bf16[1920,256]{1,0:T(8,128)(2,1)}, u32[]{:S(2)}, u32[]{:S(2)}) %collective-permute-start.7) | collective-permute-done | bytes 983072 | tf_op jit(solution)/shard_map/ppermute | solution.py:288
  324.0 42.8 %shard_map.106 = (f32[1920,256]{1,0:T(8,128)S(1)}, f32[1920,256]{1,0:T(8,128)S(1)}, f32[4,8,512]{2,1,0:T(8,128)S(1)}) custom-call(s32[128]{0:T(128)S(1)} %reshape.537.places, s32[128]{0:T(128)S(1)} %reshape.539.lens, s32[4]{0:T(128)S(1)} %get-tuple-element.24.counts, bf16[1920,512]{1,0:T(8,128)(2,1)S(1)} %copy-done.15, bf16[1920,512]{1,0:T(8,128)(2,1)} %fusion.2.b_ref, ...), custom_call_target="tpu_custom_call" | custom-call | flops 8053063680 | bytes 41943040 | tf_op jit(solution)/shard_map/pallas_call | solution.py:176
  369.5 6.9 %collective-permute-start.8 = (f32[4,8,512]{2,1,0:T(8,128)S(1)}, f32[4,8,512]{2,1,0:T(8,128)S(1)}, u32[]{:S(2)}, u32[]{:S(2)}) collective-permute-start(f32[4,8,512]{2,1,0:T(8,128)S(1)} %get-tuple-element.35.mine_ref), channel_id=1, source_target_pairs={{0,4},{4,0},{1,5},{5,1},{2,6},{6,2},{3,7},{7,3},{8,12},{12,8},{9,1... | collective-permute-start | bytes 196616 | tf_op jit(solution)/shard_map/ppermute | solution.py:288
  377.8 3.0 collective-permute-start.15
  381.4 4.8 shard_map.107
  387.6 4.7 all-to-all-start.2
  392.6 8.4 %collective-permute-done.14.refs_1_ = bf16[1920,256]{1,0:T(8,128)(2,1)S(1)} collective-permute-done((bf16[1920,256]{1,0:T(8,128)(2,1)S(1)}, bf16[1920,256]{1,0:T(8,128)(2,1)S(1)}, u32[]{:S(2)}, u32[]{:S(2)}) %collective-permute-start.14) | collective-permute-done | bytes 983072 | tf_op jit(solution)/shard_map/ppermute | solution.py:288
  402.0 15.1 %collective-permute-done.15.refs_2_ = bf16[1920,256]{1,0:T(8,128)(2,1)S(1)} collective-permute-done((bf16[1920,256]{1,0:T(8,128)(2,1)S(1)}, bf16[1920,256]{1,0:T(8,128)(2,1)S(1)}, u32[]{:S(2)}, u32[]{:S(2)}) %collective-permute-start.15) | collective-permute-done | bytes 983072 | tf_op jit(solution)/shard_map/ppermute | solution.py:288
  417.9 26.5 %collective-permute-done.9 = bf16[1920,256]{1,0:T(8,128)(2,1)} collective-permute-done((bf16[1920,256]{1,0:T(8,128)(2,1)}, bf16[1920,256]{1,0:T(8,128)(2,1)}, u32[]{:S(2)}, u32[]{:S(2)}) %collective-permute-start.9) | collective-permute-done | bytes 983072 | tf_op jit(solution)/shard_map/ppermute | solution.py:288
  448.2 4.8 convolution_multiply_fusion
  455.2 5.1 %collective-permute-done.20 = bf16[128,1024]{1,0:T(8,128)(2,1)S(1)} collective-permute-done((bf16[128,1024]{1,0:T(8,128)(2,1)S(1)}, bf16[128,1024]{1,0:T(8,128)(2,1)S(1)}, u32[]{:S(2)}, u32[]{:S(2)}) %collective-permute-start.20) | collective-permute-done | bytes 262176 | tf_op jit(solution)/shard_map/ppermute | solution.py:310
  461.1 5.5 %collective-permute-done.18 = bf16[1024,128]{0,1:T(8,128)(2,1)S(1)} collective-permute-done((bf16[1024,128]{0,1:T(8,128)(2,1)S(1)}, bf16[1024,128]{0,1:T(8,128)(2,1)S(1)}, u32[]{:S(2)}, u32[]{:S(2)}) %collective-permute-start.18) | collective-permute-done | bytes 262176 | tf_op jit(solution)/shard_map/ppermute | solution.py:310
  494.9 5.2 %shard_map.109 = (bf16[1920,256]{1,0:T(8,128)(2,1)}, bf16[1920,256]{1,0:T(8,128)(2,1)}) custom-call(bf16[1920,256]{1,0:T(8,128)(2,1)S(1)} %add_convert_fusion.refs_0_, bf16[1920,256]{1,0:T(8,128)(2,1)} %collective-permute-done.10.refs_1_, bf16[1920,256]{1,0:T(8,128)(2,1)} %collective-permute-done.11.refs_2_, ...), custom_call_target="tpu_custom_call" | custom-call | flops 2013265920 | bytes 7864320 | tf_op jit(solution)/shard_map/pallas_call | solution.py:268
  (168 shorter events, 65.1 us)
Async XLA Ops:
  14.0 11.6 %copy-start.18 = (bf16[128,2048]{1,0:T(8,128)(2,1)S(1)}, bf16[128,2048]{1,0:T(8,128)(2,1)}, u32[]{:S(2)}) copy-start(bf16[128,2048]{1,0:T(8,128)(2,1)} %param.9) | copy-start | bytes 1572868
  14.0 155.6 %all-to-all-start = ((bf16[16,2048,128]{2,1,0:T(8,128)(2,1)}), bf16[16,2048,128]{2,1,0:T(8,128)(2,1)}, u32[]{:S(2)}, u32[]{:S(2)}) async-start(bf16[16,2048,128]{2,1,0:T(8,128)(2,1)} %bitcast.73), calls=%async_computation | async-start | bytes 16777216 | tf_op jit(solution)/shard_map/all_to_all | solution.py:360
  20.8 25.4 %collective-permute-start = (s32[512]{0:T(512)S(1)}, s32[512]{0:T(512)S(1)}, u32[]{:S(2)}, u32[]{:S(2)}) collective-permute-start(s32[512]{0:T(512)S(1)} %dynamic_update_slice.5), channel_id=1, source_target_pairs={{0,1},{1,0},{2,3},{3,2},{4,5},{5,4},{6,7},{7,6},{8,9},{9,8},{10,11... | collective-permute-start | bytes 6152 | tf_op jit(solution)/shard_map/ppermute | solution.py:380
  22.9 125.1 %collective-permute-start.4 = (bf16[2048,128]{0,1:T(8,128)(2,1)S(1)}, bf16[2048,128]{0,1:T(8,128)(2,1)S(1)}, u32[]{:S(2)}, u32[]{:S(2)}) collective-permute-start(bf16[2048,128]{0,1:T(8,128)(2,1)S(1)} %copy.48), channel_id=1, source_target_pairs={{0,4},{4,0},{1,5},{5,1},{2,6},{6,2},{3,7},{7,3},{8,12},{12,8},{9,1... | collective-permute-start | bytes 1572872 | tf_op jit(solution)/shard_map/ppermute | solution.py:288
  25.6 122.9 %collective-permute-start.5 = (bf16[128,2048]{1,0:T(8,128)(2,1)S(1)}, bf16[128,2048]{1,0:T(8,128)(2,1)S(1)}, u32[]{:S(2)}, u32[]{:S(2)}) collective-permute-start(bf16[128,2048]{1,0:T(8,128)(2,1)S(1)} %copy-done.18), channel_id=1, source_target_pairs={{0,4},{4,0},{1,5},{5,1},{2,6},{6,2},{3,7},{7,3},{8,12},{12,8},{9,1... | collective-permute-start | bytes 1572872 | tf_op jit(solution)/shard_map/ppermute | solution.py:288
  46.3 95.2 %collective-permute-start.1 = (s32[512]{0:T(512)S(1)}, s32[512]{0:T(512)S(1)}, u32[]{:S(2)}, u32[]{:S(2)}) collective-permute-start(s32[512]{0:T(512)S(1)} %add_dynamic-update-slice_fusion), channel_id=1, source_target_pairs={{0,2},{2,0},{1,3},{3,1},{4,6},{6,4},{5,7},{7,5},{8,10},{10,8},{9,1... | collective-permute-start | bytes 6152 | tf_op jit(solution)/shard_map/ppermute | solution.py:380
  141.5 1.2 collective-permute-start.2
  142.7 3.6 collective-permute-start.3
  155.7 18.9 %copy-start.14 = (bf16[1920,512]{1,0:T(8,128)(2,1)}, bf16[1920,512]{1,0:T(8,128)(2,1)S(1)}, u32[]{:S(2)}) copy-start(bf16[1920,512]{1,0:T(8,128)(2,1)S(1)} %fusion.3.q_ref) | copy-start | bytes 5898244
  169.6 126.7 %all-to-all-start.1 = ((bf16[16,2048,128]{2,1,0:T(8,128)(2,1)}), bf16[16,2048,128]{2,1,0:T(8,128)(2,1)}, u32[]{:S(2)}, u32[]{:S(2)}) async-start(bf16[16,2048,128]{2,1,0:T(8,128)(2,1)} %bitcast.74), calls=%async_computation.1 | async-start | bytes 16777216 | tf_op jit(solution)/shard_map/all_to_all | solution.py:360
  220.0 47.5 %copy-start.13 = (f32[4,8,512]{2,1,0:T(8,128)}, f32[4,8,512]{2,1,0:T(8,128)S(1)}, u32[]{:S(2)}) copy-start(f32[4,8,512]{2,1,0:T(8,128)S(1)} %get-tuple-element.29.mine_ref) | copy-start | bytes 196612
  220.0 47.5 %collective-permute-start.6 = (f32[4,8,512]{2,1,0:T(8,128)S(1)}, f32[4,8,512]{2,1,0:T(8,128)S(1)}, u32[]{:S(2)}, u32[]{:S(2)}) collective-permute-start(f32[4,8,512]{2,1,0:T(8,128)S(1)} %get-tuple-element.29.mine_ref), channel_id=1, source_target_pairs={{0,4},{4,0},{1,5},{5,1},{2,6},{6,2},{3,7},{7,3},{8,12},{12,8},{9,1... | collective-permute-start | bytes 196616 | tf_op jit(solution)/shard_map/ppermute | solution.py:288
  272.9 48.1 %copy-start.17 = (bf16[1920,256]{1,0:T(8,128)(2,1)S(1)}, bf16[1920,256]{1,0:T(8,128)(2,1)}, u32[]{:S(2)}) copy-start(bf16[1920,256]{1,0:T(8,128)(2,1)} %shard_map.104) | copy-start | bytes 2949124
  272.9 48.1 %collective-permute-start.7 = (bf16[1920,256]{1,0:T(8,128)(2,1)}, bf16[1920,256]{1,0:T(8,128)(2,1)}, u32[]{:S(2)}, u32[]{:S(2)}) collective-permute-start(bf16[1920,256]{1,0:T(8,128)(2,1)} %shard_map.104), channel_id=1, source_target_pairs={{0,4},{4,0},{1,5},{5,1},{2,6},{6,2},{3,7},{7,3},{8,12},{12,8},{9,1... | collective-permute-start | bytes 2949128 | tf_op jit(solution)/shard_map/ppermute | solution.py:288
  369.5 11.3 %collective-permute-start.8 = (f32[4,8,512]{2,1,0:T(8,128)S(1)}, f32[4,8,512]{2,1,0:T(8,128)S(1)}, u32[]{:S(2)}, u32[]{:S(2)}) collective-permute-start(f32[4,8,512]{2,1,0:T(8,128)S(1)} %get-tuple-element.35.mine_ref), channel_id=1, source_target_pairs={{0,4},{4,0},{1,5},{5,1},{2,6},{6,2},{3,7},{7,3},{8,12},{12,8},{9,1... | collective-permute-start | bytes 196616 | tf_op jit(solution)/shard_map/ppermute | solution.py:288
  376.3 24.7 %collective-permute-start.14 = (bf16[1920,256]{1,0:T(8,128)(2,1)S(1)}, bf16[1920,256]{1,0:T(8,128)(2,1)S(1)}, u32[]{:S(2)}, u32[]{:S(2)}) collective-permute-start(bf16[1920,256]{1,0:T(8,128)(2,1)S(1)} %add_convert_fusion.1.refs_0_), channel_id=1, source_target_pairs={{0,1},{1,0},{2,3},{3,2},{4,5},{5,4},{6,7},{7,6},{8,9},{9,8},{10,11... | collective-permute-start | bytes 2949128 | tf_op jit(solution)/shard_map/ppermute | solution.py:288
  377.8 39.3 %collective-permute-start.15 = (bf16[1920,256]{1,0:T(8,128)(2,1)S(1)}, bf16[1920,256]{1,0:T(8,128)(2,1)S(1)}, u32[]{:S(2)}, u32[]{:S(2)}) collective-permute-start(bf16[1920,256]{1,0:T(8,128)(2,1)S(1)} %add_convert_fusion.1.refs_0_), channel_id=1, source_target_pairs={{0,2},{2,0},{1,3},{3,1},{4,6},{6,4},{5,7},{7,5},{8,10},{10,8},{9,1... | collective-permute-start | bytes 2949128 | tf_op jit(solution)/shard_map/ppermute | solution.py:288
  386.2 58.3 %collective-permute-start.9 = (bf16[1920,256]{1,0:T(8,128)(2,1)}, bf16[1920,256]{1,0:T(8,128)(2,1)}, u32[]{:S(2)}, u32[]{:S(2)}) collective-permute-start(bf16[1920,256]{1,0:T(8,128)(2,1)} %shard_map.107), channel_id=1, source_target_pairs={{0,4},{4,0},{1,5},{5,1},{2,6},{6,2},{3,7},{7,3},{8,12},{12,8},{9,1... | collective-permute-start | bytes 2949128 | tf_op jit(solution)/shard_map/ppermute | solution.py:288
  387.6 79.9 %all-to-all-start.2 = ((bf16[8,128,512]{1,2,0:T(8,128)(2,1)}), bf16[8,128,512]{1,2,0:T(8,128)(2,1)}, u32[]{:S(2)}, u32[]{:S(2)}) async-start(bf16[8,128,512]{1,2,0:T(8,128)(2,1)} %pad_maximum_fusion.1), calls=%async_computation.2 | async-start | bytes 2097152 | tf_op jit(solution)/shard_map/all_to_all | solution.py:429
  392.3 52.2 %copy-start.16 = (bf16[1920,256]{1,0:T(8,128)(2,1)S(1)}, bf16[1920,256]{1,0:T(8,128)(2,1)}, u32[]{:S(2)}) copy-start(bf16[1920,256]{1,0:T(8,128)(2,1)} %shard_map.107) | copy-start | bytes 2949124
  401.0 16.9 %copy-start.4 = (bf16[1920,256]{1,0:T(8,128)(2,1)}, bf16[1920,256]{1,0:T(8,128)(2,1)S(1)}, u32[]{:S(2)}) copy-start(bf16[1920,256]{1,0:T(8,128)(2,1)S(1)} %collective-permute-done.14.refs_1_) | copy-start | bytes 2949124
  401.9 82.9 %collective-permute-start.16 = (bf16[960,256]{1,0:T(8,128)(2,1)}, bf16[960,256]{1,0:T(8,128)(2,1)}, u32[]{:S(2)}, u32[]{:S(2)}) collective-permute-start(bf16[960,256]{1,0:T(8,128)(2,1)} %slice.49), channel_id=1, source_target_pairs={{0,2},{2,0},{1,3},{3,1},{4,6},{6,4},{5,7},{7,5},{8,10},{10,8},{9,1... | collective-permute-start | bytes 1474568 | tf_op jit(solution)/shard_map/ppermute | solution.py:288
  417.1 29.2 %copy-start.6 = (bf16[1920,256]{1,0:T(8,128)(2,1)}, bf16[1920,256]{1,0:T(8,128)(2,1)S(1)}, u32[]{:S(2)}) copy-start(bf16[1920,256]{1,0:T(8,128)(2,1)S(1)} %collective-permute-done.15.refs_2_) | copy-start | bytes 2949124
  417.9 66.9 %collective-permute-start.17 = (bf16[960,256]{1,0:T(8,128)(2,1)}, bf16[960,256]{1,0:T(8,128)(2,1)}, u32[]{:S(2)}, u32[]{:S(2)}) collective-permute-start(bf16[960,256]{1,0:T(8,128)(2,1)} %slice.50), channel_id=1, source_target_pairs={{0,1},{1,0},{2,3},{3,2},{4,5},{5,4},{6,7},{7,6},{8,9},{9,8},{10,11... | collective-permute-start | bytes 1474568 | tf_op jit(solution)/shard_map/ppermute | solution.py:288
  446.3 29.9 %collective-permute-start.10 = (bf16[1920,256]{1,0:T(8,128)(2,1)S(1)}, bf16[1920,256]{1,0:T(8,128)(2,1)}, u32[]{:S(2)}, u32[]{:S(2)}) collective-permute-start(bf16[1920,256]{1,0:T(8,128)(2,1)S(1)} %add_convert_fusion.refs_0_), channel_id=1, source_target_pairs={{0,1},{1,0},{2,3},{3,2},{4,5},{5,4},{6,7},{7,6},{8,9},{9,8},{10,11... | collective-permute-start | bytes 2949128 | tf_op jit(solution)/shard_map/ppermute | solution.py:288
  447.0 31.3 %collective-permute-start.11 = (bf16[1920,256]{1,0:T(8,128)(2,1)S(1)}, bf16[1920,256]{1,0:T(8,128)(2,1)}, u32[]{:S(2)}, u32[]{:S(2)}) collective-permute-start(bf16[1920,256]{1,0:T(8,128)(2,1)S(1)} %add_convert_fusion.refs_0_), channel_id=1, source_target_pairs={{0,2},{2,0},{1,3},{3,1},{4,6},{6,4},{5,7},{7,5},{8,10},{10,8},{9,1... | collective-permute-start | bytes 2949128 | tf_op jit(solution)/shard_map/ppermute | solution.py:288
  453.1 7.2 %collective-permute-start.20 = (bf16[128,1024]{1,0:T(8,128)(2,1)S(1)}, bf16[128,1024]{1,0:T(8,128)(2,1)S(1)}, u32[]{:S(2)}, u32[]{:S(2)}) collective-permute-start(bf16[128,1024]{1,0:T(8,128)(2,1)S(1)} %dynamic-slice_convert_fusion), channel_id=1, source_target_pairs={{0,16},{8,24},{16,0},{24,8},{1,17},{9,25},{17,1},{25,9},{2,18},{10... | collective-permute-start | bytes 786440 | tf_op jit(solution)/shard_map/ppermute | solution.py:310
  460.3 6.4 %collective-permute-start.18 = (bf16[1024,128]{0,1:T(8,128)(2,1)S(1)}, bf16[1024,128]{0,1:T(8,128)(2,1)S(1)}, u32[]{:S(2)}, u32[]{:S(2)}) collective-permute-start(bf16[1024,128]{0,1:T(8,128)(2,1)S(1)} %fusion.11), channel_id=1, source_target_pairs={{0,16},{8,24},{16,0},{24,8},{1,17},{9,25},{17,1},{25,9},{2,18},{10... | collective-permute-start | bytes 786440 | tf_op jit(solution)/shard_map/ppermute | solution.py:310
  466.7 7.2 %collective-permute-start.21 = (bf16[128,512]{1,0:T(8,128)(2,1)}, bf16[128,512]{1,0:T(8,128)(2,1)}, u32[]{:S(2)}, u32[]{:S(2)}) collective-permute-start(bf16[128,512]{1,0:T(8,128)(2,1)} %dynamic-slice_convert_fusion.2), channel_id=1, source_target_pairs={{0,8},{8,0},{16,24},{24,16},{1,9},{9,1},{17,25},{25,17},{2,10},{10... | collective-permute-start | bytes 393224 | tf_op jit(solution)/shard_map/ppermute | solution.py:310
  473.9 8.3 %collective-permute-start.19 = (bf16[512,128]{0,1:T(8,128)(2,1)}, bf16[512,128]{0,1:T(8,128)(2,1)S(1)}, u32[]{:S(2)}, u32[]{:S(2)}) collective-permute-start(bf16[512,128]{0,1:T(8,128)(2,1)} %dynamic-slice_convert_fusion.3), channel_id=1, source_target_pairs={{0,8},{8,0},{16,24},{24,16},{1,9},{9,1},{17,25},{25,17},{2,10},{10... | collective-permute-start | bytes 393224 | tf_op jit(solution)/shard_map/ppermute | solution.py:310
  478.1 13.5 %collective-permute-start.12 = (bf16[960,256]{1,0:T(8,128)(2,1)}, bf16[960,256]{1,0:T(8,128)(2,1)}, u32[]{:S(2)}, u32[]{:S(2)}) collective-permute-start(bf16[960,256]{1,0:T(8,128)(2,1)} %slice.46), channel_id=1, source_target_pairs={{0,2},{2,0},{1,3},{3,1},{4,6},{6,4},{5,7},{7,5},{8,10},{10,8},{9,1... | collective-permute-start | bytes 1474568 | tf_op jit(solution)/shard_map/ppermute | solution.py:288
  480.1 13.6 %collective-permute-start.13 = (bf16[960,256]{1,0:T(8,128)(2,1)}, bf16[960,256]{1,0:T(8,128)(2,1)}, u32[]{:S(2)}, u32[]{:S(2)}) collective-permute-start(bf16[960,256]{1,0:T(8,128)(2,1)} %slice.47), channel_id=1, source_target_pairs={{0,1},{1,0},{2,3},{3,2},{4,5},{5,4},{6,7},{7,6},{8,9},{9,8},{10,11... | collective-permute-start | bytes 1474568 | tf_op jit(solution)/shard_map/ppermute | solution.py:288
  (25 other events, 97.6 us)

commit v3 on v2

--- a/solution.py
+++ b/solution.py
@@ -46,7 +46,7 @@
         out_shape=jax.ShapeDtypeStruct(
             (groups, inner, capacity, 2, block_rows, width), cache.dtype
         ),
-        compiler_params=pltpu.CompilerParams(vmem_limit_bytes=32 << 20),
+        compiler_params=pltpu.CompilerParams(vmem_limit_bytes=58 << 20),
         cost_estimate=pl.CostEstimate(
             flops=0, transcendentals=0, bytes_accessed=groups * capacity * 2 * 262144
         ),
@@ -61,10 +61,10 @@
 
 def attention_kernel(
     places, lens, counts, q_ref, b_ref, recv_ref, co_ref, ds_ref, stat_ref,
-    kv, scores, probs, top, acc, total, dacc, columns, sems, *, slots, scale,
+    kv, scores, probs, top, acc, total, dacc, columns, sems, *, slots, scale, first,
 ):
-    patch = pl.program_id(0)
-    patches = pl.num_programs(0)
+    patch = first + pl.program_id(0)
+    patches = first + pl.num_programs(0)
     block_rows = recv_ref.shape[2]
     pair = 2 * block_rows
 
@@ -80,7 +80,7 @@
         def _(j):
             copy(which, j, places[which * slots + j]).start()
 
-    @pl.when(patch == 0)
+    @pl.when(patch == first)
     def _():
         start(patch)
 
@@ -165,16 +165,17 @@
     stat_ref[0] = jnp.transpose(columns[...])[:8]
 
 
-def attention(places, lens, counts, queries, backs, received, chunk, patch_blocks, slots, scale):
-    rows = queries.shape[0] // patch_blocks
-    total_rows = queries.shape[0]
+def attention(
+    places, lens, counts, queries, backs, received, chunk, first, patch_blocks, rows, slots, scale
+):
+    total_rows = patch_blocks * rows
     padded = pl.cdiv(rows, LANES) * LANES
     block_rows, width = received.shape[2:]
-    wide = pl.BlockSpec((rows, 2 * LANES), lambda p, *_: (p, chunk))
+    wide = pl.BlockSpec((rows, 2 * LANES), lambda p, *_: (first + p, chunk))
     out = pl.BlockSpec((rows, 2 * LANES), lambda p, *_: (p, 0))
     tiles = (slots + 1) // 2
     return pl.pallas_call(
-        functools.partial(attention_kernel, slots=slots, scale=scale),
+        functools.partial(attention_kernel, slots=slots, scale=scale, first=first),
         grid_spec=pltpu.PrefetchScalarGridSpec(
             num_scalar_prefetch=3,
             grid=(patch_blocks,),
@@ -194,7 +195,7 @@
         ),
         out_shape=[jax.ShapeDtypeStruct((total_rows, 2 * LANES), jnp.float32)] * 2
         + [jax.ShapeDtypeStruct((patch_blocks, 8, padded), jnp.float32)],
-        compiler_params=pltpu.CompilerParams(vmem_limit_bytes=48 << 20),
+        compiler_params=pltpu.CompilerParams(vmem_limit_bytes=58 << 20),
         cost_estimate=pl.CostEstimate(
             flops=8 * total_rows * slots * block_rows * width,
             transcendentals=total_rows * slots * block_rows,
@@ -225,50 +226,69 @@
         out_ref[:, lanes] = value.astype(jnp.bfloat16)
 
 
-def merge(outs, douts, mine, theirs, scale, split):
+def merge(outs, douts, mine, theirs, first, count, scale, split):
     patch_blocks, _, padded = mine.shape
     rows = outs.shape[0] // patch_blocks
-    wide = pl.BlockSpec((rows, 2 * LANES), lambda p: (p, 0))
-    flat = pl.BlockSpec((1, 8, padded), lambda p: (p, 0, 0))
+    wide = pl.BlockSpec((rows, 2 * LANES), lambda p: (first + p, 0))
+    flat = pl.BlockSpec((1, 8, padded), lambda p: (first + p, 0, 0))
     return pl.pallas_call(
         functools.partial(merge_kernel, scale=scale, split=split),
-        grid=(patch_blocks,),
+        grid=(count,),
         in_specs=[wide, wide, flat, flat],
-        out_specs=wide,
-        out_shape=jax.ShapeDtypeStruct(outs.shape, jnp.bfloat16),
+        out_specs=pl.BlockSpec((rows, 2 * LANES), lambda p: (p, 0)),
+        out_shape=jax.ShapeDtypeStruct((count * rows, 2 * LANES), jnp.bfloat16),
         cost_estimate=pl.CostEstimate(
-            flops=10 * outs.size, transcendentals=0, bytes_accessed=10 * outs.size
+            flops=20 * count * rows * LANES,
+            transcendentals=0,
+            bytes_accessed=20 * count * rows * LANES,
         ),
     )(outs, douts, mine, theirs)
 
 
-def project_kernel(*refs, count, last):
-    pieces, weights = refs[:count], refs[count]
-    value = jnp.dot(pieces[0][...], weights[0], preferred_element_type=jnp.float32)
-    for i in range(1, count):
-        value += jnp.dot(pieces[i][...], weights[i], preferred_element_type=jnp.float32)
-    rest = refs[count + 1 :]
-    if not last:
-        rest[-1][...] = value if len(rest) == 1 else rest[0][...] + value
-        return
-    if len(rest) == 3:
-        value += rest[0][...]
-    width = rest[-1].shape[1]
-    rest[-2][...] = value[:, :width].astype(jnp.bfloat16)
-    rest[-1][...] = value[:, width:].astype(jnp.bfloat16)
-
-
-def project(pieces, weights, before, last):
-    count = len(pieces)
-    total_rows, depth = pieces[0].shape
+def project_kernel(*refs, count, parts, last):
+    step = pl.program_id(0)
+    weights = refs[count * parts]
+    rest = refs[count * parts + 1 :]
+    before = rest[0] if len(rest) == (3 if last else 2) else None
+
+    def part(pieces):
+        value = jnp.dot(pieces[0][...], weights[0], preferred_element_type=jnp.float32)
+        for i in range(1, count):
+            value += jnp.dot(pieces[i][...], weights[i], preferred_element_type=jnp.float32)
+        if before is not None:
+            value += before[...]
+        if last:
+            width = rest[-1].shape[1]
+            rest[-2][...] = value[:, :width].astype(jnp.bfloat16)
+            rest[-1][...] = value[:, width:].astype(jnp.bfloat16)
+        else:
+            rest[-1][...] = value
+
+    for i in range(parts):
+        pl.when(step * parts // pl.num_programs(0) == i)(
+            functools.partial(part, refs[i * count : (i + 1) * count])
+        )
+
+
+def project(parts, weights, before, last):
+    count = len(parts[0])
+    rows, depth = parts[0][0].shape
+    total_rows = rows * len(parts)
     width = weights.shape[2]
-    tile = total_rows // 4
+    steps = 4 // len(parts)
+    tile = rows // steps
     rowwise = lambda w: pl.BlockSpec((tile, w), lambda i: (i, 0))
+
+    def within(which):
+        return pl.BlockSpec(
+            (tile, depth), lambda i: (jnp.clip(i - which * steps, 0, steps - 1), 0)
+        )
+
     halves = jax.ShapeDtypeStruct((total_rows, width // 2), jnp.bfloat16)
     return pl.pallas_call(
-        functools.partial(project_kernel, count=count, last=last),
+        functools.partial(project_kernel, count=count, parts=len(parts), last=last),
         grid=(4,),
-        in_specs=[rowwise(depth)] * count
+        in_specs=[within(i) for i in range(len(parts)) for _ in range(count)]
         + [pl.BlockSpec(weights.shape, lambda i: (0, 0, 0))]
         + ([] if before is None else [rowwise(width)]),
         out_specs=[rowwise(width // 2)] * 2 if last else rowwise(width),
@@ -281,19 +301,18 @@
             transcendentals=0,
             bytes_accessed=2 * total_rows * (depth * count + 2 * width),
         ),
-    )(*pieces, weights, *([] if before is None else [before]))
+    )(*[x for pieces in parts for x in pieces], weights, *([] if before is None else [before]))
 
 
 def swap(x, axis):
     return lax.ppermute(x, axis, [(0, 1), (1, 0)])
 
 
-def gather_half(x, zl_size, y_size):
+def gather_half(x, zl_size, y_size, y_first):
     if zl_size == 2 and y_size == 2:
-        cut = x.shape[0] // 2
         by_y = swap(x, "y")
         by_zl = swap(x, "zl")
-        corner = jnp.concatenate([swap(by_y[:cut], "zl"), swap(by_zl[cut:], "y")], axis=0)
+        corner = swap(by_y, "zl") if y_first else swap(by_zl, "y")
         return [x, by_y, by_zl, corner]
     whole = lax.all_gather(x, ("zl", "y"), axis=0, tiled=False)
     return [whole[i] for i in range(zl_size * y_size)]
@@ -361,7 +380,30 @@
             x, ("dp", "zl", "y"), split_axis=0, concat_axis=0, tiled=True
         ).reshape(groups * inner * capacity, 2, block_rows, width)
 
-    received = [exchange(pack(0))]
+    cols = jnp.concatenate(
+        [
+            output_proj.reshape(local_heads * head_size, model, columns).transpose(1, 0, 2),
+            query_proj.reshape(model, columns, local_heads * head_size).transpose(0, 2, 1),
+        ],
+        axis=2,
+    )
+    cols = lax.all_to_all(cols, ("zh", "zl", "y"), split_axis=0, concat_axis=0, tiled=True)
+
+    every_length = lax.dynamic_update_slice_in_dim(
+        jnp.zeros((owner_count * local_blocks,), jnp.int32), block_lengths, me * local_blocks, 0
+    )
+    for axis, size in (("y", y_size), ("zl", zl_size), ("dp", groups)):
+        step = 1
+        while step < size:
+            every_length += lax.ppermute(
+                every_length, axis, [(i, i ^ step) for i in range(size)]
+            )
+            step *= 2
+
+    packed, cols, every_length = lax.optimization_barrier((pack(0), cols, every_length))
+    received = [exchange(packed)]
+    cols = cols.reshape(2, inner, local_heads, head_size, 2 * columns)
+
 
     my_ids = lax.dynamic_slice_in_dim(
         neighbours, group * patch_blocks, patch_blocks, 0
@@ -371,16 +413,6 @@
     source = (owners // model) * inner + owners % inner
     in_half = ((owners % model) // inner == zh).reshape(patch_blocks, slots)
     arrival = (source * capacity + slot_of).reshape(patch_blocks, slots)
-    every_length = lax.dynamic_update_slice_in_dim(
-        jnp.zeros((owner_count * local_blocks,), jnp.int32), block_lengths, me * local_blocks, 0
-    )
-    for axis, size in (("y", y_size), ("zl", zl_size), ("dp", groups)):
-        step = 1
-        while step < size:
-            every_length += lax.ppermute(
-                every_length, axis, [(i, i ^ step) for i in range(size)]
-            )
-            step *= 2
     entry_length = every_length[my_ids].reshape(patch_blocks, slots)
     spots = jnp.arange(slots, dtype=jnp.int32)
     before = jnp.sum(
@@ -412,22 +444,6 @@
     ).astype(jnp.bfloat16)
     backs = nt_dot(cotangent, o_wide).astype(jnp.bfloat16)
 
-    places, lens, counts, queries, backs, cache = lax.optimization_barrier(
-        (places, lens, counts, queries, backs, cache)
-    )
-    for c in range(1, local_heads):
-        received.append(exchange(pack(c)))
-
-    cols = jnp.concatenate(
-        [
-            output_proj.reshape(local_heads * head_size, model, columns).transpose(1, 0, 2),
-            query_proj.reshape(model, columns, local_heads * head_size).transpose(0, 2, 1),
-        ],
-        axis=2,
-    )
-    cols, received[-1] = lax.optimization_barrier((cols, received[-1]))
-    cols = lax.all_to_all(cols, ("zh", "zl", "y"), split_axis=0, concat_axis=0, tiled=True)
-    cols = cols.reshape(2, inner, local_heads, head_size, 2 * columns)
     right = jnp.arange(2 * columns)[None, None, None, :] >= columns
     if zl_size == 2 and y_size == 2:
         order = jnp.stack([spot, spot ^ 1, spot ^ 2, spot ^ 3])
@@ -441,22 +457,51 @@
 
     finals = [tail_weights(c) for c in range(local_heads)]
 
+    places, lens, counts, queries, backs, finals, cache = lax.optimization_barrier(
+        (places, lens, counts, queries, backs, finals, cache)
+    )
+    for c in range(1, local_heads):
+        received.append(exchange(pack(c)))
+
+
+    rows = row_count // patch_blocks
+    part_count = 2 if patch_blocks % 2 == 0 else 1
+    part_patches = patch_blocks // part_count
     result = None
     own = []
     for c in range(local_heads):
-        outs, douts, mine = attention(
-            places, lens, counts, queries, backs, received[c], c, patch_blocks, slots, head_scale
-        )
-        theirs = swap(mine, "zh")
-        part = merge(outs, douts, mine, theirs, head_scale, head_size)
-        merged = (part.astype(jnp.float32) + swap(part, "zh").astype(jnp.float32)).astype(
-            jnp.bfloat16
-        )
-        if c + 1 < local_heads:
-            merged, received[c + 1] = lax.optimization_barrier((merged, received[c + 1]))
-        pieces = gather_half(merged, zl_size, y_size)
-        result = project(pieces, finals[c], result, c + 1 == local_heads)
-        own.append(lax.dynamic_slice_in_dim(merged, zh * LANES, LANES, 1))
+        final = c + 1 == local_heads
+        calls = part_count if final else 1
+        call_patches = patch_blocks // calls
+        sums = []
+        for call in range(calls):
+            outs, douts, mine = attention(
+                places, lens, counts, queries, backs, received[c], c,
+                call * call_patches, call_patches, rows, slots, head_scale,
+            )
+            theirs = swap(mine, "zh")
+            for start in range(0, call_patches, part_patches):
+                part = merge(
+                    outs, douts, mine, theirs, start, part_patches, head_scale, head_size
+                )
+                sums.append((part, swap(part, "zh")))
+            if call + 1 < calls:
+                part, places = lax.optimization_barrier((part, places))
+        if not final:
+            part, places = lax.optimization_barrier((part, places))
+        merged = [
+            (part.astype(jnp.float32) + other.astype(jnp.float32)).astype(jnp.bfloat16)
+            for part, other in sums
+        ]
+        pieces = [
+            gather_half(x, zl_size, y_size, i % 2 == 0) for i, x in enumerate(merged)
+        ]
+        result = project(pieces, finals[c], result, final)
+        own.append(
+            jnp.concatenate(
+                [lax.dynamic_slice_in_dim(x, zh * LANES, LANES, 1) for x in merged], axis=0
+            )
+        )
     attended, patch_grad = result
 
     dquery = jnp.concatenate([x[:, :head_size] for x in own], axis=1)

time: 502 us -> 539 us (1.074)
  Pallas kernels: 112 us -> 163 us
  local copies, waits for them, and re-layouts: 43 us -> 16.7 us
  starting transfers between devices: 58.4 us -> 77.2 us
  waiting for transfers between devices: 256 us -> 249 us
    ppermute x4, waiting for transfers between devices: 117 us -> 12 us  [local(): lax.ppermute(every_length, axis, [(i, i ^ step) for i in range(size)])]
    ppermute x14 -> x21, waiting for transfers between devices: 110 us -> 211 us  [swap(): return lax.ppermute(x, axis, [(0, 1), (1, 0)])]
    pallas_call x2, Pallas kernels: 9.34 us -> 37.7 us  [pack_blocks(): pl.pallas_call(functools.partial(pack_kernel, chunk=chunk, local_heads=lo...]
    pallas_call x2 -> x3, Pallas kernels: 85.7 us -> 104 us  [attention(): pl.pallas_call(functools.partial(attention_kernel, slots=slots, scale=sca...]
    unnamed x68 -> x44, local copies, waits for them, and re-layouts: 26.1 us -> 8.62 us
    all_to_all x2, starting transfers between devices: 11.4 us -> 26.8 us  [exchange(): lax.all_to_all(x, ('dp', 'zl', 'y'), split_axis=0, concat_axis=0, tiled=T...]
    ppermute x14 -> x21, starting transfers between devices: 37.9 us -> 30.1 us  [swap(): return lax.ppermute(x, axis, [(0, 1), (1, 0)])]
    slice x6 -> x0, local copies, waits for them, and re-layouts: 6.15 us -> none  [the longest x2 2.77 us: gather_half(): by_y[:cut]]
  transfers between devices with their start and end apart: 25 -> 32, of which waited for: 14 -> 17; matrix products, arithmetic and copies ran while one was open for 9% -> 7% of each run, Pallas kernels for 12% -> 29%
where the time goes in v3:
time: 539 us
  waiting for transfers between devices  249 us (46%)
  Pallas kernels  163 us (30%)
  starting transfers between devices  77.2 us (14%)
  matrix products  17 us (3%)
  local copies, waits for them, and re-layouts  16.7 us (3%)
  other arithmetic  14.3 us (3%)
    ppermute x21, waiting for transfers between devices, swap(): return lax.ppermute(x, axis, [(0, 1), (1, 0)])  211 us
    pallas_call x3, Pallas kernels, attention(): pl.pallas_call(functools.partial(attention_kernel, slots=slots, scale=sca...  104 us
    pallas_call x2, Pallas kernels, pack_blocks(): pl.pallas_call(functools.partial(pack_kernel, chunk=chunk, local_heads=lo...  37.7 us
    ppermute x21, starting transfers between devices, swap(): return lax.ppermute(x, axis, [(0, 1), (1, 0)])  30.1 us
    all_to_all x2, starting transfers between devices, exchange(): lax.all_to_all(x, ('dp', 'zl', 'y'), split_axis=0, concat_axis=0, tiled=T...  26.8 us
    all_to_all x2, waiting for transfers between devices, exchange(): lax.all_to_all(x, ('dp', 'zl', 'y'), split_axis=0, concat_axis=0, tiled=T...  15.4 us
    ppermute x4, waiting for transfers between devices, local(): lax.ppermute(every_length, axis, [(i, i ^ step) for i in range(size)])  12 us
    pallas_call x4, Pallas kernels, merge(): pl.pallas_call(functools.partial(merge_kernel, scale=scale, split=split),...  11.4 us
  transfers between devices with their start and end apart: 32, of which 17 were waited for; matrix products, arithmetic and copies ran while one was open for 7% of the time, Pallas kernels for 29%

profile of v3, /device:TPU:0, one launch (start us, length us, event | category | flops | bytes accessed | tf_op | source)
XLA Modules:
  0.0 538.5 jit_solution(12470227275486751565)
XLA Ops:
  4.1 7.3 %all-to-all-start = ((bf16[8,128,512]{1,2,0:T(8,128)(2,1)}), bf16[8,128,512]{1,2,0:T(8,128)(2,1)S(1)}, u32[]{:S(2)}, u32[]{:S(2)}) async-start(bf16[8,128,512]{1,2,0:T(8,128)(2,1)} %pad_maximum_fusion), calls=%async_computation | async-start | bytes 2097152 | tf_op jit(solution)/shard_map/all_to_all | solution.py:390
  13.8 4.5 collective-permute-done
  18.5 3.5 collective-permute-start.1
  22.1 6.5 %collective-permute-done.1 = s32[512]{0:T(512)S(1)} collective-permute-done((s32[512]{0:T(512)S(1)}, s32[512]{0:T(512)S(1)}, u32[]{:S(2)}, u32[]{:S(2)}) %collective-permute-start.1) | collective-permute-done | bytes 2080 | tf_op jit(solution)/shard_map/ppermute | solution.py:398
  32.7 18.8 %shard_map.102 = bf16[4,4,8,2,128,128]{5,4,3,2,1,0:T(8,128)(2,1)} custom-call(s32[32]{0:T(128)} %reshape.539.chosen, s32[4]{0:T(128)} %reduce_sum.89.counts, bf16[16,128,16,128]{3,2,1,0:T(8,128)(2,1)} %cache_ref.2), custom_call_target="tpu_custom_call" | custom-call | bytes 16777216 | tf_op jit(solution)/shard_map/pallas_call | solution.py:29
  51.5 7.3 %all-to-all-start.1 = ((bf16[16,2048,128]{2,1,0:T(8,128)(2,1)}), bf16[16,2048,128]{2,1,0:T(8,128)(2,1)}, u32[]{:S(2)}, u32[]{:S(2)}) async-start(bf16[16,2048,128]{2,1,0:T(8,128)(2,1)} %bitcast.71), calls=%async_computation.1 | async-start | bytes 16777216 | tf_op jit(solution)/shard_map/all_to_all | solution.py:379
  63.6 109.7 %collective-permute-done.4 = bf16[2048,128]{0,1:T(8,128)(2,1)S(1)} collective-permute-done((bf16[2048,128]{0,1:T(8,128)(2,1)S(1)}, bf16[2048,128]{0,1:T(8,128)(2,1)S(1)}, u32[]{:S(2)}, u32[]{:S(2)}) %collective-permute-start.4) | collective-permute-done | bytes 524320 | tf_op jit(solution)/shard_map/ppermute | solution.py:308
  176.7 5.4 %fusion.3.q_ref = bf16[1920,512]{1,0:T(8,128)(2,1)} fusion(bf16[2048,512]{0,1:T(8,128)(2,1)S(1)} %bitcast.83, bf16[1920,2048]{1,0:T(8,128)(2,1)S(1)} %bitcast.74), kind=kOutput, calls=%fused_computation.9 | convolution fusion | flops 4028497920 | bytes 11927552 | tf_op jit(solution)/shard_map/dot_general | solution.py:443
  182.2 5.4 %fusion.2.b_ref = bf16[1920,512]{1,0:T(8,128)(2,1)} fusion(bf16[512,2048]{1,0:T(8,128)(2,1)S(1)} %bitcast.82, bf16[1920,2048]{1,0:T(8,128)(2,1)S(1)} %bitcast.78), kind=kOutput, calls=%fused_computation.8 | convolution fusion | flops 4027514880 | bytes 11927552 | tf_op jit(solution)/shard_map/dot_general | solution.py:57
  192.6 18.9 %shard_map.105 = bf16[4,4,8,2,128,128]{5,4,3,2,1,0:T(8,128)(2,1)} custom-call(s32[32]{0:T(128)} %reshape.539.chosen, s32[4]{0:T(128)} %reduce_sum.89.counts, bf16[16,128,16,128]{3,2,1,0:T(8,128)(2,1)} %cache_ref.2), custom_call_target="tpu_custom_call" | custom-call | bytes 16777216 | tf_op jit(solution)/shard_map/pallas_call | solution.py:29
  211.5 19.5 %all-to-all-start.2 = ((bf16[16,2048,128]{2,1,0:T(8,128)(2,1)}), bf16[16,2048,128]{2,1,0:T(8,128)(2,1)}, u32[]{:S(2)}, u32[]{:S(2)}) async-start(bf16[16,2048,128]{2,1,0:T(8,128)(2,1)} %bitcast.72), calls=%async_computation.2 | async-start | bytes 16777216 | tf_op jit(solution)/shard_map/all_to_all | solution.py:379
  230.9 50.0 %shard_map.103 = (f32[1920,256]{1,0:T(8,128)}, f32[1920,256]{1,0:T(8,128)}, f32[4,8,512]{2,1,0:T(8,128)}) custom-call(s32[128]{0:T(128)} %reshape.537.places, s32[128]{0:T(128)} %reshape.544.lens, s32[4]{0:T(128)} %get-tuple-element.32.counts, bf16[1920,512]{1,0:T(8,128)(2,1)} %fusion.3.q_ref, bf16[1920,512]{1,0:T(8,128)(2,1)} %fusion.2.b_ref, ...), custom_call_target="tpu_custom_call" | custom-call | flops 8053063680 | bytes 41943040 | tf_op jit(solution)/shard_map/pallas_call | solution.py:177
  281.1 43.4 %collective-permute-done.6.theirs_ref = f32[4,8,512]{2,1,0:T(8,128)S(1)} collective-permute-done((f32[4,8,512]{2,1,0:T(8,128)}, f32[4,8,512]{2,1,0:T(8,128)S(1)}, u32[]{:S(2)}, u32[]{:S(2)}) %collective-permute-start.6) | collective-permute-done | bytes 65568 | tf_op jit(solution)/shard_map/ppermute | solution.py:308
  327.9 3.3 collective-permute-start.21
  331.2 15.4 %all-to-all-done.2 = bf16[16,2048,128]{2,1,0:T(8,128)(2,1)} async-done(((bf16[16,2048,128]{2,1,0:T(8,128)(2,1)}), bf16[16,2048,128]{2,1,0:T(8,128)(2,1)}, u32[]{:S(2)}, u32[]{:S(2)}) %all-to-all-start.2) | async-done | bytes 8388640 | tf_op jit(solution)/shard_map/all_to_all | solution.py:379
  346.6 25.0 %shard_map.106 = (f32[960,256]{1,0:T(8,128)}, f32[960,256]{1,0:T(8,128)}, f32[2,8,512]{2,1,0:T(8,128)}) custom-call(s32[128]{0:T(128)} %reshape.537.places, s32[128]{0:T(128)} %reshape.544.lens, s32[4]{0:T(128)} %get-tuple-element.32.counts, bf16[1920,512]{1,0:T(8,128)(2,1)} %fusion.3.q_ref, bf16[1920,512]{1,0:T(8,128)(2,1)} %fusion.2.b_ref, ...), custom_call_target="tpu_custom_call" | custom-call | flops 4026531840 | bytes 41943040 | tf_op jit(solution)/shard_map/pallas_call | solution.py:177
  374.5 2.9 collective-permute-start.17
  377.4 7.3 %collective-permute-done.7.theirs_ref = f32[2,8,512]{2,1,0:T(8,128)S(1)} collective-permute-done((f32[2,8,512]{2,1,0:T(8,128)}, f32[2,8,512]{2,1,0:T(8,128)S(1)}, u32[]{:S(2)}, u32[]{:S(2)}) %collective-permute-start.7) | collective-permute-done | bytes 32800 | tf_op jit(solution)/shard_map/ppermute | solution.py:308
  388.1 28.8 %shard_map.108 = (f32[960,256]{1,0:T(8,128)}, f32[960,256]{1,0:T(8,128)}, f32[2,8,512]{2,1,0:T(8,128)}) custom-call(s32[128]{0:T(128)} %reshape.537.places, s32[128]{0:T(128)} %reshape.544.lens, s32[4]{0:T(128)} %get-tuple-element.32.counts, bf16[1920,512]{1,0:T(8,128)(2,1)} %fusion.3.q_ref, bf16[1920,512]{1,0:T(8,128)(2,1)} %fusion.2.b_ref, ...), custom_call_target="tpu_custom_call" | custom-call | flops 4026531840 | bytes 41943040 | tf_op jit(solution)/shard_map/pallas_call | solution.py:177
  419.9 8.1 %collective-permute-done.12.theirs_ref = f32[2,8,512]{2,1,0:T(8,128)S(1)} collective-permute-done((f32[2,8,512]{2,1,0:T(8,128)}, f32[2,8,512]{2,1,0:T(8,128)S(1)}, u32[]{:S(2)}, u32[]{:S(2)}) %collective-permute-start.12) | collective-permute-done | bytes 32800 | tf_op jit(solution)/shard_map/ppermute | solution.py:308
  432.9 6.9 %collective-permute-start.22 = (bf16[960,256]{1,0:T(8,128)(2,1)S(1)}, bf16[960,256]{1,0:T(8,128)(2,1)S(1)}, u32[]{:S(2)}, u32[]{:S(2)}) collective-permute-start(bf16[960,256]{1,0:T(8,128)(2,1)S(1)} %add_convert_fusion.refs_4_), channel_id=1, source_target_pairs={{0,1},{1,0},{2,3},{3,2},{4,5},{5,4},{6,7},{7,6},{8,9},{9,8},{10,11... | collective-permute-start | bytes 1474568 | tf_op jit(solution)/shard_map/ppermute | solution.py:308
  444.5 4.6 collective-permute-done.13
  451.0 4.8 convolution_multiply_fusion
  455.8 5.9 %collective-permute-start.27 = (bf16[128,1024]{1,0:T(8,128)(2,1)S(1)}, bf16[128,1024]{1,0:T(8,128)(2,1)S(1)}, u32[]{:S(2)}, u32[]{:S(2)}) collective-permute-start(bf16[128,1024]{1,0:T(8,128)(2,1)S(1)} %dynamic-slice_convert_fusion), channel_id=1, source_target_pairs={{0,16},{8,24},{16,0},{24,8},{1,17},{9,25},{17,1},{25,9},{2,18},{10... | collective-permute-start | bytes 786440 | tf_op jit(solution)/shard_map/ppermute | solution.py:329
  463.3 5.6 %collective-permute-done.27 = bf16[128,1024]{1,0:T(8,128)(2,1)S(1)} collective-permute-done((bf16[128,1024]{1,0:T(8,128)(2,1)S(1)}, bf16[128,1024]{1,0:T(8,128)(2,1)S(1)}, u32[]{:S(2)}, u32[]{:S(2)}) %collective-permute-start.27) | collective-permute-done | bytes 262176 | tf_op jit(solution)/shard_map/ppermute | solution.py:329
  469.0 4.8 collective-permute-done.25
  481.7 7.5 %collective-permute-done.18.refs_1_ = bf16[960,256]{1,0:T(8,128)(2,1)} collective-permute-done((bf16[960,256]{1,0:T(8,128)(2,1)}, bf16[960,256]{1,0:T(8,128)(2,1)}, u32[]{:S(2)}, u32[]{:S(2)}) %collective-permute-start.18) | collective-permute-done | bytes 491552 | tf_op jit(solution)/shard_map/ppermute | solution.py:308
  491.3 8.5 %collective-permute-done.9.refs_1_ = bf16[960,256]{1,0:T(8,128)(2,1)} collective-permute-done((bf16[960,256]{1,0:T(8,128)(2,1)S(1)}, bf16[960,256]{1,0:T(8,128)(2,1)}, u32[]{:S(2)}, u32[]{:S(2)}) %collective-permute-start.9) | collective-permute-done | bytes 491552 | tf_op jit(solution)/shard_map/ppermute | solution.py:308
  501.8 8.5 %collective-permute-done.24.refs_7_ = bf16[960,256]{1,0:T(8,128)(2,1)} collective-permute-done((bf16[960,256]{1,0:T(8,128)(2,1)}, bf16[960,256]{1,0:T(8,128)(2,1)}, u32[]{:S(2)}, u32[]{:S(2)}) %collective-permute-start.24) | collective-permute-done | bytes 491552 | tf_op jit(solution)/shard_map/ppermute | solution.py:308
  516.9 4.6 shard_map.111.refs_9_
  522.8 9.8 %collective-permute-done.11.refs_3_ = bf16[960,256]{1,0:T(8,128)(2,1)} collective-permute-done((bf16[960,256]{1,0:T(8,128)(2,1)}, bf16[960,256]{1,0:T(8,128)(2,1)}, u32[]{:S(2)}, u32[]{:S(2)}) %collective-permute-start.11) | collective-permute-done | bytes 491552 | tf_op jit(solution)/shard_map/ppermute | solution.py:308
  532.6 5.9 %shard_map.112 = (bf16[1920,256]{1,0:T(8,128)(2,1)}, bf16[1920,256]{1,0:T(8,128)(2,1)}) custom-call(bf16[960,256]{1,0:T(8,128)(2,1)S(1)} %add_convert_fusion.3.refs_0_, bf16[960,256]{1,0:T(8,128)(2,1)} %collective-permute-done.9.refs_1_, bf16[960,256]{1,0:T(8,128)(2,1)} %collective-permute-done.10.refs_2_, bf16[960,256]{1,0:T(8,128)(2,1)} %collective-permute-done.11.refs_3_, ...), custom_call_target="tpu_custom_call" | custom-call | flops 2013265920 | bytes 7864320 | tf_op jit(solution)/shard_map/pallas_call | solution.py:288
  (160 shorter events, 68.9 us)
Async XLA Ops:
  4.1 47.4 %all-to-all-start = ((bf16[8,128,512]{1,2,0:T(8,128)(2,1)}), bf16[8,128,512]{1,2,0:T(8,128)(2,1)S(1)}, u32[]{:S(2)}, u32[]{:S(2)}) async-start(bf16[8,128,512]{1,2,0:T(8,128)(2,1)} %pad_maximum_fusion), calls=%async_computation | async-start | bytes 2097152 | tf_op jit(solution)/shard_map/all_to_all | solution.py:390
  11.6 6.7 %collective-permute-start = (s32[512]{0:T(512)S(1)}, s32[512]{0:T(512)S(1)}, u32[]{:S(2)}, u32[]{:S(2)}) collective-permute-start(s32[512]{0:T(512)S(1)} %dynamic_update_slice.5), channel_id=1, source_target_pairs={{0,1},{1,0},{2,3},{3,2},{4,5},{5,4},{6,7},{7,6},{8,9},{9,8},{10,11... | collective-permute-start | bytes 6152 | tf_op jit(solution)/shard_map/ppermute | solution.py:398
  18.5 10.1 %collective-permute-start.1 = (s32[512]{0:T(512)S(1)}, s32[512]{0:T(512)S(1)}, u32[]{:S(2)}, u32[]{:S(2)}) collective-permute-start(s32[512]{0:T(512)S(1)} %add_dynamic-update-slice_fusion), channel_id=1, source_target_pairs={{0,2},{2,0},{1,3},{3,1},{4,6},{6,4},{5,7},{7,5},{8,10},{10,8},{9,1... | collective-permute-start | bytes 6152 | tf_op jit(solution)/shard_map/ppermute | solution.py:398
  28.6 1.2 collective-permute-start.2
  29.7 21.8 %collective-permute-start.3 = (s32[512]{0:T(512)S(1)}, s32[512]{0:T(512)S(1)}, u32[]{:S(2)}, u32[]{:S(2)}) collective-permute-start(s32[512]{0:T(512)S(1)} %add.196), channel_id=1, source_target_pairs={{0,16},{8,24},{16,0},{24,8},{1,17},{9,25},{17,1},{25,9},{2,18},{10... | collective-permute-start | bytes 6152 | tf_op jit(solution)/shard_map/ppermute | solution.py:398
  51.5 160.0 %all-to-all-start.1 = ((bf16[16,2048,128]{2,1,0:T(8,128)(2,1)}), bf16[16,2048,128]{2,1,0:T(8,128)(2,1)}, u32[]{:S(2)}, u32[]{:S(2)}) async-start(bf16[16,2048,128]{2,1,0:T(8,128)(2,1)} %bitcast.71), calls=%async_computation.1 | async-start | bytes 16777216 | tf_op jit(solution)/shard_map/all_to_all | solution.py:379
  58.9 115.0 %collective-permute-start.5 = (bf16[128,2048]{1,0:T(8,128)(2,1)S(1)}, bf16[128,2048]{1,0:T(8,128)(2,1)S(1)}, u32[]{:S(2)}, u32[]{:S(2)}) collective-permute-start(bf16[128,2048]{1,0:T(8,128)(2,1)S(1)} %copy-done.2), channel_id=1, source_target_pairs={{0,4},{4,0},{1,5},{5,1},{2,6},{6,2},{3,7},{7,3},{8,12},{12,8},{9,1... | collective-permute-start | bytes 1572872 | tf_op jit(solution)/shard_map/ppermute | solution.py:308
  60.8 112.5 %collective-permute-start.4 = (bf16[2048,128]{0,1:T(8,128)(2,1)S(1)}, bf16[2048,128]{0,1:T(8,128)(2,1)S(1)}, u32[]{:S(2)}, u32[]{:S(2)}) collective-permute-start(bf16[2048,128]{0,1:T(8,128)(2,1)S(1)} %copy.49), channel_id=1, source_target_pairs={{0,4},{4,0},{1,5},{5,1},{2,6},{6,2},{3,7},{7,3},{8,12},{12,8},{9,1... | collective-permute-start | bytes 1572872 | tf_op jit(solution)/shard_map/ppermute | solution.py:308
  211.5 135.1 %all-to-all-start.2 = ((bf16[16,2048,128]{2,1,0:T(8,128)(2,1)}), bf16[16,2048,128]{2,1,0:T(8,128)(2,1)}, u32[]{:S(2)}, u32[]{:S(2)}) async-start(bf16[16,2048,128]{2,1,0:T(8,128)(2,1)} %bitcast.72), calls=%async_computation.2 | async-start | bytes 16777216 | tf_op jit(solution)/shard_map/all_to_all | solution.py:379
  281.0 43.4 %collective-permute-start.6 = (f32[4,8,512]{2,1,0:T(8,128)}, f32[4,8,512]{2,1,0:T(8,128)S(1)}, u32[]{:S(2)}, u32[]{:S(2)}) collective-permute-start(f32[4,8,512]{2,1,0:T(8,128)} %get-tuple-element.38.mine_ref), channel_id=1, source_target_pairs={{0,4},{4,0},{1,5},{5,1},{2,6},{6,2},{3,7},{7,3},{8,12},{12,8},{9,1... | collective-permute-start | bytes 196616 | tf_op jit(solution)/shard_map/ppermute | solution.py:308
  327.9 103.5 %collective-permute-start.21 = (bf16[960,256]{1,0:T(8,128)(2,1)}, bf16[960,256]{1,0:T(8,128)(2,1)}, u32[]{:S(2)}, u32[]{:S(2)}) collective-permute-start(bf16[960,256]{1,0:T(8,128)(2,1)} %shard_map.104), channel_id=1, source_target_pairs={{0,4},{4,0},{1,5},{5,1},{2,6},{6,2},{3,7},{7,3},{8,12},{12,8},{9,1... | collective-permute-start | bytes 1474568 | tf_op jit(solution)/shard_map/ppermute | solution.py:308
  371.6 13.1 %collective-permute-start.7 = (f32[2,8,512]{2,1,0:T(8,128)}, f32[2,8,512]{2,1,0:T(8,128)S(1)}, u32[]{:S(2)}, u32[]{:S(2)}) collective-permute-start(f32[2,8,512]{2,1,0:T(8,128)} %get-tuple-element.43.mine_ref), channel_id=1, source_target_pairs={{0,4},{4,0},{1,5},{5,1},{2,6},{6,2},{3,7},{7,3},{8,12},{12,8},{9,1... | collective-permute-start | bytes 98312 | tf_op jit(solution)/shard_map/ppermute | solution.py:308
  374.5 65.3 %collective-permute-start.17 = (bf16[960,256]{1,0:T(8,128)(2,1)}, bf16[960,256]{1,0:T(8,128)(2,1)}, u32[]{:S(2)}, u32[]{:S(2)}) collective-permute-start(bf16[960,256]{1,0:T(8,128)(2,1)} %shard_map.110), channel_id=1, source_target_pairs={{0,4},{4,0},{1,5},{5,1},{2,6},{6,2},{3,7},{7,3},{8,12},{12,8},{9,1... | collective-permute-start | bytes 1474568 | tf_op jit(solution)/shard_map/ppermute | solution.py:308
  416.9 11.1 %collective-permute-start.12 = (f32[2,8,512]{2,1,0:T(8,128)}, f32[2,8,512]{2,1,0:T(8,128)S(1)}, u32[]{:S(2)}, u32[]{:S(2)}) collective-permute-start(f32[2,8,512]{2,1,0:T(8,128)} %get-tuple-element.47.mine_ref), channel_id=1, source_target_pairs={{0,4},{4,0},{1,5},{5,1},{2,6},{6,2},{3,7},{7,3},{8,12},{12,8},{9,1... | collective-permute-start | bytes 98312 | tf_op jit(solution)/shard_map/ppermute | solution.py:308
  417.0 25.9 %collective-permute-start.8 = (bf16[960,256]{1,0:T(8,128)(2,1)S(1)}, bf16[960,256]{1,0:T(8,128)(2,1)}, u32[]{:S(2)}, u32[]{:S(2)}) collective-permute-start(bf16[960,256]{1,0:T(8,128)(2,1)S(1)} %copy-done.4), channel_id=1, source_target_pairs={{0,4},{4,0},{1,5},{5,1},{2,6},{6,2},{3,7},{7,3},{8,12},{12,8},{9,1... | collective-permute-start | bytes 1474568 | tf_op jit(solution)/shard_map/ppermute | solution.py:308
  431.4 17.6 %collective-permute-start.13 = (bf16[960,256]{1,0:T(8,128)(2,1)}, bf16[960,256]{1,0:T(8,128)(2,1)S(1)}, u32[]{:S(2)}, u32[]{:S(2)}) collective-permute-start(bf16[960,256]{1,0:T(8,128)(2,1)} %shard_map.109), channel_id=1, source_target_pairs={{0,4},{4,0},{1,5},{5,1},{2,6},{6,2},{3,7},{7,3},{8,12},{12,8},{9,1... | collective-permute-start | bytes 1474568 | tf_op jit(solution)/shard_map/ppermute | solution.py:308
  432.8 45.3 %collective-permute-start.23 = (bf16[960,256]{1,0:T(8,128)(2,1)S(1)}, bf16[960,256]{1,0:T(8,128)(2,1)}, u32[]{:S(2)}, u32[]{:S(2)}) collective-permute-start(bf16[960,256]{1,0:T(8,128)(2,1)S(1)} %add_convert_fusion.refs_4_), channel_id=1, source_target_pairs={{0,2},{2,0},{1,3},{3,1},{4,6},{6,4},{5,7},{7,5},{8,10},{10,8},{9,1... | collective-permute-start | bytes 1474568 | tf_op jit(solution)/shard_map/ppermute | solution.py:308
  432.9 46.1 %collective-permute-start.22 = (bf16[960,256]{1,0:T(8,128)(2,1)S(1)}, bf16[960,256]{1,0:T(8,128)(2,1)S(1)}, u32[]{:S(2)}, u32[]{:S(2)}) collective-permute-start(bf16[960,256]{1,0:T(8,128)(2,1)S(1)} %add_convert_fusion.refs_4_), channel_id=1, source_target_pairs={{0,1},{1,0},{2,3},{3,2},{4,5},{5,4},{6,7},{7,6},{8,9},{9,8},{10,11... | collective-permute-start | bytes 1474568 | tf_op jit(solution)/shard_map/ppermute | solution.py:308
  455.8 13.0 %collective-permute-start.27 = (bf16[128,1024]{1,0:T(8,128)(2,1)S(1)}, bf16[128,1024]{1,0:T(8,128)(2,1)S(1)}, u32[]{:S(2)}, u32[]{:S(2)}) collective-permute-start(bf16[128,1024]{1,0:T(8,128)(2,1)S(1)} %dynamic-slice_convert_fusion), channel_id=1, source_target_pairs={{0,16},{8,24},{16,0},{24,8},{1,17},{9,25},{17,1},{25,9},{2,18},{10... | collective-permute-start | bytes 786440 | tf_op jit(solution)/shard_map/ppermute | solution.py:329
  463.2 10.7 %collective-permute-start.25 = (bf16[1024,128]{0,1:T(8,128)(2,1)S(1)}, bf16[1024,128]{0,1:T(8,128)(2,1)S(1)}, u32[]{:S(2)}, u32[]{:S(2)}) collective-permute-start(bf16[1024,128]{0,1:T(8,128)(2,1)S(1)} %fusion.17), channel_id=1, source_target_pairs={{0,16},{8,24},{16,0},{24,8},{1,17},{9,25},{17,1},{25,9},{2,18},{10... | collective-permute-start | bytes 786440 | tf_op jit(solution)/shard_map/ppermute | solution.py:329
  469.0 7.9 %collective-permute-start.28 = (bf16[128,512]{1,0:T(8,128)(2,1)S(1)}, bf16[128,512]{1,0:T(8,128)(2,1)S(1)}, u32[]{:S(2)}, u32[]{:S(2)}) collective-permute-start(bf16[128,512]{1,0:T(8,128)(2,1)S(1)} %dynamic-slice_convert_fusion.2), channel_id=1, source_target_pairs={{0,8},{8,0},{16,24},{24,16},{1,9},{9,1},{17,25},{25,17},{2,10},{10... | collective-permute-start | bytes 393224 | tf_op jit(solution)/shard_map/ppermute | solution.py:329
  474.0 2.9 collective-permute-start.26
  474.1 15.2 %collective-permute-start.18 = (bf16[960,256]{1,0:T(8,128)(2,1)}, bf16[960,256]{1,0:T(8,128)(2,1)}, u32[]{:S(2)}, u32[]{:S(2)}) collective-permute-start(bf16[960,256]{1,0:T(8,128)(2,1)} %add_convert_fusion.1.refs_0_), channel_id=1, source_target_pairs={{0,1},{1,0},{2,3},{3,2},{4,5},{5,4},{6,7},{7,6},{8,9},{9,8},{10,11... | collective-permute-start | bytes 1474568 | tf_op jit(solution)/shard_map/ppermute | solution.py:308
  476.9 14.4 %collective-permute-start.19 = (bf16[960,256]{1,0:T(8,128)(2,1)}, bf16[960,256]{1,0:T(8,128)(2,1)}, u32[]{:S(2)}, u32[]{:S(2)}) collective-permute-start(bf16[960,256]{1,0:T(8,128)(2,1)} %add_convert_fusion.1.refs_0_), channel_id=1, source_target_pairs={{0,2},{2,0},{1,3},{3,1},{4,6},{6,4},{5,7},{7,5},{8,10},{10,8},{9,1... | collective-permute-start | bytes 1474568 | tf_op jit(solution)/shard_map/ppermute | solution.py:308
  476.9 22.9 %collective-permute-start.9 = (bf16[960,256]{1,0:T(8,128)(2,1)S(1)}, bf16[960,256]{1,0:T(8,128)(2,1)}, u32[]{:S(2)}, u32[]{:S(2)}) collective-permute-start(bf16[960,256]{1,0:T(8,128)(2,1)S(1)} %add_convert_fusion.3.refs_0_), channel_id=1, source_target_pairs={{0,1},{1,0},{2,3},{3,2},{4,5},{5,4},{6,7},{7,6},{8,9},{9,8},{10,11... | collective-permute-start | bytes 1474568 | tf_op jit(solution)/shard_map/ppermute | solution.py:308
  478.1 23.6 %collective-permute-start.15 = (bf16[960,256]{1,0:T(8,128)(2,1)}, bf16[960,256]{1,0:T(8,128)(2,1)}, u32[]{:S(2)}, u32[]{:S(2)}) collective-permute-start(bf16[960,256]{1,0:T(8,128)(2,1)} %add_convert_fusion.2.refs_4_), channel_id=1, source_target_pairs={{0,2},{2,0},{1,3},{3,1},{4,6},{6,4},{5,7},{7,5},{8,10},{10,8},{9,1... | collective-permute-start | bytes 1474568 | tf_op jit(solution)/shard_map/ppermute | solution.py:308
  479.8 30.5 %collective-permute-start.24 = (bf16[960,256]{1,0:T(8,128)(2,1)}, bf16[960,256]{1,0:T(8,128)(2,1)}, u32[]{:S(2)}, u32[]{:S(2)}) collective-permute-start(bf16[960,256]{1,0:T(8,128)(2,1)} %collective-permute-done.23.refs_6_), channel_id=1, source_target_pairs={{0,1},{1,0},{2,3},{3,2},{4,5},{5,4},{6,7},{7,6},{8,9},{9,8},{10,11... | collective-permute-start | bytes 1474568 | tf_op jit(solution)/shard_map/ppermute | solution.py:308
  489.2 26.6 %collective-permute-start.20 = (bf16[960,256]{1,0:T(8,128)(2,1)}, bf16[960,256]{1,0:T(8,128)(2,1)}, u32[]{:S(2)}, u32[]{:S(2)}) collective-permute-start(bf16[960,256]{1,0:T(8,128)(2,1)} %collective-permute-done.18.refs_1_), channel_id=1, source_target_pairs={{0,2},{2,0},{1,3},{3,1},{4,6},{6,4},{5,7},{7,5},{8,10},{10,8},{9,1... | collective-permute-start | bytes 1474568 | tf_op jit(solution)/shard_map/ppermute | solution.py:308
  491.2 31.6 %collective-permute-start.10 = (bf16[960,256]{1,0:T(8,128)(2,1)S(1)}, bf16[960,256]{1,0:T(8,128)(2,1)}, u32[]{:S(2)}, u32[]{:S(2)}) collective-permute-start(bf16[960,256]{1,0:T(8,128)(2,1)S(1)} %add_convert_fusion.3.refs_0_), channel_id=1, source_target_pairs={{0,2},{2,0},{1,3},{3,1},{4,6},{6,4},{5,7},{7,5},{8,10},{10,8},{9,1... | collective-permute-start | bytes 1474568 | tf_op jit(solution)/shard_map/ppermute | solution.py:308
  499.8 23.1 %collective-permute-start.14 = (bf16[960,256]{1,0:T(8,128)(2,1)}, bf16[960,256]{1,0:T(8,128)(2,1)}, u32[]{:S(2)}, u32[]{:S(2)}) collective-permute-start(bf16[960,256]{1,0:T(8,128)(2,1)} %add_convert_fusion.2.refs_4_), channel_id=1, source_target_pairs={{0,1},{1,0},{2,3},{3,2},{4,5},{5,4},{6,7},{7,6},{8,9},{9,8},{10,11... | collective-permute-start | bytes 1474568 | tf_op jit(solution)/shard_map/ppermute | solution.py:308
  501.8 30.8 %collective-permute-start.11 = (bf16[960,256]{1,0:T(8,128)(2,1)}, bf16[960,256]{1,0:T(8,128)(2,1)}, u32[]{:S(2)}, u32[]{:S(2)}) collective-permute-start(bf16[960,256]{1,0:T(8,128)(2,1)} %collective-permute-done.9.refs_1_), channel_id=1, source_target_pairs={{0,2},{2,0},{1,3},{3,1},{4,6},{6,4},{5,7},{7,5},{8,10},{10,8},{9,1... | collective-permute-start | bytes 1474568 | tf_op jit(solution)/shard_map/ppermute | solution.py:308
  510.3 22.3 %collective-permute-start.16 = (bf16[960,256]{1,0:T(8,128)(2,1)}, bf16[960,256]{1,0:T(8,128)(2,1)}, u32[]{:S(2)}, u32[]{:S(2)}) collective-permute-start(bf16[960,256]{1,0:T(8,128)(2,1)} %collective-permute-done.15.refs_6_), channel_id=1, source_target_pairs={{0,1},{1,0},{2,3},{3,2},{4,5},{5,4},{6,7},{7,6},{8,9},{9,8},{10,11... | collective-permute-start | bytes 1474568 | tf_op jit(solution)/shard_map/ppermute | solution.py:308
  (20 other events, 190.0 us)

commit v4 on v3

--- a/solution.py
+++ b/solution.py
@@ -11,46 +11,65 @@
 
 masked_value = -1e30
 LANES = 128
-
-
-def pack_kernel(chosen, counts, cache_ref, out_ref, *, chunk, local_heads, inner, capacity):
+MARK_ROWS = 16
+MARK_BASE = 100.0
+MARK_LEAST = 64.0
+
+
+def pack_kernel(
+    chosen, counts, lengths, cache_ref, out_ref, *, chunk, local_heads, inner, capacity
+):
     slot = pl.program_id(0) * capacity + pl.program_id(1)
 
     @pl.when(pl.program_id(1) < counts[pl.program_id(0)])
     def _():
         by_head = pltpu.einshape("rhd->hrd", cache_ref[0])
+        block_rows, width = by_head.shape[1:]
+        valid = lengths[chosen[slot]]
+        shape = (MARK_ROWS, width)
+        corner = (lax.broadcasted_iota(jnp.int32, shape, 0) == MARK_ROWS - 1) & (
+            lax.broadcasted_iota(jnp.int32, shape, 1) == 0
+        )
+        corner = corner & (valid < block_rows)
+        mark = valid.astype(jnp.float32) + MARK_BASE
         for r in range(inner):
             for half in range(2):
-                out_ref[0, r, 0, half] = by_head[(half * inner + r) * local_heads + chunk]
-
-
-def pack_blocks(chosen, counts, cache, chunk, groups, inner, capacity, local_heads):
+                tile = by_head[(half * inner + r) * local_heads + chunk]
+                out_ref[0, r, 0, half] = tile
+                last = tile[block_rows - MARK_ROWS :].astype(jnp.float32)
+                out_ref[0, r, 0, half, block_rows - MARK_ROWS :, :] = jnp.where(
+                    corner, mark, last
+                ).astype(jnp.bfloat16)
+
+
+def pack_blocks(chosen, counts, lengths, cache, chunk, groups, inner, capacity, local_heads):
     _, block_rows, heads, width = cache.shape
     return pl.pallas_call(
         functools.partial(
             pack_kernel, chunk=chunk, local_heads=local_heads, inner=inner, capacity=capacity
         ),
         grid_spec=pltpu.PrefetchScalarGridSpec(
-            num_scalar_prefetch=2,
+            num_scalar_prefetch=3,
             grid=(groups, capacity),
             in_specs=[
                 pl.BlockSpec(
                     (1, block_rows, heads, width),
-                    lambda g, s, ch, ct: (ch[g * capacity + s], 0, 0, 0),
+                    lambda g, s, ch, ct, ln: (ch[g * capacity + s], 0, 0, 0),
                 )
             ],
             out_specs=pl.BlockSpec(
-                (1, inner, 1, 2, block_rows, width), lambda g, s, ch, ct: (g, 0, s, 0, 0, 0)
+                (1, inner, 1, 2, block_rows, width),
+                lambda g, s, ch, ct, ln: (g, 0, s, 0, 0, 0),
             ),
         ),
         out_shape=jax.ShapeDtypeStruct(
             (groups, inner, capacity, 2, block_rows, width), cache.dtype
         ),
-        compiler_params=pltpu.CompilerParams(vmem_limit_bytes=58 << 20),
+        compiler_params=pltpu.CompilerParams(vmem_limit_bytes=32 << 20),
         cost_estimate=pl.CostEstimate(
             flops=0, transcendentals=0, bytes_accessed=groups * capacity * 2 * 262144
         ),
-    )(chosen, counts, cache)
+    )(chosen, counts, lengths, cache)
 
 
 def nt_dot(left, right):
@@ -60,8 +79,8 @@
 
 
 def attention_kernel(
-    places, lens, counts, q_ref, b_ref, recv_ref, co_ref, ds_ref, stat_ref,
-    kv, scores, probs, top, acc, total, dacc, columns, sems, *, slots, scale, first,
+    places, counts, q_ref, b_ref, recv_ref, co_ref, ds_ref, stat_ref,
+    kv, scores, probs, top, acc, total, dacc, columns, bias, sems, *, slots, scale, first,
 ):
     patch = first + pl.program_id(0)
     patches = first + pl.num_programs(0)
@@ -96,10 +115,18 @@
         kv[patch % 2, :, pl.ds(pl.multiple_of(j * block_rows, block_rows), block_rows), :] = (
             jnp.zeros((2, block_rows, kv.shape[3]), kv.dtype)
         )
+        bias[pl.ds(j, 1), :] = jnp.full((1, block_rows), masked_value, jnp.float32)
+
+    lane = lax.broadcasted_iota(jnp.int32, (1, block_rows), 1)
 
     @pl.loop(0, here)
     def _(j):
         copy(patch, j, 0).wait()
+        end = pl.multiple_of(j * block_rows + block_rows - MARK_ROWS, MARK_ROWS)
+        last = kv[patch % 2, 0, pl.ds(end, MARK_ROWS), :].astype(jnp.float32)[MARK_ROWS - 1 :]
+        mark = jnp.sum(jnp.where(lane == 0, last, 0.0), axis=1, keepdims=True)
+        valid = jnp.where(mark > MARK_LEAST, mark - MARK_BASE, float(block_rows))
+        bias[pl.ds(j, 1), :] = jnp.where(lane.astype(jnp.float32) < valid, 0.0, masked_value)
 
     def key_tile(t, head):
         return kv[patch % 2, head, pl.ds(pl.multiple_of(t * pair, pair), pair), :]
@@ -113,13 +140,12 @@
 
     @pl.loop(0, tiles)
     def _(t):
-        place = lax.broadcasted_iota(jnp.int32, (1, block_rows), 1)
-        seen_lo = place < lens[patch * slots + 2 * t]
-        seen_hi = place < lens[patch * slots + 2 * t + 1]
+        bias_lo = bias[pl.ds(2 * t, 1), :]
+        bias_hi = bias[pl.ds(2 * t + 1, 1), :]
         for head in range(2):
             score = nt_dot(q_ref[:, lanes[head]], key_tile(t, head))
-            low = jnp.where(seen_lo, score[:, :block_rows], masked_value)
-            high = jnp.where(seen_hi, score[:, block_rows:], masked_value)
+            low = score[:, :block_rows] + bias_lo
+            high = score[:, block_rows:] + bias_hi
             scores[head, t, :, :block_rows] = low
             scores[head, t, :, block_rows:] = high
             top[head] = jnp.maximum(top[head], jnp.maximum(low, high))
@@ -166,7 +192,7 @@
 
 
 def attention(
-    places, lens, counts, queries, backs, received, chunk, first, patch_blocks, rows, slots, scale
+    places, counts, queries, backs, received, chunk, first, patch_blocks, rows, slots, scale
 ):
     total_rows = patch_blocks * rows
     padded = pl.cdiv(rows, LANES) * LANES
@@ -177,7 +203,7 @@
     return pl.pallas_call(
         functools.partial(attention_kernel, slots=slots, scale=scale, first=first),
         grid_spec=pltpu.PrefetchScalarGridSpec(
-            num_scalar_prefetch=3,
+            num_scalar_prefetch=2,
             grid=(patch_blocks,),
             in_specs=[wide, wide, pl.BlockSpec(memory_space=pl.ANY)],
             out_specs=[out, out, pl.BlockSpec((1, 8, padded), lambda p, *_: (p, 0, 0))],
@@ -190,6 +216,7 @@
                 pltpu.VMEM((2, rows, block_rows), jnp.float32),
                 pltpu.VMEM((2, rows, width), jnp.float32),
                 pltpu.VMEM((padded, LANES), jnp.float32),
+                pltpu.VMEM((2 * tiles, block_rows), jnp.float32),
                 pltpu.SemaphoreType.DMA((2, slots)),
             ],
         ),
@@ -201,7 +228,7 @@
             transcendentals=total_rows * slots * block_rows,
             bytes_accessed=40 << 20,
         ),
-    )(places, lens, counts, queries, backs, received)
+    )(places, counts, queries, backs, received)
 
 
 def merge_kernel(co_ref, ds_ref, mine_ref, theirs_ref, out_ref, *, scale, split):
@@ -245,11 +272,25 @@
     )(outs, douts, mine, theirs)
 
 
-def project_kernel(*refs, count, parts, last):
+def project_kernel(order, *refs, count, parts, last, chunk, depth):
     step = pl.program_id(0)
-    weights = refs[count * parts]
-    rest = refs[count * parts + 1 :]
+    cols = refs[count * parts]
+    rest, weights = refs[count * parts + 1 : -1], refs[-1]
     before = rest[0] if len(rest) == (3 if last else 2) else None
+    half = cols.shape[2] // 2
+
+    @pl.when(step == 0)
+    def _():
+        empty = jnp.zeros((depth, half), weights.dtype)
+        for i in range(count):
+            for z in range(2):
+                own = cols[z * count + order[i], pl.ds(chunk * depth, depth), :]
+                grad_rows = pl.ds(2 * z * depth, depth)
+                out_rows = pl.ds((2 * z + 1) * depth, depth)
+                weights[i, grad_rows, :half] = empty
+                weights[i, grad_rows, half:] = own[:, half:]
+                weights[i, out_rows, :half] = own[:, :half]
+                weights[i, out_rows, half:] = empty
 
     def part(pieces):
         value = jnp.dot(pieces[0][...], weights[0], preferred_element_type=jnp.float32)
@@ -258,9 +299,8 @@
         if before is not None:
             value += before[...]
         if last:
-            width = rest[-1].shape[1]
-            rest[-2][...] = value[:, :width].astype(jnp.bfloat16)
-            rest[-1][...] = value[:, width:].astype(jnp.bfloat16)
+            rest[-2][...] = value[:, :half].astype(jnp.bfloat16)
+            rest[-1][...] = value[:, half:].astype(jnp.bfloat16)
         else:
             rest[-1][...] = value
 
@@ -270,28 +310,35 @@
         )
 
 
-def project(parts, weights, before, last):
+def project(parts, cols, order, before, last, chunk):
     count = len(parts[0])
     rows, depth = parts[0][0].shape
     total_rows = rows * len(parts)
-    width = weights.shape[2]
+    width = cols.shape[2]
     steps = 4 // len(parts)
     tile = rows // steps
-    rowwise = lambda w: pl.BlockSpec((tile, w), lambda i: (i, 0))
+    rowwise = lambda w: pl.BlockSpec((tile, w), lambda i, *_: (i, 0))
 
     def within(which):
         return pl.BlockSpec(
-            (tile, depth), lambda i: (jnp.clip(i - which * steps, 0, steps - 1), 0)
+            (tile, depth), lambda i, *_: (jnp.clip(i - which * steps, 0, steps - 1), 0)
         )
 
     halves = jax.ShapeDtypeStruct((total_rows, width // 2), jnp.bfloat16)
     return pl.pallas_call(
-        functools.partial(project_kernel, count=count, parts=len(parts), last=last),
-        grid=(4,),
-        in_specs=[within(i) for i in range(len(parts)) for _ in range(count)]
-        + [pl.BlockSpec(weights.shape, lambda i: (0, 0, 0))]
-        + ([] if before is None else [rowwise(width)]),
-        out_specs=[rowwise(width // 2)] * 2 if last else rowwise(width),
+        functools.partial(
+            project_kernel, count=count, parts=len(parts), last=last, chunk=chunk,
+            depth=depth // 4,
+        ),
+        grid_spec=pltpu.PrefetchScalarGridSpec(
+            num_scalar_prefetch=1,
+            grid=(4,),
+            in_specs=[within(i) for i in range(len(parts)) for _ in range(count)]
+            + [pl.BlockSpec(cols.shape, lambda i, *_: (0, 0, 0))]
+            + ([] if before is None else [rowwise(width)]),
+            out_specs=[rowwise(width // 2)] * 2 if last else rowwise(width),
+            scratch_shapes=[pltpu.VMEM((count, depth, width), jnp.bfloat16)],
+        ),
         out_shape=[halves] * 2
         if last
         else jax.ShapeDtypeStruct((total_rows, width), jnp.float32),
@@ -301,7 +348,10 @@
             transcendentals=0,
             bytes_accessed=2 * total_rows * (depth * count + 2 * width),
         ),
-    )(*[x for pieces in parts for x in pieces], weights, *([] if before is None else [before]))
+    )(
+        order, *[x for pieces in parts for x in pieces], cols,
+        *([] if before is None else [before]),
+    )
 
 
 def swap(x, axis):
@@ -372,7 +422,7 @@
 
     def pack(c):
         return pack_blocks(
-            chosen, send_counts, cache, c, groups, inner, capacity, local_heads
+            chosen, send_counts, block_lengths, cache, c, groups, inner, capacity, local_heads
         ).reshape(groups * inner, capacity * 2 * block_rows, width)
 
     def exchange(x):
@@ -380,30 +430,11 @@
             x, ("dp", "zl", "y"), split_axis=0, concat_axis=0, tiled=True
         ).reshape(groups * inner * capacity, 2, block_rows, width)
 
-    cols = jnp.concatenate(
-        [
-            output_proj.reshape(local_heads * head_size, model, columns).transpose(1, 0, 2),
-            query_proj.reshape(model, columns, local_heads * head_size).transpose(0, 2, 1),
-        ],
-        axis=2,
-    )
-    cols = lax.all_to_all(cols, ("zh", "zl", "y"), split_axis=0, concat_axis=0, tiled=True)
-
-    every_length = lax.dynamic_update_slice_in_dim(
-        jnp.zeros((owner_count * local_blocks,), jnp.int32), block_lengths, me * local_blocks, 0
-    )
-    for axis, size in (("y", y_size), ("zl", zl_size), ("dp", groups)):
-        step = 1
-        while step < size:
-            every_length += lax.ppermute(
-                every_length, axis, [(i, i ^ step) for i in range(size)]
-            )
-            step *= 2
-
-    packed, cols, every_length = lax.optimization_barrier((pack(0), cols, every_length))
-    received = [exchange(packed)]
-    cols = cols.reshape(2, inner, local_heads, head_size, 2 * columns)
-
+    received = [exchange(pack(0))]
+    q_other, o_other = swap(query_proj, "zh"), swap(output_proj, "zh")
+    for c in range(1, local_heads):
+        packed, q_other, o_other = lax.optimization_barrier((pack(c), q_other, o_other))
+        received.append(exchange(packed))
 
     my_ids = lax.dynamic_slice_in_dim(
         neighbours, group * patch_blocks, patch_blocks, 0
@@ -413,28 +444,29 @@
     source = (owners // model) * inner + owners % inner
     in_half = ((owners % model) // inner == zh).reshape(patch_blocks, slots)
     arrival = (source * capacity + slot_of).reshape(patch_blocks, slots)
-    entry_length = every_length[my_ids].reshape(patch_blocks, slots)
     spots = jnp.arange(slots, dtype=jnp.int32)
     before = jnp.sum(
         (in_half[:, None, :] & (spots[None, :] < spots[:, None])[None]).astype(jnp.int32), axis=2
     )
     at = in_half[:, :, None] & (before[:, :, None] == spots)
     places = jnp.sum(jnp.where(at, arrival[:, :, None], 0), axis=1).reshape(entry_count)
-    lens = jnp.sum(jnp.where(at, entry_length[:, :, None], 0), axis=1).reshape(entry_count)
     counts = jnp.sum(in_half.astype(jnp.int32), axis=1)
 
-    def both_halves(own):
-        other = swap(own, "zh")
+    q_other, o_other, received[0] = lax.optimization_barrier(
+        (q_other, o_other, received[0])
+    )
+
+    def both_halves(own, other):
         return jnp.where(zh == 0, own, other), jnp.where(zh == 0, other, own)
 
     q_halves = [
-        w.reshape(features, local_heads, head_size) for w in both_halves(query_proj)
+        w.reshape(features, local_heads, head_size) for w in both_halves(query_proj, q_other)
     ]
     q_wide = jnp.stack(q_halves, axis=2)
     q_wide = jnp.pad(q_wide, ((0, 0), (0, 0), (0, 0), (0, LANES - head_size)))
     q_wide = q_wide.reshape(features, local_heads * 2 * LANES)
     o_halves = [
-        w.reshape(local_heads, head_size, features) for w in both_halves(output_proj)
+        w.reshape(local_heads, head_size, features) for w in both_halves(output_proj, o_other)
     ]
     o_wide = jnp.stack(o_halves, axis=1)
     o_wide = jnp.pad(o_wide, ((0, 0), (0, 0), (LANES - head_size, 0), (0, 0)))
@@ -444,64 +476,58 @@
     ).astype(jnp.bfloat16)
     backs = nt_dot(cotangent, o_wide).astype(jnp.bfloat16)
 
-    right = jnp.arange(2 * columns)[None, None, None, :] >= columns
+    cols = jnp.concatenate(
+        [
+            output_proj.reshape(local_heads * head_size, model, columns).transpose(1, 0, 2),
+            query_proj.reshape(model, columns, local_heads * head_size).transpose(0, 2, 1),
+        ],
+        axis=2,
+    )
     if zl_size == 2 and y_size == 2:
         order = jnp.stack([spot, spot ^ 1, spot ^ 2, spot ^ 3])
     else:
         order = jnp.arange(inner, dtype=jnp.int32)
 
-    def tail_weights(c):
-        both = jnp.moveaxis(cols[:, :, c], 0, 1)
-        pair = [jnp.where(right, both, 0), jnp.where(right, 0, both)]
-        return jnp.stack(pair, axis=2).reshape(inner, 2 * LANES, 2 * columns)[order]
-
-    finals = [tail_weights(c) for c in range(local_heads)]
-
-    places, lens, counts, queries, backs, finals, cache = lax.optimization_barrier(
-        (places, lens, counts, queries, backs, finals, cache)
-    )
-    for c in range(1, local_heads):
-        received.append(exchange(pack(c)))
-
-
     rows = row_count // patch_blocks
     part_count = 2 if patch_blocks % 2 == 0 else 1
     part_patches = patch_blocks // part_count
-    result = None
+    gathered = []
     own = []
     for c in range(local_heads):
         final = c + 1 == local_heads
-        calls = part_count if final else 1
-        call_patches = patch_blocks // calls
-        sums = []
-        for call in range(calls):
-            outs, douts, mine = attention(
-                places, lens, counts, queries, backs, received[c], c,
-                call * call_patches, call_patches, rows, slots, head_scale,
-            )
-            theirs = swap(mine, "zh")
-            for start in range(0, call_patches, part_patches):
-                part = merge(
-                    outs, douts, mine, theirs, start, part_patches, head_scale, head_size
-                )
-                sums.append((part, swap(part, "zh")))
-            if call + 1 < calls:
-                part, places = lax.optimization_barrier((part, places))
+        if final:
+            cols, places, received[c] = lax.optimization_barrier((cols, places, received[c]))
+            cols = lax.all_to_all(cols, ("zh", "zl", "y"), split_axis=0, concat_axis=0, tiled=True)
+        outs, douts, mine = attention(
+            places, counts, queries, backs, received[c], c, 0, patch_blocks, rows, slots, head_scale
+        )
+        theirs = swap(mine, "zh")
+        if final:
+            theirs, cols = lax.optimization_barrier((theirs, cols))
+        parts = [
+            merge(outs, douts, mine, theirs, start, part_patches, head_scale, head_size)
+            for start in range(0, patch_blocks, part_patches)
+        ]
         if not final:
-            part, places = lax.optimization_barrier((part, places))
+            parts, places = lax.optimization_barrier((parts, places))
         merged = [
-            (part.astype(jnp.float32) + other.astype(jnp.float32)).astype(jnp.bfloat16)
-            for part, other in sums
+            (part.astype(jnp.float32) + swap(part, "zh").astype(jnp.float32)).astype(jnp.bfloat16)
+            for part in parts
         ]
         pieces = [
             gather_half(x, zl_size, y_size, i % 2 == 0) for i, x in enumerate(merged)
         ]
-        result = project(pieces, finals[c], result, final)
+        gathered.append(pieces)
+        if final:
+            merged, pieces[0][1] = lax.optimization_barrier((merged, pieces[0][1]))
         own.append(
             jnp.concatenate(
                 [lax.dynamic_slice_in_dim(x, zh * LANES, LANES, 1) for x in merged], axis=0
             )
         )
+    result = None
+    for c, pieces in enumerate(gathered):
+        result = project(pieces, cols, order, result, c + 1 == local_heads, c)
     attended, patch_grad = result
 
     dquery = jnp.concatenate([x[:, :head_size] for x in own], axis=1)

time: 539 us -> 434 us (0.81)
  waiting for transfers between devices: 249 us -> 183 us
  starting transfers between devices: 77.2 us -> 45.1 us
  Pallas kernels: 163 us -> 146 us
  local copies, waits for them, and re-layouts: 16.7 us -> 28.4 us
    ppermute x21 -> x20, waiting for transfers between devices: 211 us -> 164 us  [swap(): return lax.ppermute(x, axis, [(0, 1), (1, 0)])]
    pallas_call x2, Pallas kernels: 37.7 us -> 9.21 us  [pack_blocks(): pl.pallas_call(functools.partial(pack_kernel, chunk=chunk, local_heads=lo...]
    unnamed x44 -> x60, local copies, waits for them, and re-layouts: 8.62 us -> 23.8 us
    ppermute x4 -> x0, waiting for transfers between devices: 12 us -> none  [local(): lax.ppermute(every_length, axis, [(i, i ^ step) for i in range(size)])]
    ppermute x21 -> x20, starting transfers between devices: 30.1 us -> 18.7 us  [swap(): return lax.ppermute(x, axis, [(0, 1), (1, 0)])]
    pallas_call x3 -> x2, Pallas kernels: 104 us -> 115 us  [attention(): pl.pallas_call(functools.partial(attention_kernel, slots=slots, scale=sca...]
    all_to_all x2, starting transfers between devices: 26.8 us -> 18 us  [exchange(): lax.all_to_all(x, ('dp', 'zl', 'y'), split_axis=0, concat_axis=0, tiled=T...]
    ppermute x4 -> x0, starting transfers between devices: 7.01 us -> none  [local(): lax.ppermute(every_length, axis, [(i, i ^ step) for i in range(size)])]
  transfers between devices with their start and end apart: 32 -> 27, of which waited for: 17 -> 16; matrix products, arithmetic and copies ran while one was open for 7% -> 8% of each run, Pallas kernels for 29% -> 32%
where the time goes in v4:
time: 434 us; the launch traced here: 432 us
  waiting for transfers between devices  183 us (42%)
  Pallas kernels  146 us (34%)
  starting transfers between devices  45.1 us (10%)
  local copies, waits for them, and re-layouts  28.4 us (7%)
  matrix products  17 us (4%)
  other arithmetic  11.5 us (3%)
    ppermute x20, waiting for transfers between devices, swap(): return lax.ppermute(x, axis, [(0, 1), (1, 0)])  164 us
    pallas_call x2, Pallas kernels, attention(): pl.pallas_call(functools.partial(attention_kernel, slots=slots, scale=sca...  115 us
    unnamed x60, local copies, waits for them, and re-layouts  23.8 us
    ppermute x20, starting transfers between devices, swap(): return lax.ppermute(x, axis, [(0, 1), (1, 0)])  18.7 us
    all_to_all x2, starting transfers between devices, exchange(): lax.all_to_all(x, ('dp', 'zl', 'y'), split_axis=0, concat_axis=0, tiled=T...  18 us
    all_to_all x2, waiting for transfers between devices, exchange(): lax.all_to_all(x, ('dp', 'zl', 'y'), split_axis=0, concat_axis=0, tiled=T...  13 us
    pallas_call x4, Pallas kernels, merge(): pl.pallas_call(functools.partial(merge_kernel, scale=scale, split=split),...  11.4 us
    pallas_call x2, Pallas kernels, project(): pl.pallas_call(functools.partial(project_kernel, count=count, parts=len(p...  10.9 us
  transfers between devices with their start and end apart: 27, of which 16 were waited for; matrix products, arithmetic and copies ran while one was open for 8% of the time, Pallas kernels for 32%

profile of v4, /device:TPU:0, one launch (start us, length us, event | category | flops | bytes accessed | tf_op | source)
XLA Modules:
  0.0 432.2 jit_solution(4802829807416021629)
XLA Ops:
  2.9 3.4 copy-done
  6.9 4.3 shard_map.103
  11.3 3.3 copy-done.3
  14.6 6.7 %all-to-all-start = ((bf16[16,2048,128]{2,1,0:T(8,128)(2,1)}), bf16[16,2048,128]{2,1,0:T(8,128)(2,1)}, u32[]{:S(2)}, u32[]{:S(2)}) async-start(bf16[16,2048,128]{2,1,0:T(8,128)(2,1)} %bitcast.33), calls=%async_computation | async-start | bytes 16777216 | tf_op jit(solution)/shard_map/all_to_all | solution.py:429
  24.5 3.4 copy-done.1
  27.9 4.9 %shard_map.102 = bf16[4,4,8,2,128,128]{5,4,3,2,1,0:T(8,128)(2,1)S(1)} custom-call(s32[32]{0:T(128)S(1)} %reshape.334.chosen, s32[4]{0:T(128)S(1)} %reduce_sum.81.counts, s32[16]{0:T(128)S(1)} %copy-done.7, bf16[16,128,16,128]{3,2,1,0:T(8,128)(2,1)S(1)} %copy-done.1), custom_call_target="tpu_custom_call" | custom-call | bytes 16777216 | tf_op jit(solution)/shard_map/pallas_call | solution.py:47
  32.8 3.3 copy-done.2
  36.0 88.6 %collective-permute-done = bf16[2048,128]{0,1:T(8,128)(2,1)S(1)} collective-permute-done((bf16[2048,128]{0,1:T(8,128)(2,1)S(1)}, bf16[2048,128]{0,1:T(8,128)(2,1)S(1)}, u32[]{:S(2)}, u32[]{:S(2)}) %collective-permute-start) | collective-permute-done | bytes 524320 | tf_op jit(solution)/shard_map/ppermute | solution.py:358
  124.7 11.0 %collective-permute-done.1 = bf16[128,2048]{1,0:T(8,128)(2,1)S(1)} collective-permute-done((bf16[128,2048]{1,0:T(8,128)(2,1)S(1)}, bf16[128,2048]{1,0:T(8,128)(2,1)S(1)}, u32[]{:S(2)}, u32[]{:S(2)}) %collective-permute-start.1) | collective-permute-done | bytes 524320 | tf_op jit(solution)/shard_map/ppermute | solution.py:358
  136.5 5.2 %all-to-all-done = bf16[16,2048,128]{2,1,0:T(8,128)(2,1)} async-done(((bf16[16,2048,128]{2,1,0:T(8,128)(2,1)}), bf16[16,2048,128]{2,1,0:T(8,128)(2,1)}, u32[]{:S(2)}, u32[]{:S(2)}) %all-to-all-start) | async-done | bytes 8388640 | tf_op jit(solution)/shard_map/all_to_all | solution.py:429
  141.7 11.3 %all-to-all-start.1 = ((bf16[16,2048,128]{2,1,0:T(8,128)(2,1)}), bf16[16,2048,128]{2,1,0:T(8,128)(2,1)}, u32[]{:S(2)}, u32[]{:S(2)}) async-start(bf16[16,2048,128]{2,1,0:T(8,128)(2,1)} %bitcast.32), calls=%async_computation.1 | async-start | bytes 16777216 | tf_op jit(solution)/shard_map/all_to_all | solution.py:429
  160.3 5.4 %fusion.2.b_ref = bf16[1920,512]{1,0:T(8,128)(2,1)} fusion(bf16[512,2048]{1,0:T(8,128)(2,1)S(1)} %bitcast.40, bf16[1920,2048]{1,0:T(8,128)(2,1)S(1)} %bitcast.37), kind=kOutput, calls=%fused_computation.5 | convolution fusion | flops 4027514880 | bytes 11927552 | tf_op jit(solution)/shard_map/dot_general | solution.py:76
  165.8 5.5 %fusion.3.q_ref = bf16[1920,512]{1,0:T(8,128)(2,1)} fusion(bf16[2048,512]{0,1:T(8,128)(2,1)S(1)} %bitcast.41, bf16[1920,2048]{1,0:T(8,128)(2,1)S(1)} %bitcast.35), kind=kOutput, calls=%fused_computation.6 | convolution fusion | flops 4028497920 | bytes 11927552 | tf_op jit(solution)/shard_map/dot_general | solution.py:475
  171.2 57.4 %shard_map.104 = (f32[1920,256]{1,0:T(8,128)}, f32[1920,256]{1,0:T(8,128)}, f32[4,8,512]{2,1,0:T(8,128)}) custom-call(s32[128]{0:T(128)} %reshape.332.places, s32[4]{0:T(128)} %get-tuple-element.66.counts, bf16[1920,512]{1,0:T(8,128)(2,1)} %fusion.3.q_ref, bf16[1920,512]{1,0:T(8,128)(2,1)} %fusion.2.b_ref, bf16[128,2,128,128]{3,2,1,0:T(8,128)(2,1)} %bitcast.10.recv_ref), custom_call_target="tpu_custom_call" | custom-call | flops 8053063680 | bytes 41943040 | tf_op jit(solution)/shard_map/pallas_call | solution.py:203
  229.8 16.7 %collective-permute-done.2.theirs_ref = f32[4,8,512]{2,1,0:T(8,128)S(1)} collective-permute-done((f32[4,8,512]{2,1,0:T(8,128)}, f32[4,8,512]{2,1,0:T(8,128)S(1)}, u32[]{:S(2)}, u32[]{:S(2)}) %collective-permute-start.2) | collective-permute-done | bytes 65568 | tf_op jit(solution)/shard_map/ppermute | solution.py:358
  247.1 2.8 shard_map.106
  250.0 2.9 shard_map.105
  252.9 7.9 %all-to-all-done.1 = bf16[16,2048,128]{2,1,0:T(8,128)(2,1)} async-done(((bf16[16,2048,128]{2,1,0:T(8,128)(2,1)}), bf16[16,2048,128]{2,1,0:T(8,128)(2,1)}, u32[]{:S(2)}, u32[]{:S(2)}) %all-to-all-start.1) | async-done | bytes 8388640 | tf_op jit(solution)/shard_map/all_to_all | solution.py:429
  260.8 5.6 %all-to-all-start.2 = ((bf16[8,128,512]{2,1,0:T(8,128)(2,1)}), bf16[8,128,512]{2,1,0:T(8,128)(2,1)S(1)}, u32[]{:S(2)}, u32[]{:S(2)}) async-start(bf16[8,128,512]{2,1,0:T(8,128)(2,1)} %pad_maximum_fusion), calls=%async_computation.2 | async-start | bytes 2097152 | tf_op jit(solution)/shard_map/all_to_all | solution.py:500
  266.5 3.0 collective-permute-start.16
  269.5 57.4 %shard_map.107 = (f32[1920,256]{1,0:T(8,128)}, f32[1920,256]{1,0:T(8,128)}, f32[4,8,512]{2,1,0:T(8,128)}) custom-call(s32[128]{0:T(128)} %reshape.332.places, s32[4]{0:T(128)} %get-tuple-element.66.counts, bf16[1920,512]{1,0:T(8,128)(2,1)} %fusion.3.q_ref, bf16[1920,512]{1,0:T(8,128)(2,1)} %fusion.2.b_ref, bf16[128,2,128,128]{3,2,1,0:T(8,128)(2,1)} %bitcast.19.recv_ref), custom_call_target="tpu_custom_call" | custom-call | flops 8053063680 | bytes 41943040 | tf_op jit(solution)/shard_map/pallas_call | solution.py:203
  329.1 8.0 %collective-permute-done.12 = bf16[960,256]{1,0:T(8,128)(2,1)S(1)} collective-permute-done((bf16[960,256]{1,0:T(8,128)(2,1)}, bf16[960,256]{1,0:T(8,128)(2,1)S(1)}, u32[]{:S(2)}, u32[]{:S(2)}) %collective-permute-start.12) | collective-permute-done | bytes 491552 | tf_op jit(solution)/shard_map/ppermute | solution.py:358
  339.4 2.8 shard_map.108
  351.5 2.9 shard_map.109
  354.4 11.1 %collective-permute-done.4 = bf16[960,256]{1,0:T(8,128)(2,1)S(1)} collective-permute-done((bf16[960,256]{1,0:T(8,128)(2,1)}, bf16[960,256]{1,0:T(8,128)(2,1)S(1)}, u32[]{:S(2)}, u32[]{:S(2)}) %collective-permute-start.4) | collective-permute-done | bytes 491552 | tf_op jit(solution)/shard_map/ppermute | solution.py:358
  370.5 14.9 %collective-permute-done.15.refs_3_ = bf16[960,256]{1,0:T(8,128)(2,1)} collective-permute-done((bf16[960,256]{1,0:T(8,128)(2,1)S(1)}, bf16[960,256]{1,0:T(8,128)(2,1)}, u32[]{:S(2)}, u32[]{:S(2)}) %collective-permute-start.15) | collective-permute-done | bytes 491552 | tf_op jit(solution)/shard_map/ppermute | solution.py:358
  385.3 5.1 %shard_map.110.refs_9_ = f32[1920,512]{1,0:T(8,128)S(1)} custom-call(s32[4]{0:T(128)S(1)} %pad_add_fusion.order, bf16[960,256]{1,0:T(8,128)(2,1)S(1)} %add_convert_fusion.1.refs_0_, bf16[960,256]{1,0:T(8,128)(2,1)S(1)} %collective-permute-done.13.refs_1_, bf16[960,256]{1,0:T(8,128)(2,1)} %collective-permute-done.14.refs_2_, ...), custom_call_target="tpu_custom_call" | custom-call | flops 2013265920 | bytes 7864320 | tf_op jit(solution)/shard_map/pallas_call | solution.py:328
  394.3 4.8 %convolution_multiply_fusion.1 = f32[128,2048]{1,0:T(8,128)S(1)} fusion(bf16[1920,2048]{1,0:T(8,128)(2,1)} %param.7, bf16[1920,64]{1,0:T(8,128)(2,1)S(1)} %fusion.7, bf16[1920,64]{1,0:T(8,128)(2,1)S(1)} %slice_maximum_fusion), kind=kOutput, calls=%fused_computation.8 | convolution fusion | flops 1007878144 | bytes 9404416 | tf_op jit(solution)/shard_map/dot_general | solution.py:536
  402.7 2.2 collective-permute-done.10.refs_6_
  405.0 3.5 collective-permute-done.20
  417.7 6.6 %collective-permute-done.8.refs_3_ = bf16[960,256]{1,0:T(8,128)(2,1)} collective-permute-done((bf16[960,256]{1,0:T(8,128)(2,1)}, bf16[960,256]{1,0:T(8,128)(2,1)}, u32[]{:S(2)}, u32[]{:S(2)}) %collective-permute-start.8) | collective-permute-done | bytes 491552 | tf_op jit(solution)/shard_map/ppermute | solution.py:358
  426.4 5.8 %shard_map.111 = (bf16[1920,256]{1,0:T(8,128)(2,1)}, bf16[1920,256]{1,0:T(8,128)(2,1)}) custom-call(s32[4]{0:T(128)S(1)} %pad_add_fusion.order, bf16[960,256]{1,0:T(8,128)(2,1)S(1)} %add_convert_fusion.3.refs_0_, bf16[960,256]{1,0:T(8,128)(2,1)} %collective-permute-done.6.refs_1_, bf16[960,256]{1,0:T(8,128)(2,1)S(1)} %collective-permute-done.7.refs_2_, ...), custom_call_target="tpu_custom_call" | custom-call | flops 2013265920 | bytes 7864320 | tf_op jit(solution)/shard_map/pallas_call | solution.py:328
  (145 shorter events, 53.4 us)
Async XLA Ops:
  14.6 9.9 %copy-start.7 = (s32[16]{0:T(128)S(1)}, s32[16]{0:T(128)}, u32[]{:S(2)}) copy-start(s32[16]{0:T(128)} %lengths.3) | copy-start | bytes 196
  14.6 127.1 %all-to-all-start = ((bf16[16,2048,128]{2,1,0:T(8,128)(2,1)}), bf16[16,2048,128]{2,1,0:T(8,128)(2,1)}, u32[]{:S(2)}, u32[]{:S(2)}) async-start(bf16[16,2048,128]{2,1,0:T(8,128)(2,1)} %bitcast.33), calls=%async_computation | async-start | bytes 16777216 | tf_op jit(solution)/shard_map/all_to_all | solution.py:429
  21.5 103.2 %collective-permute-start = (bf16[2048,128]{0,1:T(8,128)(2,1)S(1)}, bf16[2048,128]{0,1:T(8,128)(2,1)S(1)}, u32[]{:S(2)}, u32[]{:S(2)}) collective-permute-start(bf16[2048,128]{0,1:T(8,128)(2,1)S(1)} %copy.28), channel_id=1, source_target_pairs={{0,4},{4,0},{1,5},{5,1},{2,6},{6,2},{3,7},{7,3},{8,12},{12,8},{9,1... | collective-permute-start | bytes 1572872 | tf_op jit(solution)/shard_map/ppermute | solution.py:358
  23.4 112.3 %collective-permute-start.1 = (bf16[128,2048]{1,0:T(8,128)(2,1)S(1)}, bf16[128,2048]{1,0:T(8,128)(2,1)S(1)}, u32[]{:S(2)}, u32[]{:S(2)}) collective-permute-start(bf16[128,2048]{1,0:T(8,128)(2,1)S(1)} %copy-done.10), channel_id=1, source_target_pairs={{0,4},{4,0},{1,5},{5,1},{2,6},{6,2},{3,7},{7,3},{8,12},{12,8},{9,1... | collective-permute-start | bytes 1572872 | tf_op jit(solution)/shard_map/ppermute | solution.py:358
  124.7 11.1 %copy-start.18 = (bf16[2048,128]{0,1:T(8,128)(2,1)}, bf16[2048,128]{0,1:T(8,128)(2,1)S(1)}, u32[]{:S(2)}) copy-start(bf16[2048,128]{0,1:T(8,128)(2,1)S(1)} %collective-permute-done) | copy-start | bytes 1572868
  141.7 119.1 %all-to-all-start.1 = ((bf16[16,2048,128]{2,1,0:T(8,128)(2,1)}), bf16[16,2048,128]{2,1,0:T(8,128)(2,1)}, u32[]{:S(2)}, u32[]{:S(2)}) async-start(bf16[16,2048,128]{2,1,0:T(8,128)(2,1)} %bitcast.32), calls=%async_computation.1 | async-start | bytes 16777216 | tf_op jit(solution)/shard_map/all_to_all | solution.py:429
  228.6 17.9 %collective-permute-start.2 = (f32[4,8,512]{2,1,0:T(8,128)}, f32[4,8,512]{2,1,0:T(8,128)S(1)}, u32[]{:S(2)}, u32[]{:S(2)}) collective-permute-start(f32[4,8,512]{2,1,0:T(8,128)} %get-tuple-element.36.mine_ref), channel_id=1, source_target_pairs={{0,4},{4,0},{1,5},{5,1},{2,6},{6,2},{3,7},{7,3},{8,12},{12,8},{9,1... | collective-permute-start | bytes 196616 | tf_op jit(solution)/shard_map/ppermute | solution.py:358
  250.0 16.4 %copy-start.14 = (bf16[960,256]{1,0:T(8,128)(2,1)S(1)}, bf16[960,256]{1,0:T(8,128)(2,1)}, u32[]{:S(2)}) copy-start(bf16[960,256]{1,0:T(8,128)(2,1)} %shard_map.106) | copy-start | bytes 1474564
  260.8 78.0 %all-to-all-start.2 = ((bf16[8,128,512]{2,1,0:T(8,128)(2,1)}), bf16[8,128,512]{2,1,0:T(8,128)(2,1)S(1)}, u32[]{:S(2)}, u32[]{:S(2)}) async-start(bf16[8,128,512]{2,1,0:T(8,128)(2,1)} %pad_maximum_fusion), calls=%async_computation.2 | async-start | bytes 2097152 | tf_op jit(solution)/shard_map/all_to_all | solution.py:500
  266.4 70.7 %copy-start.12 = (bf16[960,256]{1,0:T(8,128)(2,1)S(1)}, bf16[960,256]{1,0:T(8,128)(2,1)}, u32[]{:S(2)}) copy-start(bf16[960,256]{1,0:T(8,128)(2,1)} %shard_map.105) | copy-start | bytes 1474564
  266.5 60.5 %collective-permute-start.16 = (bf16[960,256]{1,0:T(8,128)(2,1)S(1)}, bf16[960,256]{1,0:T(8,128)(2,1)S(1)}, u32[]{:S(2)}, u32[]{:S(2)}) collective-permute-start(bf16[960,256]{1,0:T(8,128)(2,1)S(1)} %copy-done.14), channel_id=1, source_target_pairs={{0,4},{4,0},{1,5},{5,1},{2,6},{6,2},{3,7},{7,3},{8,12},{12,8},{9,1... | collective-permute-start | bytes 1474568 | tf_op jit(solution)/shard_map/ppermute | solution.py:358
  269.4 67.7 %collective-permute-start.12 = (bf16[960,256]{1,0:T(8,128)(2,1)}, bf16[960,256]{1,0:T(8,128)(2,1)S(1)}, u32[]{:S(2)}, u32[]{:S(2)}) collective-permute-start(bf16[960,256]{1,0:T(8,128)(2,1)} %shard_map.105), channel_id=1, source_target_pairs={{0,4},{4,0},{1,5},{5,1},{2,6},{6,2},{3,7},{7,3},{8,12},{12,8},{9,1... | collective-permute-start | bytes 1474568 | tf_op jit(solution)/shard_map/ppermute | solution.py:358
  326.9 11.9 %collective-permute-start.3 = (f32[4,8,512]{2,1,0:T(8,128)}, f32[4,8,512]{2,1,0:T(8,128)S(1)}, u32[]{:S(2)}, u32[]{:S(2)}) collective-permute-start(f32[4,8,512]{2,1,0:T(8,128)} %get-tuple-element.43.mine_ref), channel_id=1, source_target_pairs={{0,4},{4,0},{1,5},{5,1},{2,6},{6,2},{3,7},{7,3},{8,12},{12,8},{9,1... | collective-permute-start | bytes 196616 | tf_op jit(solution)/shard_map/ppermute | solution.py:358
  327.1 21.1 %collective-permute-start.18 = (bf16[960,256]{1,0:T(8,128)(2,1)S(1)}, bf16[960,256]{1,0:T(8,128)(2,1)S(1)}, u32[]{:S(2)}, u32[]{:S(2)}) collective-permute-start(bf16[960,256]{1,0:T(8,128)(2,1)S(1)} %add_convert_fusion.refs_4_), channel_id=1, source_target_pairs={{0,2},{2,0},{1,3},{3,1},{4,6},{6,4},{5,7},{7,5},{8,10},{10,8},{9,1... | collective-permute-start | bytes 1474568 | tf_op jit(solution)/shard_map/ppermute | solution.py:358
  337.3 14.2 %collective-permute-start.13 = (bf16[960,256]{1,0:T(8,128)(2,1)S(1)}, bf16[960,256]{1,0:T(8,128)(2,1)S(1)}, u32[]{:S(2)}, u32[]{:S(2)}) collective-permute-start(bf16[960,256]{1,0:T(8,128)(2,1)S(1)} %add_convert_fusion.1.refs_0_), channel_id=1, source_target_pairs={{0,1},{1,0},{2,3},{3,2},{4,5},{5,4},{6,7},{7,6},{8,9},{9,8},{10,11... | collective-permute-start | bytes 1474568 | tf_op jit(solution)/shard_map/ppermute | solution.py:358
  342.2 23.2 %collective-permute-start.4 = (bf16[960,256]{1,0:T(8,128)(2,1)}, bf16[960,256]{1,0:T(8,128)(2,1)S(1)}, u32[]{:S(2)}, u32[]{:S(2)}) collective-permute-start(bf16[960,256]{1,0:T(8,128)(2,1)} %shard_map.108), channel_id=1, source_target_pairs={{0,4},{4,0},{1,5},{5,1},{2,6},{6,2},{3,7},{7,3},{8,12},{12,8},{9,1... | collective-permute-start | bytes 1474568 | tf_op jit(solution)/shard_map/ppermute | solution.py:358
  342.3 25.2 %collective-permute-start.17 = (bf16[960,256]{1,0:T(8,128)(2,1)S(1)}, bf16[960,256]{1,0:T(8,128)(2,1)}, u32[]{:S(2)}, u32[]{:S(2)}) collective-permute-start(bf16[960,256]{1,0:T(8,128)(2,1)S(1)} %add_convert_fusion.refs_4_), channel_id=1, source_target_pairs={{0,1},{1,0},{2,3},{3,2},{4,5},{5,4},{6,7},{7,6},{8,9},{9,8},{10,11... | collective-permute-start | bytes 1474568 | tf_op jit(solution)/shard_map/ppermute | solution.py:358
  342.9 26.8 %collective-permute-start.14 = (bf16[960,256]{1,0:T(8,128)(2,1)S(1)}, bf16[960,256]{1,0:T(8,128)(2,1)}, u32[]{:S(2)}, u32[]{:S(2)}) collective-permute-start(bf16[960,256]{1,0:T(8,128)(2,1)S(1)} %add_convert_fusion.1.refs_0_), channel_id=1, source_target_pairs={{0,2},{2,0},{1,3},{3,1},{4,6},{6,4},{5,7},{7,5},{8,10},{10,8},{9,1... | collective-permute-start | bytes 1474568 | tf_op jit(solution)/shard_map/ppermute | solution.py:358
  348.2 22.3 %collective-permute-start.19 = (bf16[960,256]{1,0:T(8,128)(2,1)S(1)}, bf16[960,256]{1,0:T(8,128)(2,1)}, u32[]{:S(2)}, u32[]{:S(2)}) collective-permute-start(bf16[960,256]{1,0:T(8,128)(2,1)S(1)} %collective-permute-done.18.refs_6_), channel_id=1, source_target_pairs={{0,1},{1,0},{2,3},{3,2},{4,5},{5,4},{6,7},{7,6},{8,9},{9,8},{10,11... | collective-permute-start | bytes 1474568 | tf_op jit(solution)/shard_map/ppermute | solution.py:358
  351.5 33.8 %collective-permute-start.15 = (bf16[960,256]{1,0:T(8,128)(2,1)S(1)}, bf16[960,256]{1,0:T(8,128)(2,1)}, u32[]{:S(2)}, u32[]{:S(2)}) collective-permute-start(bf16[960,256]{1,0:T(8,128)(2,1)S(1)} %collective-permute-done.13.refs_1_), channel_id=1, source_target_pairs={{0,2},{2,0},{1,3},{3,1},{4,6},{6,4},{5,7},{7,5},{8,10},{10,8},{9,1... | collective-permute-start | bytes 1474568 | tf_op jit(solution)/shard_map/ppermute | solution.py:358
  366.2 24.4 %collective-permute-start.5 = (bf16[960,256]{1,0:T(8,128)(2,1)}, bf16[960,256]{1,0:T(8,128)(2,1)S(1)}, u32[]{:S(2)}, u32[]{:S(2)}) collective-permute-start(bf16[960,256]{1,0:T(8,128)(2,1)} %shard_map.109), channel_id=1, source_target_pairs={{0,4},{4,0},{1,5},{5,1},{2,6},{6,2},{3,7},{7,3},{8,12},{12,8},{9,1... | collective-permute-start | bytes 1474568 | tf_op jit(solution)/shard_map/ppermute | solution.py:358
  367.5 26.6 %collective-permute-start.6 = (bf16[960,256]{1,0:T(8,128)(2,1)S(1)}, bf16[960,256]{1,0:T(8,128)(2,1)}, u32[]{:S(2)}, u32[]{:S(2)}) collective-permute-start(bf16[960,256]{1,0:T(8,128)(2,1)S(1)} %add_convert_fusion.3.refs_0_), channel_id=1, source_target_pairs={{0,1},{1,0},{2,3},{3,2},{4,5},{5,4},{6,7},{7,6},{8,9},{9,8},{10,11... | collective-permute-start | bytes 1474568 | tf_op jit(solution)/shard_map/ppermute | solution.py:358
  369.7 21.0 %copy-start.13 = (bf16[960,256]{1,0:T(8,128)(2,1)S(1)}, bf16[960,256]{1,0:T(8,128)(2,1)}, u32[]{:S(2)}) copy-start(bf16[960,256]{1,0:T(8,128)(2,1)} %shard_map.109) | copy-start | bytes 1474564
  390.7 14.2 %collective-permute-start.10 = (bf16[960,256]{1,0:T(8,128)(2,1)S(1)}, bf16[960,256]{1,0:T(8,128)(2,1)S(1)}, u32[]{:S(2)}, u32[]{:S(2)}) collective-permute-start(bf16[960,256]{1,0:T(8,128)(2,1)S(1)} %add_convert_fusion.2.refs_4_), channel_id=1, source_target_pairs={{0,2},{2,0},{1,3},{3,1},{4,6},{6,4},{5,7},{7,5},{8,10},{10,8},{9,1... | collective-permute-start | bytes 1474568 | tf_op jit(solution)/shard_map/ppermute | solution.py:358
  390.8 26.8 %collective-permute-start.9 = (bf16[960,256]{1,0:T(8,128)(2,1)S(1)}, bf16[960,256]{1,0:T(8,128)(2,1)S(1)}, u32[]{:S(2)}, u32[]{:S(2)}) collective-permute-start(bf16[960,256]{1,0:T(8,128)(2,1)S(1)} %add_convert_fusion.2.refs_4_), channel_id=1, source_target_pairs={{0,1},{1,0},{2,3},{3,2},{4,5},{5,4},{6,7},{7,6},{8,9},{9,8},{10,11... | collective-permute-start | bytes 1474568 | tf_op jit(solution)/shard_map/ppermute | solution.py:358
  392.2 25.4 %collective-permute-start.7 = (bf16[960,256]{1,0:T(8,128)(2,1)S(1)}, bf16[960,256]{1,0:T(8,128)(2,1)S(1)}, u32[]{:S(2)}, u32[]{:S(2)}) collective-permute-start(bf16[960,256]{1,0:T(8,128)(2,1)S(1)} %add_convert_fusion.3.refs_0_), channel_id=1, source_target_pairs={{0,2},{2,0},{1,3},{3,1},{4,6},{6,4},{5,7},{7,5},{8,10},{10,8},{9,1... | collective-permute-start | bytes 1474568 | tf_op jit(solution)/shard_map/ppermute | solution.py:358
  399.1 9.3 %collective-permute-start.20 = (bf16[1024,128]{0,1:T(8,128)(2,1)S(1)}, bf16[1024,128]{0,1:T(8,128)(2,1)S(1)}, u32[]{:S(2)}, u32[]{:S(2)}) collective-permute-start(bf16[1024,128]{0,1:T(8,128)(2,1)S(1)} %fusion.17), channel_id=1, source_target_pairs={{0,16},{8,24},{16,0},{24,8},{1,17},{9,25},{17,1},{25,9},{2,18},{10... | collective-permute-start | bytes 786440 | tf_op jit(solution)/shard_map/ppermute | solution.py:379
  401.6 9.8 %collective-permute-start.22 = (bf16[128,1024]{1,0:T(8,128)(2,1)S(1)}, bf16[128,1024]{1,0:T(8,128)(2,1)S(1)}, u32[]{:S(2)}, u32[]{:S(2)}) collective-permute-start(bf16[128,1024]{1,0:T(8,128)(2,1)S(1)} %dynamic-slice_convert_fusion), channel_id=1, source_target_pairs={{0,16},{8,24},{16,0},{24,8},{1,17},{9,25},{17,1},{25,9},{2,18},{10... | collective-permute-start | bytes 786440 | tf_op jit(solution)/shard_map/ppermute | solution.py:379
  405.0 19.3 %collective-permute-start.8 = (bf16[960,256]{1,0:T(8,128)(2,1)}, bf16[960,256]{1,0:T(8,128)(2,1)}, u32[]{:S(2)}, u32[]{:S(2)}) collective-permute-start(bf16[960,256]{1,0:T(8,128)(2,1)} %collective-permute-done.6.refs_1_), channel_id=1, source_target_pairs={{0,2},{2,0},{1,3},{3,1},{4,6},{6,4},{5,7},{7,5},{8,10},{10,8},{9,1... | collective-permute-start | bytes 1474568 | tf_op jit(solution)/shard_map/ppermute | solution.py:358
  408.4 9.2 %collective-permute-start.11 = (bf16[960,256]{1,0:T(8,128)(2,1)S(1)}, bf16[960,256]{1,0:T(8,128)(2,1)}, u32[]{:S(2)}, u32[]{:S(2)}) collective-permute-start(bf16[960,256]{1,0:T(8,128)(2,1)S(1)} %collective-permute-done.10.refs_6_), channel_id=1, source_target_pairs={{0,1},{1,0},{2,3},{3,2},{4,5},{5,4},{6,7},{7,6},{8,9},{9,8},{10,11... | collective-permute-start | bytes 1474568 | tf_op jit(solution)/shard_map/ppermute | solution.py:358
  411.3 1.5 collective-permute-start.21
  412.9 3.0 collective-permute-start.23
  (23 other events, 89.3 us)

commit v5 on v4

--- a/solution.py
+++ b/solution.py
@@ -14,6 +14,8 @@
 MARK_ROWS = 16
 MARK_BASE = 100.0
 MARK_LEAST = 64.0
+GRANULE = 32
+KEY_TILE = 512
 
 
 def pack_kernel(
@@ -79,93 +81,91 @@
 
 
 def attention_kernel(
-    places, counts, q_ref, b_ref, recv_ref, co_ref, ds_ref, stat_ref,
-    kv, scores, probs, top, acc, total, dacc, columns, bias, sems, *, slots, scale, first,
+    places, counts, offsets, sizes, q_ref, b_ref, bias_ref, recv_ref, co_ref, ds_ref, stat_ref,
+    kv, scores, probs, top, acc, dacc, columns, sems, *, slots, scale,
 ):
-    patch = first + pl.program_id(0)
-    patches = first + pl.num_programs(0)
-    block_rows = recv_ref.shape[2]
-    pair = 2 * block_rows
-
-    def copy(which, j, place):
-        return pltpu.make_async_copy(
-            recv_ref.at[place],
-            kv.at[which % 2, :, pl.ds(pl.multiple_of(j * block_rows, block_rows), block_rows), :],
-            sems.at[which % 2, j],
-        )
-
-    def start(which):
+    patch = pl.program_id(0)
+    block_rows, width = recv_ref.shape[2:]
+    steps = block_rows // GRANULE
+    folds = KEY_TILE // LANES
+
+    def each_copy(which, act):
         @pl.loop(0, counts[which])
         def _(j):
-            copy(which, j, places[which * slots + j]).start()
-
-    @pl.when(patch == first)
+            entry = which * slots + j
+            at = pl.multiple_of(offsets[entry] * GRANULE, GRANULE)
+            for size in range(1, steps + 1):
+
+                @pl.when(sizes[entry] == size)
+                def _():
+                    act(
+                        pltpu.make_async_copy(
+                            recv_ref.at[places[entry], :, pl.ds(0, size * GRANULE), :],
+                            kv.at[which % 2, :, pl.ds(at, size * GRANULE), :],
+                            sems.at[which % 2, j],
+                        )
+                    )
+
+    @pl.when(patch == 0)
     def _():
-        start(patch)
-
-    @pl.when(patch + 1 < patches)
+        each_copy(patch, lambda copy: copy.start())
+
+    @pl.when(patch + 1 < pl.num_programs(0))
     def _():
-        start(patch + 1)
-
-    here = counts[patch]
-    tiles = jnp.maximum((here + 1) // 2, 1)
-
-    @pl.loop(here, 2 * tiles)
-    def _(j):
-        kv[patch % 2, :, pl.ds(pl.multiple_of(j * block_rows, block_rows), block_rows), :] = (
-            jnp.zeros((2, block_rows, kv.shape[3]), kv.dtype)
-        )
-        bias[pl.ds(j, 1), :] = jnp.full((1, block_rows), masked_value, jnp.float32)
-
-    lane = lax.broadcasted_iota(jnp.int32, (1, block_rows), 1)
-
-    @pl.loop(0, here)
-    def _(j):
-        copy(patch, j, 0).wait()
-        end = pl.multiple_of(j * block_rows + block_rows - MARK_ROWS, MARK_ROWS)
-        last = kv[patch % 2, 0, pl.ds(end, MARK_ROWS), :].astype(jnp.float32)[MARK_ROWS - 1 :]
-        mark = jnp.sum(jnp.where(lane == 0, last, 0.0), axis=1, keepdims=True)
-        valid = jnp.where(mark > MARK_LEAST, mark - MARK_BASE, float(block_rows))
-        bias[pl.ds(j, 1), :] = jnp.where(lane.astype(jnp.float32) < valid, 0.0, masked_value)
+        each_copy(patch + 1, lambda copy: copy.start())
+
+    filled = offsets[patch * slots + slots - 1] + sizes[patch * slots + slots - 1]
+    per_tile = KEY_TILE // GRANULE
+    tiles = jnp.maximum((filled + per_tile - 1) // per_tile, 1)
+
+    @pl.loop(filled, tiles * per_tile)
+    def _(g):
+        kv[patch % 2, :, pl.ds(pl.multiple_of(g * GRANULE, GRANULE), GRANULE), :] = jnp.zeros(
+            (2, GRANULE, width), kv.dtype
+        )
+
+    each_copy(patch, lambda copy: copy.wait())
 
     def key_tile(t, head):
-        return kv[patch % 2, head, pl.ds(pl.multiple_of(t * pair, pair), pair), :]
+        return kv[patch % 2, head, pl.ds(pl.multiple_of(t * KEY_TILE, KEY_TILE), KEY_TILE), :]
 
     rows = q_ref.shape[0]
     lanes = [pl.ds(head * LANES, LANES) for head in range(2)]
     top[...] = jnp.full_like(top, masked_value)
     acc[...] = jnp.zeros_like(acc)
-    total[...] = jnp.zeros_like(total)
     dacc[...] = jnp.zeros_like(dacc)
 
     @pl.loop(0, tiles)
     def _(t):
-        bias_lo = bias[pl.ds(2 * t, 1), :]
-        bias_hi = bias[pl.ds(2 * t + 1, 1), :]
         for head in range(2):
             score = nt_dot(q_ref[:, lanes[head]], key_tile(t, head))
-            low = score[:, :block_rows] + bias_lo
-            high = score[:, block_rows:] + bias_hi
-            scores[head, t, :, :block_rows] = low
-            scores[head, t, :, block_rows:] = high
-            top[head] = jnp.maximum(top[head], jnp.maximum(low, high))
+            best = top[head]
+            for fold in range(folds):
+                part = score[:, fold * LANES : (fold + 1) * LANES]
+                part = part + bias_ref[0, pl.ds(t * folds + fold, 1), :]
+                scores[head, t, :, fold * LANES : (fold + 1) * LANES] = part
+                best = jnp.maximum(best, part)
+            top[head] = best
 
     row_max = [jnp.max(top[head], axis=1, keepdims=True) for head in range(2)]
+    ones = jnp.ones((KEY_TILE, LANES), jnp.bfloat16)
 
     @pl.loop(0, tiles)
     def _(t):
         for head in range(2):
             weights = jnp.exp(scores[head, t] - row_max[head]).astype(jnp.bfloat16)
             probs[head, t] = weights
-            wide = weights.astype(jnp.float32)
-            total[head] += wide[:, :block_rows] + wide[:, block_rows:]
-            acc[head] += jnp.dot(weights, key_tile(t, head), preferred_element_type=jnp.float32)
+            acc[head] += jnp.dot(
+                weights,
+                jnp.concatenate([key_tile(t, head), ones], axis=1),
+                preferred_element_type=jnp.float32,
+            )
 
     inverse, inner, stats = [], [], []
     for head in range(2):
-        row_sum = jnp.sum(total[head], axis=1, keepdims=True)
+        row_sum = acc[head, :, width : width + 1]
         inverse.append(1.0 / row_sum)
-        outs = acc[head] * inverse[head]
+        outs = acc[head, :, :width] * inverse[head]
         co_ref[:, lanes[head]] = outs
         inner.append(
             jnp.sum(outs * b_ref[:, lanes[head]].astype(jnp.float32), axis=1, keepdims=True)
@@ -191,32 +191,35 @@
     stat_ref[0] = jnp.transpose(columns[...])[:8]
 
 
-def attention(
-    places, counts, queries, backs, received, chunk, first, patch_blocks, rows, slots, scale
-):
-    total_rows = patch_blocks * rows
+def attention(tables, bias, queries, backs, received, chunk, slots, scale):
+    patch_blocks = bias.shape[0]
+    total_rows = queries.shape[0]
+    rows = total_rows // patch_blocks
     padded = pl.cdiv(rows, LANES) * LANES
     block_rows, width = received.shape[2:]
-    wide = pl.BlockSpec((rows, 2 * LANES), lambda p, *_: (first + p, chunk))
+    tiles = pl.cdiv(slots * block_rows, KEY_TILE)
+    wide = pl.BlockSpec((rows, 2 * LANES), lambda p, *_: (p, chunk))
     out = pl.BlockSpec((rows, 2 * LANES), lambda p, *_: (p, 0))
-    tiles = (slots + 1) // 2
     return pl.pallas_call(
-        functools.partial(attention_kernel, slots=slots, scale=scale, first=first),
+        functools.partial(attention_kernel, slots=slots, scale=scale),
         grid_spec=pltpu.PrefetchScalarGridSpec(
-            num_scalar_prefetch=2,
+            num_scalar_prefetch=4,
             grid=(patch_blocks,),
-            in_specs=[wide, wide, pl.BlockSpec(memory_space=pl.ANY)],
+            in_specs=[
+                wide,
+                wide,
+                pl.BlockSpec((1,) + bias.shape[1:], lambda p, *_: (p, 0, 0)),
+                pl.BlockSpec(memory_space=pl.ANY),
+            ],
             out_specs=[out, out, pl.BlockSpec((1, 8, padded), lambda p, *_: (p, 0, 0))],
             scratch_shapes=[
-                pltpu.VMEM((2, 2, tiles * 2 * block_rows, width), jnp.bfloat16),
-                pltpu.VMEM((2, tiles, rows, 2 * block_rows), jnp.float32),
-                pltpu.VMEM((2, tiles, rows, 2 * block_rows), jnp.bfloat16),
-                pltpu.VMEM((2, rows, block_rows), jnp.float32),
-                pltpu.VMEM((2, rows, width), jnp.float32),
-                pltpu.VMEM((2, rows, block_rows), jnp.float32),
+                pltpu.VMEM((2, 2, tiles * KEY_TILE, width), jnp.bfloat16),
+                pltpu.VMEM((2, tiles, rows, KEY_TILE), jnp.float32),
+                pltpu.VMEM((2, tiles, rows, KEY_TILE), jnp.bfloat16),
+                pltpu.VMEM((2, rows, LANES), jnp.float32),
+                pltpu.VMEM((2, rows, width + LANES), jnp.float32),
                 pltpu.VMEM((2, rows, width), jnp.float32),
                 pltpu.VMEM((padded, LANES), jnp.float32),
-                pltpu.VMEM((2 * tiles, block_rows), jnp.float32),
                 pltpu.SemaphoreType.DMA((2, slots)),
             ],
         ),
@@ -228,7 +231,7 @@
             transcendentals=total_rows * slots * block_rows,
             bytes_accessed=40 << 20,
         ),
-    )(places, counts, queries, backs, received)
+    )(*tables, queries, backs, bias, received)
 
 
 def merge_kernel(co_ref, ds_ref, mine_ref, theirs_ref, out_ref, *, scale, split):
@@ -358,11 +361,12 @@
     return lax.ppermute(x, axis, [(0, 1), (1, 0)])
 
 
-def gather_half(x, zl_size, y_size, y_first):
+def gather_half(x, zl_size, y_size):
     if zl_size == 2 and y_size == 2:
         by_y = swap(x, "y")
         by_zl = swap(x, "zl")
-        corner = swap(by_y, "zl") if y_first else swap(by_zl, "y")
+        cut = x.shape[0] // 2
+        corner = jnp.concatenate([swap(by_y[:cut], "zl"), swap(by_zl[cut:], "y")], axis=0)
         return [x, by_y, by_zl, corner]
     whole = lax.all_gather(x, ("zl", "y"), axis=0, tiled=False)
     return [whole[i] for i in range(zl_size * y_size)]
@@ -452,6 +456,28 @@
     places = jnp.sum(jnp.where(at, arrival[:, :, None], 0), axis=1).reshape(entry_count)
     counts = jnp.sum(in_half.astype(jnp.int32), axis=1)
 
+    marks = received[0][:, 0, block_rows - MARK_ROWS :, :].astype(jnp.float32)
+    marks = marks[:, MARK_ROWS - 1, 0]
+    rows_of = jnp.where(marks > MARK_LEAST, marks - MARK_BASE, float(block_rows)).astype(jnp.int32)
+    arrivals = jnp.arange(rows_of.shape[0], dtype=jnp.int32)
+    valid = jnp.sum(
+        jnp.where(places[:, None] == arrivals[None, :], rows_of[None, :], 0), axis=1
+    ).reshape(patch_blocks, slots)
+    valid = jnp.where(spots[None, :] < counts[:, None], valid, 0)
+    sizes_of = (valid + GRANULE - 1) // GRANULE
+    offsets = jnp.sum(
+        jnp.where(spots[None, None, :] < spots[None, :, None], sizes_of[:, None, :], 0), axis=2
+    )
+    tile_count = pl.cdiv(slots * block_rows, KEY_TILE)
+    bias_shape = (patch_blocks, tile_count * KEY_TILE // LANES, LANES)
+    key_at = LANES * lax.broadcasted_iota(jnp.int32, bias_shape, 1) + lax.broadcasted_iota(
+        jnp.int32, bias_shape, 2
+    )
+    first_key = (offsets * GRANULE)[:, :, None, None]
+    seen = (key_at[:, None] >= first_key) & (key_at[:, None] < first_key + valid[:, :, None, None])
+    bias = jnp.where(jnp.any(seen, axis=1), 0.0, masked_value).astype(jnp.float32)
+    tables = (places, counts, offsets.reshape(entry_count), sizes_of.reshape(entry_count))
+
     q_other, o_other, received[0] = lax.optimization_barrier(
         (q_other, o_other, received[0])
     )
@@ -488,7 +514,6 @@
     else:
         order = jnp.arange(inner, dtype=jnp.int32)
 
-    rows = row_count // patch_blocks
     part_count = 2 if patch_blocks % 2 == 0 else 1
     part_patches = patch_blocks // part_count
     gathered = []
@@ -496,10 +521,10 @@
     for c in range(local_heads):
         final = c + 1 == local_heads
         if final:
-            cols, places, received[c] = lax.optimization_barrier((cols, places, received[c]))
+            cols, bias, received[c] = lax.optimization_barrier((cols, bias, received[c]))
             cols = lax.all_to_all(cols, ("zh", "zl", "y"), split_axis=0, concat_axis=0, tiled=True)
         outs, douts, mine = attention(
-            places, counts, queries, backs, received[c], c, 0, patch_blocks, rows, slots, head_scale
+            tables, bias, queries, backs, received[c], c, slots, head_scale
         )
         theirs = swap(mine, "zh")
         if final:
@@ -509,14 +534,12 @@
             for start in range(0, patch_blocks, part_patches)
         ]
         if not final:
-            parts, places = lax.optimization_barrier((parts, places))
+            parts, bias = lax.optimization_barrier((parts, bias))
         merged = [
             (part.astype(jnp.float32) + swap(part, "zh").astype(jnp.float32)).astype(jnp.bfloat16)
             for part in parts
         ]
-        pieces = [
-            gather_half(x, zl_size, y_size, i % 2 == 0) for i, x in enumerate(merged)
-        ]
+        pieces = [gather_half(x, zl_size, y_size) for x in merged]
         gathered.append(pieces)
         if final:
             merged, pieces[0][1] = lax.optimization_barrier((merged, pieces[0][1]))

time: 434 us -> 446 us (1.028)
  waiting for transfers between devices: 183 us -> 239 us
  Pallas kernels: 146 us -> 94.4 us
  starting transfers between devices: 45.1 us -> 51 us
  local copies, waits for them, and re-layouts: 28.4 us -> 23.5 us
    ppermute x20 -> x24, waiting for transfers between devices: 164 us -> 225 us  [swap(): return lax.ppermute(x, axis, [(0, 1), (1, 0)])]
    pallas_call x2, Pallas kernels: 115 us -> 64.8 us  [attention(): pl.pallas_call(functools.partial(attention_kernel, slots=slots, scale=sca...]
    unnamed x60 -> x56, local copies, waits for them, and re-layouts: 23.8 us -> 17.1 us
    ppermute x20 -> x24, starting transfers between devices: 18.7 us -> 24.1 us  [swap(): return lax.ppermute(x, axis, [(0, 1), (1, 0)])]
    ppermute x4, waiting for transfers between devices: 5.56 us -> 0.68 us  [scatter_sum(): lax.ppermute(give.astype(jnp.bfloat16), 'dp', [(i, i ^ step) for i in ran...]
  transfers between devices with their start and end apart: 27 -> 31, of which waited for: 16 -> 17; matrix products, arithmetic and copies ran while one was open for 8% -> 9% of each run, Pallas kernels for 32% -> 20%
where the time goes in v5:
time: 446 us; the launch traced here: 445 us
  waiting for transfers between devices  239 us (54%)
  Pallas kernels  94.4 us (21%)
  starting transfers between devices  51 us (11%)
  local copies, waits for them, and re-layouts  23.5 us (5%)
  matrix products  20.5 us (5%)
  other arithmetic  14.8 us (3%)
    ppermute x24, waiting for transfers between devices, swap(): return lax.ppermute(x, axis, [(0, 1), (1, 0)])  225 us
    pallas_call x2, Pallas kernels, attention(): pl.pallas_call(functools.partial(attention_kernel, slots=slots, scale=sca...  64.8 us
    ppermute x24, starting transfers between devices, swap(): return lax.ppermute(x, axis, [(0, 1), (1, 0)])  24.1 us
    all_to_all x2, starting transfers between devices, exchange(): lax.all_to_all(x, ('dp', 'zl', 'y'), split_axis=0, concat_axis=0, tiled=T...  18.5 us
    unnamed x56, local copies, waits for them, and re-layouts  17.1 us
    all_to_all x2, waiting for transfers between devices, exchange(): lax.all_to_all(x, ('dp', 'zl', 'y'), split_axis=0, concat_axis=0, tiled=T...  13.8 us
    pallas_call x4, Pallas kernels, merge(): pl.pallas_call(functools.partial(merge_kernel, scale=scale, split=split),...  11.5 us
    pallas_call x2, Pallas kernels, pack_blocks(): pl.pallas_call(functools.partial(pack_kernel, chunk=chunk, local_heads=lo...  9.48 us
  transfers between devices with their start and end apart: 31, of which 17 were waited for; matrix products, arithmetic and copies ran while one was open for 9% of the time, Pallas kernels for 20%

profile of v5, /device:TPU:0, one launch (start us, length us, event | category | flops | bytes accessed | tf_op | source)
XLA Modules:
  0.0 444.7 jit_solution(12723514138056132473)
XLA Ops:
  2.9 3.4 copy-done
  6.9 4.4 shard_map.102
  11.4 3.3 copy-done.3
  14.7 6.5 %all-to-all-start = ((bf16[16,2048,128]{2,1,0:T(8,128)(2,1)}), bf16[16,2048,128]{2,1,0:T(8,128)(2,1)}, u32[]{:S(2)}, u32[]{:S(2)}) async-start(bf16[16,2048,128]{2,1,0:T(8,128)(2,1)} %bitcast.35), calls=%async_computation | async-start | bytes 16777216 | tf_op jit(solution)/shard_map/all_to_all | solution.py:433
  24.4 3.4 copy-done.1
  27.8 5.0 %shard_map.103 = bf16[4,4,8,2,128,128]{5,4,3,2,1,0:T(8,128)(2,1)S(1)} custom-call(s32[32]{0:T(128)S(1)} %reshape.442.chosen, s32[4]{0:T(128)S(1)} %reduce_sum.99.counts, s32[16]{0:T(128)S(1)} %copy-done.7, bf16[16,128,16,128]{3,2,1,0:T(8,128)(2,1)S(1)} %copy-done.1), custom_call_target="tpu_custom_call" | custom-call | bytes 16777216 | tf_op jit(solution)/shard_map/pallas_call | solution.py:49
  32.8 3.2 copy-done.2
  36.1 88.5 %collective-permute-done = bf16[2048,128]{0,1:T(8,128)(2,1)S(1)} collective-permute-done((bf16[2048,128]{0,1:T(8,128)(2,1)S(1)}, bf16[2048,128]{0,1:T(8,128)(2,1)S(1)}, u32[]{:S(2)}, u32[]{:S(2)}) %collective-permute-start) | collective-permute-done | bytes 524320 | tf_op jit(solution)/shard_map/ppermute | solution.py:361
  124.6 11.0 %collective-permute-done.1 = bf16[128,2048]{1,0:T(8,128)(2,1)S(1)} collective-permute-done((bf16[128,2048]{1,0:T(8,128)(2,1)S(1)}, bf16[128,2048]{1,0:T(8,128)(2,1)S(1)}, u32[]{:S(2)}, u32[]{:S(2)}) %collective-permute-start.1) | collective-permute-done | bytes 524320 | tf_op jit(solution)/shard_map/ppermute | solution.py:361
  135.6 5.9 %all-to-all-done = bf16[16,2048,128]{2,1,0:T(8,128)(2,1)} async-done(((bf16[16,2048,128]{2,1,0:T(8,128)(2,1)}), bf16[16,2048,128]{2,1,0:T(8,128)(2,1)}, u32[]{:S(2)}, u32[]{:S(2)}) %all-to-all-start) | async-done | bytes 8388640 | tf_op jit(solution)/shard_map/all_to_all | solution.py:433
  141.6 12.0 %all-to-all-start.1 = ((bf16[16,2048,128]{2,1,0:T(8,128)(2,1)}), bf16[16,2048,128]{2,1,0:T(8,128)(2,1)}, u32[]{:S(2)}, u32[]{:S(2)}) async-start(bf16[16,2048,128]{2,1,0:T(8,128)(2,1)} %bitcast.34), calls=%async_computation.1 | async-start | bytes 16777216 | tf_op jit(solution)/shard_map/all_to_all | solution.py:433
  164.6 9.0 %fusion.2.b_ref = bf16[1920,512]{1,0:T(8,128)(2,1)} fusion(bf16[512,2048]{1,0:T(8,128)(2,1)S(1)} %bitcast.40, bf16[1920,2048]{1,0:T(8,128)(2,1)} %param.13), kind=kOutput, calls=%fused_computation.5 | convolution fusion | flops 4027514880 | bytes 11927552 | tf_op jit(solution)/shard_map/dot_general | solution.py:78
  173.6 5.5 %fusion.3.q_ref = bf16[1920,512]{1,0:T(8,128)(2,1)} fusion(bf16[2048,512]{0,1:T(8,128)(2,1)S(1)} %bitcast.41, bf16[1920,2048]{1,0:T(8,128)(2,1)S(1)} %bitcast.37), kind=kOutput, calls=%fused_computation.6 | convolution fusion | flops 4028497920 | bytes 11927552 | tf_op jit(solution)/shard_map/dot_general | solution.py:501
  179.1 32.4 %shard_map.104 = (f32[1920,256]{1,0:T(8,128)}, f32[1920,256]{1,0:T(8,128)}, f32[4,8,512]{2,1,0:T(8,128)}) custom-call(s32[128]{0:T(128)} %copy-done.21, s32[4]{0:T(128)} %copy-done.20, s32[128]{0:T(128)} %reshape.446.offsets, s32[128]{0:T(128)} %and_select_fusion.sizes, bf16[1920,512]{1,0:T(8,128)(2,1)} %fusion.3.q_ref, bf16[1920,512]{1,0:T(8,128)(2,1)} %fusion.2.b_ref, ...), custom_call_target="tpu_custom_call" | custom-call | flops 8053063680 | bytes 41943040 | tf_op jit(solution)/shard_map/pallas_call | solution.py:203
  212.6 34.5 %collective-permute-done.2.theirs_ref = f32[4,8,512]{2,1,0:T(8,128)S(1)} collective-permute-done((f32[4,8,512]{2,1,0:T(8,128)}, f32[4,8,512]{2,1,0:T(8,128)S(1)}, u32[]{:S(2)}, u32[]{:S(2)}) %collective-permute-start.2) | collective-permute-done | bytes 65568 | tf_op jit(solution)/shard_map/ppermute | solution.py:361
  250.6 2.9 shard_map.105
  253.5 7.8 %all-to-all-done.1 = bf16[16,2048,128]{2,1,0:T(8,128)(2,1)} async-done(((bf16[16,2048,128]{2,1,0:T(8,128)(2,1)}), bf16[16,2048,128]{2,1,0:T(8,128)(2,1)}, u32[]{:S(2)}, u32[]{:S(2)}) %all-to-all-start.1) | async-done | bytes 8388640 | tf_op jit(solution)/shard_map/all_to_all | solution.py:433
  261.3 5.7 %all-to-all-start.2 = ((bf16[8,128,512]{2,1,0:T(8,128)(2,1)}), bf16[8,128,512]{2,1,0:T(8,128)(2,1)S(1)}, u32[]{:S(2)}, u32[]{:S(2)}) async-start(bf16[8,128,512]{2,1,0:T(8,128)(2,1)} %pad_maximum_fusion.1), calls=%async_computation.2 | async-start | bytes 2097152 | tf_op jit(solution)/shard_map/all_to_all | solution.py:525
  267.0 3.0 collective-permute-start.19
  270.1 32.4 %shard_map.107 = (f32[1920,256]{1,0:T(8,128)}, f32[1920,256]{1,0:T(8,128)}, f32[4,8,512]{2,1,0:T(8,128)}) custom-call(s32[128]{0:T(128)} %copy-done.21, s32[4]{0:T(128)} %copy-done.20, s32[128]{0:T(128)} %reshape.446.offsets, s32[128]{0:T(128)} %and_select_fusion.sizes, bf16[1920,512]{1,0:T(8,128)(2,1)} %fusion.3.q_ref, bf16[1920,512]{1,0:T(8,128)(2,1)} %fusion.2.b_ref, ...), custom_call_target="tpu_custom_call" | custom-call | flops 8053063680 | bytes 41943040 | tf_op jit(solution)/shard_map/pallas_call | solution.py:203
  302.5 3.2 collective-permute-start.3
  305.7 21.5 %collective-permute-done.19 = bf16[960,256]{1,0:T(8,128)(2,1)S(1)} collective-permute-done((bf16[960,256]{1,0:T(8,128)(2,1)S(1)}, bf16[960,256]{1,0:T(8,128)(2,1)S(1)}, u32[]{:S(2)}, u32[]{:S(2)}) %collective-permute-start.19) | collective-permute-done | bytes 491552 | tf_op jit(solution)/shard_map/ppermute | solution.py:361
  328.8 8.7 %collective-permute-done.14 = bf16[960,256]{1,0:T(8,128)(2,1)S(1)} collective-permute-done((bf16[960,256]{1,0:T(8,128)(2,1)}, bf16[960,256]{1,0:T(8,128)(2,1)S(1)}, u32[]{:S(2)}, u32[]{:S(2)}) %collective-permute-start.14) | collective-permute-done | bytes 491552 | tf_op jit(solution)/shard_map/ppermute | solution.py:361
  344.3 11.6 %collective-permute-done.21.refs_6_ = bf16[960,256]{1,0:T(8,128)(2,1)S(1)} collective-permute-done((bf16[960,256]{1,0:T(8,128)(2,1)S(1)}, bf16[960,256]{1,0:T(8,128)(2,1)S(1)}, u32[]{:S(2)}, u32[]{:S(2)}) %collective-permute-start.21) | collective-permute-done | bytes 491552 | tf_op jit(solution)/shard_map/ppermute | solution.py:361
  358.9 11.1 %collective-permute-done.16.refs_2_ = bf16[960,256]{1,0:T(8,128)(2,1)} collective-permute-done((bf16[960,256]{1,0:T(8,128)(2,1)S(1)}, bf16[960,256]{1,0:T(8,128)(2,1)}, u32[]{:S(2)}, u32[]{:S(2)}) %collective-permute-start.16) | collective-permute-done | bytes 491552 | tf_op jit(solution)/shard_map/ppermute | solution.py:361
  383.0 4.4 shard_map.110.refs_9_
  387.4 14.8 %collective-permute-done.5 = bf16[960,256]{1,0:T(8,128)(2,1)S(1)} collective-permute-done((bf16[960,256]{1,0:T(8,128)(2,1)}, bf16[960,256]{1,0:T(8,128)(2,1)S(1)}, u32[]{:S(2)}, u32[]{:S(2)}) %collective-permute-start.5) | collective-permute-done | bytes 491552 | tf_op jit(solution)/shard_map/ppermute | solution.py:361
  405.4 4.7 %convolution_multiply_fusion = f32[128,2048]{1,0:T(8,128)S(1)} fusion(bf16[1920,2048]{1,0:T(8,128)(2,1)} %param.13, bf16[960,128]{1,0:T(8,128)(2,1)S(1)} %get-tuple-element.76, bf16[960,128]{1,0:T(8,128)(2,1)S(1)} %get-tuple-element.75, bf16[960,128]{1,0:T(8,128)(2,1)S(1)} %copy-done.9, bf16[960,128]{1,0:T(8,128)(2,1)S(1)} %copy-done.11), kind=kOutput, calls=%fused_computation.7 | convolution fusion | flops 1009598464 | bytes 9895936 | tf_op jit(solution)/shard_map/dot_general | solution.py:565
  411.3 4.2 collective-permute-done.10.refs_5_
  418.8 9.2 %collective-permute-done.7.refs_2_ = bf16[960,256]{1,0:T(8,128)(2,1)S(1)} collective-permute-done((bf16[960,256]{1,0:T(8,128)(2,1)S(1)}, bf16[960,256]{1,0:T(8,128)(2,1)S(1)}, u32[]{:S(2)}, u32[]{:S(2)}) %collective-permute-start.7) | collective-permute-done | bytes 491552 | tf_op jit(solution)/shard_map/ppermute | solution.py:361
  434.3 3.0 collective-permute-done.8
  437.3 4.3 shard_map.111
  (175 shorter events, 62.9 us)
Async XLA Ops:
  14.7 126.9 %all-to-all-start = ((bf16[16,2048,128]{2,1,0:T(8,128)(2,1)}), bf16[16,2048,128]{2,1,0:T(8,128)(2,1)}, u32[]{:S(2)}, u32[]{:S(2)}) async-start(bf16[16,2048,128]{2,1,0:T(8,128)(2,1)} %bitcast.35), calls=%async_computation | async-start | bytes 16777216 | tf_op jit(solution)/shard_map/all_to_all | solution.py:433
  21.4 103.2 %collective-permute-start = (bf16[2048,128]{0,1:T(8,128)(2,1)S(1)}, bf16[2048,128]{0,1:T(8,128)(2,1)S(1)}, u32[]{:S(2)}, u32[]{:S(2)}) collective-permute-start(bf16[2048,128]{0,1:T(8,128)(2,1)S(1)} %copy.25), channel_id=1, source_target_pairs={{0,4},{4,0},{1,5},{5,1},{2,6},{6,2},{3,7},{7,3},{8,12},{12,8},{9,1... | collective-permute-start | bytes 1572872 | tf_op jit(solution)/shard_map/ppermute | solution.py:361
  24.0 111.6 %collective-permute-start.1 = (bf16[128,2048]{1,0:T(8,128)(2,1)S(1)}, bf16[128,2048]{1,0:T(8,128)(2,1)S(1)}, u32[]{:S(2)}, u32[]{:S(2)}) collective-permute-start(bf16[128,2048]{1,0:T(8,128)(2,1)S(1)} %copy-done.12), channel_id=1, source_target_pairs={{0,4},{4,0},{1,5},{5,1},{2,6},{6,2},{3,7},{7,3},{8,12},{12,8},{9,1... | collective-permute-start | bytes 1572872 | tf_op jit(solution)/shard_map/ppermute | solution.py:361
  141.6 119.7 %all-to-all-start.1 = ((bf16[16,2048,128]{2,1,0:T(8,128)(2,1)}), bf16[16,2048,128]{2,1,0:T(8,128)(2,1)}, u32[]{:S(2)}, u32[]{:S(2)}) async-start(bf16[16,2048,128]{2,1,0:T(8,128)(2,1)} %bitcast.34), calls=%async_computation.1 | async-start | bytes 16777216 | tf_op jit(solution)/shard_map/all_to_all | solution.py:433
  211.5 35.6 %collective-permute-start.2 = (f32[4,8,512]{2,1,0:T(8,128)}, f32[4,8,512]{2,1,0:T(8,128)S(1)}, u32[]{:S(2)}, u32[]{:S(2)}) collective-permute-start(f32[4,8,512]{2,1,0:T(8,128)} %get-tuple-element.36.mine_ref), channel_id=1, source_target_pairs={{0,4},{4,0},{1,5},{5,1},{2,6},{6,2},{3,7},{7,3},{8,12},{12,8},{9,1... | collective-permute-start | bytes 196616 | tf_op jit(solution)/shard_map/ppermute | solution.py:361
  261.3 78.0 %all-to-all-start.2 = ((bf16[8,128,512]{2,1,0:T(8,128)(2,1)}), bf16[8,128,512]{2,1,0:T(8,128)(2,1)S(1)}, u32[]{:S(2)}, u32[]{:S(2)}) async-start(bf16[8,128,512]{2,1,0:T(8,128)(2,1)} %pad_maximum_fusion.1), calls=%async_computation.2 | async-start | bytes 2097152 | tf_op jit(solution)/shard_map/all_to_all | solution.py:525
  267.0 70.5 %copy-start.15 = (bf16[960,256]{1,0:T(8,128)(2,1)S(1)}, bf16[960,256]{1,0:T(8,128)(2,1)}, u32[]{:S(2)}) copy-start(bf16[960,256]{1,0:T(8,128)(2,1)} %shard_map.105) | copy-start | bytes 1474564
  267.0 60.1 %collective-permute-start.19 = (bf16[960,256]{1,0:T(8,128)(2,1)S(1)}, bf16[960,256]{1,0:T(8,128)(2,1)S(1)}, u32[]{:S(2)}, u32[]{:S(2)}) collective-permute-start(bf16[960,256]{1,0:T(8,128)(2,1)S(1)} %copy-done.16), channel_id=1, source_target_pairs={{0,4},{4,0},{1,5},{5,1},{2,6},{6,2},{3,7},{7,3},{8,12},{12,8},{9,1... | collective-permute-start | bytes 1474568 | tf_op jit(solution)/shard_map/ppermute | solution.py:361
  270.0 67.5 %collective-permute-start.14 = (bf16[960,256]{1,0:T(8,128)(2,1)}, bf16[960,256]{1,0:T(8,128)(2,1)S(1)}, u32[]{:S(2)}, u32[]{:S(2)}) collective-permute-start(bf16[960,256]{1,0:T(8,128)(2,1)} %shard_map.105), channel_id=1, source_target_pairs={{0,4},{4,0},{1,5},{5,1},{2,6},{6,2},{3,7},{7,3},{8,12},{12,8},{9,1... | collective-permute-start | bytes 1474568 | tf_op jit(solution)/shard_map/ppermute | solution.py:361
  302.5 36.7 %collective-permute-start.3 = (f32[4,8,512]{2,1,0:T(8,128)}, f32[4,8,512]{2,1,0:T(8,128)}, u32[]{:S(2)}, u32[]{:S(2)}) collective-permute-start(f32[4,8,512]{2,1,0:T(8,128)} %get-tuple-element.43.mine_ref), channel_id=1, source_target_pairs={{0,4},{4,0},{1,5},{5,1},{2,6},{6,2},{3,7},{7,3},{8,12},{12,8},{9,1... | collective-permute-start | bytes 196616 | tf_op jit(solution)/shard_map/ppermute | solution.py:361
  327.3 16.3 %collective-permute-start.20 = (bf16[960,256]{1,0:T(8,128)(2,1)S(1)}, bf16[960,256]{1,0:T(8,128)(2,1)S(1)}, u32[]{:S(2)}, u32[]{:S(2)}) collective-permute-start(bf16[960,256]{1,0:T(8,128)(2,1)S(1)} %add_convert_fusion.refs_4_), channel_id=1, source_target_pairs={{0,1},{1,0},{2,3},{3,2},{4,5},{5,4},{6,7},{7,6},{8,9},{9,8},{10,11... | collective-permute-start | bytes 1474568 | tf_op jit(solution)/shard_map/ppermute | solution.py:361
  328.8 27.1 %collective-permute-start.21 = (bf16[960,256]{1,0:T(8,128)(2,1)S(1)}, bf16[960,256]{1,0:T(8,128)(2,1)S(1)}, u32[]{:S(2)}, u32[]{:S(2)}) collective-permute-start(bf16[960,256]{1,0:T(8,128)(2,1)S(1)} %add_convert_fusion.refs_4_), channel_id=1, source_target_pairs={{0,2},{2,0},{1,3},{3,1},{4,6},{6,4},{5,7},{7,5},{8,10},{10,8},{9,1... | collective-permute-start | bytes 1474568 | tf_op jit(solution)/shard_map/ppermute | solution.py:361
  337.7 20.4 %collective-permute-start.15 = (bf16[960,256]{1,0:T(8,128)(2,1)S(1)}, bf16[960,256]{1,0:T(8,128)(2,1)S(1)}, u32[]{:S(2)}, u32[]{:S(2)}) collective-permute-start(bf16[960,256]{1,0:T(8,128)(2,1)S(1)} %add_convert_fusion.1.refs_0_), channel_id=1, source_target_pairs={{0,1},{1,0},{2,3},{3,2},{4,5},{5,4},{6,7},{7,6},{8,9},{9,8},{10,11... | collective-permute-start | bytes 1474568 | tf_op jit(solution)/shard_map/ppermute | solution.py:361
  339.2 30.8 %collective-permute-start.16 = (bf16[960,256]{1,0:T(8,128)(2,1)S(1)}, bf16[960,256]{1,0:T(8,128)(2,1)}, u32[]{:S(2)}, u32[]{:S(2)}) collective-permute-start(bf16[960,256]{1,0:T(8,128)(2,1)S(1)} %add_convert_fusion.1.refs_0_), channel_id=1, source_target_pairs={{0,2},{2,0},{1,3},{3,1},{4,6},{6,4},{5,7},{7,5},{8,10},{10,8},{9,1... | collective-permute-start | bytes 1474568 | tf_op jit(solution)/shard_map/ppermute | solution.py:361
  342.1 36.1 %collective-permute-start.4 = (bf16[960,256]{1,0:T(8,128)(2,1)}, bf16[960,256]{1,0:T(8,128)(2,1)}, u32[]{:S(2)}, u32[]{:S(2)}) collective-permute-start(bf16[960,256]{1,0:T(8,128)(2,1)} %shard_map.108), channel_id=1, source_target_pairs={{0,4},{4,0},{1,5},{5,1},{2,6},{6,2},{3,7},{7,3},{8,12},{12,8},{9,1... | collective-permute-start | bytes 1474568 | tf_op jit(solution)/shard_map/ppermute | solution.py:361
  343.6 31.5 %collective-permute-start.22 = (bf16[480,256]{1,0:T(8,128)(2,1)S(1)}, bf16[480,256]{1,0:T(8,128)(2,1)S(1)}, u32[]{:S(2)}, u32[]{:S(2)}) collective-permute-start(bf16[480,256]{1,0:T(8,128)(2,1)S(1)} %slice.68), channel_id=1, source_target_pairs={{0,2},{2,0},{1,3},{3,1},{4,6},{6,4},{5,7},{7,5},{8,10},{10,8},{9,1... | collective-permute-start | bytes 737288 | tf_op jit(solution)/shard_map/ppermute | solution.py:361
  355.9 19.2 %collective-permute-start.23 = (bf16[480,256]{1,0:T(8,128)(2,1)S(1)}, bf16[480,256]{1,0:T(8,128)(2,1)S(1)}, u32[]{:S(2)}, u32[]{:S(2)}) collective-permute-start(bf16[480,256]{1,0:T(8,128)(2,1)S(1)} %slice.69), channel_id=1, source_target_pairs={{0,1},{1,0},{2,3},{3,2},{4,5},{5,4},{6,7},{7,6},{8,9},{9,8},{10,11... | collective-permute-start | bytes 737288 | tf_op jit(solution)/shard_map/ppermute | solution.py:361
  358.9 22.0 %collective-permute-start.17 = (bf16[480,256]{1,0:T(8,128)(2,1)}, bf16[480,256]{1,0:T(8,128)(2,1)}, u32[]{:S(2)}, u32[]{:S(2)}) collective-permute-start(bf16[480,256]{1,0:T(8,128)(2,1)} %slice.66), channel_id=1, source_target_pairs={{0,2},{2,0},{1,3},{3,1},{4,6},{6,4},{5,7},{7,5},{8,10},{10,8},{9,1... | collective-permute-start | bytes 737288 | tf_op jit(solution)/shard_map/ppermute | solution.py:361
  371.6 9.2 %collective-permute-start.18 = (bf16[480,256]{1,0:T(8,128)(2,1)}, bf16[480,256]{1,0:T(8,128)(2,1)}, u32[]{:S(2)}, u32[]{:S(2)}) collective-permute-start(bf16[480,256]{1,0:T(8,128)(2,1)} %slice.67), channel_id=1, source_target_pairs={{0,1},{1,0},{2,3},{3,2},{4,5},{5,4},{6,7},{7,6},{8,9},{9,8},{10,11... | collective-permute-start | bytes 737288 | tf_op jit(solution)/shard_map/ppermute | solution.py:361
  378.0 24.1 %collective-permute-start.5 = (bf16[960,256]{1,0:T(8,128)(2,1)}, bf16[960,256]{1,0:T(8,128)(2,1)S(1)}, u32[]{:S(2)}, u32[]{:S(2)}) collective-permute-start(bf16[960,256]{1,0:T(8,128)(2,1)} %shard_map.109), channel_id=1, source_target_pairs={{0,4},{4,0},{1,5},{5,1},{2,6},{6,2},{3,7},{7,3},{8,12},{12,8},{9,1... | collective-permute-start | bytes 1474568 | tf_op jit(solution)/shard_map/ppermute | solution.py:361
  379.5 25.9 %collective-permute-start.6 = (bf16[960,256]{1,0:T(8,128)(2,1)S(1)}, bf16[960,256]{1,0:T(8,128)(2,1)S(1)}, u32[]{:S(2)}, u32[]{:S(2)}) collective-permute-start(bf16[960,256]{1,0:T(8,128)(2,1)S(1)} %add_convert_fusion.3.refs_0_), channel_id=1, source_target_pairs={{0,1},{1,0},{2,3},{3,2},{4,5},{5,4},{6,7},{7,6},{8,9},{9,8},{10,11... | collective-permute-start | bytes 1474568 | tf_op jit(solution)/shard_map/ppermute | solution.py:361
  402.3 13.2 %collective-permute-start.10 = (bf16[960,256]{1,0:T(8,128)(2,1)S(1)}, bf16[960,256]{1,0:T(8,128)(2,1)S(1)}, u32[]{:S(2)}, u32[]{:S(2)}) collective-permute-start(bf16[960,256]{1,0:T(8,128)(2,1)S(1)} %add_convert_fusion.2.refs_4_), channel_id=1, source_target_pairs={{0,1},{1,0},{2,3},{3,2},{4,5},{5,4},{6,7},{7,6},{8,9},{9,8},{10,11... | collective-permute-start | bytes 1474568 | tf_op jit(solution)/shard_map/ppermute | solution.py:361
  403.3 14.1 %collective-permute-start.11 = (bf16[960,256]{1,0:T(8,128)(2,1)S(1)}, bf16[960,256]{1,0:T(8,128)(2,1)S(1)}, u32[]{:S(2)}, u32[]{:S(2)}) collective-permute-start(bf16[960,256]{1,0:T(8,128)(2,1)S(1)} %add_convert_fusion.2.refs_4_), channel_id=1, source_target_pairs={{0,2},{2,0},{1,3},{3,1},{4,6},{6,4},{5,7},{7,5},{8,10},{10,8},{9,1... | collective-permute-start | bytes 1474568 | tf_op jit(solution)/shard_map/ppermute | solution.py:361
  403.3 24.7 %collective-permute-start.7 = (bf16[960,256]{1,0:T(8,128)(2,1)S(1)}, bf16[960,256]{1,0:T(8,128)(2,1)S(1)}, u32[]{:S(2)}, u32[]{:S(2)}) collective-permute-start(bf16[960,256]{1,0:T(8,128)(2,1)S(1)} %add_convert_fusion.3.refs_0_), channel_id=1, source_target_pairs={{0,2},{2,0},{1,3},{3,1},{4,6},{6,4},{5,7},{7,5},{8,10},{10,8},{9,1... | collective-permute-start | bytes 1474568 | tf_op jit(solution)/shard_map/ppermute | solution.py:361
  410.2 31.5 %collective-permute-start.26 = (bf16[128,1024]{1,0:T(8,128)(2,1)S(1)}, bf16[128,1024]{1,0:T(8,128)(2,1)S(1)}, u32[]{:S(2)}, u32[]{:S(2)}) collective-permute-start(bf16[128,1024]{1,0:T(8,128)(2,1)S(1)} %dynamic-slice_convert_fusion), channel_id=1, source_target_pairs={{0,16},{8,24},{16,0},{24,8},{1,17},{9,25},{17,1},{25,9},{2,18},{10... | collective-permute-start | bytes 786440 | tf_op jit(solution)/shard_map/ppermute | solution.py:383
  415.5 17.7 %collective-permute-start.12 = (bf16[480,256]{1,0:T(8,128)(2,1)S(1)}, bf16[480,256]{1,0:T(8,128)(2,1)S(1)}, u32[]{:S(2)}, u32[]{:S(2)}) collective-permute-start(bf16[480,256]{1,0:T(8,128)(2,1)S(1)} %slice.64), channel_id=1, source_target_pairs={{0,2},{2,0},{1,3},{3,1},{4,6},{6,4},{5,7},{7,5},{8,10},{10,8},{9,1... | collective-permute-start | bytes 737288 | tf_op jit(solution)/shard_map/ppermute | solution.py:361
  417.5 16.8 %collective-permute-start.13 = (bf16[480,256]{1,0:T(8,128)(2,1)S(1)}, bf16[480,256]{1,0:T(8,128)(2,1)S(1)}, u32[]{:S(2)}, u32[]{:S(2)}) collective-permute-start(bf16[480,256]{1,0:T(8,128)(2,1)S(1)} %slice.65), channel_id=1, source_target_pairs={{0,1},{1,0},{2,3},{3,2},{4,5},{5,4},{6,7},{7,6},{8,9},{9,8},{10,11... | collective-permute-start | bytes 737288 | tf_op jit(solution)/shard_map/ppermute | solution.py:361
  418.6 18.7 %collective-permute-start.8 = (bf16[480,256]{1,0:T(8,128)(2,1)S(1)}, bf16[480,256]{1,0:T(8,128)(2,1)S(1)}, u32[]{:S(2)}, u32[]{:S(2)}) collective-permute-start(bf16[480,256]{1,0:T(8,128)(2,1)S(1)} %slice.62), channel_id=1, source_target_pairs={{0,2},{2,0},{1,3},{3,1},{4,6},{6,4},{5,7},{7,5},{8,10},{10,8},{9,1... | collective-permute-start | bytes 737288 | tf_op jit(solution)/shard_map/ppermute | solution.py:361
  428.0 9.3 %collective-permute-start.9 = (bf16[480,256]{1,0:T(8,128)(2,1)S(1)}, bf16[480,256]{1,0:T(8,128)(2,1)S(1)}, u32[]{:S(2)}, u32[]{:S(2)}) collective-permute-start(bf16[480,256]{1,0:T(8,128)(2,1)S(1)} %slice.63), channel_id=1, source_target_pairs={{0,1},{1,0},{2,3},{3,2},{4,5},{5,4},{6,7},{7,6},{8,9},{9,8},{10,11... | collective-permute-start | bytes 737288 | tf_op jit(solution)/shard_map/ppermute | solution.py:361
  433.3 8.3 %collective-permute-start.24 = (bf16[1024,128]{0,1:T(8,128)(2,1)S(1)}, bf16[1024,128]{0,1:T(8,128)(2,1)S(1)}, u32[]{:S(2)}, u32[]{:S(2)}) collective-permute-start(bf16[1024,128]{0,1:T(8,128)(2,1)S(1)} %fusion.17), channel_id=1, source_target_pairs={{0,16},{8,24},{16,0},{24,8},{1,17},{9,25},{17,1},{25,9},{2,18},{10... | collective-permute-start | bytes 786440 | tf_op jit(solution)/shard_map/ppermute | solution.py:383
  441.7 1.4 collective-permute-start.25
  441.9 2.1 collective-permute-start.27
  (25 other events, 294.7 us)

commit v6 on v5

--- a/solution.py
+++ b/solution.py
@@ -275,19 +275,19 @@
     )(outs, douts, mine, theirs)
 
 
-def project_kernel(order, *refs, count, parts, last, chunk, depth):
+def project_kernel(*refs, count, parts, last, chunk, depth):
     step = pl.program_id(0)
     cols = refs[count * parts]
     rest, weights = refs[count * parts + 1 : -1], refs[-1]
     before = rest[0] if len(rest) == (3 if last else 2) else None
-    half = cols.shape[2] // 2
+    half = cols.shape[3] // 2
 
     @pl.when(step == 0)
     def _():
         empty = jnp.zeros((depth, half), weights.dtype)
         for i in range(count):
             for z in range(2):
-                own = cols[z * count + order[i], pl.ds(chunk * depth, depth), :]
+                own = cols[i, z, pl.ds(chunk * depth, depth), :]
                 grad_rows = pl.ds(2 * z * depth, depth)
                 out_rows = pl.ds((2 * z + 1) * depth, depth)
                 weights[i, grad_rows, :half] = empty
@@ -313,18 +313,18 @@
         )
 
 
-def project(parts, cols, order, before, last, chunk):
+def project(parts, cols, before, last, chunk):
     count = len(parts[0])
     rows, depth = parts[0][0].shape
     total_rows = rows * len(parts)
-    width = cols.shape[2]
+    width = cols.shape[3]
     steps = 4 // len(parts)
     tile = rows // steps
-    rowwise = lambda w: pl.BlockSpec((tile, w), lambda i, *_: (i, 0))
+    rowwise = lambda w: pl.BlockSpec((tile, w), lambda i: (i, 0))
 
     def within(which):
         return pl.BlockSpec(
-            (tile, depth), lambda i, *_: (jnp.clip(i - which * steps, 0, steps - 1), 0)
+            (tile, depth), lambda i: (jnp.clip(i - which * steps, 0, steps - 1), 0)
         )
 
     halves = jax.ShapeDtypeStruct((total_rows, width // 2), jnp.bfloat16)
@@ -333,15 +333,12 @@
             project_kernel, count=count, parts=len(parts), last=last, chunk=chunk,
             depth=depth // 4,
         ),
-        grid_spec=pltpu.PrefetchScalarGridSpec(
-            num_scalar_prefetch=1,
-            grid=(4,),
-            in_specs=[within(i) for i in range(len(parts)) for _ in range(count)]
-            + [pl.BlockSpec(cols.shape, lambda i, *_: (0, 0, 0))]
-            + ([] if before is None else [rowwise(width)]),
-            out_specs=[rowwise(width // 2)] * 2 if last else rowwise(width),
-            scratch_shapes=[pltpu.VMEM((count, depth, width), jnp.bfloat16)],
-        ),
+        grid=(4,),
+        in_specs=[within(i) for i in range(len(parts)) for _ in range(count)]
+        + [pl.BlockSpec(cols.shape, lambda i: (0, 0, 0, 0))]
+        + ([] if before is None else [rowwise(width)]),
+        out_specs=[rowwise(width // 2)] * 2 if last else rowwise(width),
+        scratch_shapes=[pltpu.VMEM((count, depth, width), jnp.bfloat16)],
         out_shape=[halves] * 2
         if last
         else jax.ShapeDtypeStruct((total_rows, width), jnp.float32),
@@ -351,25 +348,27 @@
             transcendentals=0,
             bytes_accessed=2 * total_rows * (depth * count + 2 * width),
         ),
-    )(
-        order, *[x for pieces in parts for x in pieces], cols,
-        *([] if before is None else [before]),
-    )
+    )(*[x for pieces in parts for x in pieces], cols, *([] if before is None else [before]))
 
 
 def swap(x, axis):
     return lax.ppermute(x, axis, [(0, 1), (1, 0)])
 
 
-def gather_half(x, zl_size, y_size):
-    if zl_size == 2 and y_size == 2:
-        by_y = swap(x, "y")
-        by_zl = swap(x, "zl")
-        cut = x.shape[0] // 2
-        corner = jnp.concatenate([swap(by_y[:cut], "zl"), swap(by_zl[cut:], "y")], axis=0)
-        return [x, by_y, by_zl, corner]
+def first_hop(x, small):
+    if small:
+        return [x, swap(x, "y"), swap(x, "zl")]
     whole = lax.all_gather(x, ("zl", "y"), axis=0, tiled=False)
-    return [whole[i] for i in range(zl_size * y_size)]
+    return [whole[i] for i in range(whole.shape[0])]
+
+
+def second_hop(pieces, small):
+    if not small:
+        return pieces
+    x, by_y, by_zl = pieces
+    cut = x.shape[0] // 2
+    corner = jnp.concatenate([swap(by_y[:cut], "zl"), swap(by_zl[cut:], "y")], axis=0)
+    return [x, by_y, by_zl, corner]
 
 
 def scatter_sum(x, size, dim):
@@ -485,16 +484,12 @@
     def both_halves(own, other):
         return jnp.where(zh == 0, own, other), jnp.where(zh == 0, other, own)
 
-    q_halves = [
-        w.reshape(features, local_heads, head_size) for w in both_halves(query_proj, q_other)
-    ]
-    q_wide = jnp.stack(q_halves, axis=2)
+    q_both = both_halves(query_proj, q_other)
+    q_wide = jnp.stack([w.reshape(features, local_heads, head_size) for w in q_both], axis=2)
     q_wide = jnp.pad(q_wide, ((0, 0), (0, 0), (0, 0), (0, LANES - head_size)))
     q_wide = q_wide.reshape(features, local_heads * 2 * LANES)
-    o_halves = [
-        w.reshape(local_heads, head_size, features) for w in both_halves(output_proj, o_other)
-    ]
-    o_wide = jnp.stack(o_halves, axis=1)
+    o_both = both_halves(output_proj, o_other)
+    o_wide = jnp.stack([w.reshape(local_heads, head_size, features) for w in o_both], axis=1)
     o_wide = jnp.pad(o_wide, ((0, 0), (0, 0), (LANES - head_size, 0), (0, 0)))
     o_wide = o_wide.reshape(local_heads * 2 * LANES, features)
     queries = (
@@ -502,17 +497,13 @@
     ).astype(jnp.bfloat16)
     backs = nt_dot(cotangent, o_wide).astype(jnp.bfloat16)
 
-    cols = jnp.concatenate(
-        [
-            output_proj.reshape(local_heads * head_size, model, columns).transpose(1, 0, 2),
-            query_proj.reshape(model, columns, local_heads * head_size).transpose(0, 2, 1),
-        ],
-        axis=2,
-    )
-    if zl_size == 2 and y_size == 2:
-        order = jnp.stack([spot, spot ^ 1, spot ^ 2, spot ^ 3])
-    else:
-        order = jnp.arange(inner, dtype=jnp.int32)
+    small = zl_size == 2 and y_size == 2
+    own_width = local_heads * head_size
+    o_blocks = jnp.stack(o_both).reshape(2, own_width, model, columns).transpose(2, 0, 1, 3)
+    q_blocks = jnp.stack(q_both).reshape(2, model, columns, own_width).transpose(1, 0, 3, 2)
+    blocks = lax.dynamic_slice_in_dim(
+        jnp.concatenate([o_blocks, q_blocks], axis=3), zh * inner, inner, 0
+    )
 
     part_count = 2 if patch_blocks % 2 == 0 else 1
     part_patches = patch_blocks // part_count
@@ -521,37 +512,56 @@
     for c in range(local_heads):
         final = c + 1 == local_heads
         if final:
-            cols, bias, received[c] = lax.optimization_barrier((cols, bias, received[c]))
-            cols = lax.all_to_all(cols, ("zh", "zl", "y"), split_axis=0, concat_axis=0, tiled=True)
+            blocks, bias, received[c] = lax.optimization_barrier((blocks, bias, received[c]))
+            if small:
+                pairs = lambda d: [(i, i ^ d) for i in range(inner)]
+                cols = [
+                    lax.ppermute(
+                        lax.dynamic_index_in_dim(blocks, spot ^ d, 0, keepdims=False),
+                        ("zl", "y"),
+                        pairs(d),
+                    )
+                    if d
+                    else lax.dynamic_index_in_dim(blocks, spot, 0, keepdims=False)
+                    for d in range(inner)
+                ]
+                cols = jnp.stack(cols)
+            else:
+                cols = lax.all_to_all(blocks, ("zl", "y"), split_axis=0, concat_axis=0, tiled=True)
         outs, douts, mine = attention(
             tables, bias, queries, backs, received[c], c, slots, head_scale
         )
         theirs = swap(mine, "zh")
         if final:
-            theirs, cols = lax.optimization_barrier((theirs, cols))
+            theirs, _ = lax.optimization_barrier((theirs, cols))
         parts = [
             merge(outs, douts, mine, theirs, start, part_patches, head_scale, head_size)
             for start in range(0, patch_blocks, part_patches)
         ]
+        if gathered:
+            gathered[-1], _ = lax.optimization_barrier((gathered[-1], parts))
+            gathered[-1] = [second_hop(x, small) for x in gathered[-1]]
         if not final:
             parts, bias = lax.optimization_barrier((parts, bias))
         merged = [
             (part.astype(jnp.float32) + swap(part, "zh").astype(jnp.float32)).astype(jnp.bfloat16)
             for part in parts
         ]
-        pieces = [gather_half(x, zl_size, y_size) for x in merged]
+        pieces = [first_hop(x, small) for x in merged]
         gathered.append(pieces)
         if final:
-            merged, pieces[0][1] = lax.optimization_barrier((merged, pieces[0][1]))
+            result = None
+            for i, earlier in enumerate(gathered[:-1]):
+                result = project(earlier, cols, result, False, i)
+            if result is not None:
+                merged, _ = lax.optimization_barrier((merged, result))
         own.append(
             jnp.concatenate(
                 [lax.dynamic_slice_in_dim(x, zh * LANES, LANES, 1) for x in merged], axis=0
             )
         )
-    result = None
-    for c, pieces in enumerate(gathered):
-        result = project(pieces, cols, order, result, c + 1 == local_heads, c)
-    attended, patch_grad = result
+    last_pieces = [second_hop(x, small) for x in gathered[-1]]
+    attended, patch_grad = project(last_pieces, cols, result, True, local_heads - 1)
 
     dquery = jnp.concatenate([x[:, :head_size] for x in own], axis=1)
     heads_out = jnp.concatenate([x[:, head_size:] for x in own], axis=1)

time: 446 us -> 426 us (0.955)
  waiting for transfers between devices: 239 us -> 193 us
  local copies, waits for them, and re-layouts: 23.5 us -> 34.4 us
  starting transfers between devices: 51 us -> 57.7 us
    ppermute x24, waiting for transfers between devices: 225 us -> 153 us  [swap(): return lax.ppermute(x, axis, [(0, 1), (1, 0)])]
    ppermute x0 -> x3, waiting for transfers between devices: none -> 15.1 us  [local(): lax.ppermute(lax.dynamic_index_in_dim(blocks, spot ^ d, 0, keepdims=False...]
    ppermute x4, waiting for transfers between devices: 0.68 us -> 7.77 us  [scatter_sum(): lax.ppermute(give.astype(jnp.bfloat16), 'dp', [(i, i ^ step) for i in ran...]
    ppermute x4, starting transfers between devices: 2.65 us -> 9.24 us  [scatter_sum(): lax.ppermute(give.astype(jnp.bfloat16), 'dp', [(i, i ^ step) for i in ran...]
    all_to_all x1 -> x0, starting transfers between devices: 5.72 us -> none  [local(): lax.all_to_all(cols, ('zh', 'zl', 'y'), split_axis=0, concat_axis=0, tile...]
    dot_general x1, matrix products: 1.36 us -> 5.94 us  [local(): lax.dot_general(patches, dquery, (((0,), (0,)), ((), ())), preferred_elem...]
    unnamed x56 -> x72, local copies, waits for them, and re-layouts: 17.1 us -> 20 us
  transfers between devices with their start and end apart: 31 -> 33, of which waited for: 17 -> 17; matrix products, arithmetic and copies ran while one was open for 9% -> 12% of each run, Pallas kernels for 20% -> 21%
where the time goes in v6:
time: 426 us; the launch traced here: 424 us
  waiting for transfers between devices  193 us (45%)
  Pallas kernels  98.3 us (23%)
  starting transfers between devices  57.7 us (14%)
  local copies, waits for them, and re-layouts  34.4 us (8%)
  matrix products  21.7 us (5%)
  other arithmetic  16.8 us (4%)
    ppermute x24, waiting for transfers between devices, swap(): return lax.ppermute(x, axis, [(0, 1), (1, 0)])  153 us
    pallas_call x2, Pallas kernels, attention(): pl.pallas_call(functools.partial(attention_kernel, slots=slots, scale=sca...  68.8 us
    ppermute x24, starting transfers between devices, swap(): return lax.ppermute(x, axis, [(0, 1), (1, 0)])  26.3 us
    unnamed x72, local copies, waits for them, and re-layouts  20 us
    all_to_all x2, starting transfers between devices, exchange(): lax.all_to_all(x, ('dp', 'zl', 'y'), split_axis=0, concat_axis=0, tiled=T...  18.6 us
    all_to_all x2, waiting for transfers between devices, exchange(): lax.all_to_all(x, ('dp', 'zl', 'y'), split_axis=0, concat_axis=0, tiled=T...  17.4 us
    ppermute x3, waiting for transfers between devices, local(): lax.ppermute(lax.dynamic_index_in_dim(blocks, spot ^ d, 0, keepdims=False...  15.1 us
    pallas_call x4, Pallas kernels, merge(): pl.pallas_call(functools.partial(merge_kernel, scale=scale, split=split),...  11.4 us
  transfers between devices with their start and end apart: 33, of which 17 were waited for; matrix products, arithmetic and copies ran while one was open for 12% of the time, Pallas kernels for 21%

profile of v6, /device:TPU:0, one launch (start us, length us, event | category | flops | bytes accessed | tf_op | source)
XLA Modules:
  0.0 423.8 jit_solution(6435830108806859194)
XLA Ops:
  2.9 3.4 copy-done
  6.9 4.0 shard_map.102
  10.9 3.3 copy-done.3
  14.2 6.2 %all-to-all-start = ((bf16[16,2048,128]{2,1,0:T(8,128)(2,1)}), bf16[16,2048,128]{2,1,0:T(8,128)(2,1)}, u32[]{:S(2)}, u32[]{:S(2)}) async-start(bf16[16,2048,128]{2,1,0:T(8,128)(2,1)} %bitcast.44), calls=%async_computation | async-start | bytes 16777216 | tf_op jit(solution)/shard_map/all_to_all | solution.py:432
  24.0 3.4 copy-done.1
  27.4 4.4 %shard_map.103 = bf16[4,4,8,2,128,128]{5,4,3,2,1,0:T(8,128)(2,1)S(1)} custom-call(s32[32]{0:T(128)S(1)} %reshape.446.chosen, s32[4]{0:T(128)S(1)} %reduce_sum.99.counts, s32[16]{0:T(128)S(1)} %copy-done.15, bf16[16,128,16,128]{3,2,1,0:T(8,128)(2,1)S(1)} %copy-done.1), custom_call_target="tpu_custom_call" | custom-call | bytes 16777216 | tf_op jit(solution)/shard_map/pallas_call | solution.py:49
  31.8 3.2 copy-done.2
  35.1 88.8 %collective-permute-done = bf16[2048,128]{0,1:T(8,128)(2,1)S(1)} collective-permute-done((bf16[2048,128]{0,1:T(8,128)(2,1)S(1)}, bf16[2048,128]{0,1:T(8,128)(2,1)S(1)}, u32[]{:S(2)}, u32[]{:S(2)}) %collective-permute-start) | collective-permute-done | bytes 524320 | tf_op jit(solution)/shard_map/ppermute | solution.py:355
  123.8 11.0 %collective-permute-done.1 = bf16[128,2048]{0,1:T(8,128)(2,1)S(1)} collective-permute-done((bf16[128,2048]{0,1:T(8,128)(2,1)S(1)}, bf16[128,2048]{0,1:T(8,128)(2,1)S(1)}, u32[]{:S(2)}, u32[]{:S(2)}) %collective-permute-start.1) | collective-permute-done | bytes 524320 | tf_op jit(solution)/shard_map/ppermute | solution.py:355
  134.9 5.9 %all-to-all-done = bf16[16,2048,128]{2,1,0:T(8,128)(2,1)} async-done(((bf16[16,2048,128]{2,1,0:T(8,128)(2,1)}), bf16[16,2048,128]{2,1,0:T(8,128)(2,1)}, u32[]{:S(2)}, u32[]{:S(2)}) %all-to-all-start) | async-done | bytes 8388640 | tf_op jit(solution)/shard_map/all_to_all | solution.py:432
  140.8 12.4 %all-to-all-start.1 = ((bf16[16,2048,128]{2,1,0:T(8,128)(2,1)}), bf16[16,2048,128]{2,1,0:T(8,128)(2,1)}, u32[]{:S(2)}, u32[]{:S(2)}) async-start(bf16[16,2048,128]{2,1,0:T(8,128)(2,1)} %bitcast.43), calls=%async_computation.1 | async-start | bytes 16777216 | tf_op jit(solution)/shard_map/all_to_all | solution.py:432
  170.0 9.0 %fusion.3.q_ref = bf16[1920,512]{1,0:T(8,128)(2,1)} fusion(bf16[2048,512]{0,1:T(8,128)(2,1)S(1)} %bitcast.54, bf16[1920,2048]{1,0:T(8,128)(2,1)} %param.7), kind=kOutput, calls=%fused_computation.6 | convolution fusion | flops 4028497920 | bytes 11927552 | tf_op jit(solution)/shard_map/dot_general | solution.py:496
  179.0 5.4 %fusion.2.b_ref = bf16[1920,512]{1,0:T(8,128)(2,1)} fusion(bf16[512,2048]{1,0:T(8,128)(2,1)S(1)} %bitcast.53, bf16[1920,2048]{1,0:T(8,128)(2,1)S(1)} %bitcast.46), kind=kOutput, calls=%fused_computation.5 | convolution fusion | flops 4027514880 | bytes 11927552 | tf_op jit(solution)/shard_map/dot_general | solution.py:78
  184.5 34.4 %shard_map.104 = (f32[1920,256]{1,0:T(8,128)}, f32[1920,256]{1,0:T(8,128)}, f32[4,8,512]{2,1,0:T(8,128)}) custom-call(s32[128]{0:T(128)} %copy-done.29, s32[4]{0:T(128)} %copy-done.28, s32[128]{0:T(128)} %reshape.450.offsets, s32[128]{0:T(128)} %and_select_fusion.sizes, bf16[1920,512]{1,0:T(8,128)(2,1)} %fusion.3.q_ref, bf16[1920,512]{1,0:T(8,128)(2,1)} %fusion.2.b_ref, ...), custom_call_target="tpu_custom_call" | custom-call | flops 8053063680 | bytes 41943040 | tf_op jit(solution)/shard_map/pallas_call | solution.py:203
  219.3 27.5 %collective-permute-done.2.theirs_ref = f32[4,8,512]{2,1,0:T(8,128)S(1)} collective-permute-done((f32[4,8,512]{2,1,0:T(8,128)}, f32[4,8,512]{2,1,0:T(8,128)S(1)}, u32[]{:S(2)}, u32[]{:S(2)}) %collective-permute-start.2) | collective-permute-done | bytes 65568 | tf_op jit(solution)/shard_map/ppermute | solution.py:355
  250.2 2.9 shard_map.106
  253.1 3.3 collective-permute-start.17
  256.5 11.5 %all-to-all-done.1 = bf16[16,2048,128]{2,1,0:T(8,128)(2,1)} async-done(((bf16[16,2048,128]{2,1,0:T(8,128)(2,1)}), bf16[16,2048,128]{2,1,0:T(8,128)(2,1)}, u32[]{:S(2)}, u32[]{:S(2)}) %all-to-all-start.1) | async-done | bytes 8388640 | tf_op jit(solution)/shard_map/all_to_all | solution.py:432
  267.9 34.4 %shard_map.107 = (f32[1920,256]{1,0:T(8,128)}, f32[1920,256]{1,0:T(8,128)}, f32[4,8,512]{2,1,0:T(8,128)}) custom-call(s32[128]{0:T(128)} %copy-done.29, s32[4]{0:T(128)} %copy-done.28, s32[128]{0:T(128)} %reshape.450.offsets, s32[128]{0:T(128)} %and_select_fusion.sizes, bf16[1920,512]{1,0:T(8,128)(2,1)} %fusion.3.q_ref, bf16[1920,512]{1,0:T(8,128)(2,1)} %fusion.2.b_ref, ...), custom_call_target="tpu_custom_call" | custom-call | flops 8053063680 | bytes 41943040 | tf_op jit(solution)/shard_map/pallas_call | solution.py:203
  302.6 3.1 collective-permute-start.5
  308.1 5.0 %collective-permute-done.6 = bf16[2,128,512]{2,1,0:T(8,128)(2,1)S(1)} collective-permute-done((bf16[2,128,512]{2,1,0:T(8,128)(2,1)S(1)}, bf16[2,128,512]{2,1,0:T(8,128)(2,1)S(1)}, u32[]{:S(2)}, u32[]{:S(2)}) %collective-permute-start.6) | collective-permute-done | bytes 262176 | tf_op jit(solution)/shard_map/ppermute | solution.py:519
  314.4 10.1 %collective-permute-done.5 = bf16[2,128,512]{2,1,0:T(8,128)(2,1)S(1)} collective-permute-done((bf16[2,128,512]{2,1,0:T(8,128)(2,1)S(1)}, bf16[2,128,512]{2,1,0:T(8,128)(2,1)S(1)}, u32[]{:S(2)}, u32[]{:S(2)}) %collective-permute-start.5) | collective-permute-done | bytes 262176 | tf_op jit(solution)/shard_map/ppermute | solution.py:519
  324.7 2.9 shard_map.108
  331.7 2.8 shard_map.109
  335.9 8.5 %collective-permute-done.19.refs_2_ = bf16[960,256]{1,0:T(8,128)(2,1)S(1)} collective-permute-done((bf16[960,256]{1,0:T(8,128)(2,1)S(1)}, bf16[960,256]{1,0:T(8,128)(2,1)S(1)}, u32[]{:S(2)}, u32[]{:S(2)}) %collective-permute-start.19) | collective-permute-done | bytes 491552 | tf_op jit(solution)/shard_map/ppermute | solution.py:355
  344.4 8.7 %collective-permute-done.22.refs_6_ = bf16[960,256]{1,0:T(8,128)(2,1)} collective-permute-done((bf16[960,256]{1,0:T(8,128)(2,1)S(1)}, bf16[960,256]{1,0:T(8,128)(2,1)}, u32[]{:S(2)}, u32[]{:S(2)}) %collective-permute-start.22) | collective-permute-done | bytes 491552 | tf_op jit(solution)/shard_map/ppermute | solution.py:355
  371.3 4.4 %shard_map.110.refs_9_ = f32[1920,512]{1,0:T(8,128)S(1)} custom-call(bf16[960,256]{1,0:T(8,128)(2,1)S(1)} %add_convert_fusion.1.refs_0_, bf16[960,256]{1,0:T(8,128)(2,1)S(1)} %collective-permute-done.18.refs_1_, bf16[960,256]{1,0:T(8,128)(2,1)S(1)} %copy-done.7, bf16[960,256]{1,0:T(8,128)(2,1)S(1)} %pad_maximum_fusion.6.refs_3_, ...), custom_call_target="tpu_custom_call" | custom-call | flops 2013265920 | bytes 7864320 | tf_op jit(solution)/shard_map/pallas_call | solution.py:331
  375.9 5.9 %convolution_multiply_fusion.1 = f32[128,2048]{1,0:T(8,128)S(1)} fusion(bf16[1920,2048]{1,0:T(8,128)(2,1)} %param.7, bf16[1920,64]{1,0:T(8,128)(2,1)S(1)} %fusion.8, bf16[1920,64]{1,0:T(8,128)(2,1)S(1)} %slice_maximum_fusion), kind=kOutput, calls=%fused_computation.8 | convolution fusion | flops 1007878144 | bytes 9404416 | tf_op jit(solution)/shard_map/dot_general | solution.py:569
  381.9 6.4 %collective-permute-start.27 = (bf16[1024,128]{0,1:T(8,128)(2,1)S(1)}, bf16[1024,128]{0,1:T(8,128)(2,1)S(1)}, u32[]{:S(2)}, u32[]{:S(2)}) collective-permute-start(bf16[1024,128]{0,1:T(8,128)(2,1)S(1)} %fusion.18), channel_id=1, source_target_pairs={{0,16},{8,24},{16,0},{24,8},{1,17},{9,25},{17,1},{25,9},{2,18},{10... | collective-permute-start | bytes 786440 | tf_op jit(solution)/shard_map/ppermute | solution.py:382
  389.7 3.5 collective-permute-done.27
  395.6 4.2 %collective-permute-done.29 = bf16[128,1024]{1,0:T(8,128)(2,1)S(1)} collective-permute-done((bf16[128,1024]{1,0:T(8,128)(2,1)S(1)}, bf16[128,1024]{1,0:T(8,128)(2,1)S(1)}, u32[]{:S(2)}, u32[]{:S(2)}) %collective-permute-start.29) | collective-permute-done | bytes 262176 | tf_op jit(solution)/shard_map/ppermute | solution.py:382
  418.5 5.3 %shard_map.111 = (bf16[1920,256]{1,0:T(8,128)(2,1)}, bf16[1920,256]{1,0:T(8,128)(2,1)}) custom-call(bf16[960,256]{1,0:T(8,128)(2,1)S(1)} %add_convert_fusion.3.refs_0_, bf16[960,256]{1,0:T(8,128)(2,1)S(1)} %copy-done.11, bf16[960,256]{1,0:T(8,128)(2,1)S(1)} %copy-done.13, bf16[960,256]{1,0:T(8,128)(2,1)S(1)} %pad_maximum_fusion.4.refs_3_, ...), custom_call_target="tpu_custom_call" | custom-call | flops 2013265920 | bytes 7864320 | tf_op jit(solution)/shard_map/pallas_call | solution.py:331
  (204 shorter events, 77.2 us)
Async XLA Ops:
  14.2 126.7 %all-to-all-start = ((bf16[16,2048,128]{2,1,0:T(8,128)(2,1)}), bf16[16,2048,128]{2,1,0:T(8,128)(2,1)}, u32[]{:S(2)}, u32[]{:S(2)}) async-start(bf16[16,2048,128]{2,1,0:T(8,128)(2,1)} %bitcast.44), calls=%async_computation | async-start | bytes 16777216 | tf_op jit(solution)/shard_map/all_to_all | solution.py:432
  20.7 103.2 %collective-permute-start = (bf16[2048,128]{0,1:T(8,128)(2,1)S(1)}, bf16[2048,128]{0,1:T(8,128)(2,1)S(1)}, u32[]{:S(2)}, u32[]{:S(2)}) collective-permute-start(bf16[2048,128]{0,1:T(8,128)(2,1)S(1)} %copy.34), channel_id=1, source_target_pairs={{0,4},{4,0},{1,5},{5,1},{2,6},{6,2},{3,7},{7,3},{8,12},{12,8},{9,1... | collective-permute-start | bytes 1572872 | tf_op jit(solution)/shard_map/ppermute | solution.py:355
  23.7 111.2 %collective-permute-start.1 = (bf16[128,2048]{0,1:T(8,128)(2,1)S(1)}, bf16[128,2048]{0,1:T(8,128)(2,1)S(1)}, u32[]{:S(2)}, u32[]{:S(2)}) collective-permute-start(bf16[128,2048]{0,1:T(8,128)(2,1)S(1)} %copy.33), channel_id=1, source_target_pairs={{0,4},{4,0},{1,5},{5,1},{2,6},{6,2},{3,7},{7,3},{8,12},{12,8},{9,1... | collective-permute-start | bytes 1572872 | tf_op jit(solution)/shard_map/ppermute | solution.py:355
  140.8 127.1 %all-to-all-start.1 = ((bf16[16,2048,128]{2,1,0:T(8,128)(2,1)}), bf16[16,2048,128]{2,1,0:T(8,128)(2,1)}, u32[]{:S(2)}, u32[]{:S(2)}) async-start(bf16[16,2048,128]{2,1,0:T(8,128)(2,1)} %bitcast.43), calls=%async_computation.1 | async-start | bytes 16777216 | tf_op jit(solution)/shard_map/all_to_all | solution.py:432
  218.9 27.9 %collective-permute-start.2 = (f32[4,8,512]{2,1,0:T(8,128)}, f32[4,8,512]{2,1,0:T(8,128)S(1)}, u32[]{:S(2)}, u32[]{:S(2)}) collective-permute-start(f32[4,8,512]{2,1,0:T(8,128)} %get-tuple-element.40.mine_ref), channel_id=1, source_target_pairs={{0,4},{4,0},{1,5},{5,1},{2,6},{6,2},{3,7},{7,3},{8,12},{12,8},{9,1... | collective-permute-start | bytes 196616 | tf_op jit(solution)/shard_map/ppermute | solution.py:355
  253.1 52.6 %collective-permute-start.17 = (bf16[960,256]{1,0:T(8,128)(2,1)S(1)}, bf16[960,256]{1,0:T(8,128)(2,1)S(1)}, u32[]{:S(2)}, u32[]{:S(2)}) collective-permute-start(bf16[960,256]{1,0:T(8,128)(2,1)S(1)} %copy-done.21), channel_id=1, source_target_pairs={{0,4},{4,0},{1,5},{5,1},{2,6},{6,2},{3,7},{7,3},{8,12},{12,8},{9,1... | collective-permute-start | bytes 1474568 | tf_op jit(solution)/shard_map/ppermute | solution.py:355
  256.4 49.8 %collective-permute-start.20 = (bf16[960,256]{1,0:T(8,128)(2,1)}, bf16[960,256]{1,0:T(8,128)(2,1)S(1)}, u32[]{:S(2)}, u32[]{:S(2)}) collective-permute-start(bf16[960,256]{1,0:T(8,128)(2,1)} %shard_map.106), channel_id=1, source_target_pairs={{0,4},{4,0},{1,5},{5,1},{2,6},{6,2},{3,7},{7,3},{8,12},{12,8},{9,1... | collective-permute-start | bytes 1474568 | tf_op jit(solution)/shard_map/ppermute | solution.py:355
  302.3 22.4 %collective-permute-start.3 = (f32[4,8,512]{2,1,0:T(8,128)}, f32[4,8,512]{2,1,0:T(8,128)}, u32[]{:S(2)}, u32[]{:S(2)}) collective-permute-start(f32[4,8,512]{2,1,0:T(8,128)} %get-tuple-element.47.mine_ref), channel_id=1, source_target_pairs={{0,4},{4,0},{1,5},{5,1},{2,6},{6,2},{3,7},{7,3},{8,12},{12,8},{9,1... | collective-permute-start | bytes 196616 | tf_op jit(solution)/shard_map/ppermute | solution.py:355
  302.5 10.6 %collective-permute-start.6 = (bf16[2,128,512]{2,1,0:T(8,128)(2,1)S(1)}, bf16[2,128,512]{2,1,0:T(8,128)(2,1)S(1)}, u32[]{:S(2)}, u32[]{:S(2)}) collective-permute-start(bf16[2,128,512]{2,1,0:T(8,128)(2,1)S(1)} %get-tuple-element.78), channel_id=1, source_target_pairs={{0,3},{1,2},{2,1},{3,0},{4,7},{5,6},{6,5},{7,4},{8,11},{9,10},{10,... | collective-permute-start | bytes 786440 | tf_op jit(solution)/shard_map/ppermute | solution.py:519
  302.6 21.8 %collective-permute-start.5 = (bf16[2,128,512]{2,1,0:T(8,128)(2,1)S(1)}, bf16[2,128,512]{2,1,0:T(8,128)(2,1)S(1)}, u32[]{:S(2)}, u32[]{:S(2)}) collective-permute-start(bf16[2,128,512]{2,1,0:T(8,128)(2,1)S(1)} %get-tuple-element.79), channel_id=1, source_target_pairs={{0,2},{1,3},{2,0},{3,1},{4,6},{5,7},{6,4},{7,5},{8,10},{9,11},{10,... | collective-permute-start | bytes 786440 | tf_op jit(solution)/shard_map/ppermute | solution.py:519
  305.7 18.8 %collective-permute-start.4 = (bf16[2,128,512]{2,1,0:T(8,128)(2,1)S(1)}, bf16[2,128,512]{2,1,0:T(8,128)(2,1)S(1)}, u32[]{:S(2)}, u32[]{:S(2)}) collective-permute-start(bf16[2,128,512]{2,1,0:T(8,128)(2,1)S(1)} %get-tuple-element.80), channel_id=1, source_target_pairs={{0,1},{1,0},{2,3},{3,2},{4,5},{5,4},{6,7},{7,6},{8,9},{9,8},{10,11... | collective-permute-start | bytes 786440 | tf_op jit(solution)/shard_map/ppermute | solution.py:519
  306.2 28.4 %collective-permute-start.18 = (bf16[960,256]{1,0:T(8,128)(2,1)S(1)}, bf16[960,256]{1,0:T(8,128)(2,1)S(1)}, u32[]{:S(2)}, u32[]{:S(2)}) collective-permute-start(bf16[960,256]{1,0:T(8,128)(2,1)S(1)} %add_convert_fusion.1.refs_0_), channel_id=1, source_target_pairs={{0,1},{1,0},{2,3},{3,2},{4,5},{5,4},{6,7},{7,6},{8,9},{9,8},{10,11... | collective-permute-start | bytes 1474568 | tf_op jit(solution)/shard_map/ppermute | solution.py:355
  313.1 31.3 %collective-permute-start.19 = (bf16[960,256]{1,0:T(8,128)(2,1)S(1)}, bf16[960,256]{1,0:T(8,128)(2,1)S(1)}, u32[]{:S(2)}, u32[]{:S(2)}) collective-permute-start(bf16[960,256]{1,0:T(8,128)(2,1)S(1)} %add_convert_fusion.1.refs_0_), channel_id=1, source_target_pairs={{0,2},{2,0},{1,3},{3,1},{4,6},{6,4},{5,7},{7,5},{8,10},{10,8},{9,1... | collective-permute-start | bytes 1474568 | tf_op jit(solution)/shard_map/ppermute | solution.py:355
  324.4 20.0 %collective-permute-start.21 = (bf16[960,256]{1,0:T(8,128)(2,1)S(1)}, bf16[960,256]{1,0:T(8,128)(2,1)S(1)}, u32[]{:S(2)}, u32[]{:S(2)}) collective-permute-start(bf16[960,256]{1,0:T(8,128)(2,1)S(1)} %add_convert_fusion.refs_4_), channel_id=1, source_target_pairs={{0,1},{1,0},{2,3},{3,2},{4,5},{5,4},{6,7},{7,6},{8,9},{9,8},{10,11... | collective-permute-start | bytes 1474568 | tf_op jit(solution)/shard_map/ppermute | solution.py:355
  324.6 28.6 %collective-permute-start.22 = (bf16[960,256]{1,0:T(8,128)(2,1)S(1)}, bf16[960,256]{1,0:T(8,128)(2,1)}, u32[]{:S(2)}, u32[]{:S(2)}) collective-permute-start(bf16[960,256]{1,0:T(8,128)(2,1)S(1)} %add_convert_fusion.refs_4_), channel_id=1, source_target_pairs={{0,2},{2,0},{1,3},{3,1},{4,6},{6,4},{5,7},{7,5},{8,10},{10,8},{9,1... | collective-permute-start | bytes 1474568 | tf_op jit(solution)/shard_map/ppermute | solution.py:355
  327.6 28.8 %collective-permute-start.7 = (bf16[960,256]{1,0:T(8,128)(2,1)}, bf16[960,256]{1,0:T(8,128)(2,1)}, u32[]{:S(2)}, u32[]{:S(2)}) collective-permute-start(bf16[960,256]{1,0:T(8,128)(2,1)} %shard_map.108), channel_id=1, source_target_pairs={{0,4},{4,0},{1,5},{5,1},{2,6},{6,2},{3,7},{7,3},{8,12},{12,8},{9,1... | collective-permute-start | bytes 1474568 | tf_op jit(solution)/shard_map/ppermute | solution.py:355
  334.6 27.8 %collective-permute-start.12 = (bf16[960,256]{1,0:T(8,128)(2,1)}, bf16[960,256]{1,0:T(8,128)(2,1)S(1)}, u32[]{:S(2)}, u32[]{:S(2)}) collective-permute-start(bf16[960,256]{1,0:T(8,128)(2,1)} %shard_map.109), channel_id=1, source_target_pairs={{0,4},{4,0},{1,5},{5,1},{2,6},{6,2},{3,7},{7,3},{8,12},{12,8},{9,1... | collective-permute-start | bytes 1474568 | tf_op jit(solution)/shard_map/ppermute | solution.py:355
  353.2 11.4 %collective-permute-start.24 = (bf16[480,256]{1,0:T(8,128)(2,1)S(1)}, bf16[480,256]{1,0:T(8,128)(2,1)S(1)}, u32[]{:S(2)}, u32[]{:S(2)}) collective-permute-start(bf16[480,256]{1,0:T(8,128)(2,1)S(1)} %slice.53), channel_id=1, source_target_pairs={{0,1},{1,0},{2,3},{3,2},{4,5},{5,4},{6,7},{7,6},{8,9},{9,8},{10,11... | collective-permute-start | bytes 737288 | tf_op jit(solution)/shard_map/ppermute | solution.py:355
  353.3 11.7 %collective-permute-start.23 = (bf16[480,256]{1,0:T(8,128)(2,1)S(1)}, bf16[480,256]{1,0:T(8,128)(2,1)S(1)}, u32[]{:S(2)}, u32[]{:S(2)}) collective-permute-start(bf16[480,256]{1,0:T(8,128)(2,1)S(1)} %slice.52), channel_id=1, source_target_pairs={{0,2},{2,0},{1,3},{3,1},{4,6},{6,4},{5,7},{7,5},{8,10},{10,8},{9,1... | collective-permute-start | bytes 737288 | tf_op jit(solution)/shard_map/ppermute | solution.py:355
  354.3 13.1 %collective-permute-start.26 = (bf16[480,256]{1,0:T(8,128)(2,1)S(1)}, bf16[480,256]{1,0:T(8,128)(2,1)S(1)}, u32[]{:S(2)}, u32[]{:S(2)}) collective-permute-start(bf16[480,256]{1,0:T(8,128)(2,1)S(1)} %slice.55), channel_id=1, source_target_pairs={{0,1},{1,0},{2,3},{3,2},{4,5},{5,4},{6,7},{7,6},{8,9},{9,8},{10,11... | collective-permute-start | bytes 737288 | tf_op jit(solution)/shard_map/ppermute | solution.py:355
  356.4 13.8 %collective-permute-start.25 = (bf16[480,256]{1,0:T(8,128)(2,1)S(1)}, bf16[480,256]{1,0:T(8,128)(2,1)S(1)}, u32[]{:S(2)}, u32[]{:S(2)}) collective-permute-start(bf16[480,256]{1,0:T(8,128)(2,1)S(1)} %slice.54), channel_id=1, source_target_pairs={{0,2},{2,0},{1,3},{3,1},{4,6},{6,4},{5,7},{7,5},{8,10},{10,8},{9,1... | collective-permute-start | bytes 737288 | tf_op jit(solution)/shard_map/ppermute | solution.py:355
  362.4 38.8 %collective-permute-start.8 = (bf16[960,256]{1,0:T(8,128)(2,1)S(1)}, bf16[960,256]{1,0:T(8,128)(2,1)S(1)}, u32[]{:S(2)}, u32[]{:S(2)}) collective-permute-start(bf16[960,256]{1,0:T(8,128)(2,1)S(1)} %add_convert_fusion.3.refs_0_), channel_id=1, source_target_pairs={{0,1},{1,0},{2,3},{3,2},{4,5},{5,4},{6,7},{7,6},{8,9},{9,8},{10,11... | collective-permute-start | bytes 1474568 | tf_op jit(solution)/shard_map/ppermute | solution.py:355
  364.6 35.4 %collective-permute-start.9 = (bf16[960,256]{1,0:T(8,128)(2,1)S(1)}, bf16[960,256]{1,0:T(8,128)(2,1)S(1)}, u32[]{:S(2)}, u32[]{:S(2)}) collective-permute-start(bf16[960,256]{1,0:T(8,128)(2,1)S(1)} %add_convert_fusion.3.refs_0_), channel_id=1, source_target_pairs={{0,2},{2,0},{1,3},{3,1},{4,6},{6,4},{5,7},{7,5},{8,10},{10,8},{9,1... | collective-permute-start | bytes 1474568 | tf_op jit(solution)/shard_map/ppermute | solution.py:355
  365.0 41.8 %collective-permute-start.13 = (bf16[960,256]{1,0:T(8,128)(2,1)S(1)}, bf16[960,256]{1,0:T(8,128)(2,1)}, u32[]{:S(2)}, u32[]{:S(2)}) collective-permute-start(bf16[960,256]{1,0:T(8,128)(2,1)S(1)} %add_convert_fusion.2.refs_4_), channel_id=1, source_target_pairs={{0,1},{1,0},{2,3},{3,2},{4,5},{5,4},{6,7},{7,6},{8,9},{9,8},{10,11... | collective-permute-start | bytes 1474568 | tf_op jit(solution)/shard_map/ppermute | solution.py:355
  367.4 36.4 %collective-permute-start.14 = (bf16[960,256]{1,0:T(8,128)(2,1)S(1)}, bf16[960,256]{1,0:T(8,128)(2,1)}, u32[]{:S(2)}, u32[]{:S(2)}) collective-permute-start(bf16[960,256]{1,0:T(8,128)(2,1)S(1)} %add_convert_fusion.2.refs_4_), channel_id=1, source_target_pairs={{0,2},{2,0},{1,3},{3,1},{4,6},{6,4},{5,7},{7,5},{8,10},{10,8},{9,1... | collective-permute-start | bytes 1474568 | tf_op jit(solution)/shard_map/ppermute | solution.py:355
  381.9 11.3 %collective-permute-start.27 = (bf16[1024,128]{0,1:T(8,128)(2,1)S(1)}, bf16[1024,128]{0,1:T(8,128)(2,1)S(1)}, u32[]{:S(2)}, u32[]{:S(2)}) collective-permute-start(bf16[1024,128]{0,1:T(8,128)(2,1)S(1)} %fusion.18), channel_id=1, source_target_pairs={{0,16},{8,24},{16,0},{24,8},{1,17},{9,25},{17,1},{25,9},{2,18},{10... | collective-permute-start | bytes 786440 | tf_op jit(solution)/shard_map/ppermute | solution.py:382
  393.2 6.6 %collective-permute-start.29 = (bf16[128,1024]{1,0:T(8,128)(2,1)S(1)}, bf16[128,1024]{1,0:T(8,128)(2,1)S(1)}, u32[]{:S(2)}, u32[]{:S(2)}) collective-permute-start(bf16[128,1024]{1,0:T(8,128)(2,1)S(1)} %dynamic-slice_convert_fusion), channel_id=1, source_target_pairs={{0,16},{8,24},{16,0},{24,8},{1,17},{9,25},{17,1},{25,9},{2,18},{10... | collective-permute-start | bytes 786440 | tf_op jit(solution)/shard_map/ppermute | solution.py:382
  400.0 9.9 %collective-permute-start.30 = (bf16[128,512]{1,0:T(8,128)(2,1)S(1)}, bf16[128,512]{1,0:T(8,128)(2,1)}, u32[]{:S(2)}, u32[]{:S(2)}) collective-permute-start(bf16[128,512]{1,0:T(8,128)(2,1)S(1)} %dynamic-slice_convert_fusion.2), channel_id=1, source_target_pairs={{0,8},{8,0},{16,24},{24,16},{1,9},{9,1},{17,25},{25,17},{2,10},{10... | collective-permute-start | bytes 393224 | tf_op jit(solution)/shard_map/ppermute | solution.py:382
  401.3 10.3 %collective-permute-start.11 = (bf16[480,256]{1,0:T(8,128)(2,1)}, bf16[480,256]{1,0:T(8,128)(2,1)}, u32[]{:S(2)}, u32[]{:S(2)}) collective-permute-start(bf16[480,256]{1,0:T(8,128)(2,1)} %slice.63), channel_id=1, source_target_pairs={{0,1},{1,0},{2,3},{3,2},{4,5},{5,4},{6,7},{7,6},{8,9},{9,8},{10,11... | collective-permute-start | bytes 737288 | tf_op jit(solution)/shard_map/ppermute | solution.py:355
  402.8 9.2 %collective-permute-start.10 = (bf16[480,256]{1,0:T(8,128)(2,1)}, bf16[480,256]{1,0:T(8,128)(2,1)}, u32[]{:S(2)}, u32[]{:S(2)}) collective-permute-start(bf16[480,256]{1,0:T(8,128)(2,1)} %slice.62), channel_id=1, source_target_pairs={{0,2},{2,0},{1,3},{3,1},{4,6},{6,4},{5,7},{7,5},{8,10},{10,8},{9,1... | collective-permute-start | bytes 737288 | tf_op jit(solution)/shard_map/ppermute | solution.py:355
  404.8 10.0 %collective-permute-start.16 = (bf16[480,256]{1,0:T(8,128)(2,1)S(1)}, bf16[480,256]{1,0:T(8,128)(2,1)S(1)}, u32[]{:S(2)}, u32[]{:S(2)}) collective-permute-start(bf16[480,256]{1,0:T(8,128)(2,1)S(1)} %slice.65), channel_id=1, source_target_pairs={{0,1},{1,0},{2,3},{3,2},{4,5},{5,4},{6,7},{7,6},{8,9},{9,8},{10,11... | collective-permute-start | bytes 737288 | tf_op jit(solution)/shard_map/ppermute | solution.py:355
  407.8 8.6 %collective-permute-start.15 = (bf16[480,256]{1,0:T(8,128)(2,1)S(1)}, bf16[480,256]{1,0:T(8,128)(2,1)S(1)}, u32[]{:S(2)}, u32[]{:S(2)}) collective-permute-start(bf16[480,256]{1,0:T(8,128)(2,1)S(1)} %slice.64), channel_id=1, source_target_pairs={{0,2},{2,0},{1,3},{3,1},{4,6},{6,4},{5,7},{7,5},{8,10},{10,8},{9,1... | collective-permute-start | bytes 737288 | tf_op jit(solution)/shard_map/ppermute | solution.py:355
  (35 other events, 336.0 us)

commit v7 on v6

--- a/solution.py
+++ b/solution.py
@@ -275,11 +275,11 @@
     )(outs, douts, mine, theirs)
 
 
-def project_kernel(*refs, count, parts, last, chunk, depth):
+def project_kernel(*refs, count, last, chunk, depth, has_before):
     step = pl.program_id(0)
-    cols = refs[count * parts]
-    rest, weights = refs[count * parts + 1 : -1], refs[-1]
-    before = rest[0] if len(rest) == (3 if last else 2) else None
+    cols = refs[count]
+    rest, weights = refs[count + 1 : -1], refs[-1]
+    before = rest[0] if has_before else None
     half = cols.shape[3] // 2
 
     @pl.when(step == 0)
@@ -295,60 +295,51 @@
                 weights[i, out_rows, :half] = own[:, :half]
                 weights[i, out_rows, half:] = empty
 
-    def part(pieces):
-        value = jnp.dot(pieces[0][...], weights[0], preferred_element_type=jnp.float32)
-        for i in range(1, count):
-            value += jnp.dot(pieces[i][...], weights[i], preferred_element_type=jnp.float32)
-        if before is not None:
-            value += before[...]
-        if last:
-            rest[-2][...] = value[:, :half].astype(jnp.bfloat16)
-            rest[-1][...] = value[:, half:].astype(jnp.bfloat16)
-        else:
-            rest[-1][...] = value
-
-    for i in range(parts):
-        pl.when(step * parts // pl.num_programs(0) == i)(
-            functools.partial(part, refs[i * count : (i + 1) * count])
-        )
-
-
-def project(parts, cols, before, last, chunk):
-    count = len(parts[0])
-    rows, depth = parts[0][0].shape
-    total_rows = rows * len(parts)
+    value = jnp.dot(refs[0][...], weights[0], preferred_element_type=jnp.float32)
+    for i in range(1, count):
+        value += jnp.dot(refs[i][...], weights[i], preferred_element_type=jnp.float32)
+    if before is not None:
+        value += before[...]
+    if last:
+        rest[-2][...] = value[:, :half].astype(jnp.bfloat16)
+        rest[-1][...] = value[:, half:].astype(jnp.bfloat16)
+    else:
+        rest[-1][...] = value
+
+
+def project(pieces, cols, before, outs, last, chunk, part, parts):
+    count = len(pieces)
+    rows, depth = pieces[0].shape
+    total_rows = rows * parts
     width = cols.shape[3]
-    steps = 4 // len(parts)
+    steps = 2
     tile = rows // steps
-    rowwise = lambda w: pl.BlockSpec((tile, w), lambda i: (i, 0))
-
-    def within(which):
-        return pl.BlockSpec(
-            (tile, depth), lambda i: (jnp.clip(i - which * steps, 0, steps - 1), 0)
-        )
-
+    rowwise = lambda w: pl.BlockSpec((tile, w), lambda i: (part * steps + i, 0))
     halves = jax.ShapeDtypeStruct((total_rows, width // 2), jnp.bfloat16)
+    shapes = [halves] * 2 if last else [jax.ShapeDtypeStruct((total_rows, width), jnp.float32)]
+    outs = list(outs or [])
+    inputs = [*pieces, cols] + ([] if before is None else [before]) + outs
     return pl.pallas_call(
         functools.partial(
-            project_kernel, count=count, parts=len(parts), last=last, chunk=chunk,
-            depth=depth // 4,
-        ),
-        grid=(4,),
-        in_specs=[within(i) for i in range(len(parts)) for _ in range(count)]
+            project_kernel, count=count, last=last, chunk=chunk, depth=depth // 4,
+            has_before=before is not None,
+        ),
+        grid=(steps,),
+        in_specs=[pl.BlockSpec((tile, depth), lambda i: (i, 0))] * count
         + [pl.BlockSpec(cols.shape, lambda i: (0, 0, 0, 0))]
-        + ([] if before is None else [rowwise(width)]),
-        out_specs=[rowwise(width // 2)] * 2 if last else rowwise(width),
+        + ([] if before is None else [rowwise(width)])
+        + [pl.BlockSpec(memory_space=pl.ANY)] * len(outs),
+        out_specs=[rowwise(width // 2)] * 2 if last else [rowwise(width)],
         scratch_shapes=[pltpu.VMEM((count, depth, width), jnp.bfloat16)],
-        out_shape=[halves] * 2
-        if last
-        else jax.ShapeDtypeStruct((total_rows, width), jnp.float32),
+        out_shape=shapes,
+        input_output_aliases={len(inputs) - len(outs) + i: i for i in range(len(outs))},
         compiler_params=pltpu.CompilerParams(vmem_limit_bytes=40 << 20),
         cost_estimate=pl.CostEstimate(
-            flops=2 * total_rows * depth * count * width,
+            flops=2 * rows * depth * count * width,
             transcendentals=0,
-            bytes_accessed=2 * total_rows * (depth * count + 2 * width),
-        ),
-    )(*[x for pieces in parts for x in pieces], cols, *([] if before is None else [before]))
+            bytes_accessed=2 * rows * (depth * count + 2 * width),
+        ),
+    )(*inputs)
 
 
 def swap(x, axis):
@@ -509,31 +500,29 @@
     part_patches = patch_blocks // part_count
     gathered = []
     own = []
+    cols = None
     for c in range(local_heads):
         final = c + 1 == local_heads
         if final:
-            blocks, bias, received[c] = lax.optimization_barrier((blocks, bias, received[c]))
+            if c:
+                blocks, _ = lax.optimization_barrier((blocks, mine))
             if small:
-                pairs = lambda d: [(i, i ^ d) for i in range(inner)]
-                cols = [
+                cols = [lax.dynamic_index_in_dim(blocks, spot, 0, keepdims=False)] + [
                     lax.ppermute(
                         lax.dynamic_index_in_dim(blocks, spot ^ d, 0, keepdims=False),
                         ("zl", "y"),
-                        pairs(d),
+                        [(i, i ^ d) for i in range(inner)],
                     )
-                    if d
-                    else lax.dynamic_index_in_dim(blocks, spot, 0, keepdims=False)
-                    for d in range(inner)
+                    for d in range(1, inner)
                 ]
                 cols = jnp.stack(cols)
             else:
                 cols = lax.all_to_all(blocks, ("zl", "y"), split_axis=0, concat_axis=0, tiled=True)
+            bias, cols = lax.optimization_barrier((bias, cols))
         outs, douts, mine = attention(
             tables, bias, queries, backs, received[c], c, slots, head_scale
         )
         theirs = swap(mine, "zh")
-        if final:
-            theirs, _ = lax.optimization_barrier((theirs, cols))
         parts = [
             merge(outs, douts, mine, theirs, start, part_patches, head_scale, head_size)
             for start in range(0, patch_blocks, part_patches)
@@ -543,25 +532,38 @@
             gathered[-1] = [second_hop(x, small) for x in gathered[-1]]
         if not final:
             parts, bias = lax.optimization_barrier((parts, bias))
-        merged = [
-            (part.astype(jnp.float32) + swap(part, "zh").astype(jnp.float32)).astype(jnp.bfloat16)
-            for part in parts
-        ]
-        pieces = [first_hop(x, small) for x in merged]
-        gathered.append(pieces)
+        merged = []
+        for part in parts:
+            if final and merged:
+                part, _ = lax.optimization_barrier((part, merged[-1]))
+            other = swap(part, "zh").astype(jnp.float32)
+            merged.append((part.astype(jnp.float32) + other).astype(jnp.bfloat16))
+        gathered.append([first_hop(x, small) for x in merged])
         if final:
-            result = None
+            results = None
             for i, earlier in enumerate(gathered[:-1]):
-                result = project(earlier, cols, result, False, i)
-            if result is not None:
-                merged, _ = lax.optimization_barrier((merged, result))
+                before = results
+                results = None
+                for j, pieces in enumerate(earlier):
+                    results = project(
+                        pieces, cols, before[0] if before else None, results, False, i, j,
+                        part_count,
+                    )
+            if results is not None:
+                merged, _ = lax.optimization_barrier((merged, results))
         own.append(
             jnp.concatenate(
                 [lax.dynamic_slice_in_dim(x, zh * LANES, LANES, 1) for x in merged], axis=0
             )
         )
-    last_pieces = [second_hop(x, small) for x in gathered[-1]]
-    attended, patch_grad = project(last_pieces, cols, result, True, local_heads - 1)
+    before = results[0] if results else None
+    final_outs = None
+    for j, pieces in enumerate(gathered[-1]):
+        final_outs = project(
+            second_hop(pieces, small), cols, before, final_outs, True, local_heads - 1, j,
+            part_count,
+        )
+    attended, patch_grad = final_outs
 
     dquery = jnp.concatenate([x[:, :head_size] for x in own], axis=1)
     heads_out = jnp.concatenate([x[:, head_size:] for x in own], axis=1)

time: 426 us -> 423 us (level)
  waiting for transfers between devices: 193 us -> 200 us
  matrix products: 21.7 us -> 17.2 us
    ppermute x24, waiting for transfers between devices: 153 us -> 190 us  [swap(): return lax.ppermute(x, axis, [(0, 1), (1, 0)])]
    ppermute x3, waiting for transfers between devices: 15.1 us -> 0.01 us  [local(): lax.ppermute(lax.dynamic_index_in_dim(blocks, spot ^ d, 0, keepdims=False...]
    all_to_all x2, waiting for transfers between devices: 17.4 us -> 5.95 us  [exchange(): lax.all_to_all(x, ('dp', 'zl', 'y'), split_axis=0, concat_axis=0, tiled=T...]
    ppermute x4, starting transfers between devices: 9.24 us -> 0.8 us  [scatter_sum(): lax.ppermute(give.astype(jnp.bfloat16), 'dp', [(i, i ^ step) for i in ran...]
    ppermute x24, starting transfers between devices: 26.3 us -> 34.1 us  [swap(): return lax.ppermute(x, axis, [(0, 1), (1, 0)])]
    dot_general x1, matrix products: 5.94 us -> 1.38 us  [local(): lax.dot_general(patches, dquery, (((0,), (0,)), ((), ())), preferred_elem...]
    pallas_call x2 -> x4, Pallas kernels: 9.66 us -> 8.69 us  [project(): pl.pallas_call(functools.partial(project_kernel, count=count, last=last,...]
    unnamed x72 -> x74, local copies, waits for them, and re-layouts: 20 us -> 19.6 us
  transfers between devices with their start and end apart: 33 -> 33, of which waited for: 17 -> 13; matrix products, arithmetic and copies ran while one was open for 12% -> 11% of each run, Pallas kernels for 21% -> 21%
where the time goes in v7:
time: 423 us; the launch traced here: 422 us
  waiting for transfers between devices  200 us (47%)
  Pallas kernels  96.4 us (23%)
  starting transfers between devices  56 us (13%)
  local copies, waits for them, and re-layouts  33.7 us (8%)
  matrix products  17.2 us (4%)
  other arithmetic  16.9 us (4%)
    ppermute x24, waiting for transfers between devices, swap(): return lax.ppermute(x, axis, [(0, 1), (1, 0)])  190 us
    pallas_call x2, Pallas kernels, attention(): pl.pallas_call(functools.partial(attention_kernel, slots=slots, scale=sca...  65.4 us
    ppermute x24, starting transfers between devices, swap(): return lax.ppermute(x, axis, [(0, 1), (1, 0)])  34.1 us
    unnamed x74, local copies, waits for them, and re-layouts  19.6 us
    all_to_all x2, starting transfers between devices, exchange(): lax.all_to_all(x, ('dp', 'zl', 'y'), split_axis=0, concat_axis=0, tiled=T...  17.5 us
    pallas_call x4, Pallas kernels, merge(): pl.pallas_call(functools.partial(merge_kernel, scale=scale, split=split),...  11.4 us
    pallas_call x2, Pallas kernels, pack_blocks(): pl.pallas_call(functools.partial(pack_kernel, chunk=chunk, local_heads=lo...  10.8 us
    dot_general x1, matrix products, nt_dot(): lax.dot_general(left, right, (((1,), (1,)), ((), ())), preferred_element_...  8.98 us
  transfers between devices with their start and end apart: 33, of which 13 were waited for; matrix products, arithmetic and copies ran while one was open for 11% of the time, Pallas kernels for 21%

profile of v7, /device:TPU:0, one launch (start us, length us, event | category | flops | bytes accessed | tf_op | source)
XLA Modules:
  0.0 421.7 jit_solution(13947797758911788268)
XLA Ops:
  2.9 3.4 copy-done.2
  6.9 5.0 %shard_map.102 = bf16[4,4,8,2,128,128]{5,4,3,2,1,0:T(8,128)(2,1)S(1)} custom-call(s32[32]{0:T(128)S(1)} %reshape.446.chosen, s32[4]{0:T(128)S(1)} %reduce_sum.99.counts, s32[16]{0:T(128)S(1)} %copy-done.6, bf16[16,128,16,128]{3,2,1,0:T(8,128)(2,1)S(1)} %copy-done.2), custom_call_target="tpu_custom_call" | custom-call | bytes 16777216 | tf_op jit(solution)/shard_map/pallas_call | solution.py:49
  12.0 3.3 copy-done.5
  15.3 5.4 %all-to-all-start = ((bf16[16,2048,128]{2,1,0:T(8,128)(2,1)}), bf16[16,2048,128]{2,1,0:T(8,128)(2,1)}, u32[]{:S(2)}, u32[]{:S(2)}) async-start(bf16[16,2048,128]{2,1,0:T(8,128)(2,1)} %bitcast.44), calls=%async_computation | async-start | bytes 16777216 | tf_op jit(solution)/shard_map/all_to_all | solution.py:423
  24.3 3.4 copy-done.3
  27.6 5.8 %shard_map.103 = bf16[4,4,8,2,128,128]{5,4,3,2,1,0:T(8,128)(2,1)S(1)} custom-call(s32[32]{0:T(128)S(1)} %reshape.446.chosen, s32[4]{0:T(128)S(1)} %reduce_sum.99.counts, s32[16]{0:T(128)S(1)} %copy-done.7, bf16[16,128,16,128]{3,2,1,0:T(8,128)(2,1)S(1)} %copy-done.3), custom_call_target="tpu_custom_call" | custom-call | bytes 16777216 | tf_op jit(solution)/shard_map/pallas_call | solution.py:49
  33.5 3.2 copy-done.4
  36.7 87.4 %collective-permute-done = bf16[2048,128]{0,1:T(8,128)(2,1)S(1)} collective-permute-done((bf16[2048,128]{0,1:T(8,128)(2,1)S(1)}, bf16[2048,128]{0,1:T(8,128)(2,1)S(1)}, u32[]{:S(2)}, u32[]{:S(2)}) %collective-permute-start) | collective-permute-done | bytes 524320 | tf_op jit(solution)/shard_map/ppermute | solution.py:346
  124.1 11.0 %collective-permute-done.1 = bf16[128,2048]{0,1:T(8,128)(2,1)S(1)} collective-permute-done((bf16[128,2048]{0,1:T(8,128)(2,1)S(1)}, bf16[128,2048]{0,1:T(8,128)(2,1)S(1)}, u32[]{:S(2)}, u32[]{:S(2)}) %collective-permute-start.1) | collective-permute-done | bytes 524320 | tf_op jit(solution)/shard_map/ppermute | solution.py:346
  135.2 5.9 %all-to-all-done = bf16[16,2048,128]{2,1,0:T(8,128)(2,1)} async-done(((bf16[16,2048,128]{2,1,0:T(8,128)(2,1)}), bf16[16,2048,128]{2,1,0:T(8,128)(2,1)}, u32[]{:S(2)}, u32[]{:S(2)}) %all-to-all-start) | async-done | bytes 8388640 | tf_op jit(solution)/shard_map/all_to_all | solution.py:423
  141.1 12.1 %all-to-all-start.1 = ((bf16[16,2048,128]{2,1,0:T(8,128)(2,1)}), bf16[16,2048,128]{2,1,0:T(8,128)(2,1)}, u32[]{:S(2)}, u32[]{:S(2)}) async-start(bf16[16,2048,128]{2,1,0:T(8,128)(2,1)} %bitcast.43), calls=%async_computation.1 | async-start | bytes 16777216 | tf_op jit(solution)/shard_map/all_to_all | solution.py:423
  171.3 9.0 %fusion.2.b_ref = bf16[1920,512]{1,0:T(8,128)(2,1)} fusion(bf16[512,2048]{1,0:T(8,128)(2,1)S(1)} %bitcast.55, bf16[1920,2048]{1,0:T(8,128)(2,1)} %param.13), kind=kOutput, calls=%fused_computation.5 | convolution fusion | flops 4027514880 | bytes 11927552 | tf_op jit(solution)/shard_map/dot_general | solution.py:78
  180.2 5.4 %fusion.3.q_ref = bf16[1920,512]{1,0:T(8,128)(2,1)} fusion(bf16[2048,512]{0,1:T(8,128)(2,1)S(1)} %bitcast.56, bf16[1920,2048]{1,0:T(8,128)(2,1)S(1)} %bitcast.46), kind=kOutput, calls=%fused_computation.6 | convolution fusion | flops 4028497920 | bytes 11927552 | tf_op jit(solution)/shard_map/dot_general | solution.py:487
  185.7 32.8 %shard_map.104 = (f32[1920,256]{1,0:T(8,128)}, f32[1920,256]{1,0:T(8,128)}, f32[4,8,512]{2,1,0:T(8,128)}) custom-call(s32[128]{0:T(128)} %copy-done.28, s32[4]{0:T(128)} %copy-done.27, s32[128]{0:T(128)} %reshape.450.offsets, s32[128]{0:T(128)} %and_select_fusion.sizes, bf16[1920,512]{1,0:T(8,128)(2,1)} %fusion.3.q_ref, bf16[1920,512]{1,0:T(8,128)(2,1)} %fusion.2.b_ref, ...), custom_call_target="tpu_custom_call" | custom-call | flops 8053063680 | bytes 41943040 | tf_op jit(solution)/shard_map/pallas_call | solution.py:203
  222.1 40.3 %collective-permute-done.2.theirs_ref = f32[4,8,512]{2,1,0:T(8,128)S(1)} collective-permute-done((f32[4,8,512]{2,1,0:T(8,128)}, f32[4,8,512]{2,1,0:T(8,128)S(1)}, u32[]{:S(2)}, u32[]{:S(2)}) %collective-permute-start.2) | collective-permute-done | bytes 65568 | tf_op jit(solution)/shard_map/ppermute | solution.py:346
  263.1 2.8 shard_map.106
  265.9 2.9 shard_map.105
  268.8 3.3 collective-permute-start.16
  274.0 32.7 %shard_map.107 = (f32[1920,256]{1,0:T(8,128)}, f32[1920,256]{1,0:T(8,128)}, f32[4,8,512]{2,1,0:T(8,128)}) custom-call(s32[128]{0:T(128)} %copy-done.28, s32[4]{0:T(128)} %copy-done.27, s32[128]{0:T(128)} %reshape.450.offsets, s32[128]{0:T(128)} %and_select_fusion.sizes, bf16[1920,512]{1,0:T(8,128)(2,1)} %fusion.3.q_ref, bf16[1920,512]{1,0:T(8,128)(2,1)} %fusion.2.b_ref, ...), custom_call_target="tpu_custom_call" | custom-call | flops 8053063680 | bytes 41943040 | tf_op jit(solution)/shard_map/pallas_call | solution.py:203
  306.7 2.9 collective-permute-start.6
  310.9 4.2 collective-permute-start.18
  318.4 2.8 shard_map.109
  321.3 3.3 collective-permute-start.7
  326.0 2.8 shard_map.108
  328.9 9.4 %collective-permute-done.18.refs_2_ = bf16[960,256]{1,0:T(8,128)(2,1)} collective-permute-done((bf16[960,256]{1,0:T(8,128)(2,1)S(1)}, bf16[960,256]{1,0:T(8,128)(2,1)}, u32[]{:S(2)}, u32[]{:S(2)}) %collective-permute-start.18) | collective-permute-done | bytes 491552 | tf_op jit(solution)/shard_map/ppermute | solution.py:346
  338.3 10.4 %collective-permute-done.15.refs_2_ = bf16[960,256]{1,0:T(8,128)(2,1)S(1)} collective-permute-done((bf16[960,256]{1,0:T(8,128)(2,1)S(1)}, bf16[960,256]{1,0:T(8,128)(2,1)S(1)}, u32[]{:S(2)}, u32[]{:S(2)}) %collective-permute-start.15) | collective-permute-done | bytes 491552 | tf_op jit(solution)/shard_map/ppermute | solution.py:346
  355.4 2.8 collective-permute-start.8
  364.4 4.5 %collective-permute-done.19 = bf16[480,256]{1,0:T(8,128)(2,1)S(1)} collective-permute-done((bf16[480,256]{1,0:T(8,128)(2,1)S(1)}, bf16[480,256]{1,0:T(8,128)(2,1)S(1)}, u32[]{:S(2)}, u32[]{:S(2)}) %collective-permute-start.19) | collective-permute-done | bytes 245792 | tf_op jit(solution)/shard_map/ppermute | solution.py:346
  371.9 7.8 %collective-permute-done.8 = bf16[960,256]{1,0:T(8,128)(2,1)S(1)} collective-permute-done((bf16[960,256]{1,0:T(8,128)(2,1)}, bf16[960,256]{1,0:T(8,128)(2,1)S(1)}, u32[]{:S(2)}, u32[]{:S(2)}) %collective-permute-start.8) | collective-permute-done | bytes 491552 | tf_op jit(solution)/shard_map/ppermute | solution.py:346
  387.9 11.0 %collective-permute-done.25 = bf16[480,256]{1,0:T(8,128)(2,1)S(1)} collective-permute-done((bf16[480,256]{1,0:T(8,128)(2,1)S(1)}, bf16[480,256]{1,0:T(8,128)(2,1)S(1)}, u32[]{:S(2)}, u32[]{:S(2)}) %collective-permute-start.25) | collective-permute-done | bytes 245792 | tf_op jit(solution)/shard_map/ppermute | solution.py:346
  401.4 4.6 %collective-permute-done.29 = bf16[128,1024]{1,0:T(8,128)(2,1)S(1)} collective-permute-done((bf16[128,1024]{1,0:T(8,128)(2,1)S(1)}, bf16[128,1024]{1,0:T(8,128)(2,1)S(1)}, u32[]{:S(2)}, u32[]{:S(2)}) %collective-permute-start.29) | collective-permute-done | bytes 262176 | tf_op jit(solution)/shard_map/ppermute | solution.py:373
  410.1 5.2 %collective-permute-done.11 = bf16[480,256]{1,0:T(8,128)(2,1)} collective-permute-done((bf16[480,256]{1,0:T(8,128)(2,1)S(1)}, bf16[480,256]{1,0:T(8,128)(2,1)}, u32[]{:S(2)}, u32[]{:S(2)}) %collective-permute-start.11) | collective-permute-done | bytes 245792 | tf_op jit(solution)/shard_map/ppermute | solution.py:346
  (209 shorter events, 73.2 us)
Async XLA Ops:
  15.3 125.8 %all-to-all-start = ((bf16[16,2048,128]{2,1,0:T(8,128)(2,1)}), bf16[16,2048,128]{2,1,0:T(8,128)(2,1)}, u32[]{:S(2)}, u32[]{:S(2)}) async-start(bf16[16,2048,128]{2,1,0:T(8,128)(2,1)} %bitcast.44), calls=%async_computation | async-start | bytes 16777216 | tf_op jit(solution)/shard_map/all_to_all | solution.py:423
  20.9 103.2 %collective-permute-start = (bf16[2048,128]{0,1:T(8,128)(2,1)S(1)}, bf16[2048,128]{0,1:T(8,128)(2,1)S(1)}, u32[]{:S(2)}, u32[]{:S(2)}) collective-permute-start(bf16[2048,128]{0,1:T(8,128)(2,1)S(1)} %copy.37), channel_id=1, source_target_pairs={{0,4},{4,0},{1,5},{5,1},{2,6},{6,2},{3,7},{7,3},{8,12},{12,8},{9,1... | collective-permute-start | bytes 1572872 | tf_op jit(solution)/shard_map/ppermute | solution.py:346
  23.9 111.3 %collective-permute-start.1 = (bf16[128,2048]{0,1:T(8,128)(2,1)S(1)}, bf16[128,2048]{0,1:T(8,128)(2,1)S(1)}, u32[]{:S(2)}, u32[]{:S(2)}) collective-permute-start(bf16[128,2048]{0,1:T(8,128)(2,1)S(1)} %copy.36), channel_id=1, source_target_pairs={{0,4},{4,0},{1,5},{5,1},{2,6},{6,2},{3,7},{7,3},{8,12},{12,8},{9,1... | collective-permute-start | bytes 1572872 | tf_op jit(solution)/shard_map/ppermute | solution.py:346
  141.1 132.9 %all-to-all-start.1 = ((bf16[16,2048,128]{2,1,0:T(8,128)(2,1)}), bf16[16,2048,128]{2,1,0:T(8,128)(2,1)}, u32[]{:S(2)}, u32[]{:S(2)}) async-start(bf16[16,2048,128]{2,1,0:T(8,128)(2,1)} %bitcast.43), calls=%async_computation.1 | async-start | bytes 16777216 | tf_op jit(solution)/shard_map/all_to_all | solution.py:423
  218.6 53.6 %collective-permute-start.3 = (bf16[2,128,512]{2,1,0:T(8,128)(2,1)S(1)}, bf16[2,128,512]{2,1,0:T(8,128)(2,1)S(1)}, u32[]{:S(2)}, u32[]{:S(2)}) collective-permute-start(bf16[2,128,512]{2,1,0:T(8,128)(2,1)S(1)} %get-tuple-element.84), channel_id=1, source_target_pairs={{0,1},{1,0},{2,3},{3,2},{4,5},{5,4},{6,7},{7,6},{8,9},{9,8},{10,11... | collective-permute-start | bytes 786440 | tf_op jit(solution)/shard_map/ppermute | solution.py:511
  220.5 51.7 %collective-permute-start.4 = (bf16[2,128,512]{2,1,0:T(8,128)(2,1)S(1)}, bf16[2,128,512]{2,1,0:T(8,128)(2,1)S(1)}, u32[]{:S(2)}, u32[]{:S(2)}) collective-permute-start(bf16[2,128,512]{2,1,0:T(8,128)(2,1)S(1)} %get-tuple-element.83), channel_id=1, source_target_pairs={{0,2},{1,3},{2,0},{3,1},{4,6},{5,7},{6,4},{7,5},{8,10},{9,11},{10,... | collective-permute-start | bytes 786440 | tf_op jit(solution)/shard_map/ppermute | solution.py:511
  222.0 50.2 %collective-permute-start.5 = (bf16[2,128,512]{2,1,0:T(8,128)(2,1)S(1)}, bf16[2,128,512]{2,1,0:T(8,128)(2,1)S(1)}, u32[]{:S(2)}, u32[]{:S(2)}) collective-permute-start(bf16[2,128,512]{2,1,0:T(8,128)(2,1)S(1)} %get-tuple-element.82), channel_id=1, source_target_pairs={{0,3},{1,2},{2,1},{3,0},{4,7},{5,6},{6,5},{7,4},{8,11},{9,10},{10,... | collective-permute-start | bytes 786440 | tf_op jit(solution)/shard_map/ppermute | solution.py:511
  222.1 40.3 %collective-permute-start.2 = (f32[4,8,512]{2,1,0:T(8,128)}, f32[4,8,512]{2,1,0:T(8,128)S(1)}, u32[]{:S(2)}, u32[]{:S(2)}) collective-permute-start(f32[4,8,512]{2,1,0:T(8,128)} %get-tuple-element.42.mine_ref), channel_id=1, source_target_pairs={{0,4},{4,0},{1,5},{5,1},{2,6},{6,2},{3,7},{7,3},{8,12},{12,8},{9,1... | collective-permute-start | bytes 196616 | tf_op jit(solution)/shard_map/ppermute | solution.py:346
  268.8 40.7 %collective-permute-start.16 = (bf16[960,256]{1,0:T(8,128)(2,1)S(1)}, bf16[960,256]{1,0:T(8,128)(2,1)S(1)}, u32[]{:S(2)}, u32[]{:S(2)}) collective-permute-start(bf16[960,256]{1,0:T(8,128)(2,1)S(1)} %copy-done.21), channel_id=1, source_target_pairs={{0,4},{4,0},{1,5},{5,1},{2,6},{6,2},{3,7},{7,3},{8,12},{12,8},{9,1... | collective-permute-start | bytes 1474568 | tf_op jit(solution)/shard_map/ppermute | solution.py:346
  272.1 44.3 %collective-permute-start.13 = (bf16[960,256]{1,0:T(8,128)(2,1)}, bf16[960,256]{1,0:T(8,128)(2,1)S(1)}, u32[]{:S(2)}, u32[]{:S(2)}) collective-permute-start(bf16[960,256]{1,0:T(8,128)(2,1)} %shard_map.105), channel_id=1, source_target_pairs={{0,4},{4,0},{1,5},{5,1},{2,6},{6,2},{3,7},{7,3},{8,12},{12,8},{9,1... | collective-permute-start | bytes 1474568 | tf_op jit(solution)/shard_map/ppermute | solution.py:346
  306.7 11.7 %collective-permute-start.6 = (f32[4,8,512]{2,1,0:T(8,128)}, f32[4,8,512]{2,1,0:T(8,128)}, u32[]{:S(2)}, u32[]{:S(2)}) collective-permute-start(f32[4,8,512]{2,1,0:T(8,128)} %get-tuple-element.49.mine_ref), channel_id=1, source_target_pairs={{0,4},{4,0},{1,5},{5,1},{2,6},{6,2},{3,7},{7,3},{8,12},{12,8},{9,1... | collective-permute-start | bytes 196616 | tf_op jit(solution)/shard_map/ppermute | solution.py:346
  309.7 19.2 %collective-permute-start.17 = (bf16[960,256]{1,0:T(8,128)(2,1)S(1)}, bf16[960,256]{1,0:T(8,128)(2,1)S(1)}, u32[]{:S(2)}, u32[]{:S(2)}) collective-permute-start(bf16[960,256]{1,0:T(8,128)(2,1)S(1)} %add_convert_fusion.refs_0_), channel_id=1, source_target_pairs={{0,1},{1,0},{2,3},{3,2},{4,5},{5,4},{6,7},{7,6},{8,9},{9,8},{10,11... | collective-permute-start | bytes 1474568 | tf_op jit(solution)/shard_map/ppermute | solution.py:346
  310.9 27.4 %collective-permute-start.18 = (bf16[960,256]{1,0:T(8,128)(2,1)S(1)}, bf16[960,256]{1,0:T(8,128)(2,1)}, u32[]{:S(2)}, u32[]{:S(2)}) collective-permute-start(bf16[960,256]{1,0:T(8,128)(2,1)S(1)} %add_convert_fusion.refs_0_), channel_id=1, source_target_pairs={{0,2},{2,0},{1,3},{3,1},{4,6},{6,4},{5,7},{7,5},{8,10},{10,8},{9,1... | collective-permute-start | bytes 1474568 | tf_op jit(solution)/shard_map/ppermute | solution.py:346
  316.6 21.8 %collective-permute-start.14 = (bf16[960,256]{1,0:T(8,128)(2,1)S(1)}, bf16[960,256]{1,0:T(8,128)(2,1)S(1)}, u32[]{:S(2)}, u32[]{:S(2)}) collective-permute-start(bf16[960,256]{1,0:T(8,128)(2,1)S(1)} %add_convert_fusion.1.refs_0_), channel_id=1, source_target_pairs={{0,1},{1,0},{2,3},{3,2},{4,5},{5,4},{6,7},{7,6},{8,9},{9,8},{10,11... | collective-permute-start | bytes 1474568 | tf_op jit(solution)/shard_map/ppermute | solution.py:346
  317.6 31.2 %collective-permute-start.15 = (bf16[960,256]{1,0:T(8,128)(2,1)S(1)}, bf16[960,256]{1,0:T(8,128)(2,1)S(1)}, u32[]{:S(2)}, u32[]{:S(2)}) collective-permute-start(bf16[960,256]{1,0:T(8,128)(2,1)S(1)} %add_convert_fusion.1.refs_0_), channel_id=1, source_target_pairs={{0,2},{2,0},{1,3},{3,1},{4,6},{6,4},{5,7},{7,5},{8,10},{10,8},{9,1... | collective-permute-start | bytes 1474568 | tf_op jit(solution)/shard_map/ppermute | solution.py:346
  321.3 32.8 %collective-permute-start.7 = (bf16[960,256]{1,0:T(8,128)(2,1)}, bf16[960,256]{1,0:T(8,128)(2,1)}, u32[]{:S(2)}, u32[]{:S(2)}) collective-permute-start(bf16[960,256]{1,0:T(8,128)(2,1)} %shard_map.109), channel_id=1, source_target_pairs={{0,4},{4,0},{1,5},{5,1},{2,6},{6,2},{3,7},{7,3},{8,12},{12,8},{9,1... | collective-permute-start | bytes 1474568 | tf_op jit(solution)/shard_map/ppermute | solution.py:346
  348.8 11.4 %collective-permute-start.21 = (bf16[480,256]{1,0:T(8,128)(2,1)S(1)}, bf16[480,256]{1,0:T(8,128)(2,1)S(1)}, u32[]{:S(2)}, u32[]{:S(2)}) collective-permute-start(bf16[480,256]{1,0:T(8,128)(2,1)S(1)} %slice.52), channel_id=1, source_target_pairs={{0,2},{2,0},{1,3},{3,1},{4,6},{6,4},{5,7},{7,5},{8,10},{10,8},{9,1... | collective-permute-start | bytes 737288 | tf_op jit(solution)/shard_map/ppermute | solution.py:346
  348.9 12.1 %collective-permute-start.22 = (bf16[480,256]{1,0:T(8,128)(2,1)S(1)}, bf16[480,256]{1,0:T(8,128)(2,1)S(1)}, u32[]{:S(2)}, u32[]{:S(2)}) collective-permute-start(bf16[480,256]{1,0:T(8,128)(2,1)S(1)} %slice.53), channel_id=1, source_target_pairs={{0,1},{1,0},{2,3},{3,2},{4,5},{5,4},{6,7},{7,6},{8,9},{9,8},{10,11... | collective-permute-start | bytes 737288 | tf_op jit(solution)/shard_map/ppermute | solution.py:346
  349.5 19.5 %collective-permute-start.19 = (bf16[480,256]{1,0:T(8,128)(2,1)S(1)}, bf16[480,256]{1,0:T(8,128)(2,1)S(1)}, u32[]{:S(2)}, u32[]{:S(2)}) collective-permute-start(bf16[480,256]{1,0:T(8,128)(2,1)S(1)} %slice.50), channel_id=1, source_target_pairs={{0,2},{2,0},{1,3},{3,1},{4,6},{6,4},{5,7},{7,5},{8,10},{10,8},{9,1... | collective-permute-start | bytes 737288 | tf_op jit(solution)/shard_map/ppermute | solution.py:346
  352.5 16.4 %collective-permute-start.20 = (bf16[480,256]{1,0:T(8,128)(2,1)S(1)}, bf16[480,256]{1,0:T(8,128)(2,1)S(1)}, u32[]{:S(2)}, u32[]{:S(2)}) collective-permute-start(bf16[480,256]{1,0:T(8,128)(2,1)S(1)} %slice.51), channel_id=1, source_target_pairs={{0,1},{1,0},{2,3},{3,2},{4,5},{5,4},{6,7},{7,6},{8,9},{9,8},{10,11... | collective-permute-start | bytes 737288 | tf_op jit(solution)/shard_map/ppermute | solution.py:346
  355.4 24.3 %collective-permute-start.8 = (bf16[960,256]{1,0:T(8,128)(2,1)}, bf16[960,256]{1,0:T(8,128)(2,1)S(1)}, u32[]{:S(2)}, u32[]{:S(2)}) collective-permute-start(bf16[960,256]{1,0:T(8,128)(2,1)} %shard_map.108), channel_id=1, source_target_pairs={{0,4},{4,0},{1,5},{5,1},{2,6},{6,2},{3,7},{7,3},{8,12},{12,8},{9,1... | collective-permute-start | bytes 1474568 | tf_op jit(solution)/shard_map/ppermute | solution.py:346
  360.1 21.6 %collective-permute-start.23 = (bf16[960,256]{1,0:T(8,128)(2,1)S(1)}, bf16[960,256]{1,0:T(8,128)(2,1)S(1)}, u32[]{:S(2)}, u32[]{:S(2)}) collective-permute-start(bf16[960,256]{1,0:T(8,128)(2,1)S(1)} %add_convert_fusion.3.refs_0_), channel_id=1, source_target_pairs={{0,1},{1,0},{2,3},{3,2},{4,5},{5,4},{6,7},{7,6},{8,9},{9,8},{10,11... | collective-permute-start | bytes 1474568 | tf_op jit(solution)/shard_map/ppermute | solution.py:346
  361.0 23.4 %collective-permute-start.24 = (bf16[960,256]{1,0:T(8,128)(2,1)S(1)}, bf16[960,256]{1,0:T(8,128)(2,1)S(1)}, u32[]{:S(2)}, u32[]{:S(2)}) collective-permute-start(bf16[960,256]{1,0:T(8,128)(2,1)S(1)} %add_convert_fusion.3.refs_0_), channel_id=1, source_target_pairs={{0,2},{2,0},{1,3},{3,1},{4,6},{6,4},{5,7},{7,5},{8,10},{10,8},{9,1... | collective-permute-start | bytes 1474568 | tf_op jit(solution)/shard_map/ppermute | solution.py:346
  379.8 26.9 %collective-permute-start.9 = (bf16[960,256]{1,0:T(8,128)(2,1)S(1)}, bf16[960,256]{1,0:T(8,128)(2,1)S(1)}, u32[]{:S(2)}, u32[]{:S(2)}) collective-permute-start(bf16[960,256]{1,0:T(8,128)(2,1)S(1)} %add_convert_fusion.2.refs_0_), channel_id=1, source_target_pairs={{0,1},{1,0},{2,3},{3,2},{4,5},{5,4},{6,7},{7,6},{8,9},{9,8},{10,11... | collective-permute-start | bytes 1474568 | tf_op jit(solution)/shard_map/ppermute | solution.py:346
  380.7 26.1 %collective-permute-start.10 = (bf16[960,256]{1,0:T(8,128)(2,1)S(1)}, bf16[960,256]{1,0:T(8,128)(2,1)S(1)}, u32[]{:S(2)}, u32[]{:S(2)}) collective-permute-start(bf16[960,256]{1,0:T(8,128)(2,1)S(1)} %add_convert_fusion.2.refs_0_), channel_id=1, source_target_pairs={{0,2},{2,0},{1,3},{3,1},{4,6},{6,4},{5,7},{7,5},{8,10},{10,8},{9,1... | collective-permute-start | bytes 1474568 | tf_op jit(solution)/shard_map/ppermute | solution.py:346
  381.7 17.2 %collective-permute-start.25 = (bf16[480,256]{1,0:T(8,128)(2,1)S(1)}, bf16[480,256]{1,0:T(8,128)(2,1)S(1)}, u32[]{:S(2)}, u32[]{:S(2)}) collective-permute-start(bf16[480,256]{1,0:T(8,128)(2,1)S(1)} %slice.64), channel_id=1, source_target_pairs={{0,2},{2,0},{1,3},{3,1},{4,6},{6,4},{5,7},{7,5},{8,10},{10,8},{9,1... | collective-permute-start | bytes 737288 | tf_op jit(solution)/shard_map/ppermute | solution.py:346
  384.4 14.5 %collective-permute-start.26 = (bf16[480,256]{1,0:T(8,128)(2,1)S(1)}, bf16[480,256]{1,0:T(8,128)(2,1)S(1)}, u32[]{:S(2)}, u32[]{:S(2)}) collective-permute-start(bf16[480,256]{1,0:T(8,128)(2,1)S(1)} %slice.65), channel_id=1, source_target_pairs={{0,1},{1,0},{2,3},{3,2},{4,5},{5,4},{6,7},{7,6},{8,9},{9,8},{10,11... | collective-permute-start | bytes 737288 | tf_op jit(solution)/shard_map/ppermute | solution.py:346
  387.2 14.1 %collective-permute-start.27 = (bf16[1024,128]{0,1:T(8,128)(2,1)S(1)}, bf16[1024,128]{0,1:T(8,128)(2,1)S(1)}, u32[]{:S(2)}, u32[]{:S(2)}) collective-permute-start(bf16[1024,128]{0,1:T(8,128)(2,1)S(1)} %fusion.18), channel_id=1, source_target_pairs={{0,16},{8,24},{16,0},{24,8},{1,17},{9,25},{17,1},{25,9},{2,18},{10... | collective-permute-start | bytes 786440 | tf_op jit(solution)/shard_map/ppermute | solution.py:373
  398.9 7.1 %collective-permute-start.29 = (bf16[128,1024]{1,0:T(8,128)(2,1)S(1)}, bf16[128,1024]{1,0:T(8,128)(2,1)S(1)}, u32[]{:S(2)}, u32[]{:S(2)}) collective-permute-start(bf16[128,1024]{1,0:T(8,128)(2,1)S(1)} %dynamic-slice_convert_fusion), channel_id=1, source_target_pairs={{0,16},{8,24},{16,0},{24,8},{1,17},{9,25},{17,1},{25,9},{2,18},{10... | collective-permute-start | bytes 786440 | tf_op jit(solution)/shard_map/ppermute | solution.py:373
  401.3 6.3 %collective-permute-start.28 = (bf16[512,128]{0,1:T(8,128)(2,1)S(1)}, bf16[512,128]{0,1:T(8,128)(2,1)S(1)}, u32[]{:S(2)}, u32[]{:S(2)}) collective-permute-start(bf16[512,128]{0,1:T(8,128)(2,1)S(1)} %dynamic-slice_convert_fusion.3), channel_id=1, source_target_pairs={{0,8},{8,0},{16,24},{24,16},{1,9},{9,1},{17,25},{25,17},{2,10},{10... | collective-permute-start | bytes 393224 | tf_op jit(solution)/shard_map/ppermute | solution.py:373
  406.8 8.5 %collective-permute-start.11 = (bf16[480,256]{1,0:T(8,128)(2,1)S(1)}, bf16[480,256]{1,0:T(8,128)(2,1)}, u32[]{:S(2)}, u32[]{:S(2)}) collective-permute-start(bf16[480,256]{1,0:T(8,128)(2,1)S(1)} %slice.62), channel_id=1, source_target_pairs={{0,2},{2,0},{1,3},{3,1},{4,6},{6,4},{5,7},{7,5},{8,10},{10,8},{9,1... | collective-permute-start | bytes 737288 | tf_op jit(solution)/shard_map/ppermute | solution.py:346
  407.6 8.7 %collective-permute-start.12 = (bf16[480,256]{1,0:T(8,128)(2,1)}, bf16[480,256]{1,0:T(8,128)(2,1)}, u32[]{:S(2)}, u32[]{:S(2)}) collective-permute-start(bf16[480,256]{1,0:T(8,128)(2,1)} %slice.63), channel_id=1, source_target_pairs={{0,1},{1,0},{2,3},{3,2},{4,5},{5,4},{6,7},{7,6},{8,9},{9,8},{10,11... | collective-permute-start | bytes 737288 | tf_op jit(solution)/shard_map/ppermute | solution.py:346
  (36 other events, 257.6 us)

commit v8 on v7

--- a/solution.py
+++ b/solution.py
@@ -275,69 +275,56 @@
     )(outs, douts, mine, theirs)
 
 
-def project_kernel(*refs, count, last, chunk, depth, has_before):
-    step = pl.program_id(0)
+def project_kernel(*refs, count, chunk, depth, has_before):
     cols = refs[count]
-    rest, weights = refs[count + 1 : -1], refs[-1]
-    before = rest[0] if has_before else None
-    half = cols.shape[3] // 2
-
-    @pl.when(step == 0)
-    def _():
-        empty = jnp.zeros((depth, half), weights.dtype)
-        for i in range(count):
+    before = refs[count + 1] if has_before else None
+    out, weights = refs[-2], refs[-1]
+    dests, width = cols.shape[1], cols.shape[4]
+    half = width // 2
+    empty = jnp.zeros((depth, half), weights.dtype)
+    for i in range(count):
+        for dest in range(dests):
+            low = pl.ds(dest * width, half)
+            high = pl.ds(dest * width + half, half)
             for z in range(2):
-                own = cols[i, z, pl.ds(chunk * depth, depth), :]
+                own = cols[i, dest, z, pl.ds(chunk * depth, depth), :]
                 grad_rows = pl.ds(2 * z * depth, depth)
                 out_rows = pl.ds((2 * z + 1) * depth, depth)
-                weights[i, grad_rows, :half] = empty
-                weights[i, grad_rows, half:] = own[:, half:]
-                weights[i, out_rows, :half] = own[:, :half]
-                weights[i, out_rows, half:] = empty
-
-    value = jnp.dot(refs[0][...], weights[0], preferred_element_type=jnp.float32)
-    for i in range(1, count):
-        value += jnp.dot(refs[i][...], weights[i], preferred_element_type=jnp.float32)
-    if before is not None:
-        value += before[...]
-    if last:
-        rest[-2][...] = value[:, :half].astype(jnp.bfloat16)
-        rest[-1][...] = value[:, half:].astype(jnp.bfloat16)
-    else:
-        rest[-1][...] = value
-
-
-def project(pieces, cols, before, outs, last, chunk, part, parts):
+                weights[i, grad_rows, low] = empty
+                weights[i, grad_rows, high] = own[:, half:]
+                weights[i, out_rows, low] = own[:, :half]
+                weights[i, out_rows, high] = empty
+    for dest in range(dests):
+        lanes = pl.ds(dest * width, width)
+        value = jnp.dot(refs[0][...], weights[0, :, lanes], preferred_element_type=jnp.float32)
+        for i in range(1, count):
+            value += jnp.dot(
+                refs[i][...], weights[i, :, lanes], preferred_element_type=jnp.float32
+            )
+        if has_before:
+            value += before[dest]
+        out[dest] = value.astype(out.dtype)
+
+
+def project(pieces, cols, before, last, chunk):
     count = len(pieces)
     rows, depth = pieces[0].shape
-    total_rows = rows * parts
-    width = cols.shape[3]
-    steps = 2
-    tile = rows // steps
-    rowwise = lambda w: pl.BlockSpec((tile, w), lambda i: (part * steps + i, 0))
-    halves = jax.ShapeDtypeStruct((total_rows, width // 2), jnp.bfloat16)
-    shapes = [halves] * 2 if last else [jax.ShapeDtypeStruct((total_rows, width), jnp.float32)]
-    outs = list(outs or [])
-    inputs = [*pieces, cols] + ([] if before is None else [before]) + outs
+    dests, width = cols.shape[1], cols.shape[4]
+    inputs = [*pieces, cols] + ([] if before is None else [before])
     return pl.pallas_call(
         functools.partial(
-            project_kernel, count=count, last=last, chunk=chunk, depth=depth // 4,
+            project_kernel, count=count, chunk=chunk, depth=depth // 4,
             has_before=before is not None,
         ),
-        grid=(steps,),
-        in_specs=[pl.BlockSpec((tile, depth), lambda i: (i, 0))] * count
-        + [pl.BlockSpec(cols.shape, lambda i: (0, 0, 0, 0))]
-        + ([] if before is None else [rowwise(width)])
-        + [pl.BlockSpec(memory_space=pl.ANY)] * len(outs),
-        out_specs=[rowwise(width // 2)] * 2 if last else [rowwise(width)],
-        scratch_shapes=[pltpu.VMEM((count, depth, width), jnp.bfloat16)],
-        out_shape=shapes,
-        input_output_aliases={len(inputs) - len(outs) + i: i for i in range(len(outs))},
+        out_shape=jax.ShapeDtypeStruct(
+            (dests, rows, width), jnp.bfloat16 if last else jnp.float32
+        ),
+        scratch_shapes=[pltpu.VMEM((count, depth, dests * width), jnp.bfloat16)],
         compiler_params=pltpu.CompilerParams(vmem_limit_bytes=40 << 20),
         cost_estimate=pl.CostEstimate(
-            flops=2 * rows * depth * count * width,
+            flops=2 * rows * depth * count * width * dests,
             transcendentals=0,
-            bytes_accessed=2 * rows * (depth * count + 2 * width),
+            bytes_accessed=2 * rows * (depth * count + 2 * width) + 2 * cols.size,
         ),
     )(*inputs)
 
@@ -346,20 +333,35 @@
     return lax.ppermute(x, axis, [(0, 1), (1, 0)])
 
 
-def first_hop(x, small):
-    if small:
-        return [x, swap(x, "y"), swap(x, "zl")]
-    whole = lax.all_gather(x, ("zl", "y"), axis=0, tiled=False)
-    return [whole[i] for i in range(whole.shape[0])]
-
-
-def second_hop(pieces, small):
+def trade(blocks, spot, small):
+    count = blocks.shape[0]
+    if not small:
+        whole = lax.all_to_all(blocks, ("zl", "y"), split_axis=0, concat_axis=0, tiled=True)
+        return [whole[i] for i in range(count)]
+    return [
+        across(lax.dynamic_index_in_dim(blocks, spot ^ d, 0, keepdims=False), d, count)
+        for d in range(count)
+    ]
+
+
+def across(x, d, count):
+    if d == 0:
+        return x
+    return lax.ppermute(x, ("zl", "y"), [(i, i ^ d) for i in range(count)])
+
+
+def in_order(pieces, spot, small):
     if not small:
         return pieces
-    x, by_y, by_zl = pieces
-    cut = x.shape[0] // 2
-    corner = jnp.concatenate([swap(by_y[:cut], "zl"), swap(by_zl[cut:], "y")], axis=0)
-    return [x, by_y, by_zl, corner]
+    low, high = spot % 2 == 1, spot // 2 == 1
+    return [
+        jnp.where(
+            high,
+            jnp.where(low, pieces[i ^ 3], pieces[i ^ 2]),
+            jnp.where(low, pieces[i ^ 1], pieces[i]),
+        )
+        for i in range(len(pieces))
+    ]
 
 
 def scatter_sum(x, size, dim):
@@ -498,27 +500,18 @@
 
     part_count = 2 if patch_blocks % 2 == 0 else 1
     part_patches = patch_blocks // part_count
-    gathered = []
+    results = [None] * part_count
+    traded = []
     own = []
-    cols = None
     for c in range(local_heads):
         final = c + 1 == local_heads
         if final:
             if c:
                 blocks, _ = lax.optimization_barrier((blocks, mine))
             if small:
-                cols = [lax.dynamic_index_in_dim(blocks, spot, 0, keepdims=False)] + [
-                    lax.ppermute(
-                        lax.dynamic_index_in_dim(blocks, spot ^ d, 0, keepdims=False),
-                        ("zl", "y"),
-                        [(i, i ^ d) for i in range(inner)],
-                    )
-                    for d in range(1, inner)
-                ]
-                cols = jnp.stack(cols)
+                cols = jnp.stack([across(blocks, d, inner) for d in range(inner)])
             else:
-                cols = lax.all_to_all(blocks, ("zl", "y"), split_axis=0, concat_axis=0, tiled=True)
-            bias, cols = lax.optimization_barrier((bias, cols))
+                cols = lax.all_gather(blocks, ("zl", "y"), axis=0, tiled=False)
         outs, douts, mine = attention(
             tables, bias, queries, backs, received[c], c, slots, head_scale
         )
@@ -527,9 +520,6 @@
             merge(outs, douts, mine, theirs, start, part_patches, head_scale, head_size)
             for start in range(0, patch_blocks, part_patches)
         ]
-        if gathered:
-            gathered[-1], _ = lax.optimization_barrier((gathered[-1], parts))
-            gathered[-1] = [second_hop(x, small) for x in gathered[-1]]
         if not final:
             parts, bias = lax.optimization_barrier((parts, bias))
         merged = []
@@ -538,32 +528,31 @@
                 part, _ = lax.optimization_barrier((part, merged[-1]))
             other = swap(part, "zh").astype(jnp.float32)
             merged.append((part.astype(jnp.float32) + other).astype(jnp.bfloat16))
-        gathered.append([first_hop(x, small) for x in merged])
-        if final:
-            results = None
-            for i, earlier in enumerate(gathered[:-1]):
-                before = results
-                results = None
-                for j, pieces in enumerate(earlier):
-                    results = project(
-                        pieces, cols, before[0] if before else None, results, False, i, j,
-                        part_count,
-                    )
-            if results is not None:
-                merged, _ = lax.optimization_barrier((merged, results))
-        own.append(
-            jnp.concatenate(
-                [lax.dynamic_slice_in_dim(x, zh * LANES, LANES, 1) for x in merged], axis=0
-            )
-        )
-    before = results[0] if results else None
-    final_outs = None
-    for j, pieces in enumerate(gathered[-1]):
-        final_outs = project(
-            second_hop(pieces, small), cols, before, final_outs, True, local_heads - 1, j,
-            part_count,
-        )
-    attended, patch_grad = final_outs
+        by_rows = [
+            trade(x.reshape(inner, x.shape[0] // inner, x.shape[1]), spot, small) for x in merged
+        ]
+        if not final:
+            traded.append(by_rows)
+            own.append(merged)
+            continue
+        for i, earlier in enumerate(traded):
+            results = [
+                project(pieces, cols, before, False, i)
+                for pieces, before in zip(earlier, results)
+            ]
+        behind = merged
+        if traded:
+            behind, _ = lax.optimization_barrier((merged, results))
+        own.append(behind)
+        outputs = []
+        for pieces, before in zip(by_rows, results):
+            outputs += in_order(trade(project(pieces, cols, before, True, c), spot, small), spot, small)
+    attended = jnp.concatenate([x[:, :columns] for x in outputs], axis=0)
+    patch_grad = jnp.concatenate([x[:, columns:] for x in outputs], axis=0)
+    own = [
+        jnp.concatenate([lax.dynamic_slice_in_dim(x, zh * LANES, LANES, 1) for x in xs], axis=0)
+        for xs in own
+    ]
 
     dquery = jnp.concatenate([x[:, :head_size] for x in own], axis=1)
     heads_out = jnp.concatenate([x[:, head_size:] for x in own], axis=1)

time: 423 us -> 420 us (level)
  Pallas kernels: 96.4 us -> 82.8 us
  starting transfers between devices: 56 us -> 67.8 us
  waiting for transfers between devices: 200 us -> 208 us
  local copies, waits for them, and re-layouts: 33.7 us -> 27.2 us
    ppermute x24 -> x8, waiting for transfers between devices: 190 us -> 155 us  [swap(): return lax.ppermute(x, axis, [(0, 1), (1, 0)])]
    ppermute x3 -> x21, starting transfers between devices: 3.55 us -> 29.3 us  [across(): return lax.ppermute(x, ('zl', 'y'), [(i, i ^ d) for i in range(count)])]
    ppermute x3 -> x21, waiting for transfers between devices: 0.01 us -> 22.6 us  [across(): return lax.ppermute(x, ('zl', 'y'), [(i, i ^ d) for i in range(count)])]
    all_to_all x2, waiting for transfers between devices: 5.95 us -> 28.1 us  [exchange(): lax.all_to_all(x, ('dp', 'zl', 'y'), split_axis=0, concat_axis=0, tiled=T...]
    ppermute x24 -> x8, starting transfers between devices: 34.1 us -> 16.4 us  [swap(): return lax.ppermute(x, axis, [(0, 1), (1, 0)])]
    pallas_call x2, Pallas kernels: 65.4 us -> 58.5 us  [attention(): pl.pallas_call(functools.partial(attention_kernel, slots=slots, scale=sca...]
    unnamed x74 -> x65, local copies, waits for them, and re-layouts: 19.6 us -> 18.6 us
  transfers between devices with their start and end apart: 33 -> 35, of which waited for: 13 -> 18; matrix products, arithmetic and copies ran while one was open for 11% -> 9% of each run, Pallas kernels for 21% -> 19%
where the time goes in v8:
time: 420 us; the launch traced here: 419 us
  waiting for transfers between devices  208 us (50%)
  Pallas kernels  82.8 us (20%)
  starting transfers between devices  67.8 us (16%)
  local copies, waits for them, and re-layouts  27.2 us (6%)
  matrix products  17.2 us (4%)
  other arithmetic  14.6 us (3%)
    ppermute x8, waiting for transfers between devices, swap(): return lax.ppermute(x, axis, [(0, 1), (1, 0)])  155 us
    pallas_call x2, Pallas kernels, attention(): pl.pallas_call(functools.partial(attention_kernel, slots=slots, scale=sca...  58.5 us
    ppermute x21, starting transfers between devices, across(): return lax.ppermute(x, ('zl', 'y'), [(i, i ^ d) for i in range(count)])  29.3 us
    all_to_all x2, waiting for transfers between devices, exchange(): lax.all_to_all(x, ('dp', 'zl', 'y'), split_axis=0, concat_axis=0, tiled=T...  28.1 us
    ppermute x21, waiting for transfers between devices, across(): return lax.ppermute(x, ('zl', 'y'), [(i, i ^ d) for i in range(count)])  22.6 us
    all_to_all x2, starting transfers between devices, exchange(): lax.all_to_all(x, ('dp', 'zl', 'y'), split_axis=0, concat_axis=0, tiled=T...  19.8 us
    unnamed x65, local copies, waits for them, and re-layouts  18.6 us
    ppermute x8, starting transfers between devices, swap(): return lax.ppermute(x, axis, [(0, 1), (1, 0)])  16.4 us
  transfers between devices with their start and end apart: 35, of which 18 were waited for; matrix products, arithmetic and copies ran while one was open for 9% of the time, Pallas kernels for 19%

profile of v8, /device:TPU:0, one launch (start us, length us, event | category | flops | bytes accessed | tf_op | source)
XLA Modules:
  0.0 419.0 jit_solution(8404765702983592802)
XLA Ops:
  2.9 3.4 copy-done
  6.9 3.8 shard_map.102
  10.8 3.3 copy-done.3
  14.1 7.1 %all-to-all-start = ((bf16[16,2048,128]{2,1,0:T(8,128)(2,1)}), bf16[16,2048,128]{2,1,0:T(8,128)(2,1)}, u32[]{:S(2)}, u32[]{:S(2)}) async-start(bf16[16,2048,128]{2,1,0:T(8,128)(2,1)} %bitcast.109), calls=%async_computation | async-start | bytes 16777216 | tf_op jit(solution)/shard_map/all_to_all | solution.py:425
  21.4 3.3 collective-permute-start
  25.1 3.4 copy-done.1
  28.4 4.3 %shard_map.103 = bf16[4,4,8,2,128,128]{5,4,3,2,1,0:T(8,128)(2,1)S(1)} custom-call(s32[32]{0:T(128)S(1)} %reshape.458.chosen, s32[4]{0:T(128)S(1)} %reduce_sum.99.counts, s32[16]{0:T(128)S(1)} %copy-done.5, bf16[16,128,16,128]{3,2,1,0:T(8,128)(2,1)S(1)} %copy-done.1), custom_call_target="tpu_custom_call" | custom-call | bytes 16777216 | tf_op jit(solution)/shard_map/pallas_call | solution.py:49
  32.7 3.3 copy-done.2
  36.0 88.6 %collective-permute-done = bf16[2048,128]{0,1:T(8,128)(2,1)S(1)} collective-permute-done((bf16[2048,128]{0,1:T(8,128)(2,1)S(1)}, bf16[2048,128]{0,1:T(8,128)(2,1)S(1)}, u32[]{:S(2)}, u32[]{:S(2)}) %collective-permute-start) | collective-permute-done | bytes 524320 | tf_op jit(solution)/shard_map/ppermute | solution.py:333
  124.6 11.0 %collective-permute-done.1 = bf16[128,2048]{0,1:T(8,128)(2,1)S(1)} collective-permute-done((bf16[128,2048]{0,1:T(8,128)(2,1)S(1)}, bf16[128,2048]{0,1:T(8,128)(2,1)S(1)}, u32[]{:S(2)}, u32[]{:S(2)}) %collective-permute-start.1) | collective-permute-done | bytes 524320 | tf_op jit(solution)/shard_map/ppermute | solution.py:333
  136.4 5.2 %all-to-all-done = bf16[16,2048,128]{2,1,0:T(8,128)(2,1)} async-done(((bf16[16,2048,128]{2,1,0:T(8,128)(2,1)}), bf16[16,2048,128]{2,1,0:T(8,128)(2,1)}, u32[]{:S(2)}, u32[]{:S(2)}) %all-to-all-start) | async-done | bytes 8388640 | tf_op jit(solution)/shard_map/all_to_all | solution.py:425
  141.6 12.7 %all-to-all-start.1 = ((bf16[16,2048,128]{2,1,0:T(8,128)(2,1)}), bf16[16,2048,128]{2,1,0:T(8,128)(2,1)}, u32[]{:S(2)}, u32[]{:S(2)}) async-start(bf16[16,2048,128]{2,1,0:T(8,128)(2,1)} %bitcast.108), calls=%async_computation.1 | async-start | bytes 16777216 | tf_op jit(solution)/shard_map/all_to_all | solution.py:425
  168.5 9.0 %fusion.3.q_ref = bf16[1920,512]{1,0:T(8,128)(2,1)} fusion(bf16[2048,512]{0,1:T(8,128)(2,1)S(1)} %bitcast.126, bf16[1920,2048]{1,0:T(8,128)(2,1)} %param.7), kind=kOutput, calls=%fused_computation.7 | convolution fusion | flops 4028497920 | bytes 11927552 | tf_op jit(solution)/shard_map/dot_general | solution.py:489
  177.4 5.5 %fusion.2.b_ref = bf16[1920,512]{1,0:T(8,128)(2,1)} fusion(bf16[512,2048]{1,0:T(8,128)(2,1)S(1)} %bitcast.125, bf16[1920,2048]{1,0:T(8,128)(2,1)S(1)} %bitcast.113), kind=kOutput, calls=%fused_computation.6 | convolution fusion | flops 4027514880 | bytes 11927552 | tf_op jit(solution)/shard_map/dot_general | solution.py:78
  182.9 29.3 %shard_map.104 = (f32[1920,256]{1,0:T(8,128)}, f32[1920,256]{1,0:T(8,128)}, f32[4,8,512]{2,1,0:T(8,128)}) custom-call(s32[128]{0:T(128)} %copy-done.20, s32[4]{0:T(128)} %copy-done.19, s32[128]{0:T(128)} %reshape.462.offsets, s32[128]{0:T(128)} %and_select_fusion.sizes, bf16[1920,512]{1,0:T(8,128)(2,1)} %fusion.3.q_ref, bf16[1920,512]{1,0:T(8,128)(2,1)} %fusion.2.b_ref, ...), custom_call_target="tpu_custom_call" | custom-call | flops 8053063680 | bytes 41943040 | tf_op jit(solution)/shard_map/pallas_call | solution.py:203
  212.2 6.5 %collective-permute-start.2 = (f32[4,8,512]{2,1,0:T(8,128)}, f32[4,8,512]{2,1,0:T(8,128)S(1)}, u32[]{:S(2)}, u32[]{:S(2)}) collective-permute-start(f32[4,8,512]{2,1,0:T(8,128)} %get-tuple-element.30.mine_ref), channel_id=1, source_target_pairs={{0,4},{4,0},{1,5},{5,1},{2,6},{6,2},{3,7},{7,3},{8,12},{12,8},{9,1... | collective-permute-start | bytes 196616 | tf_op jit(solution)/shard_map/ppermute | solution.py:333
  223.4 24.7 %collective-permute-done.2.theirs_ref = f32[4,8,512]{2,1,0:T(8,128)S(1)} collective-permute-done((f32[4,8,512]{2,1,0:T(8,128)}, f32[4,8,512]{2,1,0:T(8,128)S(1)}, u32[]{:S(2)}, u32[]{:S(2)}) %collective-permute-start.2) | collective-permute-done | bytes 65568 | tf_op jit(solution)/shard_map/ppermute | solution.py:333
  251.6 2.9 shard_map.106
  254.5 3.3 collective-permute-start.22
  257.9 22.9 %all-to-all-done.1 = bf16[16,2048,128]{2,1,0:T(8,128)(2,1)} async-done(((bf16[16,2048,128]{2,1,0:T(8,128)(2,1)}), bf16[16,2048,128]{2,1,0:T(8,128)(2,1)}, u32[]{:S(2)}, u32[]{:S(2)}) %all-to-all-start.1) | async-done | bytes 8388640 | tf_op jit(solution)/shard_map/all_to_all | solution.py:425
  280.8 29.2 %shard_map.107 = (f32[1920,256]{1,0:T(8,128)}, f32[1920,256]{1,0:T(8,128)}, f32[4,8,512]{2,1,0:T(8,128)}) custom-call(s32[128]{0:T(128)} %copy-done.20, s32[4]{0:T(128)} %copy-done.19, s32[128]{0:T(128)} %reshape.462.offsets, s32[128]{0:T(128)} %and_select_fusion.sizes, bf16[1920,512]{1,0:T(8,128)(2,1)} %fusion.3.q_ref, bf16[1920,512]{1,0:T(8,128)(2,1)} %fusion.2.b_ref, ...), custom_call_target="tpu_custom_call" | custom-call | flops 8053063680 | bytes 41943040 | tf_op jit(solution)/shard_map/pallas_call | solution.py:203
  312.7 3.3 collective-permute-start.3
  316.9 6.3 %collective-permute-done.11 = bf16[960,256]{1,0:T(8,128)(2,1)S(1)} collective-permute-done((bf16[960,256]{1,0:T(8,128)(2,1)S(1)}, bf16[960,256]{1,0:T(8,128)(2,1)S(1)}, u32[]{:S(2)}, u32[]{:S(2)}) %collective-permute-start.11) | collective-permute-done | bytes 491552 | tf_op jit(solution)/shard_map/ppermute | solution.py:333
  325.3 6.0 %collective-permute-done.3.theirs_ref = f32[4,8,512]{2,1,0:T(8,128)S(1)} collective-permute-done((f32[4,8,512]{2,1,0:T(8,128)}, f32[4,8,512]{2,1,0:T(8,128)S(1)}, u32[]{:S(2)}, u32[]{:S(2)}) %collective-permute-start.3) | collective-permute-done | bytes 65568 | tf_op jit(solution)/shard_map/ppermute | solution.py:333
  331.9 2.8 shard_map.108
  335.5 2.8 shard_map.111
  338.4 2.9 collective-permute-start.25
  344.3 13.5 %collective-permute-done.4 = bf16[960,256]{1,0:T(8,128)(2,1)S(1)} collective-permute-done((bf16[960,256]{1,0:T(8,128)(2,1)}, bf16[960,256]{1,0:T(8,128)(2,1)S(1)}, u32[]{:S(2)}, u32[]{:S(2)}) %collective-permute-start.4) | collective-permute-done | bytes 491552 | tf_op jit(solution)/shard_map/ppermute | solution.py:333
  358.0 3.0 collective-permute-start.14
  370.6 7.3 %collective-permute-done.6.refs_2_ = bf16[240,256]{1,0:T(8,128)(2,1)S(1)} collective-permute-done((bf16[240,256]{1,0:T(8,128)(2,1)S(1)}, bf16[240,256]{1,0:T(8,128)(2,1)S(1)}, u32[]{:S(2)}, u32[]{:S(2)}) %collective-permute-start.6) | collective-permute-done | bytes 122912 | tf_op jit(solution)/shard_map/ppermute | solution.py:350
  392.8 6.3 %collective-permute-start.15 = (bf16[240,512]{1,0:T(8,128)(2,1)S(1)}, bf16[240,512]{1,0:T(8,128)(2,1)S(1)}, u32[]{:S(2)}, u32[]{:S(2)}) collective-permute-start(bf16[240,512]{1,0:T(8,128)(2,1)S(1)} %get-tuple-element.74), channel_id=1, source_target_pairs={{0,3},{1,2},{2,1},{3,0},{4,7},{5,6},{6,5},{7,4},{8,11},{9,10},{10,... | collective-permute-start | bytes 737288 | tf_op jit(solution)/shard_map/ppermute | solution.py:350
  408.9 4.4 %collective-permute-done.27 = bf16[240,512]{1,0:T(8,128)(2,1)S(1)} collective-permute-done((bf16[240,512]{1,0:T(8,128)(2,1)S(1)}, bf16[240,512]{1,0:T(8,128)(2,1)S(1)}, u32[]{:S(2)}, u32[]{:S(2)}) %collective-permute-start.27) | collective-permute-done | bytes 245792 | tf_op jit(solution)/shard_map/ppermute | solution.py:350
  (199 shorter events, 76.4 us)
Async XLA Ops:
  14.1 127.5 %all-to-all-start = ((bf16[16,2048,128]{2,1,0:T(8,128)(2,1)}), bf16[16,2048,128]{2,1,0:T(8,128)(2,1)}, u32[]{:S(2)}, u32[]{:S(2)}) async-start(bf16[16,2048,128]{2,1,0:T(8,128)(2,1)} %bitcast.109), calls=%async_computation | async-start | bytes 16777216 | tf_op jit(solution)/shard_map/all_to_all | solution.py:425
  21.4 103.2 %collective-permute-start = (bf16[2048,128]{0,1:T(8,128)(2,1)S(1)}, bf16[2048,128]{0,1:T(8,128)(2,1)S(1)}, u32[]{:S(2)}, u32[]{:S(2)}) collective-permute-start(bf16[2048,128]{0,1:T(8,128)(2,1)S(1)} %copy.34), channel_id=1, source_target_pairs={{0,4},{4,0},{1,5},{5,1},{2,6},{6,2},{3,7},{7,3},{8,12},{12,8},{9,1... | collective-permute-start | bytes 1572872 | tf_op jit(solution)/shard_map/ppermute | solution.py:333
  24.9 110.7 %collective-permute-start.1 = (bf16[128,2048]{0,1:T(8,128)(2,1)S(1)}, bf16[128,2048]{0,1:T(8,128)(2,1)S(1)}, u32[]{:S(2)}, u32[]{:S(2)}) collective-permute-start(bf16[128,2048]{0,1:T(8,128)(2,1)S(1)} %copy.33), channel_id=1, source_target_pairs={{0,4},{4,0},{1,5},{5,1},{2,6},{6,2},{3,7},{7,3},{8,12},{12,8},{9,1... | collective-permute-start | bytes 1572872 | tf_op jit(solution)/shard_map/ppermute | solution.py:333
  141.6 139.2 %all-to-all-start.1 = ((bf16[16,2048,128]{2,1,0:T(8,128)(2,1)}), bf16[16,2048,128]{2,1,0:T(8,128)(2,1)}, u32[]{:S(2)}, u32[]{:S(2)}) async-start(bf16[16,2048,128]{2,1,0:T(8,128)(2,1)} %bitcast.108), calls=%async_computation.1 | async-start | bytes 16777216 | tf_op jit(solution)/shard_map/all_to_all | solution.py:425
  212.2 35.9 %collective-permute-start.2 = (f32[4,8,512]{2,1,0:T(8,128)}, f32[4,8,512]{2,1,0:T(8,128)S(1)}, u32[]{:S(2)}, u32[]{:S(2)}) collective-permute-start(f32[4,8,512]{2,1,0:T(8,128)} %get-tuple-element.30.mine_ref), channel_id=1, source_target_pairs={{0,4},{4,0},{1,5},{5,1},{2,6},{6,2},{3,7},{7,3},{8,12},{12,8},{9,1... | collective-permute-start | bytes 196616 | tf_op jit(solution)/shard_map/ppermute | solution.py:333
  219.9 118.5 %collective-permute-start.10 = (bf16[4,2,128,512]{3,2,1,0:T(8,128)(2,1)S(1)}, bf16[4,2,128,512]{3,2,1,0:T(8,128)(2,1)}, u32[]{:S(2)}, u32[]{:S(2)}) collective-permute-start(bf16[4,2,128,512]{3,2,1,0:T(8,128)(2,1)S(1)} %fusion.5), channel_id=1, source_target_pairs={{0,3},{1,2},{2,1},{3,0},{4,7},{5,6},{6,5},{7,4},{8,11},{9,10},{10,... | collective-permute-start | bytes 3145736 | tf_op jit(solution)/shard_map/ppermute | solution.py:350
  222.7 115.7 %collective-permute-start.9 = (bf16[4,2,128,512]{3,2,1,0:T(8,128)(2,1)S(1)}, bf16[4,2,128,512]{3,2,1,0:T(8,128)(2,1)}, u32[]{:S(2)}, u32[]{:S(2)}) collective-permute-start(bf16[4,2,128,512]{3,2,1,0:T(8,128)(2,1)S(1)} %fusion.5), channel_id=1, source_target_pairs={{0,2},{1,3},{2,0},{3,1},{4,6},{5,7},{6,4},{7,5},{8,10},{9,11},{10,... | collective-permute-start | bytes 3145736 | tf_op jit(solution)/shard_map/ppermute | solution.py:350
  223.2 118.1 %collective-permute-start.8 = (bf16[4,2,128,512]{3,2,1,0:T(8,128)(2,1)S(1)}, bf16[4,2,128,512]{3,2,1,0:T(8,128)(2,1)}, u32[]{:S(2)}, u32[]{:S(2)}) collective-permute-start(bf16[4,2,128,512]{3,2,1,0:T(8,128)(2,1)S(1)} %fusion.5), channel_id=1, source_target_pairs={{0,1},{1,0},{2,3},{3,2},{4,5},{5,4},{6,7},{7,6},{8,9},{9,8},{10,11... | collective-permute-start | bytes 3145736 | tf_op jit(solution)/shard_map/ppermute | solution.py:350
  254.5 58.1 %collective-permute-start.22 = (bf16[960,256]{1,0:T(8,128)(2,1)}, bf16[960,256]{1,0:T(8,128)(2,1)S(1)}, u32[]{:S(2)}, u32[]{:S(2)}) collective-permute-start(bf16[960,256]{1,0:T(8,128)(2,1)} %shard_map.106), channel_id=1, source_target_pairs={{0,4},{4,0},{1,5},{5,1},{2,6},{6,2},{3,7},{7,3},{8,12},{12,8},{9,1... | collective-permute-start | bytes 1474568 | tf_op jit(solution)/shard_map/ppermute | solution.py:333
  257.8 65.3 %collective-permute-start.11 = (bf16[960,256]{1,0:T(8,128)(2,1)S(1)}, bf16[960,256]{1,0:T(8,128)(2,1)S(1)}, u32[]{:S(2)}, u32[]{:S(2)}) collective-permute-start(bf16[960,256]{1,0:T(8,128)(2,1)S(1)} %copy-done.8), channel_id=1, source_target_pairs={{0,4},{4,0},{1,5},{5,1},{2,6},{6,2},{3,7},{7,3},{8,12},{12,8},{9,1... | collective-permute-start | bytes 1474568 | tf_op jit(solution)/shard_map/ppermute | solution.py:333
  312.7 18.6 %collective-permute-start.3 = (f32[4,8,512]{2,1,0:T(8,128)}, f32[4,8,512]{2,1,0:T(8,128)S(1)}, u32[]{:S(2)}, u32[]{:S(2)}) collective-permute-start(f32[4,8,512]{2,1,0:T(8,128)} %get-tuple-element.35.mine_ref), channel_id=1, source_target_pairs={{0,4},{4,0},{1,5},{5,1},{2,6},{6,2},{3,7},{7,3},{8,12},{12,8},{9,1... | collective-permute-start | bytes 196616 | tf_op jit(solution)/shard_map/ppermute | solution.py:333
  323.1 34.8 %collective-permute-start.23 = (bf16[240,256]{1,0:T(8,128)(2,1)}, bf16[240,256]{1,0:T(8,128)(2,1)S(1)}, u32[]{:S(2)}, u32[]{:S(2)}) collective-permute-start(bf16[240,256]{1,0:T(8,128)(2,1)} %get-tuple-element.77), channel_id=1, source_target_pairs={{0,1},{1,0},{2,3},{3,2},{4,5},{5,4},{6,7},{7,6},{8,9},{9,8},{10,11... | collective-permute-start | bytes 368648 | tf_op jit(solution)/shard_map/ppermute | solution.py:350
  334.8 23.0 %collective-permute-start.4 = (bf16[960,256]{1,0:T(8,128)(2,1)}, bf16[960,256]{1,0:T(8,128)(2,1)S(1)}, u32[]{:S(2)}, u32[]{:S(2)}) collective-permute-start(bf16[960,256]{1,0:T(8,128)(2,1)} %shard_map.108), channel_id=1, source_target_pairs={{0,4},{4,0},{1,5},{5,1},{2,6},{6,2},{3,7},{7,3},{8,12},{12,8},{9,1... | collective-permute-start | bytes 1474568 | tf_op jit(solution)/shard_map/ppermute | solution.py:333
  338.4 22.6 %collective-permute-start.24 = (bf16[240,256]{1,0:T(8,128)(2,1)}, bf16[240,256]{1,0:T(8,128)(2,1)S(1)}, u32[]{:S(2)}, u32[]{:S(2)}) collective-permute-start(bf16[240,256]{1,0:T(8,128)(2,1)} %get-tuple-element.76), channel_id=1, source_target_pairs={{0,2},{1,3},{2,0},{3,1},{4,6},{5,7},{6,4},{7,5},{8,10},{9,11},{10,... | collective-permute-start | bytes 368648 | tf_op jit(solution)/shard_map/ppermute | solution.py:350
  338.4 22.6 %collective-permute-start.25 = (bf16[240,256]{1,0:T(8,128)(2,1)}, bf16[240,256]{1,0:T(8,128)(2,1)S(1)}, u32[]{:S(2)}, u32[]{:S(2)}) collective-permute-start(bf16[240,256]{1,0:T(8,128)(2,1)} %get-tuple-element.75), channel_id=1, source_target_pairs={{0,3},{1,2},{2,1},{3,0},{4,7},{5,6},{6,5},{7,4},{8,11},{9,10},{10,... | collective-permute-start | bytes 368648 | tf_op jit(solution)/shard_map/ppermute | solution.py:350
  341.3 20.4 %collective-permute-start.12 = (bf16[240,256]{1,0:T(8,128)(2,1)}, bf16[240,256]{1,0:T(8,128)(2,1)S(1)}, u32[]{:S(2)}, u32[]{:S(2)}) collective-permute-start(bf16[240,256]{1,0:T(8,128)(2,1)} %get-tuple-element.85), channel_id=1, source_target_pairs={{0,1},{1,0},{2,3},{3,2},{4,5},{5,4},{6,7},{7,6},{8,9},{9,8},{10,11... | collective-permute-start | bytes 368648 | tf_op jit(solution)/shard_map/ppermute | solution.py:350
  358.0 11.4 %collective-permute-start.14 = (bf16[240,256]{1,0:T(8,128)(2,1)S(1)}, bf16[240,256]{1,0:T(8,128)(2,1)S(1)}, u32[]{:S(2)}, u32[]{:S(2)}) collective-permute-start(bf16[240,256]{1,0:T(8,128)(2,1)S(1)} %get-tuple-element.83), channel_id=1, source_target_pairs={{0,3},{1,2},{2,1},{3,0},{4,7},{5,6},{6,5},{7,4},{8,11},{9,10},{10,... | collective-permute-start | bytes 368648 | tf_op jit(solution)/shard_map/ppermute | solution.py:350
  361.0 23.9 %collective-permute-start.18 = (bf16[960,256]{1,0:T(8,128)(2,1)S(1)}, bf16[960,256]{1,0:T(8,128)(2,1)S(1)}, u32[]{:S(2)}, u32[]{:S(2)}) collective-permute-start(bf16[960,256]{1,0:T(8,128)(2,1)S(1)} %copy-done.7), channel_id=1, source_target_pairs={{0,4},{4,0},{1,5},{5,1},{2,6},{6,2},{3,7},{7,3},{8,12},{12,8},{9,1... | collective-permute-start | bytes 1474568 | tf_op jit(solution)/shard_map/ppermute | solution.py:333
  361.0 9.6 %collective-permute-start.5 = (bf16[240,256]{1,0:T(8,128)(2,1)S(1)}, bf16[240,256]{1,0:T(8,128)(2,1)S(1)}, u32[]{:S(2)}, u32[]{:S(2)}) collective-permute-start(bf16[240,256]{1,0:T(8,128)(2,1)S(1)} %get-tuple-element.89), channel_id=1, source_target_pairs={{0,1},{1,0},{2,3},{3,2},{4,5},{5,4},{6,7},{7,6},{8,9},{9,8},{10,11... | collective-permute-start | bytes 368648 | tf_op jit(solution)/shard_map/ppermute | solution.py:350
  361.7 16.2 %collective-permute-start.6 = (bf16[240,256]{1,0:T(8,128)(2,1)S(1)}, bf16[240,256]{1,0:T(8,128)(2,1)S(1)}, u32[]{:S(2)}, u32[]{:S(2)}) collective-permute-start(bf16[240,256]{1,0:T(8,128)(2,1)S(1)} %get-tuple-element.88), channel_id=1, source_target_pairs={{0,2},{1,3},{2,0},{3,1},{4,6},{5,7},{6,4},{7,5},{8,10},{9,11},{10,... | collective-permute-start | bytes 368648 | tf_op jit(solution)/shard_map/ppermute | solution.py:350
  364.1 15.3 %collective-permute-start.7 = (bf16[240,256]{1,0:T(8,128)(2,1)S(1)}, bf16[240,256]{1,0:T(8,128)(2,1)S(1)}, u32[]{:S(2)}, u32[]{:S(2)}) collective-permute-start(bf16[240,256]{1,0:T(8,128)(2,1)S(1)} %get-tuple-element.87), channel_id=1, source_target_pairs={{0,3},{1,2},{2,1},{3,0},{4,7},{5,6},{6,5},{7,4},{8,11},{9,10},{10,... | collective-permute-start | bytes 368648 | tf_op jit(solution)/shard_map/ppermute | solution.py:350
  380.7 22.9 %collective-permute-start.17 = (bf16[240,512]{1,0:T(8,128)(2,1)S(1)}, bf16[240,512]{1,0:T(8,128)(2,1)S(1)}, u32[]{:S(2)}, u32[]{:S(2)}) collective-permute-start(bf16[240,512]{1,0:T(8,128)(2,1)S(1)} %get-tuple-element.72), channel_id=1, source_target_pairs={{0,1},{1,0},{2,3},{3,2},{4,5},{5,4},{6,7},{7,6},{8,9},{9,8},{10,11... | collective-permute-start | bytes 737288 | tf_op jit(solution)/shard_map/ppermute | solution.py:350
  387.3 11.8 %collective-permute-start.20 = (bf16[240,256]{1,0:T(8,128)(2,1)S(1)}, bf16[240,256]{1,0:T(8,128)(2,1)S(1)}, u32[]{:S(2)}, u32[]{:S(2)}) collective-permute-start(bf16[240,256]{1,0:T(8,128)(2,1)S(1)} %get-tuple-element.80), channel_id=1, source_target_pairs={{0,2},{1,3},{2,0},{3,1},{4,6},{5,7},{6,4},{7,5},{8,10},{9,11},{10,... | collective-permute-start | bytes 368648 | tf_op jit(solution)/shard_map/ppermute | solution.py:350
  387.9 11.2 %collective-permute-start.21 = (bf16[240,256]{1,0:T(8,128)(2,1)S(1)}, bf16[240,256]{1,0:T(8,128)(2,1)S(1)}, u32[]{:S(2)}, u32[]{:S(2)}) collective-permute-start(bf16[240,256]{1,0:T(8,128)(2,1)S(1)} %get-tuple-element.79), channel_id=1, source_target_pairs={{0,3},{1,2},{2,1},{3,0},{4,7},{5,6},{6,5},{7,4},{8,11},{9,10},{10,... | collective-permute-start | bytes 368648 | tf_op jit(solution)/shard_map/ppermute | solution.py:350
  391.6 9.8 %collective-permute-start.29 = (bf16[1024,128]{0,1:T(8,128)(2,1)S(1)}, bf16[1024,128]{0,1:T(8,128)(2,1)S(1)}, u32[]{:S(2)}, u32[]{:S(2)}) collective-permute-start(bf16[1024,128]{0,1:T(8,128)(2,1)S(1)} %fusion.18), channel_id=1, source_target_pairs={{0,16},{8,24},{16,0},{24,8},{1,17},{9,25},{17,1},{25,9},{2,18},{10... | collective-permute-start | bytes 786440 | tf_op jit(solution)/shard_map/ppermute | solution.py:375
  392.8 13.4 %collective-permute-start.15 = (bf16[240,512]{1,0:T(8,128)(2,1)S(1)}, bf16[240,512]{1,0:T(8,128)(2,1)S(1)}, u32[]{:S(2)}, u32[]{:S(2)}) collective-permute-start(bf16[240,512]{1,0:T(8,128)(2,1)S(1)} %get-tuple-element.74), channel_id=1, source_target_pairs={{0,3},{1,2},{2,1},{3,0},{4,7},{5,6},{6,5},{7,4},{8,11},{9,10},{10,... | collective-permute-start | bytes 737288 | tf_op jit(solution)/shard_map/ppermute | solution.py:350
  399.1 9.8 %collective-permute-start.16 = (bf16[240,512]{1,0:T(8,128)(2,1)S(1)}, bf16[240,512]{1,0:T(8,128)(2,1)S(1)}, u32[]{:S(2)}, u32[]{:S(2)}) collective-permute-start(bf16[240,512]{1,0:T(8,128)(2,1)S(1)} %get-tuple-element.73), channel_id=1, source_target_pairs={{0,2},{1,3},{2,0},{3,1},{4,6},{5,7},{6,4},{7,5},{8,10},{9,11},{10,... | collective-permute-start | bytes 737288 | tf_op jit(solution)/shard_map/ppermute | solution.py:350
  401.4 11.8 %collective-permute-start.27 = (bf16[240,512]{1,0:T(8,128)(2,1)S(1)}, bf16[240,512]{1,0:T(8,128)(2,1)S(1)}, u32[]{:S(2)}, u32[]{:S(2)}) collective-permute-start(bf16[240,512]{1,0:T(8,128)(2,1)S(1)} %get-tuple-element.70), channel_id=1, source_target_pairs={{0,2},{1,3},{2,0},{3,1},{4,6},{5,7},{6,4},{7,5},{8,10},{9,11},{10,... | collective-permute-start | bytes 737288 | tf_op jit(solution)/shard_map/ppermute | solution.py:350
  403.5 12.5 %collective-permute-start.26 = (bf16[240,512]{1,0:T(8,128)(2,1)S(1)}, bf16[240,512]{1,0:T(8,128)(2,1)S(1)}, u32[]{:S(2)}, u32[]{:S(2)}) collective-permute-start(bf16[240,512]{1,0:T(8,128)(2,1)S(1)} %get-tuple-element.71), channel_id=1, source_target_pairs={{0,3},{1,2},{2,1},{3,0},{4,7},{5,6},{6,5},{7,4},{8,11},{9,10},{10,... | collective-permute-start | bytes 737288 | tf_op jit(solution)/shard_map/ppermute | solution.py:350
  405.5 10.5 %collective-permute-start.28 = (bf16[240,512]{1,0:T(8,128)(2,1)S(1)}, bf16[240,512]{1,0:T(8,128)(2,1)S(1)}, u32[]{:S(2)}, u32[]{:S(2)}) collective-permute-start(bf16[240,512]{1,0:T(8,128)(2,1)S(1)} %get-tuple-element.69), channel_id=1, source_target_pairs={{0,1},{1,0},{2,3},{3,2},{4,5},{5,4},{6,7},{7,6},{8,9},{9,8},{10,11... | collective-permute-start | bytes 737288 | tf_op jit(solution)/shard_map/ppermute | solution.py:350
  406.2 10.3 %collective-permute-start.30 = (bf16[512,128]{0,1:T(8,128)(2,1)S(1)}, bf16[512,128]{0,1:T(8,128)(2,1)S(1)}, u32[]{:S(2)}, u32[]{:S(2)}) collective-permute-start(bf16[512,128]{0,1:T(8,128)(2,1)S(1)} %dynamic-slice_convert_fusion.3), channel_id=1, source_target_pairs={{0,8},{8,0},{16,24},{24,16},{1,9},{9,1},{17,25},{25,17},{2,10},{10... | collective-permute-start | bytes 393224 | tf_op jit(solution)/shard_map/ppermute | solution.py:375
  408.9 9.4 %collective-permute-start.32 = (bf16[128,512]{1,0:T(8,128)(2,1)S(1)}, bf16[128,512]{1,0:T(8,128)(2,1)S(1)}, u32[]{:S(2)}, u32[]{:S(2)}) collective-permute-start(bf16[128,512]{1,0:T(8,128)(2,1)S(1)} %dynamic-slice_convert_fusion.2), channel_id=1, source_target_pairs={{0,8},{8,0},{16,24},{24,16},{1,9},{9,1},{17,25},{25,17},{2,10},{10... | collective-permute-start | bytes 393224 | tf_op jit(solution)/shard_map/ppermute | solution.py:375
  (30 other events, 263.1 us)

commit v9 on v8

--- a/solution.py
+++ b/solution.py
@@ -506,8 +506,7 @@
     for c in range(local_heads):
         final = c + 1 == local_heads
         if final:
-            if c:
-                blocks, _ = lax.optimization_barrier((blocks, mine))
+            blocks, _ = lax.optimization_barrier((blocks, received[c]))
             if small:
                 cols = jnp.stack([across(blocks, d, inner) for d in range(inner)])
             else:

time: 420 us -> 426 us (1.014)
  Pallas kernels: 82.8 us -> 94.7 us
  starting transfers between devices: 67.8 us -> 58.8 us
    ppermute x8, waiting for transfers between devices: 155 us -> 178 us  [swap(): return lax.ppermute(x, axis, [(0, 1), (1, 0)])]
    all_to_all x2, waiting for transfers between devices: 28.1 us -> 10.2 us  [exchange(): lax.all_to_all(x, ('dp', 'zl', 'y'), split_axis=0, concat_axis=0, tiled=T...]
    pallas_call x2, Pallas kernels: 58.5 us -> 72 us  [attention(): pl.pallas_call(functools.partial(attention_kernel, slots=slots, scale=sca...]
    ppermute x8, starting transfers between devices: 16.4 us -> 10 us  [swap(): return lax.ppermute(x, axis, [(0, 1), (1, 0)])]
    unnamed x65 -> x63, local copies, waits for them, and re-layouts: 18.6 us -> 17.1 us
  transfers between devices with their start and end apart: 35 -> 35, of which waited for: 18 -> 17; matrix products, arithmetic and copies ran while one was open for 9% -> 10% of each run, Pallas kernels for 19% -> 22%
where the time goes in v9:
time: 426 us; the launch traced here: 424 us
  waiting for transfers between devices  207 us (49%)
  Pallas kernels  94.7 us (22%)
  starting transfers between devices  58.8 us (14%)
  local copies, waits for them, and re-layouts  25.8 us (6%)
  matrix products  20.5 us (5%)
  other arithmetic  15.7 us (4%)
    ppermute x8, waiting for transfers between devices, swap(): return lax.ppermute(x, axis, [(0, 1), (1, 0)])  178 us
    pallas_call x2, Pallas kernels, attention(): pl.pallas_call(functools.partial(attention_kernel, slots=slots, scale=sca...  72 us
    ppermute x21, starting transfers between devices, across(): return lax.ppermute(x, ('zl', 'y'), [(i, i ^ d) for i in range(count)])  28.1 us
    ppermute x21, waiting for transfers between devices, across(): return lax.ppermute(x, ('zl', 'y'), [(i, i ^ d) for i in range(count)])  18.8 us
    all_to_all x2, starting transfers between devices, exchange(): lax.all_to_all(x, ('dp', 'zl', 'y'), split_axis=0, concat_axis=0, tiled=T...  18.5 us
    unnamed x63, local copies, waits for them, and re-layouts  17.1 us
    pallas_call x4, Pallas kernels, merge(): pl.pallas_call(functools.partial(merge_kernel, scale=scale, split=split),...  11.4 us
    all_to_all x2, waiting for transfers between devices, exchange(): lax.all_to_all(x, ('dp', 'zl', 'y'), split_axis=0, concat_axis=0, tiled=T...  10.2 us
  transfers between devices with their start and end apart: 35, of which 17 were waited for; matrix products, arithmetic and copies ran while one was open for 10% of the time, Pallas kernels for 22%

profile of v9, /device:TPU:0, one launch (start us, length us, event | category | flops | bytes accessed | tf_op | source)
XLA Modules:
  0.0 424.2 jit_solution(14106040704779617140)
XLA Ops:
  2.9 3.4 copy-done
  6.9 3.1 shard_map.102
  10.1 3.3 copy-done.3
  13.4 6.8 %all-to-all-start = ((bf16[16,2048,128]{2,1,0:T(8,128)(2,1)}), bf16[16,2048,128]{2,1,0:T(8,128)(2,1)}, u32[]{:S(2)}, u32[]{:S(2)}) async-start(bf16[16,2048,128]{2,1,0:T(8,128)(2,1)} %bitcast.109), calls=%async_computation | async-start | bytes 16777216 | tf_op jit(solution)/shard_map/all_to_all | solution.py:425
  20.4 3.1 collective-permute-start
  23.9 3.4 copy-done.1
  27.3 3.4 shard_map.103
  30.7 3.3 copy-done.2
  33.9 89.8 %collective-permute-done = bf16[2048,128]{0,1:T(8,128)(2,1)S(1)} collective-permute-done((bf16[2048,128]{0,1:T(8,128)(2,1)S(1)}, bf16[2048,128]{0,1:T(8,128)(2,1)S(1)}, u32[]{:S(2)}, u32[]{:S(2)}) %collective-permute-start) | collective-permute-done | bytes 524320 | tf_op jit(solution)/shard_map/ppermute | solution.py:333
  123.8 11.0 %collective-permute-done.1 = bf16[128,2048]{0,1:T(8,128)(2,1)S(1)} collective-permute-done((bf16[128,2048]{0,1:T(8,128)(2,1)S(1)}, bf16[128,2048]{0,1:T(8,128)(2,1)S(1)}, u32[]{:S(2)}, u32[]{:S(2)}) %collective-permute-start.1) | collective-permute-done | bytes 524320 | tf_op jit(solution)/shard_map/ppermute | solution.py:333
  134.8 5.8 %all-to-all-done = bf16[16,2048,128]{2,1,0:T(8,128)(2,1)} async-done(((bf16[16,2048,128]{2,1,0:T(8,128)(2,1)}), bf16[16,2048,128]{2,1,0:T(8,128)(2,1)}, u32[]{:S(2)}, u32[]{:S(2)}) %all-to-all-start) | async-done | bytes 8388640 | tf_op jit(solution)/shard_map/all_to_all | solution.py:425
  140.7 11.7 %all-to-all-start.1 = ((bf16[16,2048,128]{2,1,0:T(8,128)(2,1)}), bf16[16,2048,128]{2,1,0:T(8,128)(2,1)}, u32[]{:S(2)}, u32[]{:S(2)}) async-start(bf16[16,2048,128]{2,1,0:T(8,128)(2,1)} %bitcast.108), calls=%async_computation.1 | async-start | bytes 16777216 | tf_op jit(solution)/shard_map/all_to_all | solution.py:425
  166.8 9.0 %fusion.2.b_ref = bf16[1920,512]{1,0:T(8,128)(2,1)} fusion(bf16[512,2048]{1,0:T(8,128)(2,1)S(1)} %bitcast.123, bf16[1920,2048]{1,0:T(8,128)(2,1)} %param.13), kind=kOutput, calls=%fused_computation.6 | convolution fusion | flops 4027514880 | bytes 11927552 | tf_op jit(solution)/shard_map/dot_general | solution.py:78
  175.8 5.4 %fusion.3.q_ref = bf16[1920,512]{1,0:T(8,128)(2,1)} fusion(bf16[2048,512]{0,1:T(8,128)(2,1)S(1)} %bitcast.124, bf16[1920,2048]{1,0:T(8,128)(2,1)S(1)} %bitcast.111), kind=kOutput, calls=%fused_computation.7 | convolution fusion | flops 4028497920 | bytes 11927552 | tf_op jit(solution)/shard_map/dot_general | solution.py:489
  181.2 36.0 %shard_map.104 = (f32[1920,256]{1,0:T(8,128)}, f32[1920,256]{1,0:T(8,128)}, f32[4,8,512]{2,1,0:T(8,128)}) custom-call(s32[128]{0:T(128)} %copy-done.21, s32[4]{0:T(128)} %copy-done.20, s32[128]{0:T(128)} %reshape.462.offsets, s32[128]{0:T(128)} %and_select_fusion.sizes, bf16[1920,512]{1,0:T(8,128)(2,1)} %fusion.3.q_ref, bf16[1920,512]{1,0:T(8,128)(2,1)} %fusion.2.b_ref, ...), custom_call_target="tpu_custom_call" | custom-call | flops 8053063680 | bytes 41943040 | tf_op jit(solution)/shard_map/pallas_call | solution.py:203
  218.5 27.4 %collective-permute-done.2.theirs_ref = f32[4,8,512]{2,1,0:T(8,128)S(1)} collective-permute-done((f32[4,8,512]{2,1,0:T(8,128)}, f32[4,8,512]{2,1,0:T(8,128)S(1)}, u32[]{:S(2)}, u32[]{:S(2)}) %collective-permute-start.2) | collective-permute-done | bytes 65568 | tf_op jit(solution)/shard_map/ppermute | solution.py:333
  246.5 2.8 shard_map.106
  249.4 2.9 shard_map.105
  252.3 3.3 collective-permute-start.11
  255.6 4.4 %all-to-all-done.1 = bf16[16,2048,128]{2,1,0:T(8,128)(2,1)} async-done(((bf16[16,2048,128]{2,1,0:T(8,128)(2,1)}), bf16[16,2048,128]{2,1,0:T(8,128)(2,1)}, u32[]{:S(2)}, u32[]{:S(2)}) %all-to-all-start.1) | async-done | bytes 8388640 | tf_op jit(solution)/shard_map/all_to_all | solution.py:425
  261.6 6.8 %collective-permute-start.9 = (bf16[4,2,128,512]{3,2,1,0:T(8,128)(2,1)S(1)}, bf16[4,2,128,512]{3,2,1,0:T(8,128)(2,1)}, u32[]{:S(2)}, u32[]{:S(2)}) collective-permute-start(bf16[4,2,128,512]{3,2,1,0:T(8,128)(2,1)S(1)} %fusion.5), channel_id=1, source_target_pairs={{0,2},{1,3},{2,0},{3,1},{4,6},{5,7},{6,4},{7,5},{8,10},{9,11},{10,... | collective-permute-start | bytes 3145736 | tf_op jit(solution)/shard_map/ppermute | solution.py:350
  268.4 36.0 %shard_map.107 = (f32[1920,256]{1,0:T(8,128)}, f32[1920,256]{1,0:T(8,128)}, f32[4,8,512]{2,1,0:T(8,128)}) custom-call(s32[128]{0:T(128)} %copy-done.21, s32[4]{0:T(128)} %copy-done.20, s32[128]{0:T(128)} %reshape.462.offsets, s32[128]{0:T(128)} %and_select_fusion.sizes, bf16[1920,512]{1,0:T(8,128)(2,1)} %fusion.3.q_ref, bf16[1920,512]{1,0:T(8,128)(2,1)} %fusion.2.b_ref, ...), custom_call_target="tpu_custom_call" | custom-call | flops 8053063680 | bytes 41943040 | tf_op jit(solution)/shard_map/pallas_call | solution.py:203
  307.0 16.5 %collective-permute-done.3.theirs_ref = f32[4,8,512]{2,1,0:T(8,128)S(1)} collective-permute-done((f32[4,8,512]{2,1,0:T(8,128)}, f32[4,8,512]{2,1,0:T(8,128)S(1)}, u32[]{:S(2)}, u32[]{:S(2)}) %collective-permute-start.3) | collective-permute-done | bytes 65568 | tf_op jit(solution)/shard_map/ppermute | solution.py:333
  324.1 2.8 shard_map.108
  326.9 3.3 collective-permute-start.4
  331.1 2.9 shard_map.111
  333.9 18.9 %collective-permute-done.4 = bf16[960,256]{1,0:T(8,128)(2,1)} collective-permute-done((bf16[960,256]{1,0:T(8,128)(2,1)}, bf16[960,256]{1,0:T(8,128)(2,1)}, u32[]{:S(2)}, u32[]{:S(2)}) %collective-permute-start.4) | collective-permute-done | bytes 491552 | tf_op jit(solution)/shard_map/ppermute | solution.py:333
  354.1 3.1 collective-permute-start.13
  363.2 14.5 %collective-permute-done.18 = bf16[960,256]{1,0:T(8,128)(2,1)S(1)} collective-permute-done((bf16[960,256]{1,0:T(8,128)(2,1)}, bf16[960,256]{1,0:T(8,128)(2,1)S(1)}, u32[]{:S(2)}, u32[]{:S(2)}) %collective-permute-start.18) | collective-permute-done | bytes 491552 | tf_op jit(solution)/shard_map/ppermute | solution.py:333
  385.6 4.7 %convolution_multiply_fusion = f32[128,2048]{1,0:T(8,128)S(1)} fusion(bf16[1920,2048]{1,0:T(8,128)(2,1)} %param.13, bf16[960,128]{1,0:T(8,128)(2,1)S(1)} %get-tuple-element.114, bf16[960,128]{1,0:T(8,128)(2,1)S(1)} %get-tuple-element.113, bf16[960,128]{1,0:T(8,128)(2,1)S(1)} %constant_dynamic-slice_fusion.2, ...), kind=kOutput, calls=%fused_computation.8 | convolution fusion | flops 1009598464 | bytes 9895936 | tf_op jit(solution)/shard_map/dot_general | solution.py:565
  407.9 3.2 collective-permute-done.15
  411.7 3.3 collective-permute-done.16
  (196 shorter events, 67.3 us)
Async XLA Ops:
  13.4 127.3 %all-to-all-start = ((bf16[16,2048,128]{2,1,0:T(8,128)(2,1)}), bf16[16,2048,128]{2,1,0:T(8,128)(2,1)}, u32[]{:S(2)}, u32[]{:S(2)}) async-start(bf16[16,2048,128]{2,1,0:T(8,128)(2,1)} %bitcast.109), calls=%async_computation | async-start | bytes 16777216 | tf_op jit(solution)/shard_map/all_to_all | solution.py:425
  20.4 103.4 %collective-permute-start = (bf16[2048,128]{0,1:T(8,128)(2,1)S(1)}, bf16[2048,128]{0,1:T(8,128)(2,1)S(1)}, u32[]{:S(2)}, u32[]{:S(2)}) collective-permute-start(bf16[2048,128]{0,1:T(8,128)(2,1)S(1)} %copy.34), channel_id=1, source_target_pairs={{0,4},{4,0},{1,5},{5,1},{2,6},{6,2},{3,7},{7,3},{8,12},{12,8},{9,1... | collective-permute-start | bytes 1572872 | tf_op jit(solution)/shard_map/ppermute | solution.py:333
  23.8 111.0 %collective-permute-start.1 = (bf16[128,2048]{0,1:T(8,128)(2,1)S(1)}, bf16[128,2048]{0,1:T(8,128)(2,1)S(1)}, u32[]{:S(2)}, u32[]{:S(2)}) collective-permute-start(bf16[128,2048]{0,1:T(8,128)(2,1)S(1)} %copy.33), channel_id=1, source_target_pairs={{0,4},{4,0},{1,5},{5,1},{2,6},{6,2},{3,7},{7,3},{8,12},{12,8},{9,1... | collective-permute-start | bytes 1572872 | tf_op jit(solution)/shard_map/ppermute | solution.py:333
  140.7 119.3 %all-to-all-start.1 = ((bf16[16,2048,128]{2,1,0:T(8,128)(2,1)}), bf16[16,2048,128]{2,1,0:T(8,128)(2,1)}, u32[]{:S(2)}, u32[]{:S(2)}) async-start(bf16[16,2048,128]{2,1,0:T(8,128)(2,1)} %bitcast.108), calls=%async_computation.1 | async-start | bytes 16777216 | tf_op jit(solution)/shard_map/all_to_all | solution.py:425
  217.2 28.7 %collective-permute-start.2 = (f32[4,8,512]{2,1,0:T(8,128)}, f32[4,8,512]{2,1,0:T(8,128)S(1)}, u32[]{:S(2)}, u32[]{:S(2)}) collective-permute-start(f32[4,8,512]{2,1,0:T(8,128)} %get-tuple-element.30.mine_ref), channel_id=1, source_target_pairs={{0,4},{4,0},{1,5},{5,1},{2,6},{6,2},{3,7},{7,3},{8,12},{12,8},{9,1... | collective-permute-start | bytes 196616 | tf_op jit(solution)/shard_map/ppermute | solution.py:333
  252.3 52.2 %collective-permute-start.11 = (bf16[960,256]{1,0:T(8,128)(2,1)}, bf16[960,256]{1,0:T(8,128)(2,1)S(1)}, u32[]{:S(2)}, u32[]{:S(2)}) collective-permute-start(bf16[960,256]{1,0:T(8,128)(2,1)} %shard_map.105), channel_id=1, source_target_pairs={{0,4},{4,0},{1,5},{5,1},{2,6},{6,2},{3,7},{7,3},{8,12},{12,8},{9,1... | collective-permute-start | bytes 1474568 | tf_op jit(solution)/shard_map/ppermute | solution.py:333
  255.5 49.9 %collective-permute-start.22 = (bf16[960,256]{1,0:T(8,128)(2,1)S(1)}, bf16[960,256]{1,0:T(8,128)(2,1)S(1)}, u32[]{:S(2)}, u32[]{:S(2)}) collective-permute-start(bf16[960,256]{1,0:T(8,128)(2,1)S(1)} %copy-done.6), channel_id=1, source_target_pairs={{0,4},{4,0},{1,5},{5,1},{2,6},{6,2},{3,7},{7,3},{8,12},{12,8},{9,1... | collective-permute-start | bytes 1474568 | tf_op jit(solution)/shard_map/ppermute | solution.py:333
  260.0 94.1 %collective-permute-start.8 = (bf16[4,2,128,512]{3,2,1,0:T(8,128)(2,1)S(1)}, bf16[4,2,128,512]{3,2,1,0:T(8,128)(2,1)}, u32[]{:S(2)}, u32[]{:S(2)}) collective-permute-start(bf16[4,2,128,512]{3,2,1,0:T(8,128)(2,1)S(1)} %fusion.5), channel_id=1, source_target_pairs={{0,1},{1,0},{2,3},{3,2},{4,5},{5,4},{6,7},{7,6},{8,9},{9,8},{10,11... | collective-permute-start | bytes 3145736 | tf_op jit(solution)/shard_map/ppermute | solution.py:350
  261.6 95.6 %collective-permute-start.9 = (bf16[4,2,128,512]{3,2,1,0:T(8,128)(2,1)S(1)}, bf16[4,2,128,512]{3,2,1,0:T(8,128)(2,1)}, u32[]{:S(2)}, u32[]{:S(2)}) collective-permute-start(bf16[4,2,128,512]{3,2,1,0:T(8,128)(2,1)S(1)} %fusion.5), channel_id=1, source_target_pairs={{0,2},{1,3},{2,0},{3,1},{4,6},{5,7},{6,4},{7,5},{8,10},{9,11},{10,... | collective-permute-start | bytes 3145736 | tf_op jit(solution)/shard_map/ppermute | solution.py:350
  268.4 89.1 %collective-permute-start.10 = (bf16[4,2,128,512]{3,2,1,0:T(8,128)(2,1)S(1)}, bf16[4,2,128,512]{3,2,1,0:T(8,128)(2,1)}, u32[]{:S(2)}, u32[]{:S(2)}) collective-permute-start(bf16[4,2,128,512]{3,2,1,0:T(8,128)(2,1)S(1)} %fusion.5), channel_id=1, source_target_pairs={{0,3},{1,2},{2,1},{3,0},{4,7},{5,6},{6,5},{7,4},{8,11},{9,10},{10,... | collective-permute-start | bytes 3145736 | tf_op jit(solution)/shard_map/ppermute | solution.py:350
  304.4 19.0 %collective-permute-start.3 = (f32[4,8,512]{2,1,0:T(8,128)}, f32[4,8,512]{2,1,0:T(8,128)S(1)}, u32[]{:S(2)}, u32[]{:S(2)}) collective-permute-start(f32[4,8,512]{2,1,0:T(8,128)} %get-tuple-element.35.mine_ref), channel_id=1, source_target_pairs={{0,4},{4,0},{1,5},{5,1},{2,6},{6,2},{3,7},{7,3},{8,12},{12,8},{9,1... | collective-permute-start | bytes 196616 | tf_op jit(solution)/shard_map/ppermute | solution.py:333
  305.4 55.8 %collective-permute-start.12 = (bf16[240,256]{1,0:T(8,128)(2,1)}, bf16[240,256]{1,0:T(8,128)(2,1)S(1)}, u32[]{:S(2)}, u32[]{:S(2)}) collective-permute-start(bf16[240,256]{1,0:T(8,128)(2,1)} %get-tuple-element.85), channel_id=1, source_target_pairs={{0,1},{1,0},{2,3},{3,2},{4,5},{5,4},{6,7},{7,6},{8,9},{9,8},{10,11... | collective-permute-start | bytes 368648 | tf_op jit(solution)/shard_map/ppermute | solution.py:350
  326.9 25.8 %collective-permute-start.4 = (bf16[960,256]{1,0:T(8,128)(2,1)}, bf16[960,256]{1,0:T(8,128)(2,1)}, u32[]{:S(2)}, u32[]{:S(2)}) collective-permute-start(bf16[960,256]{1,0:T(8,128)(2,1)} %shard_map.108), channel_id=1, source_target_pairs={{0,4},{4,0},{1,5},{5,1},{2,6},{6,2},{3,7},{7,3},{8,12},{12,8},{9,1... | collective-permute-start | bytes 1474568 | tf_op jit(solution)/shard_map/ppermute | solution.py:333
  353.9 23.8 %collective-permute-start.18 = (bf16[960,256]{1,0:T(8,128)(2,1)}, bf16[960,256]{1,0:T(8,128)(2,1)S(1)}, u32[]{:S(2)}, u32[]{:S(2)}) collective-permute-start(bf16[960,256]{1,0:T(8,128)(2,1)} %shard_map.111), channel_id=1, source_target_pairs={{0,4},{4,0},{1,5},{5,1},{2,6},{6,2},{3,7},{7,3},{8,12},{12,8},{9,1... | collective-permute-start | bytes 1474568 | tf_op jit(solution)/shard_map/ppermute | solution.py:333
  354.1 23.8 %collective-permute-start.13 = (bf16[240,256]{1,0:T(8,128)(2,1)S(1)}, bf16[240,256]{1,0:T(8,128)(2,1)S(1)}, u32[]{:S(2)}, u32[]{:S(2)}) collective-permute-start(bf16[240,256]{1,0:T(8,128)(2,1)S(1)} %copy-done.17), channel_id=1, source_target_pairs={{0,2},{1,3},{2,0},{3,1},{4,6},{5,7},{6,4},{7,5},{8,10},{9,11},{10,... | collective-permute-start | bytes 368648 | tf_op jit(solution)/shard_map/ppermute | solution.py:350
  357.2 21.5 %collective-permute-start.14 = (bf16[240,256]{1,0:T(8,128)(2,1)S(1)}, bf16[240,256]{1,0:T(8,128)(2,1)S(1)}, u32[]{:S(2)}, u32[]{:S(2)}) collective-permute-start(bf16[240,256]{1,0:T(8,128)(2,1)S(1)} %get-tuple-element.83), channel_id=1, source_target_pairs={{0,3},{1,2},{2,1},{3,0},{4,7},{5,6},{6,5},{7,4},{8,11},{9,10},{10,... | collective-permute-start | bytes 368648 | tf_op jit(solution)/shard_map/ppermute | solution.py:350
  357.5 25.1 %collective-permute-start.23 = (bf16[240,256]{1,0:T(8,128)(2,1)}, bf16[240,256]{1,0:T(8,128)(2,1)S(1)}, u32[]{:S(2)}, u32[]{:S(2)}) collective-permute-start(bf16[240,256]{1,0:T(8,128)(2,1)} %get-tuple-element.77), channel_id=1, source_target_pairs={{0,1},{1,0},{2,3},{3,2},{4,5},{5,4},{6,7},{7,6},{8,9},{9,8},{10,11... | collective-permute-start | bytes 368648 | tf_op jit(solution)/shard_map/ppermute | solution.py:350
  361.2 21.7 %collective-permute-start.24 = (bf16[240,256]{1,0:T(8,128)(2,1)S(1)}, bf16[240,256]{1,0:T(8,128)(2,1)S(1)}, u32[]{:S(2)}, u32[]{:S(2)}) collective-permute-start(bf16[240,256]{1,0:T(8,128)(2,1)S(1)} %copy-done.16), channel_id=1, source_target_pairs={{0,2},{1,3},{2,0},{3,1},{4,6},{5,7},{6,4},{7,5},{8,10},{9,11},{10,... | collective-permute-start | bytes 368648 | tf_op jit(solution)/shard_map/ppermute | solution.py:350
  377.9 16.2 %collective-permute-start.5 = (bf16[240,256]{1,0:T(8,128)(2,1)S(1)}, bf16[240,256]{1,0:T(8,128)(2,1)S(1)}, u32[]{:S(2)}, u32[]{:S(2)}) collective-permute-start(bf16[240,256]{1,0:T(8,128)(2,1)S(1)} %get-tuple-element.89), channel_id=1, source_target_pairs={{0,1},{1,0},{2,3},{3,2},{4,5},{5,4},{6,7},{7,6},{8,9},{9,8},{10,11... | collective-permute-start | bytes 368648 | tf_op jit(solution)/shard_map/ppermute | solution.py:350
  378.7 16.1 %collective-permute-start.6 = (bf16[240,256]{1,0:T(8,128)(2,1)S(1)}, bf16[240,256]{1,0:T(8,128)(2,1)S(1)}, u32[]{:S(2)}, u32[]{:S(2)}) collective-permute-start(bf16[240,256]{1,0:T(8,128)(2,1)S(1)} %get-tuple-element.88), channel_id=1, source_target_pairs={{0,2},{1,3},{2,0},{3,1},{4,6},{5,7},{6,4},{7,5},{8,10},{9,11},{10,... | collective-permute-start | bytes 368648 | tf_op jit(solution)/shard_map/ppermute | solution.py:350
  382.6 13.4 %collective-permute-start.7 = (bf16[240,256]{1,0:T(8,128)(2,1)S(1)}, bf16[240,256]{1,0:T(8,128)(2,1)S(1)}, u32[]{:S(2)}, u32[]{:S(2)}) collective-permute-start(bf16[240,256]{1,0:T(8,128)(2,1)S(1)} %get-tuple-element.87), channel_id=1, source_target_pairs={{0,3},{1,2},{2,1},{3,0},{4,7},{5,6},{6,5},{7,4},{8,11},{9,10},{10,... | collective-permute-start | bytes 368648 | tf_op jit(solution)/shard_map/ppermute | solution.py:350
  390.4 16.0 %collective-permute-start.31 = (bf16[128,1024]{1,0:T(8,128)(2,1)S(1)}, bf16[128,1024]{1,0:T(8,128)(2,1)S(1)}, u32[]{:S(2)}, u32[]{:S(2)}) collective-permute-start(bf16[128,1024]{1,0:T(8,128)(2,1)S(1)} %dynamic-slice_convert_fusion), channel_id=1, source_target_pairs={{0,16},{8,24},{16,0},{24,8},{1,17},{9,25},{17,1},{25,9},{2,18},{10... | collective-permute-start | bytes 786440 | tf_op jit(solution)/shard_map/ppermute | solution.py:375
  391.9 19.2 %collective-permute-start.29 = (bf16[1024,128]{0,1:T(8,128)(2,1)S(1)}, bf16[1024,128]{0,1:T(8,128)(2,1)S(1)}, u32[]{:S(2)}, u32[]{:S(2)}) collective-permute-start(bf16[1024,128]{0,1:T(8,128)(2,1)S(1)} %fusion.18), channel_id=1, source_target_pairs={{0,16},{8,24},{16,0},{24,8},{1,17},{9,25},{17,1},{25,9},{2,18},{10... | collective-permute-start | bytes 786440 | tf_op jit(solution)/shard_map/ppermute | solution.py:375
  394.0 7.2 %collective-permute-start.19 = (bf16[240,256]{1,0:T(8,128)(2,1)S(1)}, bf16[240,256]{1,0:T(8,128)(2,1)S(1)}, u32[]{:S(2)}, u32[]{:S(2)}) collective-permute-start(bf16[240,256]{1,0:T(8,128)(2,1)S(1)} %get-tuple-element.81), channel_id=1, source_target_pairs={{0,1},{1,0},{2,3},{3,2},{4,5},{5,4},{6,7},{7,6},{8,9},{9,8},{10,11... | collective-permute-start | bytes 368648 | tf_op jit(solution)/shard_map/ppermute | solution.py:350
  396.0 8.4 %collective-permute-start.21 = (bf16[240,256]{1,0:T(8,128)(2,1)S(1)}, bf16[240,256]{1,0:T(8,128)(2,1)S(1)}, u32[]{:S(2)}, u32[]{:S(2)}) collective-permute-start(bf16[240,256]{1,0:T(8,128)(2,1)S(1)} %get-tuple-element.79), channel_id=1, source_target_pairs={{0,3},{1,2},{2,1},{3,0},{4,7},{5,6},{6,5},{7,4},{8,11},{9,10},{10,... | collective-permute-start | bytes 368648 | tf_op jit(solution)/shard_map/ppermute | solution.py:350
  401.2 9.9 %collective-permute-start.15 = (bf16[240,512]{1,0:T(8,128)(2,1)S(1)}, bf16[240,512]{1,0:T(8,128)(2,1)S(1)}, u32[]{:S(2)}, u32[]{:S(2)}) collective-permute-start(bf16[240,512]{1,0:T(8,128)(2,1)S(1)} %get-tuple-element.74), channel_id=1, source_target_pairs={{0,3},{1,2},{2,1},{3,0},{4,7},{5,6},{6,5},{7,4},{8,11},{9,10},{10,... | collective-permute-start | bytes 737288 | tf_op jit(solution)/shard_map/ppermute | solution.py:350
  401.2 13.8 %collective-permute-start.16 = (bf16[240,512]{1,0:T(8,128)(2,1)S(1)}, bf16[240,512]{1,0:T(8,128)(2,1)S(1)}, u32[]{:S(2)}, u32[]{:S(2)}) collective-permute-start(bf16[240,512]{1,0:T(8,128)(2,1)S(1)} %get-tuple-element.73), channel_id=1, source_target_pairs={{0,2},{1,3},{2,0},{3,1},{4,6},{5,7},{6,4},{7,5},{8,10},{9,11},{10,... | collective-permute-start | bytes 737288 | tf_op jit(solution)/shard_map/ppermute | solution.py:350
  404.4 12.6 %collective-permute-start.17 = (bf16[240,512]{1,0:T(8,128)(2,1)S(1)}, bf16[240,512]{1,0:T(8,128)(2,1)S(1)}, u32[]{:S(2)}, u32[]{:S(2)}) collective-permute-start(bf16[240,512]{1,0:T(8,128)(2,1)S(1)} %get-tuple-element.72), channel_id=1, source_target_pairs={{0,1},{1,0},{2,3},{3,2},{4,5},{5,4},{6,7},{7,6},{8,9},{9,8},{10,11... | collective-permute-start | bytes 737288 | tf_op jit(solution)/shard_map/ppermute | solution.py:350
  406.4 13.0 %collective-permute-start.26 = (bf16[240,512]{1,0:T(8,128)(2,1)S(1)}, bf16[240,512]{1,0:T(8,128)(2,1)S(1)}, u32[]{:S(2)}, u32[]{:S(2)}) collective-permute-start(bf16[240,512]{1,0:T(8,128)(2,1)S(1)} %get-tuple-element.71), channel_id=1, source_target_pairs={{0,3},{1,2},{2,1},{3,0},{4,7},{5,6},{6,5},{7,4},{8,11},{9,10},{10,... | collective-permute-start | bytes 737288 | tf_op jit(solution)/shard_map/ppermute | solution.py:350
  411.1 10.3 %collective-permute-start.27 = (bf16[240,512]{1,0:T(8,128)(2,1)S(1)}, bf16[240,512]{1,0:T(8,128)(2,1)S(1)}, u32[]{:S(2)}, u32[]{:S(2)}) collective-permute-start(bf16[240,512]{1,0:T(8,128)(2,1)S(1)} %get-tuple-element.70), channel_id=1, source_target_pairs={{0,2},{1,3},{2,0},{3,1},{4,6},{5,7},{6,4},{7,5},{8,10},{9,11},{10,... | collective-permute-start | bytes 737288 | tf_op jit(solution)/shard_map/ppermute | solution.py:350
  411.1 10.8 %collective-permute-start.28 = (bf16[240,512]{1,0:T(8,128)(2,1)S(1)}, bf16[240,512]{1,0:T(8,128)(2,1)S(1)}, u32[]{:S(2)}, u32[]{:S(2)}) collective-permute-start(bf16[240,512]{1,0:T(8,128)(2,1)S(1)} %get-tuple-element.69), channel_id=1, source_target_pairs={{0,1},{1,0},{2,3},{3,2},{4,5},{5,4},{6,7},{7,6},{8,9},{9,8},{10,11... | collective-permute-start | bytes 737288 | tf_op jit(solution)/shard_map/ppermute | solution.py:350
  415.0 8.4 %collective-permute-start.32 = (bf16[128,512]{1,0:T(8,128)(2,1)S(1)}, bf16[128,512]{1,0:T(8,128)(2,1)S(1)}, u32[]{:S(2)}, u32[]{:S(2)}) collective-permute-start(bf16[128,512]{1,0:T(8,128)(2,1)S(1)} %dynamic-slice_convert_fusion.2), channel_id=1, source_target_pairs={{0,8},{8,0},{16,24},{24,16},{1,9},{9,1},{17,25},{25,17},{2,10},{10... | collective-permute-start | bytes 393224 | tf_op jit(solution)/shard_map/ppermute | solution.py:375
  (29 other events, 269.7 us)

commit v10 on v9

--- a/solution.py
+++ b/solution.py
@@ -275,58 +275,60 @@
     )(outs, douts, mine, theirs)
 
 
-def project_kernel(*refs, count, chunk, depth, has_before):
-    cols = refs[count]
-    before = refs[count + 1] if has_before else None
+def project_kernel(spot, *refs, count, dests, chunk, depth, has_before):
+    cols = refs[count : count + dests]
+    before = refs[count + dests] if has_before else None
     out, weights = refs[-2], refs[-1]
-    dests, width = cols.shape[1], cols.shape[4]
-    half = width // 2
+    half = weights.shape[3] // 2
     empty = jnp.zeros((depth, half), weights.dtype)
-    for i in range(count):
-        for dest in range(dests):
-            low = pl.ds(dest * width, half)
-            high = pl.ds(dest * width + half, half)
+    for j in range(dests):
+        dest = spot[j]
+        for i in range(count):
             for z in range(2):
-                own = cols[i, dest, z, pl.ds(chunk * depth, depth), :]
+                own = cols[j][i, z, pl.ds(chunk * depth, depth), :]
                 grad_rows = pl.ds(2 * z * depth, depth)
                 out_rows = pl.ds((2 * z + 1) * depth, depth)
-                weights[i, grad_rows, low] = empty
-                weights[i, grad_rows, high] = own[:, half:]
-                weights[i, out_rows, low] = own[:, :half]
-                weights[i, out_rows, high] = empty
+                weights[dest, i, grad_rows, :half] = empty
+                weights[dest, i, grad_rows, half:] = own[:, half:]
+                weights[dest, i, out_rows, :half] = own[:, :half]
+                weights[dest, i, out_rows, half:] = empty
     for dest in range(dests):
-        lanes = pl.ds(dest * width, width)
-        value = jnp.dot(refs[0][...], weights[0, :, lanes], preferred_element_type=jnp.float32)
+        value = jnp.dot(refs[0][...], weights[dest, 0], preferred_element_type=jnp.float32)
         for i in range(1, count):
-            value += jnp.dot(
-                refs[i][...], weights[i, :, lanes], preferred_element_type=jnp.float32
-            )
+            value += jnp.dot(refs[i][...], weights[dest, i], preferred_element_type=jnp.float32)
         if has_before:
             value += before[dest]
         out[dest] = value.astype(out.dtype)
 
 
-def project(pieces, cols, before, last, chunk):
-    count = len(pieces)
+def project(pieces, cols, order, before, last, chunk):
+    count, dests = len(pieces), len(cols)
     rows, depth = pieces[0].shape
-    dests, width = cols.shape[1], cols.shape[4]
-    inputs = [*pieces, cols] + ([] if before is None else [before])
+    width = cols[0].shape[3]
+    inputs = [*pieces, *cols] + ([] if before is None else [before])
+    full = lambda x: pl.BlockSpec(x.shape, lambda i, *_: (0,) * x.ndim)
+    result = jax.ShapeDtypeStruct((dests, rows, width), jnp.bfloat16 if last else jnp.float32)
     return pl.pallas_call(
         functools.partial(
-            project_kernel, count=count, chunk=chunk, depth=depth // 4,
+            project_kernel, count=count, dests=dests, chunk=chunk, depth=depth // 4,
             has_before=before is not None,
         ),
-        out_shape=jax.ShapeDtypeStruct(
-            (dests, rows, width), jnp.bfloat16 if last else jnp.float32
-        ),
-        scratch_shapes=[pltpu.VMEM((count, depth, dests * width), jnp.bfloat16)],
+        grid_spec=pltpu.PrefetchScalarGridSpec(
+            num_scalar_prefetch=1,
+            grid=(1,),
+            in_specs=[full(x) for x in inputs],
+            out_specs=full(result),
+            scratch_shapes=[pltpu.VMEM((dests, count, depth, width), jnp.bfloat16)],
+        ),
+        out_shape=result,
         compiler_params=pltpu.CompilerParams(vmem_limit_bytes=40 << 20),
         cost_estimate=pl.CostEstimate(
             flops=2 * rows * depth * count * width * dests,
             transcendentals=0,
-            bytes_accessed=2 * rows * (depth * count + 2 * width) + 2 * cols.size,
-        ),
-    )(*inputs)
+            bytes_accessed=2 * rows * (depth * count + 2 * width)
+            + 2 * sum(x.size for x in cols),
+        ),
+    )(order, *inputs)
 
 
 def swap(x, axis):
@@ -507,10 +509,27 @@
         final = c + 1 == local_heads
         if final:
             blocks, _ = lax.optimization_barrier((blocks, received[c]))
-            if small:
-                cols = jnp.stack([across(blocks, d, inner) for d in range(inner)])
+            if small and groups == inner:
+                cols = [
+                    jnp.stack(
+                        [
+                            across(
+                                lax.dynamic_index_in_dim(blocks, group, 0, keepdims=False),
+                                d,
+                                inner,
+                            )
+                            for d in range(inner)
+                        ]
+                    )
+                ]
+                flip = lambda x, d: lax.ppermute(x, "dp", [(i, i ^ d) for i in range(groups)])
+                cols.append(flip(cols[0], 1))
+                cols += [flip(cols[0], 2), flip(cols[1], 2)]
+                order = group ^ jnp.arange(inner, dtype=jnp.int32)
             else:
-                cols = lax.all_gather(blocks, ("zl", "y"), axis=0, tiled=False)
+                whole = lax.all_gather(blocks, ("zl", "y"), axis=0, tiled=False)
+                cols = [whole[:, i] for i in range(inner)]
+                order = jnp.arange(inner, dtype=jnp.int32)
         outs, douts, mine = attention(
             tables, bias, queries, backs, received[c], c, slots, head_scale
         )
@@ -521,31 +540,37 @@
         ]
         if not final:
             parts, bias = lax.optimization_barrier((parts, bias))
-        merged = []
+        merged, by_rows = [], []
         for part in parts:
-            if final and merged:
+            behind_rows = final and bool(merged)
+            if behind_rows:
                 part, _ = lax.optimization_barrier((part, merged[-1]))
-            other = swap(part, "zh").astype(jnp.float32)
-            merged.append((part.astype(jnp.float32) + other).astype(jnp.bfloat16))
-        by_rows = [
-            trade(x.reshape(inner, x.shape[0] // inner, x.shape[1]), spot, small) for x in merged
-        ]
+            other = swap(part, "zh")
+            if behind_rows:
+                other, _ = lax.optimization_barrier((other, (by_rows, traded)))
+            x = (part.astype(jnp.float32) + other.astype(jnp.float32)).astype(jnp.bfloat16)
+            merged.append(x)
+            by_rows.append(
+                trade(x.reshape(inner, x.shape[0] // inner, x.shape[1]), spot, small)
+            )
         if not final:
             traded.append(by_rows)
             own.append(merged)
             continue
         for i, earlier in enumerate(traded):
             results = [
-                project(pieces, cols, before, False, i)
+                project(pieces, cols, order, before, False, i)
                 for pieces, before in zip(earlier, results)
             ]
-        behind = merged
-        if traded:
-            behind, _ = lax.optimization_barrier((merged, results))
+        outputs = [
+            project(pieces, cols, order, before, True, c)
+            for pieces, before in zip(by_rows, results)
+        ]
+        behind, _ = lax.optimization_barrier((merged, outputs))
         own.append(behind)
-        outputs = []
-        for pieces, before in zip(by_rows, results):
-            outputs += in_order(trade(project(pieces, cols, before, True, c), spot, small), spot, small)
+        outputs = [
+            x for part in outputs for x in in_order(trade(part, spot, small), spot, small)
+        ]
     attended = jnp.concatenate([x[:, :columns] for x in outputs], axis=0)
     patch_grad = jnp.concatenate([x[:, columns:] for x in outputs], axis=0)
     own = [

time: 426 us -> 438 us (1.028)
  local copies, waits for them, and re-layouts: 25.8 us -> 34.3 us
  Pallas kernels: 94.7 us -> 101 us
    ppermute x8, waiting for transfers between devices: 178 us -> 148 us  [swap(): return lax.ppermute(x, axis, [(0, 1), (1, 0)])]
    ppermute x0 -> x3, waiting for transfers between devices: none -> 16.5 us  [local(): lax.ppermute(x, 'dp', [(i, i ^ d) for i in range(groups)])]
    pallas_call x4, Pallas kernels: 4.72 us -> 13.9 us  [project(): pl.pallas_call(functools.partial(project_kernel, count=count, dests=dests...]
    all_to_all x2, waiting for transfers between devices: 10.2 us -> 17.6 us  [exchange(): lax.all_to_all(x, ('dp', 'zl', 'y'), split_axis=0, concat_axis=0, tiled=T...]
    ppermute x21, waiting for transfers between devices: 18.8 us -> 24.9 us  [across(): return lax.ppermute(x, ('zl', 'y'), [(i, i ^ d) for i in range(count)])]
    unnamed x63 -> x103, local copies, waits for them, and re-layouts: 17.1 us -> 22.2 us
  transfers between devices with their start and end apart: 35 -> 38, of which waited for: 17 -> 18; matrix products, arithmetic and copies ran while one was open for 10% -> 10% of each run, Pallas kernels for 22% -> 20%
where the time goes in v10:
time: 438 us; the launch traced here: 436 us
  waiting for transfers between devices  211 us (48%)
  Pallas kernels  101 us (23%)
  starting transfers between devices  55.5 us (13%)
  local copies, waits for them, and re-layouts  34.3 us (8%)
  matrix products  17.3 us (4%)
  other arithmetic  15.3 us (3%)
    ppermute x8, waiting for transfers between devices, swap(): return lax.ppermute(x, axis, [(0, 1), (1, 0)])  148 us
    pallas_call x2, Pallas kernels, attention(): pl.pallas_call(functools.partial(attention_kernel, slots=slots, scale=sca...  68.2 us
    ppermute x21, waiting for transfers between devices, across(): return lax.ppermute(x, ('zl', 'y'), [(i, i ^ d) for i in range(count)])  24.9 us
    ppermute x21, starting transfers between devices, across(): return lax.ppermute(x, ('zl', 'y'), [(i, i ^ d) for i in range(count)])  24.4 us
    unnamed x103, local copies, waits for them, and re-layouts  22.2 us
    all_to_all x2, starting transfers between devices, exchange(): lax.all_to_all(x, ('dp', 'zl', 'y'), split_axis=0, concat_axis=0, tiled=T...  18.9 us
    all_to_all x2, waiting for transfers between devices, exchange(): lax.all_to_all(x, ('dp', 'zl', 'y'), split_axis=0, concat_axis=0, tiled=T...  17.6 us
    ppermute x3, waiting for transfers between devices, local(): lax.ppermute(x, 'dp', [(i, i ^ d) for i in range(groups)])  16.5 us
  transfers between devices with their start and end apart: 38, of which 18 were waited for; matrix products, arithmetic and copies ran while one was open for 10% of the time, Pallas kernels for 20%

profile of v10, /device:TPU:0, one launch (start us, length us, event | category | flops | bytes accessed | tf_op | source)
XLA Modules:
  0.0 435.9 jit_solution(11789614589876288700)
XLA Ops:
  2.9 3.4 copy-done
  6.9 3.6 shard_map.102
  10.5 3.3 copy-done.3
  13.9 7.6 %all-to-all-start = ((bf16[16,2048,128]{2,1,0:T(8,128)(2,1)}), bf16[16,2048,128]{2,1,0:T(8,128)(2,1)}, u32[]{:S(2)}, u32[]{:S(2)}) async-start(bf16[16,2048,128]{2,1,0:T(8,128)(2,1)} %bitcast.110), calls=%async_computation | async-start | bytes 16777216 | tf_op jit(solution)/shard_map/all_to_all | solution.py:427
  25.1 3.4 copy-done.1
  28.5 4.0 shard_map.103
  32.5 3.3 copy-done.2
  35.8 89.2 %collective-permute-done = bf16[2048,128]{0,1:T(8,128)(2,1)S(1)} collective-permute-done((bf16[2048,128]{0,1:T(8,128)(2,1)S(1)}, bf16[2048,128]{0,1:T(8,128)(2,1)S(1)}, u32[]{:S(2)}, u32[]{:S(2)}) %collective-permute-start) | collective-permute-done | bytes 524320 | tf_op jit(solution)/shard_map/ppermute | solution.py:335
  125.0 11.0 %collective-permute-done.1 = bf16[128,2048]{0,1:T(8,128)(2,1)S(1)} collective-permute-done((bf16[128,2048]{0,1:T(8,128)(2,1)S(1)}, bf16[128,2048]{0,1:T(8,128)(2,1)S(1)}, u32[]{:S(2)}, u32[]{:S(2)}) %collective-permute-start.1) | collective-permute-done | bytes 524320 | tf_op jit(solution)/shard_map/ppermute | solution.py:335
  136.0 5.9 %all-to-all-done = bf16[16,2048,128]{2,1,0:T(8,128)(2,1)} async-done(((bf16[16,2048,128]{2,1,0:T(8,128)(2,1)}), bf16[16,2048,128]{2,1,0:T(8,128)(2,1)}, u32[]{:S(2)}, u32[]{:S(2)}) %all-to-all-start) | async-done | bytes 8388640 | tf_op jit(solution)/shard_map/all_to_all | solution.py:427
  142.0 11.2 %all-to-all-start.1 = ((bf16[16,2048,128]{2,1,0:T(8,128)(2,1)}), bf16[16,2048,128]{2,1,0:T(8,128)(2,1)}, u32[]{:S(2)}, u32[]{:S(2)}) async-start(bf16[16,2048,128]{2,1,0:T(8,128)(2,1)} %bitcast.109), calls=%async_computation.1 | async-start | bytes 16777216 | tf_op jit(solution)/shard_map/all_to_all | solution.py:427
  165.9 9.0 %fusion.3.q_ref = bf16[1920,512]{1,0:T(8,128)(2,1)} fusion(bf16[2048,512]{0,1:T(8,128)(2,1)S(1)} %bitcast.126, bf16[1920,2048]{1,0:T(8,128)(2,1)} %param.7), kind=kOutput, calls=%fused_computation.6 | convolution fusion | flops 4028497920 | bytes 11927552 | tf_op jit(solution)/shard_map/dot_general | solution.py:491
  174.9 5.5 %fusion.2.b_ref = bf16[1920,512]{1,0:T(8,128)(2,1)} fusion(bf16[512,2048]{1,0:T(8,128)(2,1)S(1)} %bitcast.125, bf16[1920,2048]{1,0:T(8,128)(2,1)S(1)} %bitcast.114), kind=kOutput, calls=%fused_computation.5 | convolution fusion | flops 4027514880 | bytes 11927552 | tf_op jit(solution)/shard_map/dot_general | solution.py:78
  180.4 34.1 %shard_map.104 = (f32[1920,256]{1,0:T(8,128)}, f32[1920,256]{1,0:T(8,128)}, f32[4,8,512]{2,1,0:T(8,128)}) custom-call(s32[128]{0:T(128)} %copy-done.39, s32[4]{0:T(128)} %copy-done.38, s32[128]{0:T(128)} %reshape.462.offsets, s32[128]{0:T(128)} %and_select_fusion.sizes, bf16[1920,512]{1,0:T(8,128)(2,1)} %fusion.3.q_ref, bf16[1920,512]{1,0:T(8,128)(2,1)} %fusion.2.b_ref, ...), custom_call_target="tpu_custom_call" | custom-call | flops 8053063680 | bytes 41943040 | tf_op jit(solution)/shard_map/pallas_call | solution.py:203
  216.0 30.7 %collective-permute-done.2.theirs_ref = f32[4,8,512]{2,1,0:T(8,128)S(1)} collective-permute-done((f32[4,8,512]{2,1,0:T(8,128)}, f32[4,8,512]{2,1,0:T(8,128)S(1)}, u32[]{:S(2)}, u32[]{:S(2)}) %collective-permute-start.2) | collective-permute-done | bytes 65568 | tf_op jit(solution)/shard_map/ppermute | solution.py:335
  250.2 2.9 shard_map.106
  253.1 3.3 collective-permute-start.14
  256.4 11.7 %all-to-all-done.1 = bf16[16,2048,128]{2,1,0:T(8,128)(2,1)} async-done(((bf16[16,2048,128]{2,1,0:T(8,128)(2,1)}), bf16[16,2048,128]{2,1,0:T(8,128)(2,1)}, u32[]{:S(2)}, u32[]{:S(2)}) %all-to-all-start.1) | async-done | bytes 8388640 | tf_op jit(solution)/shard_map/all_to_all | solution.py:427
  271.7 34.1 %shard_map.107 = (f32[1920,256]{1,0:T(8,128)}, f32[1920,256]{1,0:T(8,128)}, f32[4,8,512]{2,1,0:T(8,128)}) custom-call(s32[128]{0:T(128)} %copy-done.39, s32[4]{0:T(128)} %copy-done.38, s32[128]{0:T(128)} %reshape.462.offsets, s32[128]{0:T(128)} %and_select_fusion.sizes, bf16[1920,512]{1,0:T(8,128)(2,1)} %fusion.3.q_ref, bf16[1920,512]{1,0:T(8,128)(2,1)} %fusion.2.b_ref, ...), custom_call_target="tpu_custom_call" | custom-call | flops 8053063680 | bytes 41943040 | tf_op jit(solution)/shard_map/pallas_call | solution.py:203
  306.2 5.4 %collective-permute-done.3.theirs_ref = f32[4,8,512]{2,1,0:T(8,128)S(1)} collective-permute-done((f32[4,8,512]{2,1,0:T(8,128)}, f32[4,8,512]{2,1,0:T(8,128)S(1)}, u32[]{:S(2)}, u32[]{:S(2)}) %collective-permute-start.3) | collective-permute-done | bytes 65568 | tf_op jit(solution)/shard_map/ppermute | solution.py:335
  312.3 2.8 shard_map.108
  322.6 3.0 shard_map.111
  325.6 12.1 %collective-permute-done.4 = bf16[960,256]{1,0:T(8,128)(2,1)} collective-permute-done((bf16[960,256]{1,0:T(8,128)(2,1)}, bf16[960,256]{1,0:T(8,128)(2,1)}, u32[]{:S(2)}, u32[]{:S(2)}) %collective-permute-start.4) | collective-permute-done | bytes 491552 | tf_op jit(solution)/shard_map/ppermute | solution.py:335
  348.7 4.8 %collective-permute-done.24.refs_2_ = bf16[240,256]{1,0:T(8,128)(2,1)S(1)} collective-permute-done((bf16[240,256]{1,0:T(8,128)(2,1)S(1)}, bf16[240,256]{1,0:T(8,128)(2,1)S(1)}, u32[]{:S(2)}, u32[]{:S(2)}) %collective-permute-start.24) | collective-permute-done | bytes 122912 | tf_op jit(solution)/shard_map/ppermute | solution.py:352
  355.6 6.7 %collective-permute-done.25.refs_3_ = bf16[240,256]{1,0:T(8,128)(2,1)} collective-permute-done((bf16[240,256]{1,0:T(8,128)(2,1)}, bf16[240,256]{1,0:T(8,128)(2,1)}, u32[]{:S(2)}, u32[]{:S(2)}) %collective-permute-start.25) | collective-permute-done | bytes 122912 | tf_op jit(solution)/shard_map/ppermute | solution.py:352
  374.8 16.5 %collective-permute-done.13.refs_7_ = bf16[4,2,128,512]{3,2,1,0:T(8,128)(2,1)} collective-permute-done((bf16[4,2,128,512]{3,2,1,0:T(8,128)(2,1)S(1)}, bf16[4,2,128,512]{3,2,1,0:T(8,128)(2,1)}, u32[]{:S(2)}, u32[]{:S(2)}) %collective-permute-start.13) | collective-permute-done | bytes 1048608 | tf_op jit(solution)/shard_map/ppermute | solution.py:525
  391.3 3.3 shard_map.112.refs_8_
  394.7 3.6 shard_map.113
  399.2 3.5 shard_map.109.refs_8_
  402.7 3.5 shard_map.110
  418.0 2.9 collective-permute-done.29
  422.6 4.7 %collective-permute-done.31 = bf16[240,512]{1,0:T(8,128)(2,1)S(1)} collective-permute-done((bf16[240,512]{1,0:T(8,128)(2,1)}, bf16[240,512]{1,0:T(8,128)(2,1)S(1)}, u32[]{:S(2)}, u32[]{:S(2)}) %collective-permute-start.31) | collective-permute-done | bytes 245792 | tf_op jit(solution)/shard_map/ppermute | solution.py:352
  (246 shorter events, 84.2 us)
Async XLA Ops:
  13.9 128.1 %all-to-all-start = ((bf16[16,2048,128]{2,1,0:T(8,128)(2,1)}), bf16[16,2048,128]{2,1,0:T(8,128)(2,1)}, u32[]{:S(2)}, u32[]{:S(2)}) async-start(bf16[16,2048,128]{2,1,0:T(8,128)(2,1)} %bitcast.110), calls=%async_computation | async-start | bytes 16777216 | tf_op jit(solution)/shard_map/all_to_all | solution.py:427
  21.8 103.2 %collective-permute-start = (bf16[2048,128]{0,1:T(8,128)(2,1)S(1)}, bf16[2048,128]{0,1:T(8,128)(2,1)S(1)}, u32[]{:S(2)}, u32[]{:S(2)}) collective-permute-start(bf16[2048,128]{0,1:T(8,128)(2,1)S(1)} %copy.34), channel_id=1, source_target_pairs={{0,4},{4,0},{1,5},{5,1},{2,6},{6,2},{3,7},{7,3},{8,12},{12,8},{9,1... | collective-permute-start | bytes 1572872 | tf_op jit(solution)/shard_map/ppermute | solution.py:335
  23.8 112.2 %collective-permute-start.1 = (bf16[128,2048]{0,1:T(8,128)(2,1)S(1)}, bf16[128,2048]{0,1:T(8,128)(2,1)S(1)}, u32[]{:S(2)}, u32[]{:S(2)}) collective-permute-start(bf16[128,2048]{0,1:T(8,128)(2,1)S(1)} %copy.33), channel_id=1, source_target_pairs={{0,4},{4,0},{1,5},{5,1},{2,6},{6,2},{3,7},{7,3},{8,12},{12,8},{9,1... | collective-permute-start | bytes 1572872 | tf_op jit(solution)/shard_map/ppermute | solution.py:335
  142.0 126.2 %all-to-all-start.1 = ((bf16[16,2048,128]{2,1,0:T(8,128)(2,1)}), bf16[16,2048,128]{2,1,0:T(8,128)(2,1)}, u32[]{:S(2)}, u32[]{:S(2)}) async-start(bf16[16,2048,128]{2,1,0:T(8,128)(2,1)} %bitcast.109), calls=%async_computation.1 | async-start | bytes 16777216 | tf_op jit(solution)/shard_map/all_to_all | solution.py:427
  214.5 32.2 %collective-permute-start.2 = (f32[4,8,512]{2,1,0:T(8,128)}, f32[4,8,512]{2,1,0:T(8,128)S(1)}, u32[]{:S(2)}, u32[]{:S(2)}) collective-permute-start(f32[4,8,512]{2,1,0:T(8,128)} %get-tuple-element.31.mine_ref), channel_id=1, source_target_pairs={{0,4},{4,0},{1,5},{5,1},{2,6},{6,2},{3,7},{7,3},{8,12},{12,8},{9,1... | collective-permute-start | bytes 196616 | tf_op jit(solution)/shard_map/ppermute | solution.py:335
  253.1 62.0 %collective-permute-start.14 = (bf16[960,256]{1,0:T(8,128)(2,1)S(1)}, bf16[960,256]{1,0:T(8,128)(2,1)}, u32[]{:S(2)}, u32[]{:S(2)}) collective-permute-start(bf16[960,256]{1,0:T(8,128)(2,1)S(1)} %copy-done.27), channel_id=1, source_target_pairs={{0,4},{4,0},{1,5},{5,1},{2,6},{6,2},{3,7},{7,3},{8,12},{12,8},{9,1... | collective-permute-start | bytes 1474568 | tf_op jit(solution)/shard_map/ppermute | solution.py:335
  256.4 62.6 %collective-permute-start.22 = (bf16[960,256]{1,0:T(8,128)(2,1)}, bf16[960,256]{1,0:T(8,128)(2,1)S(1)}, u32[]{:S(2)}, u32[]{:S(2)}) collective-permute-start(bf16[960,256]{1,0:T(8,128)(2,1)} %shard_map.106), channel_id=1, source_target_pairs={{0,4},{4,0},{1,5},{5,1},{2,6},{6,2},{3,7},{7,3},{8,12},{12,8},{9,1... | collective-permute-start | bytes 1474568 | tf_op jit(solution)/shard_map/ppermute | solution.py:335
  268.1 37.7 %collective-permute-start.10 = (bf16[2,128,512]{2,1,0:T(8,128)(2,1)S(1)}, bf16[2,128,512]{2,1,0:T(8,128)(2,1)S(1)}, u32[]{:S(2)}, u32[]{:S(2)}) collective-permute-start(bf16[2,128,512]{2,1,0:T(8,128)(2,1)S(1)} %fusion.53), channel_id=1, source_target_pairs={{0,3},{1,2},{2,1},{3,0},{4,7},{5,6},{6,5},{7,4},{8,11},{9,10},{10,... | collective-permute-start | bytes 786440 | tf_op jit(solution)/shard_map/ppermute | solution.py:352
  268.7 37.3 %collective-permute-start.9 = (bf16[2,128,512]{2,1,0:T(8,128)(2,1)S(1)}, bf16[2,128,512]{2,1,0:T(8,128)(2,1)S(1)}, u32[]{:S(2)}, u32[]{:S(2)}) collective-permute-start(bf16[2,128,512]{2,1,0:T(8,128)(2,1)S(1)} %fusion.53), channel_id=1, source_target_pairs={{0,2},{1,3},{2,0},{3,1},{4,6},{5,7},{6,4},{7,5},{8,10},{9,11},{10,... | collective-permute-start | bytes 786440 | tf_op jit(solution)/shard_map/ppermute | solution.py:352
  271.1 34.8 %collective-permute-start.8 = (bf16[2,128,512]{2,1,0:T(8,128)(2,1)S(1)}, bf16[2,128,512]{2,1,0:T(8,128)(2,1)S(1)}, u32[]{:S(2)}, u32[]{:S(2)}) collective-permute-start(bf16[2,128,512]{2,1,0:T(8,128)(2,1)S(1)} %fusion.53), channel_id=1, source_target_pairs={{0,1},{1,0},{2,3},{3,2},{4,5},{5,4},{6,7},{7,6},{8,9},{9,8},{10,11... | collective-permute-start | bytes 786440 | tf_op jit(solution)/shard_map/ppermute | solution.py:352
  306.1 40.1 %collective-permute-start.11 = (bf16[4,2,128,512]{3,2,1,0:T(8,128)(2,1)S(1)}, bf16[4,2,128,512]{3,2,1,0:T(8,128)(2,1)S(1)}, u32[]{:S(2)}, u32[]{:S(2)}) collective-permute-start(bf16[4,2,128,512]{3,2,1,0:T(8,128)(2,1)S(1)} %pad_maximum_fusion.1.refs_4_), channel_id=1, source_target_pairs={{0,8},{8,0},{16,24},{24,16},{1,9},{9,1},{17,25},{25,17},{2,10},{10... | collective-permute-start | bytes 3145736 | tf_op jit(solution)/shard_map/ppermute | solution.py:525
  315.1 22.6 %collective-permute-start.4 = (bf16[960,256]{1,0:T(8,128)(2,1)}, bf16[960,256]{1,0:T(8,128)(2,1)}, u32[]{:S(2)}, u32[]{:S(2)}) collective-permute-start(bf16[960,256]{1,0:T(8,128)(2,1)} %shard_map.108), channel_id=1, source_target_pairs={{0,4},{4,0},{1,5},{5,1},{2,6},{6,2},{3,7},{7,3},{8,12},{12,8},{9,1... | collective-permute-start | bytes 1474568 | tf_op jit(solution)/shard_map/ppermute | solution.py:335
  317.1 22.7 %collective-permute-start.15 = (bf16[240,256]{1,0:T(8,128)(2,1)}, bf16[240,256]{1,0:T(8,128)(2,1)S(1)}, u32[]{:S(2)}, u32[]{:S(2)}) collective-permute-start(bf16[240,256]{1,0:T(8,128)(2,1)} %get-tuple-element.87), channel_id=1, source_target_pairs={{0,1},{1,0},{2,3},{3,2},{4,5},{5,4},{6,7},{7,6},{8,9},{9,8},{10,11... | collective-permute-start | bytes 368648 | tf_op jit(solution)/shard_map/ppermute | solution.py:352
  318.5 23.4 %collective-permute-start.16 = (bf16[240,256]{1,0:T(8,128)(2,1)S(1)}, bf16[240,256]{1,0:T(8,128)(2,1)S(1)}, u32[]{:S(2)}, u32[]{:S(2)}) collective-permute-start(bf16[240,256]{1,0:T(8,128)(2,1)S(1)} %get-tuple-element.86), channel_id=1, source_target_pairs={{0,2},{1,3},{2,0},{3,1},{4,6},{5,7},{6,4},{7,5},{8,10},{9,11},{10,... | collective-permute-start | bytes 368648 | tf_op jit(solution)/shard_map/ppermute | solution.py:352
  319.7 23.6 %collective-permute-start.17 = (bf16[240,256]{1,0:T(8,128)(2,1)S(1)}, bf16[240,256]{1,0:T(8,128)(2,1)S(1)}, u32[]{:S(2)}, u32[]{:S(2)}) collective-permute-start(bf16[240,256]{1,0:T(8,128)(2,1)S(1)} %get-tuple-element.85), channel_id=1, source_target_pairs={{0,3},{1,2},{2,1},{3,0},{4,7},{5,6},{6,5},{7,4},{8,11},{9,10},{10,... | collective-permute-start | bytes 368648 | tf_op jit(solution)/shard_map/ppermute | solution.py:352
  339.1 30.0 %collective-permute-start.21 = (bf16[960,256]{1,0:T(8,128)(2,1)}, bf16[960,256]{1,0:T(8,128)(2,1)}, u32[]{:S(2)}, u32[]{:S(2)}) collective-permute-start(bf16[960,256]{1,0:T(8,128)(2,1)} %shard_map.111), channel_id=1, source_target_pairs={{0,4},{4,0},{1,5},{5,1},{2,6},{6,2},{3,7},{7,3},{8,12},{12,8},{9,1... | collective-permute-start | bytes 1474568 | tf_op jit(solution)/shard_map/ppermute | solution.py:335
  342.5 11.0 %collective-permute-start.24 = (bf16[240,256]{1,0:T(8,128)(2,1)S(1)}, bf16[240,256]{1,0:T(8,128)(2,1)S(1)}, u32[]{:S(2)}, u32[]{:S(2)}) collective-permute-start(bf16[240,256]{1,0:T(8,128)(2,1)S(1)} %get-tuple-element.82), channel_id=1, source_target_pairs={{0,2},{1,3},{2,0},{3,1},{4,6},{5,7},{6,4},{7,5},{8,10},{9,11},{10,... | collective-permute-start | bytes 368648 | tf_op jit(solution)/shard_map/ppermute | solution.py:352
  344.0 30.8 %collective-permute-start.12 = (bf16[4,2,128,512]{3,2,1,0:T(8,128)(2,1)S(1)}, bf16[4,2,128,512]{3,2,1,0:T(8,128)(2,1)S(1)}, u32[]{:S(2)}, u32[]{:S(2)}) collective-permute-start(bf16[4,2,128,512]{3,2,1,0:T(8,128)(2,1)S(1)} %pad_maximum_fusion.1.refs_4_), channel_id=1, source_target_pairs={{0,16},{8,24},{16,0},{24,8},{1,17},{9,25},{17,1},{25,9},{2,18},{10... | collective-permute-start | bytes 3145736 | tf_op jit(solution)/shard_map/ppermute | solution.py:525
  346.2 45.1 %collective-permute-start.13 = (bf16[4,2,128,512]{3,2,1,0:T(8,128)(2,1)S(1)}, bf16[4,2,128,512]{3,2,1,0:T(8,128)(2,1)}, u32[]{:S(2)}, u32[]{:S(2)}) collective-permute-start(bf16[4,2,128,512]{3,2,1,0:T(8,128)(2,1)S(1)} %collective-permute-done.11.refs_5_), channel_id=1, source_target_pairs={{0,16},{8,24},{16,0},{24,8},{1,17},{9,25},{17,1},{25,9},{2,18},{10... | collective-permute-start | bytes 3145736 | tf_op jit(solution)/shard_map/ppermute | solution.py:525
  347.6 14.7 %collective-permute-start.25 = (bf16[240,256]{1,0:T(8,128)(2,1)}, bf16[240,256]{1,0:T(8,128)(2,1)}, u32[]{:S(2)}, u32[]{:S(2)}) collective-permute-start(bf16[240,256]{1,0:T(8,128)(2,1)} %get-tuple-element.81), channel_id=1, source_target_pairs={{0,3},{1,2},{2,1},{3,0},{4,7},{5,6},{6,5},{7,4},{8,11},{9,10},{10,... | collective-permute-start | bytes 368648 | tf_op jit(solution)/shard_map/ppermute | solution.py:352
  354.2 8.1 %collective-permute-start.5 = (bf16[240,256]{1,0:T(8,128)(2,1)}, bf16[240,256]{1,0:T(8,128)(2,1)}, u32[]{:S(2)}, u32[]{:S(2)}) collective-permute-start(bf16[240,256]{1,0:T(8,128)(2,1)} %get-tuple-element.91), channel_id=1, source_target_pairs={{0,1},{1,0},{2,3},{3,2},{4,5},{5,4},{6,7},{7,6},{8,9},{9,8},{10,11... | collective-permute-start | bytes 368648 | tf_op jit(solution)/shard_map/ppermute | solution.py:352
  362.3 6.8 %collective-permute-start.7 = (bf16[240,256]{1,0:T(8,128)(2,1)}, bf16[240,256]{1,0:T(8,128)(2,1)S(1)}, u32[]{:S(2)}, u32[]{:S(2)}) collective-permute-start(bf16[240,256]{1,0:T(8,128)(2,1)} %get-tuple-element.89), channel_id=1, source_target_pairs={{0,3},{1,2},{2,1},{3,0},{4,7},{5,6},{6,5},{7,4},{8,11},{9,10},{10,... | collective-permute-start | bytes 368648 | tf_op jit(solution)/shard_map/ppermute | solution.py:352
  370.4 24.2 %collective-permute-start.26 = (bf16[240,256]{1,0:T(8,128)(2,1)S(1)}, bf16[240,256]{1,0:T(8,128)(2,1)S(1)}, u32[]{:S(2)}, u32[]{:S(2)}) collective-permute-start(bf16[240,256]{1,0:T(8,128)(2,1)S(1)} %get-tuple-element.79), channel_id=1, source_target_pairs={{0,1},{1,0},{2,3},{3,2},{4,5},{5,4},{6,7},{7,6},{8,9},{9,8},{10,11... | collective-permute-start | bytes 368648 | tf_op jit(solution)/shard_map/ppermute | solution.py:352
  371.8 22.8 %collective-permute-start.27 = (bf16[240,256]{1,0:T(8,128)(2,1)S(1)}, bf16[240,256]{1,0:T(8,128)(2,1)S(1)}, u32[]{:S(2)}, u32[]{:S(2)}) collective-permute-start(bf16[240,256]{1,0:T(8,128)(2,1)S(1)} %get-tuple-element.78), channel_id=1, source_target_pairs={{0,2},{1,3},{2,0},{3,1},{4,6},{5,7},{6,4},{7,5},{8,10},{9,11},{10,... | collective-permute-start | bytes 368648 | tf_op jit(solution)/shard_map/ppermute | solution.py:352
  372.4 22.2 %collective-permute-start.28 = (bf16[240,256]{1,0:T(8,128)(2,1)S(1)}, bf16[240,256]{1,0:T(8,128)(2,1)S(1)}, u32[]{:S(2)}, u32[]{:S(2)}) collective-permute-start(bf16[240,256]{1,0:T(8,128)(2,1)S(1)} %get-tuple-element.77), channel_id=1, source_target_pairs={{0,3},{1,2},{2,1},{3,0},{4,7},{5,6},{6,5},{7,4},{8,11},{9,10},{10,... | collective-permute-start | bytes 368648 | tf_op jit(solution)/shard_map/ppermute | solution.py:352
  406.3 9.2 %collective-permute-start.30 = (bf16[240,512]{1,0:T(8,128)(2,1)}, bf16[240,512]{1,0:T(8,128)(2,1)S(1)}, u32[]{:S(2)}, u32[]{:S(2)}) collective-permute-start(bf16[240,512]{1,0:T(8,128)(2,1)} %get-tuple-element.72), channel_id=1, source_target_pairs={{0,2},{1,3},{2,0},{3,1},{4,6},{5,7},{6,4},{7,5},{8,10},{9,11},{10,... | collective-permute-start | bytes 737288 | tf_op jit(solution)/shard_map/ppermute | solution.py:352
  407.4 13.5 %collective-permute-start.29 = (bf16[240,512]{1,0:T(8,128)(2,1)}, bf16[240,512]{1,0:T(8,128)(2,1)S(1)}, u32[]{:S(2)}, u32[]{:S(2)}) collective-permute-start(bf16[240,512]{1,0:T(8,128)(2,1)} %get-tuple-element.73), channel_id=1, source_target_pairs={{0,3},{1,2},{2,1},{3,0},{4,7},{5,6},{6,5},{7,4},{8,11},{9,10},{10,... | collective-permute-start | bytes 737288 | tf_op jit(solution)/shard_map/ppermute | solution.py:352
  408.5 18.8 %collective-permute-start.31 = (bf16[240,512]{1,0:T(8,128)(2,1)}, bf16[240,512]{1,0:T(8,128)(2,1)S(1)}, u32[]{:S(2)}, u32[]{:S(2)}) collective-permute-start(bf16[240,512]{1,0:T(8,128)(2,1)} %get-tuple-element.71), channel_id=1, source_target_pairs={{0,1},{1,0},{2,3},{3,2},{4,5},{5,4},{6,7},{7,6},{8,9},{9,8},{10,11... | collective-permute-start | bytes 737288 | tf_op jit(solution)/shard_map/ppermute | solution.py:352
  409.9 20.5 %collective-permute-start.20 = (bf16[240,512]{1,0:T(8,128)(2,1)S(1)}, bf16[240,512]{1,0:T(8,128)(2,1)S(1)}, u32[]{:S(2)}, u32[]{:S(2)}) collective-permute-start(bf16[240,512]{1,0:T(8,128)(2,1)S(1)} %get-tuple-element.74), channel_id=1, source_target_pairs={{0,1},{1,0},{2,3},{3,2},{4,5},{5,4},{6,7},{7,6},{8,9},{9,8},{10,11... | collective-permute-start | bytes 737288 | tf_op jit(solution)/shard_map/ppermute | solution.py:352
  410.5 19.8 %collective-permute-start.18 = (bf16[240,512]{1,0:T(8,128)(2,1)S(1)}, bf16[240,512]{1,0:T(8,128)(2,1)S(1)}, u32[]{:S(2)}, u32[]{:S(2)}) collective-permute-start(bf16[240,512]{1,0:T(8,128)(2,1)S(1)} %get-tuple-element.76), channel_id=1, source_target_pairs={{0,3},{1,2},{2,1},{3,0},{4,7},{5,6},{6,5},{7,4},{8,11},{9,10},{10,... | collective-permute-start | bytes 737288 | tf_op jit(solution)/shard_map/ppermute | solution.py:352
  415.5 14.9 %collective-permute-start.19 = (bf16[240,512]{1,0:T(8,128)(2,1)S(1)}, bf16[240,512]{1,0:T(8,128)(2,1)S(1)}, u32[]{:S(2)}, u32[]{:S(2)}) collective-permute-start(bf16[240,512]{1,0:T(8,128)(2,1)S(1)} %get-tuple-element.75), channel_id=1, source_target_pairs={{0,2},{1,3},{2,0},{3,1},{4,6},{5,7},{6,4},{7,5},{8,10},{9,11},{10,... | collective-permute-start | bytes 737288 | tf_op jit(solution)/shard_map/ppermute | solution.py:352
  420.9 9.8 %collective-permute-start.32 = (bf16[1024,128]{0,1:T(8,128)(2,1)S(1)}, bf16[1024,128]{0,1:T(8,128)(2,1)S(1)}, u32[]{:S(2)}, u32[]{:S(2)}) collective-permute-start(bf16[1024,128]{0,1:T(8,128)(2,1)S(1)} %fusion.18), channel_id=1, source_target_pairs={{0,16},{8,24},{16,0},{24,8},{1,17},{9,25},{17,1},{25,9},{2,18},{10... | collective-permute-start | bytes 786440 | tf_op jit(solution)/shard_map/ppermute | solution.py:377
  (52 other events, 347.1 us)
